TPU v7x, 256 devices: a whole 4x4x8 slice. The times are simulated.
256 devices in a mesh: lat: 8 (over z), lon: 32 (over x, y, core).
Axes of the slice: x: 4, y: 4, z: 8, core: 2. Of those that a mesh axis runs over, the one named last changes fastest.
Arguments:
- surface_forcing: float32 [4320, 2048], P('lon', 'lat'), may hold values from -40 to 40
- ocean_mask: int32 [4320, 2048], P('lon', 'lat'), may hold values 0 or 1
- self_coupling: float32 [4320, 2048], P('lon', 'lat'), may hold values from 0.2 to 2
- east_coupling: float32 [4320, 2048], P('lon', 'lat'), may hold values from 0.3 to 3
- north_coupling: float32 [4320, 2048], P('lon', 'lat'), may hold values from 0.3 to 3
- zonal_weight: float32 [2048], P('lat'), may hold values from 0.5 to 50
- aligned_inverse: float32 [16, 128, 128], P('lat'), may hold values from -1 to 4, as said below
- staggered_inverse: float32 [16, 128, 128], P('lat'), may hold values from -1 to 4, as said below
Outputs:
- solution: float32 [4320, 2048], P('lon', 'lat')
- residual: float32 [4320, 2048], P('lon', 'lat')
- direction: float32 [4320, 2048], P('lon', 'lat')
Inputs may be any that keep to these rules, and one draw needn't show every extreme that they name: `aligned_inverse`: each block is symmetric and positive definite. `staggered_inverse`: each block is symmetric and positive definite.
All inputs are finite; a program needn't handle non-finite values. No bound on the sum of `ocean_mask` on one device may be relied on, other than what follows from the above.
Results may differ from a plain program's by a relative error of at most 0.00023.
Values sent between devices are 32-bit elements; how exact they have to be, the bound alone decides.
No kernel may reach another device: no remote copies, remote signals or barrier semaphores. Data moves between devices by JAX's collectives and lax.ppermute only.
A program may use at most 64 MiB of HBM per device.

v0:
```python
import jax
import jax.numpy as jnp
import numpy as np
from jax import lax
from jax.experimental import pallas as pl
from jax.experimental.pallas import tpu as pltpu
from jax.sharding import Mesh
from jax.sharding import PartitionSpec as P

LON = ("lon_0", "lon_1", "lon_2")
LAT_LON = ("lat", "lon_0", "lon_1", "lon_2")
HIGHEST = lax.Precision.HIGHEST
TURN = 2.0 * np.pi
ROWS = 8
WIDE = 256
HALO = 136
FOLD = 68
SCALARS = 208


def tables(groups, length):
    period = groups * length
    index = np.arange(length)
    inner = TURN * (np.outer(index, index) % length) / length
    wave_of = np.zeros(groups, np.int64)
    wave_of[1] = groups // 2
    for m in range(1, groups // 2):
        wave_of[2 * m] = wave_of[2 * m + 1] = m
    turn = TURN * (np.outer(wave_of, index) % period) / period
    matrices = np.zeros((2, WIDE, WIDE))
    matrices[0, :length, :length] = np.cos(inner)
    matrices[1, :length, :length] = np.sin(inner)
    twiddle = np.zeros((2, groups, WIDE))
    twiddle[0, :, :length] = np.cos(turn)
    twiddle[1, :, :length] = np.sin(turn)
    chunk = np.arange(groups)
    outer = np.zeros((2, groups, groups))
    for c in range(groups):
        phase = TURN * (chunk * wave_of[c] % groups) / groups
        if c < 2:
            outer[0, :, c] = outer[1, :, c] = np.cos(phase)
        elif c % 2 == 0:
            outer[0, :, c], outer[1, :, c] = 2 * np.cos(phase), -2 * np.sin(phase)
        else:
            outer[0, :, c], outer[1, :, c] = -2 * np.sin(phase), -2 * np.cos(phase)
    modes = wave_of[:, None] + groups * index[None, :]
    wave = np.zeros((groups, WIDE))
    wave[:, :length] = 4.0 * np.sin(np.pi * modes / period) ** 2
    return (
        matrices.astype(np.float32),
        (matrices / period).astype(np.float32),
        twiddle.astype(np.float32),
        outer.astype(np.float32),
        wave.astype(np.float32),
    )


def real_fft(values):
    count = len(values)
    if count == 2:
        return [(values[0] + values[1], None), (values[0] - values[1], None)]
    even, odd = real_fft(values[0::2]), real_fft(values[1::2])
    out = [None] * (count // 2 + 1)
    for k in range(count // 4 + 1):
        (er, ei), (re, im) = even[k], odd[k]
        if k == 0:
            out[0], out[count // 2] = (er + re, None), (er - re, None)
        elif k == count // 4:
            out[k] = (er, -re)
        else:
            c, s = float(np.cos(TURN * k / count)), float(-np.sin(TURN * k / count))
            tr, ti = re * c - im * s, im * c + re * s
            out[k], out[count // 2 - k] = (er + tr, ei + ti), (er - tr, ti - ei)
    return out


def real_ifft(spectrum):
    count = 2 * (len(spectrum) - 1)
    if count == 2:
        return [spectrum[0][0] + spectrum[1][0], spectrum[0][0] - spectrum[1][0]]
    even, odd = [], []
    for k in range(count // 4 + 1):
        (ar, ai), (br, bi) = spectrum[k], spectrum[count // 2 - k]
        if k == 0:
            even.append((ar + br, None))
            odd.append((ar - br, None))
        elif k == count // 4:
            even.append((2.0 * ar, None))
            odd.append((-2.0 * ai, None))
        else:
            c, s = float(np.cos(TURN * k / count)), float(np.sin(TURN * k / count))
            dr, di = ar - br, ai + bi
            even.append((ar + br, ai - bi))
            odd.append((dr * c - di * s, dr * s + di * c))
    first, second = real_ifft(even), real_ifft(odd)
    out = []
    for a, b in zip(first, second, strict=True):
        out += [a, b]
    return out


def dot(a, b):
    return jnp.dot(a, b, precision=HIGHEST, preferred_element_type=jnp.float32)


def rows_of(p):
    return slice(ROWS * p, ROWS * (p + 1))


def lanes(shape):
    return lax.broadcasted_iota(jnp.int32, shape, len(shape) - 1)


def transform(chunks, matrix_ref, twiddle_ref, left, right):
    groups = len(chunks)
    mixed = real_fft(chunks)
    for m in range(groups // 2 + 1):
        re, im = mixed[m]
        if m == 0:
            left[rows_of(0), :] = re
            right[rows_of(0), :] = re
            continue
        c = 1 if m == groups // 2 else 2 * m
        cos, sin = twiddle_ref[0, c : c + 1, :], twiddle_ref[1, c : c + 1, :]
        if m == groups // 2:
            left[rows_of(1), :] = re * (cos + sin)
            right[rows_of(1), :] = re * (cos - sin)
        else:
            tr, ti = re * cos + im * sin, im * cos - re * sin
            left[rows_of(c), :] = tr
            right[rows_of(c), :] = ti
            left[rows_of(c + 1), :] = ti
            right[rows_of(c + 1), :] = -tr
    return dot(left[...], matrix_ref[0]) + dot(right[...], matrix_ref[1])


def transform_back(spectrum, groups, scaled_ref, twiddle_ref):
    pc, ps = dot(spectrum, scaled_ref[0]), dot(spectrum, scaled_ref[1])
    mixed = []
    for m in range(groups // 2 + 1):
        if m == 0:
            mixed.append((pc[rows_of(0)] + ps[rows_of(0)], None))
            continue
        c = 1 if m == groups // 2 else 2 * m
        cos, sin = twiddle_ref[0, c : c + 1, :], twiddle_ref[1, c : c + 1, :]
        if m == groups // 2:
            mixed.append((pc[rows_of(1)] * (cos + sin) + ps[rows_of(1)] * (cos - sin), None))
        else:
            hr = pc[rows_of(c)] - ps[rows_of(c + 1)]
            hi = ps[rows_of(c)] + pc[rows_of(c + 1)]
            mixed.append((hr * cos - hi * sin, hi * cos + hr * sin))
    return real_ifft(mixed)


def row_back(spectrum, scaled_ref, twiddle_ref, outer_ref):
    pc, ps = dot(spectrum, scaled_ref[0]), dot(spectrum, scaled_ref[1])
    cos, sin = twiddle_ref[0], twiddle_ref[1]
    return dot(outer_ref[0], pc * cos - ps * sin) + dot(outer_ref[1], ps * cos + pc * sin)


def forward_kernel(groups, field_ref, matrix_ref, twiddle_ref, out_ref, left, right):
    chunks = [field_ref[rows_of(p), :WIDE] for p in range(groups)]
    out_ref[...] = transform(chunks, matrix_ref, twiddle_ref, left, right)


def blocks_kernel(spec_ref, scale_ref, aligned_ref, scaled_ref, part_ref, down_ref, up_ref):
    count, block = aligned_ref.shape[0], aligned_ref.shape[1]
    half, rows = block // 2, count * block
    scaled = spec_ref[...] * scale_ref[...]
    scaled_ref[...] = scaled
    for b in range(count):
        part_ref[b * block : (b + 1) * block, :] = dot(
            aligned_ref[b], scaled[b * block : (b + 1) * block]
        )
    down_ref[:half, :] = scaled[:half]
    down_ref[half : half + 8, :] = part_ref[:8, :]
    down_ref[half + 8 :, :] = scale_ref[:8, :]
    up_ref[:half, :] = scaled[rows - half :]
    up_ref[half : half + 8, :] = part_ref[rows - 8 :, :]
    up_ref[half + 8 :, :] = scale_ref[rows - 8 :, :]


def combine(scaled_ref, part_ref, scale_ref, above_ref, below_ref, stag_ref, stag_below_ref):
    count, block = stag_ref.shape[0], stag_ref.shape[1]
    half, rows = block // 2, count * block
    before = dot(
        stag_below_ref[...],
        jnp.concatenate([below_ref[:half, :], scaled_ref[:half, :]], axis=0),
    )
    pieces = [before[half:]]
    for b in range(count - 1):
        pieces.append(dot(stag_ref[b], scaled_ref[half + b * block : half + (b + 1) * block, :]))
    after = dot(
        stag_ref[count - 1],
        jnp.concatenate([scaled_ref[rows - half :, :], above_ref[:half, :]], axis=0),
    )
    pieces.append(after[:half])
    full = (part_ref[...] + jnp.concatenate(pieces, axis=0)) * scale_ref[...]
    return full, before, after


def halo_kernel(
    scaled_ref, part_ref, scale_ref, above_ref, below_ref, stag_ref, stag_below_ref, out_ref, low, high
):
    half = stag_ref.shape[1] // 2
    full, before, after = combine(
        scaled_ref, part_ref, scale_ref, above_ref, below_ref, stag_ref, stag_below_ref
    )
    row_below = (before[half - 1 : half] + below_ref[half + 7 : half + 8, :]) * below_ref[
        half + 15 : half + 16, :
    ]
    row_above = (after[half : half + 1] + above_ref[half : half + 1, :]) * above_ref[
        half + 8 : half + 9, :
    ]
    out_ref[:, :128] = full[:, :128]
    low[...] = full[:, :128]
    high[...] = full[:, 128:]
    groups = full.shape[0] // ROWS

    def strided(start):
        at = pl.ds(start, groups, stride=ROWS)
        return jnp.concatenate([low[at, :], high[at, :]], axis=1)

    row = lax.broadcasted_iota(jnp.int32, (groups, WIDE), 0)
    up = jnp.where(row == 0, row_below, pltpu.roll(strided(ROWS - 1), 1, 0))
    down = jnp.where(row == groups - 1, row_above, pltpu.roll(strided(0), groups - 1, 0))
    lane = lanes((groups, 128)) + 128
    for s, part in enumerate(
        (
            pltpu.roll(up, HALO, 1),
            pltpu.roll(up, HALO - FOLD, 1),
            pltpu.roll(down, HALO, 1),
            pltpu.roll(down, HALO - FOLD, 1),
        )
    ):
        at = pl.ds(s, groups, stride=ROWS)
        high[at, :] = jnp.where(lane >= HALO, part[:, 128:], high[at, :])
    out_ref[:, 128:] = high[...]


def sums_kernel(
    weight,
    length,
    scaled_ref,
    part_ref,
    scale_ref,
    above_ref,
    below_ref,
    stag_ref,
    stag_below_ref,
    image_ref,
    rhs_ref,
    weight_ref,
    sums_ref,
    out_ref,
):
    full, _, _ = combine(
        scaled_ref, part_ref, scale_ref, above_ref, below_ref, stag_ref, stag_below_ref
    )
    lane = lanes(full.shape)
    held = lane < length
    norm = weight_ref[0, 0]
    own = jnp.sum(jnp.where(held, full * image_ref[...], 0.0)) * norm
    cross = jnp.sum(jnp.where(held, full * rhs_ref[...], 0.0)) * norm
    out = jnp.where(lane == SCALARS, sums_ref[0, 0], full)
    out = jnp.where(lane == SCALARS + 1, sums_ref[0, 1], out)
    out = jnp.where(lane == SCALARS + 2, own, out)
    out_ref[...] = jnp.where(lane == SCALARS + 3, cross, out)


def step_kernel(
    groups,
    length,
    spec_ref,
    rhs_ref,
    diagonal_ref,
    wet_ref,
    east_ref,
    west_ref,
    north_ref,
    south_ref,
    matrix_ref,
    inverse_ref,
    twiddle_ref,
    outer_ref,
    out_ref,
    first_ref,
    image_ref,
    sums_ref,
    left,
    right,
    low,
    high,
    tail,
):
    lane_row = lanes((groups, WIDE))
    stride = 3 * ROWS
    tail[...] = spec_ref[:, 128:]

    def halo_row(s):
        blank = jnp.zeros((groups, 128), jnp.float32)
        parts = [
            jnp.concatenate([tail[pl.ds(s + n, groups, stride=ROWS), :], blank], axis=1)
            for n in range(2)
        ]
        row = jnp.where(
            lane_row < FOLD,
            pltpu.roll(parts[0], WIDE - (HALO - 128), 1),
            pltpu.roll(parts[1], FOLD - (HALO - 128), 1),
        )
        return row_back(row, inverse_ref, twiddle_ref, outer_ref)

    for start, s in ((ROWS - 1, 0), (2 * ROWS, 2)):
        row = halo_row(s)
        low[pl.ds(start, groups, stride=stride), :] = row[:, :128]
        high[pl.ds(start, groups, stride=stride), :] = row[:, 128:]

    def neighbour(start):
        at = slice(start, start + ROWS)
        return jnp.concatenate([low[at, :], high[at, :]], axis=1)

    cells = transform_back(spec_ref[...], groups, inverse_ref, twiddle_ref)
    for p in range(groups):
        v = cells[p] * wet_ref[rows_of(p), :]
        first_ref[rows_of(p), :] = v
        low[stride * p + ROWS : stride * p + 2 * ROWS, :] = v[:, :128]
        high[stride * p + ROWS : stride * p + 2 * ROWS, :] = v[:, 128:]
    lane = lanes((ROWS, WIDE))
    rz = jnp.zeros((ROWS, WIDE), jnp.float32)
    curvature = jnp.zeros((ROWS, WIDE), jnp.float32)
    images = []
    for p in range(groups):
        at = rows_of(p)
        v = first_ref[at, :]
        after = first_ref[rows_of((p + 1) % groups), 0:1]
        before = first_ref[rows_of((p - 1) % groups), length - 1 : length]
        ring = jnp.where(lane == length, after, jnp.where(lane == WIDE - 1, before, v))
        base = stride * p + ROWS
        image = diagonal_ref[at, :] * v
        image = image + east_ref[at, :] * (v - pltpu.roll(ring, WIDE - 1, 1))
        image = image + west_ref[at, :] * (v - pltpu.roll(ring, 1, 1))
        image = image + north_ref[at, :] * (v - neighbour(base + 1))
        image = image + south_ref[at, :] * (v - neighbour(base - 1))
        image_ref[at, :] = image
        images.append(image)
        rz = rz + rhs_ref[at, :WIDE] * v
        curvature = curvature + v * image
    small = lanes((8, 128))
    sums_ref[...] = jnp.where(
        small == 0, jnp.sum(rz), jnp.where(small == 1, jnp.sum(curvature), 0.0)
    )
    out_ref[...] = transform(images, matrix_ref, twiddle_ref, left, right)


def last_kernel(
    groups,
    length,
    spec_ref,
    wet_ref,
    first_ref,
    image_ref,
    inverse_ref,
    twiddle_ref,
    out_ref,
    sums_ref,
):
    riders = jnp.sum(spec_ref[:, 128:], axis=0, keepdims=True) * (1.0 / ROWS)
    sums_ref[...] = jnp.broadcast_to(riders, (8, 128))
    cells = transform_back(spec_ref[...], groups, inverse_ref, twiddle_ref)
    blank = jnp.zeros((ROWS, WIDE), jnp.float32)
    for p in range(groups):
        at = rows_of(p)
        parts = [first_ref[at, :], image_ref[at, :], cells[p] * wet_ref[at, :]]
        packed = jnp.concatenate([parts[0], blank], axis=1)
        for n in (1, 2):
            shifted = pltpu.roll(jnp.concatenate([parts[n], blank], axis=1), n * length, 1)
            packed = packed + shifted
        out_ref[at, :] = packed


def call(kernel, out_shapes, scratch=(), name=None):
    single = not isinstance(out_shapes, (list, tuple)) or isinstance(out_shapes[0], int)
    shapes = [out_shapes] if single else out_shapes
    outs = [jax.ShapeDtypeStruct(s, jnp.float32) for s in shapes]
    return pl.pallas_call(
        kernel,
        out_shape=outs[0] if single else outs,
        scratch_shapes=[pltpu.VMEM(s, jnp.float32) for s in scratch],
        compiler_params=pltpu.CompilerParams(vmem_limit_bytes=48 * 2**20),
        name=name,
    )


def exchanged(value):
    groups = lax.axis_size(LON)
    parts = value.reshape(groups, ROWS, value.shape[1])
    return lax.all_to_all(parts, LON, split_axis=0, concat_axis=0, tiled=True).reshape(value.shape)


def from_lat(value, steps, ring):
    count = lax.axis_size("lat")
    pairs = [(d + steps, d) for d in range(count)]
    if ring:
        pairs = [(s % count, d) for s, d in pairs]
    return lax.ppermute(value, "lat", [(s, d) for s, d in pairs if 0 <= s < count])


def from_slab(value, steps):
    count = lax.axis_size("lat") * lax.axis_size(LON)
    pairs = [(d + steps, d) for d in range(count)]
    return lax.ppermute(value, LAT_LON, [(s, d) for s, d in pairs if 0 <= s < count])


def widened(value):
    return jnp.pad(value, [(0, 0)] * (value.ndim - 1) + [(0, WIDE - value.shape[-1])])


def local(
    surface_forcing,
    ocean_mask,
    self_coupling,
    east_coupling,
    north_coupling,
    zonal_weight,
    aligned_inverse,
    staggered_inverse,
):
    groups = lax.axis_size(LON)
    length, rows = surface_forcing.shape
    matrices, inverse, twiddle, outer, wave = tables(groups, length)
    channel = lax.axis_index(LON)
    count, block = aligned_inverse.shape[0], aligned_inverse.shape[1]
    half = block // 2

    wet_cells = ocean_mask.astype(jnp.float32)
    rhs_cells = wet_cells * surface_forcing
    fields = [
        rhs_cells,
        wet_cells * self_coupling,
        wet_cells * east_coupling,
        wet_cells * north_coupling,
    ]
    stacked = jnp.concatenate(fields, axis=0)
    stacked = jnp.pad(stacked, ((0, -stacked.shape[0] % 128), (0, 0)))
    slab = exchanged(stacked.T)

    def field(n):
        return slab[:, n * length : (n + 1) * length].reshape(groups, ROWS, length)

    own, east, north = field(1), field(2), field(3)
    ocean = own > 0.0
    wet = ocean.astype(jnp.float32)
    wet_next = jnp.concatenate([wet[:, :, 1:], jnp.roll(wet[:, :, :1], -1, axis=0)], axis=2)
    east = east * wet_next
    west = jnp.concatenate([jnp.roll(east[:, :, -1:], 1, axis=0), east[:, :, :-1]], axis=2)
    wet_above = from_slab(wet[:, 0, :], 1)
    north_below = from_slab(north[:, -1, :], -1)
    south = jnp.concatenate([north_below[:, None, :], north[:, :-1, :]], axis=1) * wet
    north = north * jnp.concatenate([wet[:, 1:, :], wet_above[:, None, :]], axis=1)
    diagonal = jnp.where(ocean, own, 1.0)
    flat = [widened(v).reshape(rows, WIDE) for v in (diagonal, wet, east, west, north, south)]
    wet_slab = flat[1]

    scale = lax.rsqrt(1.0 + zonal_weight[:, None] * lax.dynamic_slice_in_dim(wave, channel, 1, 0))
    stag_below = from_lat(staggered_inverse[count - 1], -1, False)
    weight = jnp.where(channel < 2, 1.0, 2.0).astype(jnp.float32) / (groups * length)

    wide = (rows, WIDE)
    edge = (half + 16, WIDE)
    transforms = [wide, wide]

    def blocks(spectrum):
        scaled, part, down, up = call(blocks_kernel, [wide, wide, edge, edge], name="blocks")(
            spectrum, scale, aligned_inverse
        )
        above, below = from_lat(down, 1, False), from_lat(up, -1, False)
        return scaled, part, scale, above, below, staggered_inverse, stag_below

    spec_rhs = exchanged(
        call(lambda *r: forward_kernel(groups, *r), wide, transforms, name="forward")(
            slab, matrices, twiddle
        )
    )
    filtered = exchanged(call(halo_kernel, wide, [(rows, 128)] * 2, name="halo")(*blocks(spec_rhs)))
    spec, first, image, sums = call(
        lambda *r: step_kernel(groups, length, *r),
        [wide, wide, wide, (8, 128)],
        transforms + [(3 * rows, 128)] * 2 + [(rows, 128)],
        name="step",
    )(filtered, slab, *flat, matrices, inverse, twiddle, outer)
    spec_image = exchanged(spec)
    smem = pl.BlockSpec(memory_space=pltpu.SMEM)
    vmem = pl.BlockSpec(memory_space=pltpu.VMEM)
    filtered = pl.pallas_call(
        lambda *r: sums_kernel(None, length, *r),
        out_shape=jax.ShapeDtypeStruct(wide, jnp.float32),
        in_specs=[vmem] * 9 + [smem, smem],
        out_specs=vmem,
        compiler_params=pltpu.CompilerParams(vmem_limit_bytes=48 * 2**20),
        name="sums",
    )(*blocks(spec_image), spec_image, spec_rhs, weight.reshape(1, 1), sums)
    packed, lon_sums = call(
        lambda *r: last_kernel(groups, length, *r), [(rows, 2 * WIDE), (8, 128)], name="last"
    )(exchanged(filtered), wet_slab, first, image, inverse, twiddle)

    behind = from_lat(lon_sums, -1, True)
    pair = lon_sums + behind
    three = pair + from_lat(lon_sums, 1, True)
    totals = three + from_lat(three, 3, True) + from_lat(pair, -2, True)
    at = SCALARS - 128
    rz, curvature, own_sum, cross = [totals[0, at + n] for n in range(4)]
    alpha = rz / curvature
    rz_next = rz - alpha * curvature - alpha * cross + alpha * alpha * own_sum

    back = exchanged(packed).T
    first, image, image_back = [back[n * length : (n + 1) * length] for n in range(3)]
    solution = alpha * first
    residual = rhs_cells - alpha * image
    direction = (first - alpha * image_back) + rz_next / rz * first
    return (solution, residual, direction)


def solution(mesh):
    torus = Mesh(
        mesh.devices.reshape(mesh.shape["lat"], 4, 4, 2), ("lat", "lon_0", "lon_1", "lon_2")
    )
    return jax.shard_map(
        local,
        mesh=torus,
        in_specs=(
            P(LON, "lat"),
            P(LON, "lat"),
            P(LON, "lat"),
            P(LON, "lat"),
            P(LON, "lat"),
            P("lat"),
            P("lat", None, None),
            P("lat", None, None),
        ),
        out_specs=(P(LON, "lat"), P(LON, "lat"), P(LON, "lat")),
        check_vma=False,
    )
```

profile of v0, /device:TPU:1, one launch (start us, length us, event | category | flops | bytes accessed | tf_op | source)
XLA Modules:
  0.0 138.6 jit_solution(4210889407184082093)
XLA Ops:
  0.6 1.2 convert_multiply_fusion.3
  1.9 0.6 copy-done.21
  2.6 1.1 copy.97
  3.7 8.7 %all-to-all-start = ((f32[32,8,640]{2,1,0:T(8,128)}), f32[32,8,640]{2,1,0:T(8,128)S(1)}, u32[]{:S(2)}, u32[]{:S(2)}) async-start(f32[32,8,640]{2,1,0:T(8,128)} %bitcast.1), calls=%async_computation | async-start | bytes 1310720 | tf_op jit(solution)/shard_map/all_to_all | solution.py:397
  12.4 0.6 slice_bitcast_fusion.3
  13.1 3.5 %collective-permute-start.2 = (f32[128,128]{1,0:T(8,128)}, f32[128,128]{1,0:T(8,128)S(1)}, u32[]{:S(2)}, u32[]{:S(2)}) collective-permute-start(f32[128,128]{1,0:T(8,128)} %slice_bitcast_fusion.3), channel_id=1, source_target_pairs={{0,32},{32,64},{64,96},{96,128},{128,160},{160,192},{192,224},{1,3... | collective-permute-start | bytes 196616 | tf_op jit(solution)/shard_map/ppermute | solution.py:405
  16.6 0.7 constant_dynamic-slice_fusion
  17.3 0.7 copy-done.31
  18.1 7.2 %all-to-all-done = f32[32,8,640]{2,1,0:T(8,128)S(1)} async-done(((f32[32,8,640]{2,1,0:T(8,128)}), f32[32,8,640]{2,1,0:T(8,128)S(1)}, u32[]{:S(2)}, u32[]{:S(2)}) %all-to-all-start) | async-done | bytes 655392 | tf_op jit(solution)/shard_map/all_to_all | solution.py:397
  27.0 1.9 %collective-permute-start.3 = (f32[32,135]{1,0:T(8,128)S(1)}, f32[32,135]{1,0:T(8,128)S(1)}, u32[]{:S(2)}, u32[]{:S(2)}) collective-permute-start(f32[32,135]{1,0:T(8,128)S(1)} %slice_bitcast_fusion.5), channel_id=1, source_target_pairs={{1,0},{2,1},{3,2},{4,3},{5,4},{6,5},{7,6},{8,7},{9,8},{10,9},{11,1... | collective-permute-start | bytes 51848 | tf_op jit(solution)/shard_map/ppermute | solution.py:411
  29.3 0.9 copy.112
  30.3 1.4 %forward.1 = f32[256,256]{1,0:T(8,128)} custom-call(f32[256,640]{1,0:T(8,128)S(1)} %bitcast.49, f32[2,256,256]{2,1,0:T(8,128)S(1)} %copy-done.1, f32[2,32,256]{2,1,0:T(8,128)S(1)} %copy-done.6), custom_call_target="tpu_custom_call" | custom-call | tf_op jit(solution)/shard_map/forward/pallas_call | solution.py:480
  31.8 5.2 %all-to-all-start.1 = ((f32[32,8,256]{2,1,0:T(8,128)}), f32[32,8,256]{2,1,0:T(8,128)S(1)}, u32[]{:S(2)}, u32[]{:S(2)}) async-start(f32[32,8,256]{2,1,0:T(8,128)} %bitcast.3), calls=%async_computation.1 | async-start | bytes 524288 | tf_op jit(solution)/shard_map/all_to_all | solution.py:397
  37.0 0.6 copy-done.30
  37.6 1.6 %fusion.6 = (f32[32,8,135]{2,0,1:T(8,128)S(1)}, f32[32,8,135]{2,0,1:T(8,128)}) fusion(f32[32,8,135]{2,1,0:T(8,128)S(1)} %get-tuple-element.45, f32[32,1,135]{2,0,1:T(8,128)} %bitcast.63, f32[32,7,135]{2,0,1:T(8,128)S(1)} %slice-done), kind=kLoop, calls=%fused_computation.38 | loop fusion | flops 69120 | bytes 552960 | tf_op jit(solution)/shard_map/reshape | solution.py:448
  39.2 3.5 %collective-permute-start.4 = (f32[32,135]{1,0:T(8,128)S(1)}, f32[32,135]{1,0:T(8,128)S(1)}, u32[]{:S(2)}, u32[]{:S(2)}) collective-permute-start(f32[32,135]{1,0:T(8,128)S(1)} %slice_bitcast_fusion.4), channel_id=1, source_target_pairs={{0,1},{1,2},{2,3},{3,4},{4,5},{5,6},{6,7},{7,8},{8,9},{9,10},{10,1... | collective-permute-start | bytes 51848 | tf_op jit(solution)/shard_map/ppermute | solution.py:411
  42.7 3.2 %all-to-all-done.1 = f32[32,8,256]{2,1,0:T(8,128)S(1)} async-done(((f32[32,8,256]{2,1,0:T(8,128)}), f32[32,8,256]{2,1,0:T(8,128)S(1)}, u32[]{:S(2)}, u32[]{:S(2)}) %all-to-all-start.1) | async-done | bytes 262176 | tf_op jit(solution)/shard_map/all_to_all | solution.py:397
  46.3 1.3 collective-permute-start
  47.7 4.5 %collective-permute-start.1 = (f32[80,256]{1,0:T(8,128)S(1)}, f32[80,256]{1,0:T(8,128)S(1)}, u32[]{:S(2)}, u32[]{:S(2)}) collective-permute-start(f32[80,256]{1,0:T(8,128)S(1)} %get-tuple-element.20), channel_id=1, source_target_pairs={{0,32},{32,64},{64,96},{96,128},{128,160},{160,192},{192,224},{1,3... | collective-permute-start | bytes 245768 | tf_op jit(solution)/shard_map/ppermute | solution.py:405
  52.2 0.7 slice.106
  53.3 0.9 copy.115
  54.1 1.3 halo.1
  55.4 4.3 %all-to-all-start.2 = ((f32[32,8,256]{2,1,0:T(8,128)}), f32[32,8,256]{2,1,0:T(8,128)S(1)}, u32[]{:S(2)}, u32[]{:S(2)}) async-start(f32[32,8,256]{2,1,0:T(8,128)} %bitcast.7), calls=%async_computation.2 | async-start | bytes 524288 | tf_op jit(solution)/shard_map/all_to_all | solution.py:397
  60.4 0.9 maximum_select_fusion
  61.7 0.9 copy-done.26
  62.6 0.8 pad_bitcast_fusion
  63.4 5.5 %all-to-all-done.2 = f32[32,8,256]{2,1,0:T(8,128)S(1)} async-done(((f32[32,8,256]{2,1,0:T(8,128)}), f32[32,8,256]{2,1,0:T(8,128)S(1)}, u32[]{:S(2)}, u32[]{:S(2)}) %all-to-all-start.2) | async-done | bytes 262176 | tf_op jit(solution)/shard_map/all_to_all | solution.py:397
  68.9 0.9 copy-done.2
  69.8 0.9 copy-done.3
  70.8 0.8 copy-done.7
  71.6 0.8 copy-done.17
  72.4 3.2 %step.1 = (f32[256,256]{1,0:T(8,128)S(1)}, f32[256,256]{1,0:T(8,128)S(1)}, f32[256,256]{1,0:T(8,128)S(1)}, f32[8,128]{1,0:T(8,128)S(1)}) custom-call(f32[256,256]{1,0:T(8,128)S(1)} %bitcast.55, f32[256,640]{1,0:T(8,128)S(1)} %bitcast.50, f32[256,256]{1,0:T(8,128)S(1)} %pad_bitcast_fusion.5.r_2_, f32[256,256]{1,0:T(8,128)S(1)} %pad_bitcast_fusion.4.r_3_.r_1_, ...), custom_call_target="tpu_custom_call" | custom-call | tf_op jit(solution)/shard_map/step/pallas_call | solution.py:485
  75.6 12.6 %all_to_all.30 = f32[32,8,256]{2,1,0:T(8,128)S(1)} all-to-all(f32[32,8,256]{2,1,0:T(8,128)S(1)} %bitcast.58), channel_id=1, replica_groups=mesh['lat'=8,'lon_0'=4,'lon_1'=4,'lon_2'=2] {'lon_0','lon_1','lon_2'}, dimensions={0} | all-to-all | bytes 524288 | tf_op jit(solution)/shard_map/all_to_all | solution.py:397
  88.6 1.3 collective-permute-start.5
  89.9 4.7 %collective-permute-start.6 = (f32[80,256]{1,0:T(8,128)S(1)}, f32[80,256]{1,0:T(8,128)S(1)}, u32[]{:S(2)}, u32[]{:S(2)}) collective-permute-start(f32[80,256]{1,0:T(8,128)S(1)} %get-tuple-element.25), channel_id=1, source_target_pairs={{0,32},{32,64},{64,96},{96,128},{128,160},{160,192},{192,224},{1,3... | collective-permute-start | bytes 245768 | tf_op jit(solution)/shard_map/ppermute | solution.py:405
  94.7 0.8 collective-permute-done.5.r_3_
  95.5 0.9 collective-permute-done.6.r_4_
  96.3 1.2 sums.1
  97.6 13.3 %all_to_all.31 = f32[32,8,256]{2,1,0:T(8,128)S(1)} all-to-all(f32[32,8,256]{2,1,0:T(8,128)S(1)} %bitcast.56), channel_id=1, replica_groups=mesh['lat'=8,'lon_0'=4,'lon_1'=4,'lon_2'=2] {'lon_0','lon_1','lon_2'}, dimensions={0} | all-to-all | bytes 524288 | tf_op jit(solution)/shard_map/all_to_all | solution.py:397
  110.9 1.6 %last.1 = (f32[256,512]{1,0:T(8,128)}, f32[8,128]{1,0:T(8,128)S(1)}) custom-call(f32[256,256]{1,0:T(8,128)S(1)} %bitcast.57, f32[256,256]{1,0:T(8,128)S(1)} %pad_bitcast_fusion.4.r_3_.r_1_, f32[256,256]{1,0:T(8,128)S(1)} %copy-done.12, f32[256,256]{1,0:T(8,128)S(1)} %copy-done.14, f32[2,256,256]{2,1,0:T(8,128)S(1)} %copy-done, f32[2,32,256]{2,1,0:T(8,128)S(1)} %copy-done.8), custom_call_target="tpu_custom_call" | custom-call | tf_op jit(solution)/shard_map/last/pallas_call | solution.py:502
  112.5 8.7 %collective-permute-start.8 = (f32[8,128]{1,0:T(8,128)S(1)}, f32[8,128]{1,0:T(8,128)S(1)}, u32[]{:S(2)}, u32[]{:S(2)}) collective-permute-start(f32[8,128]{1,0:T(8,128)S(1)} %get-tuple-element.29), channel_id=1, source_target_pairs={{32,0},{64,32},{96,64},{128,96},{160,128},{192,160},{224,192},{0,2... | collective-permute-start | bytes 12296 | tf_op jit(solution)/shard_map/ppermute | solution.py:405
  121.2 4.0 %all-to-all-start.5 = ((f32[32,8,512]{2,1,0:T(8,128)}), f32[32,8,512]{2,1,0:T(8,128)S(1)}, u32[]{:S(2)}, u32[]{:S(2)}) async-start(f32[32,8,512]{2,1,0:T(8,128)} %bitcast.29), calls=%async_computation.5 | async-start | bytes 1048576 | tf_op jit(solution)/shard_map/all_to_all | solution.py:397
  125.3 5.0 %collective-permute-start.9 = (f32[8,128]{1,0:T(8,128)S(1)}, f32[8,128]{1,0:T(8,128)S(1)}, u32[]{:S(2)}, u32[]{:S(2)}) collective-permute-start(f32[8,128]{1,0:T(8,128)S(1)} %get-tuple-element.43), channel_id=1, source_target_pairs={{96,0},{128,32},{160,64},{192,96},{224,128},{0,160},{32,192},{64,2... | collective-permute-start | bytes 12296 | tf_op jit(solution)/shard_map/ppermute | solution.py:405
  130.3 0.8 collective-permute-done.9
  131.1 0.7 fusion.7
  136.3 0.6 all-to-all-done.5
  137.1 0.7 copy-done.22
  137.8 0.8 fusion.2
  (92 shorter events, 4.7 us)
Async XLA Ops:
  1.9 0.7 copy-start.21
  3.7 8.7 %copy-start.4 = (f32[2,128,128]{2,1,0:T(8,128)S(1)}, f32[2,128,128]{2,1,0:T(8,128)}, u32[]{:S(2)}) copy-start(f32[2,128,128]{2,1,0:T(8,128)} %r_5_.2) | copy-start | bytes 393220
  3.7 21.7 %all-to-all-start = ((f32[32,8,640]{2,1,0:T(8,128)}), f32[32,8,640]{2,1,0:T(8,128)S(1)}, u32[]{:S(2)}, u32[]{:S(2)}) async-start(f32[32,8,640]{2,1,0:T(8,128)} %bitcast.1), calls=%async_computation | async-start | bytes 1310720 | tf_op jit(solution)/shard_map/all_to_all | solution.py:397
  13.1 41.1 %collective-permute-start.2 = (f32[128,128]{1,0:T(8,128)}, f32[128,128]{1,0:T(8,128)S(1)}, u32[]{:S(2)}, u32[]{:S(2)}) collective-permute-start(f32[128,128]{1,0:T(8,128)} %slice_bitcast_fusion.3), channel_id=1, source_target_pairs={{0,32},{32,64},{64,96},{96,128},{128,160},{160,192},{192,224},{1,3... | collective-permute-start | bytes 196616 | tf_op jit(solution)/shard_map/ppermute | solution.py:405
  17.3 0.7 copy-start.31
  25.6 0.7 copy-start.19
  26.3 2.9 %copy-start.18 = (f32[32,8,135]{2,0,1:T(8,128)}, f32[32,8,135]{2,0,1:T(8,128)S(1)}, u32[]{:S(2)}) copy-start(f32[32,8,135]{2,0,1:T(8,128)S(1)} %fusion.4) | copy-start | bytes 414724
  27.0 10.0 %collective-permute-start.3 = (f32[32,135]{1,0:T(8,128)S(1)}, f32[32,135]{1,0:T(8,128)S(1)}, u32[]{:S(2)}, u32[]{:S(2)}) collective-permute-start(f32[32,135]{1,0:T(8,128)S(1)} %slice_bitcast_fusion.5), channel_id=1, source_target_pairs={{1,0},{2,1},{3,2},{4,3},{5,4},{6,5},{7,6},{8,7},{9,8},{10,9},{11,1... | collective-permute-start | bytes 51848 | tf_op jit(solution)/shard_map/ppermute | solution.py:411
  29.3 1.0 copy-start.1
  29.3 1.0 copy-start.6
  31.8 5.8 %slice-start = ((f32[32,8,135]{2,0,1:T(8,128)}), f32[32,7,135]{2,0,1:T(8,128)S(1)}, s32[]{:S(2)}) async-start(f32[32,8,135]{2,0,1:T(8,128)} %copy-done.18), calls=%async_computation.6 | async-start | bytes 458752 | tf_op jit(solution)/shard_map/slice | solution.py:459
  31.8 14.2 %all-to-all-start.1 = ((f32[32,8,256]{2,1,0:T(8,128)}), f32[32,8,256]{2,1,0:T(8,128)S(1)}, u32[]{:S(2)}, u32[]{:S(2)}) async-start(f32[32,8,256]{2,1,0:T(8,128)} %bitcast.3), calls=%async_computation.1 | async-start | bytes 524288 | tf_op jit(solution)/shard_map/all_to_all | solution.py:397
  37.0 0.6 copy-start.30
  37.6 8.4 %copy-start.9 = (f32[2,128,128]{2,1,0:T(8,128)S(1)}, f32[2,128,128]{2,1,0:T(8,128)}, u32[]{:S(2)}) copy-start(f32[2,128,128]{2,1,0:T(8,128)} %aligned_ref.3) | copy-start | bytes 393220
  39.2 6.7 %copy-start.24 = (f32[32,8,135]{2,0,1:T(8,128)}, f32[32,8,135]{2,0,1:T(8,128)S(1)}, u32[]{:S(2)}) copy-start(f32[32,8,135]{2,0,1:T(8,128)S(1)} %get-tuple-element.53) | copy-start | bytes 414724
  39.2 20.6 %collective-permute-start.4 = (f32[32,135]{1,0:T(8,128)S(1)}, f32[32,135]{1,0:T(8,128)S(1)}, u32[]{:S(2)}, u32[]{:S(2)}) collective-permute-start(f32[32,135]{1,0:T(8,128)S(1)} %slice_bitcast_fusion.4), channel_id=1, source_target_pairs={{0,1},{1,2},{2,3},{3,4},{4,5},{5,6},{6,7},{7,8},{8,9},{9,10},{10,1... | collective-permute-start | bytes 51848 | tf_op jit(solution)/shard_map/ppermute | solution.py:411
  45.9 6.2 %copy-start.23 = (f32[32,8,135]{2,1,0:T(8,128)S(1)}, f32[32,8,135]{2,1,0:T(8,128)}, u32[]{:S(2)}) copy-start(f32[32,8,135]{2,1,0:T(8,128)} %copy.112) | copy-start | bytes 414724
  46.3 7.8 %collective-permute-start = (f32[80,256]{1,0:T(8,128)S(1)}, f32[80,256]{1,0:T(8,128)S(1)}, u32[]{:S(2)}, u32[]{:S(2)}) collective-permute-start(f32[80,256]{1,0:T(8,128)S(1)} %get-tuple-element.19), channel_id=1, source_target_pairs={{32,0},{64,32},{96,64},{128,96},{160,128},{192,160},{224,192},{33,... | collective-permute-start | bytes 245768 | tf_op jit(solution)/shard_map/ppermute | solution.py:405
  47.6 4.6 %copy-start.25 = (f32[32,8,135]{2,0,1:T(8,128)S(1)}, f32[32,8,135]{2,0,1:T(8,128)}, u32[]{:S(2)}) copy-start(f32[32,8,135]{2,0,1:T(8,128)} %copy-done.24) | copy-start | bytes 414724
  47.7 6.5 %collective-permute-start.1 = (f32[80,256]{1,0:T(8,128)S(1)}, f32[80,256]{1,0:T(8,128)S(1)}, u32[]{:S(2)}, u32[]{:S(2)}) collective-permute-start(f32[80,256]{1,0:T(8,128)S(1)} %get-tuple-element.20), channel_id=1, source_target_pairs={{0,32},{32,64},{64,96},{96,128},{128,160},{160,192},{192,224},{1,3... | collective-permute-start | bytes 245768 | tf_op jit(solution)/shard_map/ppermute | solution.py:405
  52.2 1.0 copy-start.27
  54.1 1.3 copy-start.15
  55.4 5.0 %copy-start.20 = (f32[32,8,135]{2,1,0:T(8,128)S(1)}, f32[32,8,135]{2,1,0:T(8,128)}, u32[]{:S(2)}) copy-start(f32[32,8,135]{2,1,0:T(8,128)} %copy-done.19) | copy-start | bytes 414724
  55.4 5.0 %copy-start.28 = (f32[32,7,135]{2,0,1:T(8,128)S(1)}, f32[32,7,135]{2,0,1:T(8,128)}, u32[]{:S(2)}) copy-start(f32[32,7,135]{2,0,1:T(8,128)} %slice.106) | copy-start | bytes 362884
  55.4 13.4 %all-to-all-start.2 = ((f32[32,8,256]{2,1,0:T(8,128)}), f32[32,8,256]{2,1,0:T(8,128)S(1)}, u32[]{:S(2)}, u32[]{:S(2)}) async-start(f32[32,8,256]{2,1,0:T(8,128)} %bitcast.7), calls=%async_computation.2 | async-start | bytes 524288 | tf_op jit(solution)/shard_map/all_to_all | solution.py:397
  59.8 0.6 copy-start.29
  61.6 1.0 copy-start.26
  62.6 6.3 %copy-start = (f32[2,256,256]{2,1,0:T(8,128)S(1)}, f32[2,256,256]{2,1,0:T(8,128)}, u32[]{:S(2)}) copy-start(f32[2,256,256]{2,1,0:T(8,128)} %constant.44.clone.r_9_.r_4_) | copy-start | bytes 1572868
  68.9 1.0 copy-start.2
  69.8 0.9 copy-start.3
  70.8 0.8 copy-start.7
  71.6 0.8 copy-start.17
  75.6 12.6 %copy-start.11 = (f32[256,256]{1,0:T(8,128)}, f32[256,256]{1,0:T(8,128)S(1)}, u32[]{:S(2)}) copy-start(f32[256,256]{1,0:T(8,128)S(1)} %get-tuple-element.27.r_2_) | copy-start | bytes 786436
  75.6 12.6 %copy-start.13 = (f32[256,256]{1,0:T(8,128)}, f32[256,256]{1,0:T(8,128)S(1)}, u32[]{:S(2)}) copy-start(f32[256,256]{1,0:T(8,128)S(1)} %get-tuple-element.28.r_3_) | copy-start | bytes 786436
  75.6 12.6 %copy-start.10 = (f32[2,128,128]{2,1,0:T(8,128)S(1)}, f32[2,128,128]{2,1,0:T(8,128)}, u32[]{:S(2)}) copy-start(f32[2,128,128]{2,1,0:T(8,128)} %aligned_ref.3) | copy-start | bytes 393220
  88.2 8.1 %copy-start.5 = (f32[2,128,128]{2,1,0:T(8,128)S(1)}, f32[2,128,128]{2,1,0:T(8,128)}, u32[]{:S(2)}) copy-start(f32[2,128,128]{2,1,0:T(8,128)} %r_5_.2) | copy-start | bytes 393220
  88.2 8.1 %copy-start.16 = (f32[128,128]{1,0:T(8,128)S(1)}, f32[128,128]{1,0:T(8,128)}, u32[]{:S(2)}) copy-start(f32[128,128]{1,0:T(8,128)} %copy-done.15) | copy-start | bytes 196612
  88.6 6.8 %collective-permute-start.5 = (f32[80,256]{1,0:T(8,128)S(1)}, f32[80,256]{1,0:T(8,128)S(1)}, u32[]{:S(2)}, u32[]{:S(2)}) collective-permute-start(f32[80,256]{1,0:T(8,128)S(1)} %get-tuple-element.24), channel_id=1, source_target_pairs={{32,0},{64,32},{96,64},{128,96},{160,128},{192,160},{224,192},{33,... | collective-permute-start | bytes 245768 | tf_op jit(solution)/shard_map/ppermute | solution.py:405
  89.9 6.4 %collective-permute-start.6 = (f32[80,256]{1,0:T(8,128)S(1)}, f32[80,256]{1,0:T(8,128)S(1)}, u32[]{:S(2)}, u32[]{:S(2)}) collective-permute-start(f32[80,256]{1,0:T(8,128)S(1)} %get-tuple-element.25), channel_id=1, source_target_pairs={{0,32},{32,64},{64,96},{96,128},{128,160},{160,192},{192,224},{1,3... | collective-permute-start | bytes 245768 | tf_op jit(solution)/shard_map/ppermute | solution.py:405
  96.3 14.5 %copy-start.14 = (f32[256,256]{1,0:T(8,128)S(1)}, f32[256,256]{1,0:T(8,128)}, u32[]{:S(2)}) copy-start(f32[256,256]{1,0:T(8,128)} %copy-done.13) | copy-start | bytes 786436
  97.6 13.3 %copy-start.8 = (f32[2,32,256]{2,1,0:T(8,128)S(1)}, f32[2,32,256]{2,1,0:T(8,128)}, u32[]{:S(2)}) copy-start(f32[2,32,256]{2,1,0:T(8,128)} %constant.43.clone.r_2_.r_10_.r_5_) | copy-start | bytes 196612
  97.6 13.3 %copy-start.12 = (f32[256,256]{1,0:T(8,128)S(1)}, f32[256,256]{1,0:T(8,128)}, u32[]{:S(2)}) copy-start(f32[256,256]{1,0:T(8,128)} %copy-done.11) | copy-start | bytes 786436
  112.5 12.7 %collective-permute-start.8 = (f32[8,128]{1,0:T(8,128)S(1)}, f32[8,128]{1,0:T(8,128)S(1)}, u32[]{:S(2)}, u32[]{:S(2)}) collective-permute-start(f32[8,128]{1,0:T(8,128)S(1)} %get-tuple-element.29), channel_id=1, source_target_pairs={{32,0},{64,32},{96,64},{128,96},{160,128},{192,160},{224,192},{0,2... | collective-permute-start | bytes 12296 | tf_op jit(solution)/shard_map/ppermute | solution.py:405
  121.2 4.0 %collective-permute-start.7 = (f32[8,128]{1,0:T(8,128)S(1)}, f32[8,128]{1,0:T(8,128)S(1)}, u32[]{:S(2)}, u32[]{:S(2)}) collective-permute-start(f32[8,128]{1,0:T(8,128)S(1)} %get-tuple-element.29), channel_id=1, source_target_pairs={{224,0},{0,32},{32,64},{64,96},{96,128},{128,160},{160,192},{192,2... | collective-permute-start | bytes 12296 | tf_op jit(solution)/shard_map/ppermute | solution.py:405
  121.2 15.8 %all-to-all-start.5 = ((f32[32,8,512]{2,1,0:T(8,128)}), f32[32,8,512]{2,1,0:T(8,128)S(1)}, u32[]{:S(2)}, u32[]{:S(2)}) async-start(f32[32,8,512]{2,1,0:T(8,128)} %bitcast.29), calls=%async_computation.5 | async-start | bytes 1048576 | tf_op jit(solution)/shard_map/all_to_all | solution.py:397
  125.2 5.1 %collective-permute-start.10 = (f32[8,128]{1,0:T(8,128)S(1)}, f32[8,128]{1,0:T(8,128)S(1)}, u32[]{:S(2)}, u32[]{:S(2)}) collective-permute-start(f32[8,128]{1,0:T(8,128)S(1)} %get-tuple-element.44), channel_id=1, source_target_pairs={{192,0},{224,32},{0,64},{32,96},{64,128},{96,160},{128,192},{160,2... | collective-permute-start | bytes 12296 | tf_op jit(solution)/shard_map/ppermute | solution.py:405
  125.3 5.8 %collective-permute-start.9 = (f32[8,128]{1,0:T(8,128)S(1)}, f32[8,128]{1,0:T(8,128)S(1)}, u32[]{:S(2)}, u32[]{:S(2)}) collective-permute-start(f32[8,128]{1,0:T(8,128)S(1)} %get-tuple-element.43), channel_id=1, source_target_pairs={{96,0},{128,32},{160,64},{192,96},{224,128},{0,160},{32,192},{64,2... | collective-permute-start | bytes 12296 | tf_op jit(solution)/shard_map/ppermute | solution.py:405
  136.9 0.9 copy-start.22
where the time goes:
time: 140 us; the launch traced here: 139 us
  starting transfers between devices  56.9 us (41%)
  blocking collectives  25.9 us (18%)
  waiting for transfers between devices  18.9 us (13%)
  local copies, waits for them, and re-layouts  16.7 us (12%)
  Pallas kernels  9.55 us (7%)
  between operations  5.69 us (4%)
  other arithmetic  5.05 us (4%)
    ppermute x9, starting transfers between devices, from_lat(): lax.ppermute(value, 'lat', [(s, d) for s, d in pairs if 0 <= s < count])  29.2 us
    all_to_all x2, blocking collectives, exchanged(): lax.all_to_all(parts, LON, split_axis=0, concat_axis=0, tiled=True)  25.9 us
    all_to_all x4, starting transfers between devices, exchanged(): lax.all_to_all(parts, LON, split_axis=0, concat_axis=0, tiled=True)  22.3 us
    all_to_all x4, waiting for transfers between devices, exchanged(): lax.all_to_all(parts, LON, split_axis=0, concat_axis=0, tiled=True)  16.5 us
    unnamed x70, local copies, waits for them, and re-layouts  11.2 us
    ppermute x2, starting transfers between devices, from_slab(): lax.ppermute(value, LAT_LON, [(s, d) for s, d in pairs if 0 <= s < count])  5.45 us
    pallas_call x1, Pallas kernels, local(): call(lambda *r: step_kernel(groups, length, *r), [wide, wide, wide, (8, 1...  3.21 us
  transfers between devices with their start and end apart: 15, of which 7 were waited for; matrix products, arithmetic and copies ran while one was open for 7% of the time, Pallas kernels for 2%

commit v1 on v0

v1 whole, which is shorter than its diff:
```python
import jax
import jax.numpy as jnp
import numpy as np
from jax import lax
from jax.experimental import pallas as pl
from jax.experimental.pallas import tpu as pltpu
from jax.sharding import Mesh
from jax.sharding import PartitionSpec as P

LON = ("lon_0", "lon_1", "lon_2")
LAT_LON = ("lat", "lon_0", "lon_1", "lon_2")
TURN = 2.0 * np.pi
ROWS = 8
WIDE = 256
HALO = 136
FOLD = 68
LATE = HALO + FOLD
SCALARS = WIDE - 4


def tables(groups, length):
    period = groups * length
    index = np.arange(length)
    inner = TURN * (np.outer(index, index) % length) / length
    wave_of = np.zeros(groups, np.int64)
    wave_of[1] = groups // 2
    for m in range(1, groups // 2):
        wave_of[2 * m] = wave_of[2 * m + 1] = m
    turn = TURN * (np.outer(wave_of, index) % period) / period
    matrices = np.zeros((2, WIDE, WIDE), np.float32)
    matrices[0, :length, :length] = np.cos(inner)
    matrices[1, :length, :length] = np.sin(inner)
    coarse = matrices.astype(jnp.bfloat16)
    rest = (matrices - coarse.astype(np.float32)).astype(jnp.bfloat16)
    twiddle = np.zeros((2, groups, WIDE))
    twiddle[0, :, :length] = np.cos(turn)
    twiddle[1, :, :length] = np.sin(turn)
    chunk = np.arange(groups)
    outer = np.zeros((2, groups, groups))
    for c in range(groups):
        phase = TURN * (chunk * wave_of[c] % groups) / groups
        if c < 2:
            outer[0, :, c] = outer[1, :, c] = np.cos(phase)
        elif c % 2 == 0:
            outer[0, :, c], outer[1, :, c] = 2 * np.cos(phase), -2 * np.sin(phase)
        else:
            outer[0, :, c], outer[1, :, c] = -2 * np.sin(phase), -2 * np.cos(phase)
    modes = wave_of[:, None] + groups * index[None, :]
    wave = np.zeros((groups, WIDE))
    wave[:, :length] = 4.0 * np.sin(np.pi * modes / period) ** 2
    return (
        np.stack([coarse, rest]),
        twiddle.astype(np.float32),
        outer.astype(np.float32),
        wave.astype(np.float32),
    )


def real_fft(values):
    count = len(values)
    if count == 2:
        return [(values[0] + values[1], None), (values[0] - values[1], None)]
    even, odd = real_fft(values[0::2]), real_fft(values[1::2])
    out = [None] * (count // 2 + 1)
    for k in range(count // 4 + 1):
        (er, ei), (re, im) = even[k], odd[k]
        if k == 0:
            out[0], out[count // 2] = (er + re, None), (er - re, None)
        elif k == count // 4:
            out[k] = (er, -re)
        else:
            c, s = float(np.cos(TURN * k / count)), float(-np.sin(TURN * k / count))
            tr, ti = re * c - im * s, im * c + re * s
            out[k], out[count // 2 - k] = (er + tr, ei + ti), (er - tr, ti - ei)
    return out


def real_ifft(spectrum):
    count = 2 * (len(spectrum) - 1)
    if count == 2:
        return [spectrum[0][0] + spectrum[1][0], spectrum[0][0] - spectrum[1][0]]
    even, odd = [], []
    for k in range(count // 4 + 1):
        (ar, ai), (br, bi) = spectrum[k], spectrum[count // 2 - k]
        if k == 0:
            even.append((ar + br, None))
            odd.append((ar - br, None))
        elif k == count // 4:
            even.append((2.0 * ar, None))
            odd.append((-2.0 * ai, None))
        else:
            c, s = float(np.cos(TURN * k / count)), float(np.sin(TURN * k / count))
            dr, di = ar - br, ai + bi
            even.append((ar + br, ai - bi))
            odd.append((dr * c - di * s, dr * s + di * c))
    first, second = real_ifft(even), real_ifft(odd)
    out = []
    for a, b in zip(first, second, strict=True):
        out += [a, b]
    return out


def split(a):
    coarse = a.astype(jnp.bfloat16)
    return coarse, (a - coarse.astype(jnp.float32)).astype(jnp.bfloat16)


def product(a, b):
    (ac, ar), (bc, br) = a, b

    def one(x, y):
        return jnp.dot(x, y, preferred_element_type=jnp.float32)

    return one(ac, bc) + (one(ac, br) + one(ar, bc))


def dot(a, b):
    return product(split(a), split(b))


def table(matrix_ref, n):
    return matrix_ref[0, n], matrix_ref[1, n]


def rows_of(p):
    return slice(ROWS * p, ROWS * (p + 1))


def lanes(shape):
    return lax.broadcasted_iota(jnp.int32, shape, len(shape) - 1)


def sublanes(shape):
    return lax.broadcasted_iota(jnp.int32, shape, len(shape) - 2)


def shifted(value, lanes_right):
    return pltpu.roll(value, lanes_right % value.shape[1], 1)


def pack_kernel(forcing_ref, mask_ref, self_ref, out_ref, tall):
    length = forcing_ref.shape[0]
    wet = mask_ref[...].astype(jnp.float32)
    tall[:length, :] = wet * forcing_ref[...]
    tall[length:, :] = (wet * self_ref[...])[: WIDE - length]
    out_ref[...] = tall[...].T


def pack_rest_kernel(mask_ref, self_ref, east_ref, north_ref, out_ref, late_ref, tall, short):
    length, rows = mask_ref.shape
    cut = WIDE - length
    n_at = 2 * length - cut
    e_at = n_at + length
    count = WIDE + 128 - e_at
    wet = mask_ref[...].astype(jnp.float32)
    east = wet * east_ref[...]
    tall[:length, :] = jnp.zeros((length, rows), jnp.float32)
    tall[length:n_at, :] = (wet * self_ref[...])[cut:]
    tall[n_at:e_at, :] = wet * north_ref[...]
    tall[e_at:, :] = east[:count]
    out_ref[...] = tall[...].T
    short[...] = jnp.zeros((128, rows), jnp.float32)
    short[LATE - 128 : LATE - 128 + length - count, :] = east[count:]
    late_ref[...] = short[...].T


def coefficients_kernel(
    groups,
    length,
    slab_ref,
    second_ref,
    diagonal_ref,
    wet_ref,
    next_ref,
    east_ref,
    north_ref,
    south_ref,
    low_row_ref,
    top_row_ref,
):
    cut = WIDE - length
    n_at = 2 * length - cut
    e_at = n_at + length
    count = WIDE + 128 - e_at
    lane, row = lanes((ROWS, WIDE)), sublanes((ROWS, WIDE))
    held = lane < length

    def one(p):
        at = rows_of(p)
        late = second_ref[at, :]
        own = jnp.where(
            lane < cut,
            shifted(slab_ref[at, :], -length),
            jnp.where(held, shifted(late, cut - length)[:, :WIDE], 0.0),
        )
        return late, own, (own > 0.0).astype(jnp.float32)

    for p in range(groups):
        wet_ref[rows_of(p), :] = one(p)[2]
    for p in range(groups):
        at = rows_of(p)
        late, own, wet = one(p)
        after = wet_ref[rows_of((p + 1) % groups), 0:1]
        north = jnp.where(held, shifted(late, -n_at)[:, :WIDE], 0.0)
        diagonal_ref[at, :] = jnp.where(wet > 0.0, own, 1.0)
        next_ref[at, :] = shifted(jnp.where(lane == length, after, wet), -1)
        east_ref[at, :] = jnp.where(lane < count, shifted(late, -e_at)[:, :WIDE], 0.0)
        north_ref[at, :] = north * jnp.where(row == ROWS - 1, 1.0, pltpu.roll(wet, ROWS - 1, 0))
        south_ref[at, :] = wet * jnp.where(row == 0, 1.0, pltpu.roll(north, 1, 0))
        low_row_ref[p : p + 1, :] = wet[:1]
        top_row_ref[p : p + 1, :] = north[ROWS - 1 :]


def transform(chunks, matrix_ref, twiddle_ref, left, right):
    groups = len(chunks)
    mixed = real_fft(chunks)
    for m in range(groups // 2 + 1):
        re, im = mixed[m]
        if m == 0:
            left[rows_of(0), :] = re
            right[rows_of(0), :] = re
            continue
        c = 1 if m == groups // 2 else 2 * m
        cos, sin = twiddle_ref[0, c : c + 1, :], twiddle_ref[1, c : c + 1, :]
        if m == groups // 2:
            left[rows_of(1), :] = re * (cos + sin)
            right[rows_of(1), :] = re * (cos - sin)
        else:
            tr, ti = re * cos + im * sin, im * cos - re * sin
            left[rows_of(c), :] = tr
            right[rows_of(c), :] = ti
            left[rows_of(c + 1), :] = ti
            right[rows_of(c + 1), :] = -tr
    return product(split(left[...]), table(matrix_ref, 0)) + product(
        split(right[...]), table(matrix_ref, 1)
    )


def transform_back(spectrum, groups, matrix_ref, twiddle_ref):
    parts = split(spectrum)
    pc, ps = product(parts, table(matrix_ref, 0)), product(parts, table(matrix_ref, 1))
    mixed = []
    for m in range(groups // 2 + 1):
        if m == 0:
            mixed.append((pc[rows_of(0)] + ps[rows_of(0)], None))
            continue
        c = 1 if m == groups // 2 else 2 * m
        cos, sin = twiddle_ref[0, c : c + 1, :], twiddle_ref[1, c : c + 1, :]
        if m == groups // 2:
            mixed.append((pc[rows_of(1)] * (cos + sin) + ps[rows_of(1)] * (cos - sin), None))
        else:
            hr = pc[rows_of(c)] - ps[rows_of(c + 1)]
            hi = ps[rows_of(c)] + pc[rows_of(c + 1)]
            mixed.append((hr * cos - hi * sin, hi * cos + hr * sin))
    return real_ifft(mixed)


def row_back(spectrum, matrix_ref, twiddle_ref, outer_ref):
    parts = split(spectrum)
    pc, ps = product(parts, table(matrix_ref, 0)), product(parts, table(matrix_ref, 1))
    cos, sin = twiddle_ref[0], twiddle_ref[1]
    return dot(outer_ref[0], pc * cos - ps * sin) + dot(outer_ref[1], ps * cos + pc * sin)


def forward_kernel(groups, field_ref, rest_ref, matrix_ref, twiddle_ref, out_ref, left, right):
    chunks = [field_ref[rows_of(p), :] for p in range(groups)]
    spectrum = transform(chunks, matrix_ref, twiddle_ref, left, right)
    out_ref[:, :WIDE] = spectrum + rest_ref[:, :WIDE]
    out_ref[:, WIDE:] = rest_ref[:, WIDE:]


def blocks_kernel(spec_ref, scale_ref, aligned_ref, scaled_ref, part_ref, down_ref, up_ref):
    count, block = aligned_ref.shape[0], aligned_ref.shape[1]
    half, rows = block // 2, count * block
    scaled = spec_ref[:, :WIDE] * scale_ref[...]
    scaled_ref[...] = scaled
    for b in range(count):
        part_ref[b * block : (b + 1) * block, :] = dot(
            aligned_ref[b], scaled[b * block : (b + 1) * block]
        )
    down_ref[:half, :] = scaled[:half]
    down_ref[half : half + 8, :] = part_ref[:8, :]
    down_ref[half + 8 :, :] = scale_ref[:8, :]
    up_ref[:half, :] = scaled[rows - half :]
    up_ref[half : half + 8, :] = part_ref[rows - 8 :, :]
    up_ref[half + 8 :, :] = scale_ref[rows - 8 :, :]


def combine(norm, scaled_ref, part_ref, scale_ref, above_ref, below_ref, stag_ref, stag_below_ref):
    count, block = stag_ref.shape[0], stag_ref.shape[1]
    half, rows = block // 2, count * block
    before = dot(
        stag_below_ref[...],
        jnp.concatenate([below_ref[:half, :], scaled_ref[:half, :]], axis=0),
    )
    pieces = [before[half:]]
    for b in range(count - 1):
        pieces.append(dot(stag_ref[b], scaled_ref[half + b * block : half + (b + 1) * block, :]))
    after = dot(
        stag_ref[count - 1],
        jnp.concatenate([scaled_ref[rows - half :, :], above_ref[:half, :]], axis=0),
    )
    pieces.append(after[:half])
    full = (part_ref[...] + jnp.concatenate(pieces, axis=0)) * (scale_ref[...] * norm)
    return full, before, after


def halo_kernel(
    norm,
    scaled_ref,
    part_ref,
    scale_ref,
    above_ref,
    below_ref,
    stag_ref,
    stag_below_ref,
    late_ref,
    out_ref,
    low,
    high,
):
    half = stag_ref.shape[1] // 2
    full, before, after = combine(
        norm, scaled_ref, part_ref, scale_ref, above_ref, below_ref, stag_ref, stag_below_ref
    )
    row_below = (before[half - 1 : half] + below_ref[half + 7 : half + 8, :]) * (
        below_ref[half + 15 : half + 16, :] * norm
    )
    row_above = (after[half : half + 1] + above_ref[half : half + 1, :]) * (
        above_ref[half + 8 : half + 9, :] * norm
    )
    out_ref[:, :128] = full[:, :128]
    low[...] = full[:, :128]
    high[...] = full[:, 128:]
    groups = full.shape[0] // ROWS

    def strided(start):
        at = pl.ds(start, groups, stride=ROWS)
        return jnp.concatenate([low[at, :], high[at, :]], axis=1)

    row = lax.broadcasted_iota(jnp.int32, (groups, WIDE), 0)
    up = jnp.where(row == 0, row_below, pltpu.roll(strided(ROWS - 1), 1, 0))
    down = jnp.where(row == groups - 1, row_above, pltpu.roll(strided(0), groups - 1, 0))
    lane = lanes((groups, 128)) + 128
    for s, part in enumerate(
        (
            pltpu.roll(up, HALO, 1),
            pltpu.roll(up, HALO - FOLD, 1),
            pltpu.roll(down, HALO, 1),
            pltpu.roll(down, HALO - FOLD, 1),
        )
    ):
        at = pl.ds(s, groups, stride=ROWS)
        high[at, :] = jnp.where(lane >= HALO, part[:, 128:], high[at, :])
    out_ref[:, 128:] = jnp.where(
        lanes(high.shape) < LATE - 128, high[...], late_ref[...]
    )


def sums_kernel(
    norm,
    length,
    scaled_ref,
    part_ref,
    scale_ref,
    above_ref,
    below_ref,
    stag_ref,
    stag_below_ref,
    spec_ref,
    rhs_ref,
    image_ref,
    weight_ref,
    sums_ref,
    out_ref,
):
    full, _, _ = combine(
        norm, scaled_ref, part_ref, scale_ref, above_ref, below_ref, stag_ref, stag_below_ref
    )
    lane = lanes(full.shape)
    held = jnp.where(lane < length, full, 0.0)
    weight = weight_ref[0, 0]
    own = jnp.sum(held * spec_ref[...]) * weight
    cross = jnp.sum(held * rhs_ref[:, :WIDE]) * weight
    out = jnp.where(lane < length, full, shifted(image_ref[...], length))
    for n, value in enumerate((sums_ref[0, 0], sums_ref[0, 1], own, cross)):
        out = jnp.where(lane == SCALARS + n, value, out)
    out_ref[...] = out


def step_kernel(
    groups,
    length,
    spec_ref,
    rhs_ref,
    diagonal_ref,
    wet_ref,
    next_ref,
    east_ref,
    north_ref,
    south_ref,
    wet_above_ref,
    north_below_ref,
    matrix_ref,
    twiddle_ref,
    outer_ref,
    out_ref,
    first_ref,
    image_ref,
    sums_ref,
    left,
    right,
    low,
    high,
    tail,
):
    lane_row = lanes((groups, WIDE))
    stride = 3 * ROWS
    tail[...] = spec_ref[:, 128:]

    def halo_row(s):
        blank = jnp.zeros((groups, 128), jnp.float32)
        parts = [
            jnp.concatenate([tail[pl.ds(s + n, groups, stride=ROWS), :], blank], axis=1)
            for n in range(2)
        ]
        row = jnp.where(
            lane_row < FOLD, shifted(parts[0], 128 - HALO), shifted(parts[1], FOLD + 128 - HALO)
        )
        return row_back(row, matrix_ref, twiddle_ref, outer_ref)

    for start, s in ((ROWS - 1, 0), (2 * ROWS, 2)):
        row = halo_row(s)
        low[pl.ds(start, groups, stride=stride), :] = row[:, :128]
        high[pl.ds(start, groups, stride=stride), :] = row[:, 128:]

    def neighbour(start):
        at = slice(start, start + ROWS)
        return jnp.concatenate([low[at, :], high[at, :]], axis=1)

    cells = transform_back(spec_ref[...], groups, matrix_ref, twiddle_ref)
    for p in range(groups):
        v = cells[p] * wet_ref[rows_of(p), :]
        first_ref[rows_of(p), :] = v
        low[stride * p + ROWS : stride * p + 2 * ROWS, :] = v[:, :128]
        high[stride * p + ROWS : stride * p + 2 * ROWS, :] = v[:, 128:]
    lane, row = lanes((ROWS, WIDE)), sublanes((ROWS, WIDE))
    count = WIDE + 128 - (2 * length - (WIDE - length)) - length
    rz = jnp.zeros((ROWS, WIDE), jnp.float32)
    curvature = jnp.zeros((ROWS, WIDE), jnp.float32)
    images, fluxes = [], []
    for p in range(groups):
        at = rows_of(p)
        v = first_ref[at, :]
        after = first_ref[rows_of((p + 1) % groups), 0:1]
        east = jnp.where(lane < count, east_ref[at, :], shifted(spec_ref[at, :], count - LATE))
        flux = v - shifted(jnp.where(lane == length, after, v), -1)
        fluxes.append(jnp.where(lane < length, east * next_ref[at, :] * flux, 0.0))
    for p in range(groups):
        at = rows_of(p)
        v = first_ref[at, :]
        before = fluxes[(p - 1) % groups][:, length - 1 : length]
        flux = fluxes[p]
        north, south = north_ref[at, :], south_ref[at, :]
        north = jnp.where(row == ROWS - 1, north * wet_above_ref[p : p + 1, :], north)
        south = jnp.where(row == 0, south * north_below_ref[p : p + 1, :], south)
        base = stride * p + ROWS
        image = diagonal_ref[at, :] * v
        image = image + (flux - shifted(jnp.where(lane == WIDE - 1, before, flux), 1))
        image = image + north * (v - neighbour(base + 1))
        image = image + south * (v - neighbour(base - 1))
        image = jnp.where(lane < length, image, 0.0)
        image_ref[at, :] = image
        images.append(image)
        rz = rz + rhs_ref[at, :] * v
        curvature = curvature + v * image
    small = lanes((8, 128))
    sums_ref[...] = jnp.where(
        small == 0, jnp.sum(rz), jnp.where(small == 1, jnp.sum(curvature), 0.0)
    )
    spectrum = transform(images, matrix_ref, twiddle_ref, left, right)
    out_ref[...] = jnp.where(
        lanes(out_ref.shape) < length, spectrum, shifted(first_ref[...], length)
    )


def gather_kernel(spec_ref, sums_ref):
    riders = jnp.sum(spec_ref[:, 128:], axis=0, keepdims=True) * (1.0 / ROWS)
    sums_ref[...] = jnp.broadcast_to(riders, (8, 128))


def last_kernel(
    groups, length, spec_ref, wet_ref, first_ref, image_ref, matrix_ref, twiddle_ref, out_ref
):
    cells = transform_back(spec_ref[...], groups, matrix_ref, twiddle_ref)
    lane = lanes((ROWS, WIDE))
    cut = WIDE - length
    image_cut = SCALARS - length
    image_at = 2 * length - cut
    for p in range(groups):
        at = rows_of(p)
        out = jnp.where(
            lane < length, cells[p] * wet_ref[at, :], shifted(first_ref[at, :], length - cut)
        )
        out_ref[at, :] = jnp.where(
            lane < image_at, out, shifted(image_ref[at, :], image_at - image_cut)
        )


def unpack_kernel(length, count, slab_ref, out_ref):
    turned = slab_ref[:, 128:].T
    out_ref[:count, :] = turned[length - 128 : length - 128 + count]


def finish_kernel(
    length,
    back_ref,
    first_ref,
    image_ref,
    forcing_ref,
    mask_ref,
    three_ref,
    others_ref,
    pair_ref,
    solution_ref,
    residual_ref,
    direction_ref,
):
    at = SCALARS - 128
    totals = three_ref[:1, :] + others_ref[:1, :] + pair_ref[:1, :]
    rz, curvature, own, cross = [totals[:, at + n : at + n + 1] for n in range(4)]
    alpha = rz / curvature
    rz_next = rz - alpha * curvature - alpha * cross + alpha * alpha * own
    beta = rz_next / rz
    back = back_ref[...].T
    cut = WIDE - length
    image_cut = SCALARS - length
    image_at = 2 * length - cut
    rhs = mask_ref[...].astype(jnp.float32) * forcing_ref[...]

    def store(where, rows_back, first):
        solution_ref[where, :] = alpha * first
        direction_ref[where, :] = (first - alpha * rows_back) + beta * first

    store(slice(0, cut), back[:cut], first_ref[:cut, :])
    store(slice(cut, length), back[cut:length], back[length:image_at])
    residual_ref[:image_cut, :] = rhs[:image_cut] - alpha * image_ref[:image_cut, :]
    residual_ref[image_cut:, :] = (
        rhs[image_cut:] - alpha * back[image_at : image_at + length - image_cut]
    )


def call(kernel, out_shapes, scratch=(), name=None):
    single = not isinstance(out_shapes, (list, tuple)) or isinstance(out_shapes[0], int)
    shapes = [out_shapes] if single else out_shapes
    outs = [jax.ShapeDtypeStruct(s, jnp.float32) for s in shapes]
    return pl.pallas_call(
        kernel,
        out_shape=outs[0] if single else outs,
        scratch_shapes=[pltpu.VMEM(s, jnp.float32) for s in scratch],
        compiler_params=pltpu.CompilerParams(vmem_limit_bytes=16 * 2**20),
        name=name,
    )


def exchanged(value):
    groups = lax.axis_size(LON)
    parts = value.reshape(groups, ROWS, value.shape[-1])
    return lax.all_to_all(parts, LON, split_axis=0, concat_axis=0, tiled=True).reshape(value.shape)


def from_lat(value, steps, ring):
    count = lax.axis_size("lat")
    pairs = [(d + steps, d) for d in range(count)]
    if ring:
        pairs = [(s % count, d) for s, d in pairs]
    return lax.ppermute(value, "lat", [(s, d) for s, d in pairs if 0 <= s < count])


def from_slab(value, steps):
    count = lax.axis_size("lat") * lax.axis_size(LON)
    pairs = [(d + steps, d) for d in range(count)]
    return lax.ppermute(value, LAT_LON, [(s, d) for s, d in pairs if 0 <= s < count])


def after(value, *others):
    return lax.optimization_barrier((value, *others))[0]


def local(
    surface_forcing,
    ocean_mask,
    self_coupling,
    east_coupling,
    north_coupling,
    zonal_weight,
    aligned_inverse,
    staggered_inverse,
):
    groups = lax.axis_size(LON)
    length, rows = surface_forcing.shape
    norm = 1.0 / (groups * length)
    matrices, twiddle, outer, wave = tables(groups, length)
    channel = lax.axis_index(LON)
    count, block = aligned_inverse.shape[0], aligned_inverse.shape[1]
    half = block // 2
    wide = (rows, WIDE)
    transforms = [wide, wide]

    packed = call(pack_kernel, wide, [wide], name="pack")(
        surface_forcing, ocean_mask, self_coupling
    )
    slab = exchanged(packed)
    rest, late = call(
        pack_rest_kernel,
        [(rows, WIDE + 128), (rows, 128)],
        [(WIDE + 128, rows), (128, rows)],
        name="pack_rest",
    )(after(ocean_mask, packed), self_coupling, east_coupling, north_coupling)
    scale = lax.rsqrt(1.0 + zonal_weight[:, None] * lax.dynamic_slice_in_dim(wave, channel, 1, 0))
    stag_below = from_lat(after(staggered_inverse[count - 1], packed), -1, False)
    weight = jnp.where(channel < 2, 1.0, 2.0).astype(jnp.float32)

    edge = (half + 16, WIDE)

    def blocks(spectrum):
        scaled, part, down, up = call(blocks_kernel, [wide, wide, edge, edge], name="blocks")(
            spectrum, scale, aligned_inverse
        )
        above, below = from_lat(down, 1, False), from_lat(up, -1, False)
        return scaled, part, scale, above, below, staggered_inverse, stag_below

    spec_rhs = exchanged(
        call(lambda *r: forward_kernel(groups, *r), (rows, WIDE + 128), transforms, name="forward")(
            slab, rest, matrices, twiddle
        )
    )
    pieces = blocks(spec_rhs)
    *flat, low_row, top_row = call(
        lambda *r: coefficients_kernel(groups, length, *r),
        [wide] * 6 + [(groups, WIDE)] * 2,
        name="coefficients",
    )(slab, after(spec_rhs, pieces[0]))
    wet_slab = flat[1]
    wet_above, north_below = from_slab(low_row, 1), from_slab(top_row, -1)
    filtered = exchanged(
        call(lambda *r: halo_kernel(norm, *r), wide, [(rows, 128)] * 2, name="halo")(*pieces, late)
    )
    spec, first, image, sums = call(
        lambda *r: step_kernel(groups, length, *r),
        [wide, wide, wide, (8, 128)],
        transforms + [(3 * rows, 128)] * 2 + [(rows, 128)],
        name="step",
    )(filtered, slab, *flat, wet_above, north_below, matrices, twiddle, outer)
    spec_image = exchanged(spec)
    smem = pl.BlockSpec(memory_space=pltpu.SMEM)
    vmem = pl.BlockSpec(memory_space=pltpu.VMEM)
    summed = pl.pallas_call(
        lambda *r: sums_kernel(norm, length, *r),
        out_shape=jax.ShapeDtypeStruct(wide, jnp.float32),
        in_specs=[vmem] * 10 + [smem, smem],
        out_specs=vmem,
        compiler_params=pltpu.CompilerParams(vmem_limit_bytes=16 * 2**20),
        name="sums",
    )(*blocks(spec_image), spec_image, spec_rhs, image, weight.reshape(1, 1), sums)
    cut, image_cut = WIDE - length, SCALARS - length
    first_cells = call(
        lambda *r: unpack_kernel(length, cut, *r), (length, rows), name="unpack_first"
    )(after(spec_image, summed))
    filtered = exchanged(summed)
    lon_sums = call(gather_kernel, (8, 128), name="gather")(filtered)
    behind, ahead = from_lat(lon_sums, -1, True), from_lat(lon_sums, 1, True)
    packed = call(lambda *r: last_kernel(groups, length, *r), wide, name="last")(
        filtered, wet_slab, first, image, matrices, twiddle
    )
    image_cells = call(
        lambda *r: unpack_kernel(length, image_cut, *r), (length, rows), name="unpack_image"
    )(after(filtered, packed))

    pair = lon_sums + behind
    three = pair + ahead
    others, last_pair = from_lat(three, 3, True), from_lat(pair, -2, True)
    cells = (length, rows)
    return tuple(
        call(lambda *r: finish_kernel(length, *r), [cells] * 3, name="finish")(
            exchanged(packed),
            first_cells,
            image_cells,
            surface_forcing,
            ocean_mask,
            three,
            others,
            last_pair,
        )
    )


def solution(mesh):
    torus = Mesh(
        mesh.devices.reshape(mesh.shape["lat"], 4, 4, 2), ("lat", "lon_0", "lon_1", "lon_2")
    )
    return jax.shard_map(
        local,
        mesh=torus,
        in_specs=(
            P(LON, "lat"),
            P(LON, "lat"),
            P(LON, "lat"),
            P(LON, "lat"),
            P(LON, "lat"),
            P("lat"),
            P("lat", None, None),
            P("lat", None, None),
        ),
        out_specs=(P(LON, "lat"), P(LON, "lat"), P(LON, "lat")),
        check_vma=False,
    )
```

time: 140 us -> 143 us (1.021)
  the two profiles are of different devices: /device:TPU:1 before, /device:TPU:70 now
where the time goes in v1:
time: 143 us; the launch traced here: 142 us
  starting transfers between devices  60.7 us (42%)
  waiting for transfers between devices  29.7 us (21%)
  blocking collectives  25.4 us (18%)
  local copies, waits for them, and re-layouts  12.6 us (9%)
  Pallas kernels  12.2 us (9%)
    ppermute x9, starting transfers between devices, from_lat(): lax.ppermute(value, 'lat', [(s, d) for s, d in pairs if 0 <= s < count])  29 us
    all_to_all x2, blocking collectives, exchanged(): lax.all_to_all(parts, LON, split_axis=0, concat_axis=0, tiled=True)  25.4 us
    all_to_all x4, starting transfers between devices, exchanged(): lax.all_to_all(parts, LON, split_axis=0, concat_axis=0, tiled=True)  25.1 us
    all_to_all x4, waiting for transfers between devices, exchanged(): lax.all_to_all(parts, LON, split_axis=0, concat_axis=0, tiled=True)  13.3 us
    unnamed x48, local copies, waits for them, and re-layouts  11.9 us
    ppermute x9, waiting for transfers between devices, from_lat(): lax.ppermute(value, 'lat', [(s, d) for s, d in pairs if 0 <= s < count])  11.6 us
    ppermute x2, starting transfers between devices, from_slab(): lax.ppermute(value, LAT_LON, [(s, d) for s, d in pairs if 0 <= s < count])  6.52 us
    ppermute x2, waiting for transfers between devices, from_slab(): lax.ppermute(value, LAT_LON, [(s, d) for s, d in pairs if 0 <= s < count])  4.79 us
  transfers between devices with their start and end apart: 15, of which 9 were waited for; matrix products, arithmetic and copies ran while one was open for 1% of the time, Pallas kernels for 2%

profile of v1, /device:TPU:70, one launch (start us, length us, event | category | flops | bytes accessed | tf_op | source)
XLA Modules:
  0.0 141.6 jit_solution(18180475658828194770)
XLA Ops:
  0.6 0.9 copy-done.1
  1.5 0.9 copy-done.5
  2.4 0.9 copy-done.7
  3.4 0.9 pack.1
  4.2 7.7 %all-to-all-start = ((f32[32,8,256]{2,1,0:T(8,128)}), f32[32,8,256]{2,1,0:T(8,128)S(1)}, u32[]{:S(2)}, u32[]{:S(2)}) async-start(f32[32,8,256]{2,1,0:T(8,128)} %bitcast), calls=%async_computation | async-start | bytes 524288 | tf_op jit(solution)/shard_map/all_to_all | solution.py:569
  12.2 6.7 %all-to-all-done = f32[32,8,256]{2,1,0:T(8,128)S(1)} async-done(((f32[32,8,256]{2,1,0:T(8,128)}), f32[32,8,256]{2,1,0:T(8,128)S(1)}, u32[]{:S(2)}, u32[]{:S(2)}) %all-to-all-start) | async-done | bytes 262176 | tf_op jit(solution)/shard_map/all_to_all | solution.py:569
  19.0 1.2 forward.1
  20.1 5.8 %all-to-all-start.1 = ((f32[32,8,384]{2,1,0:T(8,128)}), f32[32,8,384]{2,1,0:T(8,128)S(1)}, u32[]{:S(2)}, u32[]{:S(2)}) async-start(f32[32,8,384]{2,1,0:T(8,128)} %bitcast.2), calls=%async_computation.1 | async-start | bytes 786432 | tf_op jit(solution)/shard_map/all_to_all | solution.py:569
  26.0 0.7 constant_dynamic-slice_fusion
  26.7 0.7 copy-done.23
  27.5 6.5 %all-to-all-done.1 = f32[32,8,384]{2,1,0:T(8,128)S(1)} async-done(((f32[32,8,384]{2,1,0:T(8,128)}), f32[32,8,384]{2,1,0:T(8,128)S(1)}, u32[]{:S(2)}, u32[]{:S(2)}) %all-to-all-start.1) | async-done | bytes 393248 | tf_op jit(solution)/shard_map/all_to_all | solution.py:569
  34.3 2.0 %collective-permute-start = (f32[80,256]{1,0:T(8,128)S(1)}, f32[80,256]{1,0:T(8,128)S(1)}, u32[]{:S(2)}, u32[]{:S(2)}) collective-permute-start(f32[80,256]{1,0:T(8,128)S(1)} %get-tuple-element.34), channel_id=1, source_target_pairs={{32,0},{64,32},{96,64},{128,96},{160,128},{192,160},{224,192},{33,... | collective-permute-start | bytes 245768 | tf_op jit(solution)/shard_map/ppermute | solution.py:577
  36.3 3.8 %collective-permute-start.1 = (f32[80,256]{1,0:T(8,128)S(1)}, f32[80,256]{1,0:T(8,128)S(1)}, u32[]{:S(2)}, u32[]{:S(2)}) collective-permute-start(f32[80,256]{1,0:T(8,128)S(1)} %get-tuple-element.35), channel_id=1, source_target_pairs={{0,32},{32,64},{64,96},{96,128},{128,160},{160,192},{192,224},{1,3... | collective-permute-start | bytes 245768 | tf_op jit(solution)/shard_map/ppermute | solution.py:577
  40.2 5.0 %collective-permute-start.2 = (f32[128,128]{1,0:T(8,128)S(1)}, f32[128,128]{1,0:T(8,128)S(1)}, u32[]{:S(2)}, u32[]{:S(2)}) collective-permute-start(f32[128,128]{1,0:T(8,128)S(1)} %slice_bitcast_fusion), channel_id=1, source_target_pairs={{0,32},{32,64},{64,96},{96,128},{128,160},{160,192},{192,224},{1,3... | collective-permute-start | bytes 196616 | tf_op jit(solution)/shard_map/ppermute | solution.py:577
  45.3 1.9 %collective-permute-done.2.r_6_ = f32[128,128]{1,0:T(8,128)S(1)} collective-permute-done((f32[128,128]{1,0:T(8,128)S(1)}, f32[128,128]{1,0:T(8,128)S(1)}, u32[]{:S(2)}, u32[]{:S(2)}) %collective-permute-start.2) | collective-permute-done | bytes 65568 | tf_op jit(solution)/shard_map/ppermute | solution.py:577
  47.1 1.1 halo.1
  48.3 5.8 %all-to-all-start.2 = ((f32[32,8,256]{2,1,0:T(8,128)}), f32[32,8,256]{2,1,0:T(8,128)S(1)}, u32[]{:S(2)}, u32[]{:S(2)}) async-start(f32[32,8,256]{2,1,0:T(8,128)} %bitcast.6), calls=%async_computation.2 | async-start | bytes 524288 | tf_op jit(solution)/shard_map/all_to_all | solution.py:569
  54.0 2.4 %coefficients.1 = (f32[256,256]{1,0:T(8,128)S(1)}, f32[256,256]{1,0:T(8,128)S(1)}, f32[256,256]{1,0:T(8,128)S(1)}, f32[256,256]{1,0:T(8,128)S(1)}, f32[256,256]{...) custom-call(f32[256,256]{1,0:T(8,128)S(1)} %bitcast.23, ...), custom_call_target="tpu_custom_call" | custom-call | tf_op jit(solution)/shard_map/coefficients/pallas_call | solution.py:639
  56.5 0.7 copy-done.10
  57.2 0.7 copy-done.12
  57.9 0.7 copy-done.14
  58.6 4.6 %collective-permute-start.3 = (f32[32,256]{1,0:T(8,128)S(1)}, f32[32,256]{1,0:T(8,128)S(1)}, u32[]{:S(2)}, u32[]{:S(2)}) collective-permute-start(f32[32,256]{1,0:T(8,128)S(1)} %get-tuple-element.45), channel_id=1, source_target_pairs={{1,0},{2,1},{3,2},{4,3},{5,4},{6,5},{7,6},{8,7},{9,8},{10,9},{11,1... | collective-permute-start | bytes 98312 | tf_op jit(solution)/shard_map/ppermute | solution.py:583
  63.2 1.9 %collective-permute-start.4 = (f32[32,256]{1,0:T(8,128)S(1)}, f32[32,256]{1,0:T(8,128)S(1)}, u32[]{:S(2)}, u32[]{:S(2)}) collective-permute-start(f32[32,256]{1,0:T(8,128)S(1)} %get-tuple-element.46), channel_id=1, source_target_pairs={{0,1},{1,2},{2,3},{3,4},{4,5},{5,6},{6,7},{7,8},{8,9},{9,10},{10,1... | collective-permute-start | bytes 98312 | tf_op jit(solution)/shard_map/ppermute | solution.py:583
  65.2 0.6 copy-done.19
  65.8 4.8 %collective-permute-done.4.r_9_ = f32[32,256]{1,0:T(8,128)S(1)} collective-permute-done((f32[32,256]{1,0:T(8,128)S(1)}, f32[32,256]{1,0:T(8,128)S(1)}, u32[]{:S(2)}, u32[]{:S(2)}) %collective-permute-start.4) | collective-permute-done | bytes 32800 | tf_op jit(solution)/shard_map/ppermute | solution.py:583
  70.6 0.6 copy-done.21
  71.2 0.9 copy-done.11
  72.2 0.9 copy-done.13
  73.1 0.9 copy-done.15
  74.1 0.8 copy-done.18
  74.8 0.8 copy-done.20
  75.6 0.8 copy-done.22
  76.3 2.4 %step.1 = (f32[256,256]{1,0:T(8,128)S(1)}, f32[256,256]{1,0:T(8,128)S(1)}, f32[256,256]{1,0:T(8,128)S(1)}, f32[8,128]{1,0:T(8,128)S(1)}) custom-call(f32[256,256]{1,0:T(8,128)S(1)} %bitcast.30, f32[256,256]{1,0:T(8,128)S(1)} %bitcast.24, f32[256,256]{1,0:T(8,128)S(1)} %get-tuple-element.39.r_2_, f32[256,256]{1,0:T(8,128)S(1)} %get-tuple-element.40.r_3_.r_1_, ...), custom_call_target="tpu_custom_call" | custom-call | tf_op jit(solution)/shard_map/step/pallas_call | solution.py:649
  78.7 13.1 %all_to_all.30 = f32[32,8,256]{2,1,0:T(8,128)S(1)} all-to-all(f32[32,8,256]{2,1,0:T(8,128)S(1)} %bitcast.31), channel_id=1, replica_groups=mesh['lat'=8,'lon_0'=4,'lon_1'=4,'lon_2'=2] {'lon_0','lon_1','lon_2'}, dimensions={0} | all-to-all | bytes 524288 | tf_op jit(solution)/shard_map/all_to_all | solution.py:569
  92.1 1.9 %collective-permute-start.5 = (f32[80,256]{1,0:T(8,128)S(1)}, f32[80,256]{1,0:T(8,128)S(1)}, u32[]{:S(2)}, u32[]{:S(2)}) collective-permute-start(f32[80,256]{1,0:T(8,128)S(1)} %get-tuple-element.50), channel_id=1, source_target_pairs={{32,0},{64,32},{96,64},{128,96},{160,128},{192,160},{224,192},{33,... | collective-permute-start | bytes 245768 | tf_op jit(solution)/shard_map/ppermute | solution.py:577
  94.0 4.6 %collective-permute-start.6 = (f32[80,256]{1,0:T(8,128)S(1)}, f32[80,256]{1,0:T(8,128)S(1)}, u32[]{:S(2)}, u32[]{:S(2)}) collective-permute-start(f32[80,256]{1,0:T(8,128)S(1)} %get-tuple-element.51), channel_id=1, source_target_pairs={{0,32},{32,64},{64,96},{96,128},{128,160},{160,192},{192,224},{1,3... | collective-permute-start | bytes 245768 | tf_op jit(solution)/shard_map/ppermute | solution.py:577
  98.7 0.9 collective-permute-done.5.r_3_
  99.6 1.2 collective-permute-done.6.r_4_
  100.8 1.1 sums.1
  101.9 12.4 %all_to_all.31 = f32[32,8,256]{2,1,0:T(8,128)S(1)} all-to-all(f32[32,8,256]{2,1,0:T(8,128)S(1)} %bitcast.29), channel_id=1, replica_groups=mesh['lat'=8,'lon_0'=4,'lon_1'=4,'lon_2'=2] {'lon_0','lon_1','lon_2'}, dimensions={0} | all-to-all | bytes 524288 | tf_op jit(solution)/shard_map/all_to_all | solution.py:569
  114.2 1.2 last.1
  115.4 5.8 %all-to-all-start.5 = ((f32[32,8,256]{2,1,0:T(8,128)}), f32[32,8,256]{2,1,0:T(8,128)S(1)}, u32[]{:S(2)}, u32[]{:S(2)}) async-start(f32[32,8,256]{2,1,0:T(8,128)} %bitcast.13), calls=%async_computation.5 | async-start | bytes 524288 | tf_op jit(solution)/shard_map/all_to_all | solution.py:569
  121.4 4.8 %collective-permute-start.7 = (f32[8,128]{1,0:T(8,128)S(1)}, f32[8,128]{1,0:T(8,128)S(1)}, u32[]{:S(2)}, u32[]{:S(2)}) collective-permute-start(f32[8,128]{1,0:T(8,128)S(1)} %gather.1), channel_id=1, source_target_pairs={{224,0},{0,32},{32,64},{64,96},{96,128},{128,160},{160,192},{192,2... | collective-permute-start | bytes 12296 | tf_op jit(solution)/shard_map/ppermute | solution.py:577
  126.2 1.5 %collective-permute-done.8 = f32[8,128]{1,0:T(8,128)S(1)} collective-permute-done((f32[8,128]{1,0:T(8,128)S(1)}, f32[8,128]{1,0:T(8,128)S(1)}, u32[]{:S(2)}, u32[]{:S(2)}) %collective-permute-start.8) | collective-permute-done | bytes 4128 | tf_op jit(solution)/shard_map/ppermute | solution.py:577
  127.7 6.3 %collective-permute-start.10 = (f32[8,128]{1,0:T(8,128)S(1)}, f32[8,128]{1,0:T(8,128)S(1)}, u32[]{:S(2)}, u32[]{:S(2)}) collective-permute-start(f32[8,128]{1,0:T(8,128)S(1)} %get-tuple-element.58), channel_id=1, source_target_pairs={{192,0},{224,32},{0,64},{32,96},{64,128},{96,160},{128,192},{160,2... | collective-permute-start | bytes 12296 | tf_op jit(solution)/shard_map/ppermute | solution.py:577
  134.6 0.8 collective-permute-done.10.r_7_
  135.4 5.3 %collective-permute-done.9.r_6_ = f32[8,128]{1,0:T(8,128)S(1)} collective-permute-done((f32[8,128]{1,0:T(8,128)S(1)}, f32[8,128]{1,0:T(8,128)S(1)}, u32[]{:S(2)}, u32[]{:S(2)}) %collective-permute-start.9) | collective-permute-done | bytes 4128 | tf_op jit(solution)/shard_map/ppermute | solution.py:577
  140.7 1.0 finish.1
  (50 shorter events, 1.6 us)
Async XLA Ops:
  0.6 0.9 copy-start.1
  1.5 0.9 copy-start.5
  2.4 0.9 copy-start.7
  3.4 8.6 %copy-start.2 = (s32[135,256]{1,0:T(8,128)S(1)}, s32[135,256]{1,0:T(8,128)}, u32[]{:S(2)}) copy-start(s32[135,256]{1,0:T(8,128)} %r_4_.2) | copy-start | bytes 414724
  3.4 8.6 %copy-start.8 = (f32[135,256]{1,0:T(8,128)S(1)}, f32[135,256]{1,0:T(8,128)}, u32[]{:S(2)}) copy-start(f32[135,256]{1,0:T(8,128)} %self_ref.3) | copy-start | bytes 414724
  3.4 8.6 %copy-start.16 = (f32[135,256]{1,0:T(8,128)S(1)}, f32[135,256]{1,0:T(8,128)}, u32[]{:S(2)}) copy-start(f32[135,256]{1,0:T(8,128)} %east_ref.1) | copy-start | bytes 414724
  3.4 8.6 %copy-start.17 = (f32[135,256]{1,0:T(8,128)S(1)}, f32[135,256]{1,0:T(8,128)}, u32[]{:S(2)}) copy-start(f32[135,256]{1,0:T(8,128)} %north_ref.1) | copy-start | bytes 414724
  4.2 14.7 %copy-start = (bf16[2,2,256,256]{3,2,1,0:T(8,128)(2,1)S(1)}, bf16[2,2,256,256]{3,2,1,0:T(8,128)(2,1)}, u32[]{:S(2)}) copy-start(bf16[2,2,256,256]{3,2,1,0:T(8,128)(2,1)} %constant.33.clone.r_2_.r_10_.r_4_) | copy-start | bytes 1572868
  4.2 14.7 %all-to-all-start = ((f32[32,8,256]{2,1,0:T(8,128)}), f32[32,8,256]{2,1,0:T(8,128)S(1)}, u32[]{:S(2)}, u32[]{:S(2)}) async-start(f32[32,8,256]{2,1,0:T(8,128)} %bitcast), calls=%async_computation | async-start | bytes 524288 | tf_op jit(solution)/shard_map/all_to_all | solution.py:569
  12.0 7.0 %copy-start.4 = (f32[2,32,256]{2,1,0:T(8,128)S(1)}, f32[2,32,256]{2,1,0:T(8,128)}, u32[]{:S(2)}) copy-start(f32[2,32,256]{2,1,0:T(8,128)} %constant.34.clone.r_3_.r_11_.r_5_) | copy-start | bytes 196612
  20.1 13.9 %all-to-all-start.1 = ((f32[32,8,384]{2,1,0:T(8,128)}), f32[32,8,384]{2,1,0:T(8,128)S(1)}, u32[]{:S(2)}, u32[]{:S(2)}) async-start(f32[32,8,384]{2,1,0:T(8,128)} %bitcast.2), calls=%async_computation.1 | async-start | bytes 786432 | tf_op jit(solution)/shard_map/all_to_all | solution.py:569
  26.7 0.7 copy-start.23
  27.4 6.6 %copy-start.9 = (f32[2,128,128]{2,1,0:T(8,128)S(1)}, f32[2,128,128]{2,1,0:T(8,128)}, u32[]{:S(2)}) copy-start(f32[2,128,128]{2,1,0:T(8,128)} %aligned_ref.3) | copy-start | bytes 393220
  34.0 6.2 %copy-start.3 = (f32[2,128,128]{2,1,0:T(8,128)S(1)}, f32[2,128,128]{2,1,0:T(8,128)}, u32[]{:S(2)}) copy-start(f32[2,128,128]{2,1,0:T(8,128)} %r_5_.4) | copy-start | bytes 393220
  34.3 12.8 %collective-permute-start = (f32[80,256]{1,0:T(8,128)S(1)}, f32[80,256]{1,0:T(8,128)S(1)}, u32[]{:S(2)}, u32[]{:S(2)}) collective-permute-start(f32[80,256]{1,0:T(8,128)S(1)} %get-tuple-element.34), channel_id=1, source_target_pairs={{32,0},{64,32},{96,64},{128,96},{160,128},{192,160},{224,192},{33,... | collective-permute-start | bytes 245768 | tf_op jit(solution)/shard_map/ppermute | solution.py:577
  36.3 10.8 %collective-permute-start.1 = (f32[80,256]{1,0:T(8,128)S(1)}, f32[80,256]{1,0:T(8,128)S(1)}, u32[]{:S(2)}, u32[]{:S(2)}) collective-permute-start(f32[80,256]{1,0:T(8,128)S(1)} %get-tuple-element.35), channel_id=1, source_target_pairs={{0,32},{32,64},{64,96},{96,128},{128,160},{160,192},{192,224},{1,3... | collective-permute-start | bytes 245768 | tf_op jit(solution)/shard_map/ppermute | solution.py:577
  40.2 6.9 %collective-permute-start.2 = (f32[128,128]{1,0:T(8,128)S(1)}, f32[128,128]{1,0:T(8,128)S(1)}, u32[]{:S(2)}, u32[]{:S(2)}) collective-permute-start(f32[128,128]{1,0:T(8,128)S(1)} %slice_bitcast_fusion), channel_id=1, source_target_pairs={{0,32},{32,64},{64,96},{96,128},{128,160},{160,192},{192,224},{1,3... | collective-permute-start | bytes 196616 | tf_op jit(solution)/shard_map/ppermute | solution.py:577
  48.3 22.9 %all-to-all-start.2 = ((f32[32,8,256]{2,1,0:T(8,128)}), f32[32,8,256]{2,1,0:T(8,128)S(1)}, u32[]{:S(2)}, u32[]{:S(2)}) async-start(f32[32,8,256]{2,1,0:T(8,128)} %bitcast.6), calls=%async_computation.2 | async-start | bytes 524288 | tf_op jit(solution)/shard_map/all_to_all | solution.py:569
  56.5 0.7 copy-start.10
  57.2 0.7 copy-start.12
  57.9 0.7 copy-start.14
  58.6 6.5 %collective-permute-start.3 = (f32[32,256]{1,0:T(8,128)S(1)}, f32[32,256]{1,0:T(8,128)S(1)}, u32[]{:S(2)}, u32[]{:S(2)}) collective-permute-start(f32[32,256]{1,0:T(8,128)S(1)} %get-tuple-element.45), channel_id=1, source_target_pairs={{1,0},{2,1},{3,2},{4,3},{5,4},{6,5},{7,6},{8,7},{9,8},{10,9},{11,1... | collective-permute-start | bytes 98312 | tf_op jit(solution)/shard_map/ppermute | solution.py:583
  63.2 7.3 %collective-permute-start.4 = (f32[32,256]{1,0:T(8,128)S(1)}, f32[32,256]{1,0:T(8,128)S(1)}, u32[]{:S(2)}, u32[]{:S(2)}) collective-permute-start(f32[32,256]{1,0:T(8,128)S(1)} %get-tuple-element.46), channel_id=1, source_target_pairs={{0,1},{1,2},{2,3},{3,4},{4,5},{5,6},{6,7},{7,8},{8,9},{9,10},{10,1... | collective-permute-start | bytes 98312 | tf_op jit(solution)/shard_map/ppermute | solution.py:583
  65.2 0.6 copy-start.19
  70.6 0.6 copy-start.21
  71.2 1.0 copy-start.11
  72.2 0.9 copy-start.13
  73.1 0.9 copy-start.15
  74.1 0.8 copy-start.18
  74.8 0.8 copy-start.20
  75.6 0.8 copy-start.22
  92.1 7.5 %collective-permute-start.5 = (f32[80,256]{1,0:T(8,128)S(1)}, f32[80,256]{1,0:T(8,128)S(1)}, u32[]{:S(2)}, u32[]{:S(2)}) collective-permute-start(f32[80,256]{1,0:T(8,128)S(1)} %get-tuple-element.50), channel_id=1, source_target_pairs={{32,0},{64,32},{96,64},{128,96},{160,128},{192,160},{224,192},{33,... | collective-permute-start | bytes 245768 | tf_op jit(solution)/shard_map/ppermute | solution.py:577
  94.0 6.8 %collective-permute-start.6 = (f32[80,256]{1,0:T(8,128)S(1)}, f32[80,256]{1,0:T(8,128)S(1)}, u32[]{:S(2)}, u32[]{:S(2)}) collective-permute-start(f32[80,256]{1,0:T(8,128)S(1)} %get-tuple-element.51), channel_id=1, source_target_pairs={{0,32},{32,64},{64,96},{96,128},{128,160},{160,192},{192,224},{1,3... | collective-permute-start | bytes 245768 | tf_op jit(solution)/shard_map/ppermute | solution.py:577
  115.4 25.2 %all-to-all-start.5 = ((f32[32,8,256]{2,1,0:T(8,128)}), f32[32,8,256]{2,1,0:T(8,128)S(1)}, u32[]{:S(2)}, u32[]{:S(2)}) async-start(f32[32,8,256]{2,1,0:T(8,128)} %bitcast.13), calls=%async_computation.5 | async-start | bytes 524288 | tf_op jit(solution)/shard_map/all_to_all | solution.py:569
  121.3 6.4 %collective-permute-start.8 = (f32[8,128]{1,0:T(8,128)S(1)}, f32[8,128]{1,0:T(8,128)S(1)}, u32[]{:S(2)}, u32[]{:S(2)}) collective-permute-start(f32[8,128]{1,0:T(8,128)S(1)} %gather.1), channel_id=1, source_target_pairs={{32,0},{64,32},{96,64},{128,96},{160,128},{192,160},{224,192},{0,2... | collective-permute-start | bytes 12296 | tf_op jit(solution)/shard_map/ppermute | solution.py:577
  121.4 6.3 %collective-permute-start.7 = (f32[8,128]{1,0:T(8,128)S(1)}, f32[8,128]{1,0:T(8,128)S(1)}, u32[]{:S(2)}, u32[]{:S(2)}) collective-permute-start(f32[8,128]{1,0:T(8,128)S(1)} %gather.1), channel_id=1, source_target_pairs={{224,0},{0,32},{32,64},{64,96},{96,128},{128,160},{160,192},{192,2... | collective-permute-start | bytes 12296 | tf_op jit(solution)/shard_map/ppermute | solution.py:577
  127.7 7.7 %collective-permute-start.10 = (f32[8,128]{1,0:T(8,128)S(1)}, f32[8,128]{1,0:T(8,128)S(1)}, u32[]{:S(2)}, u32[]{:S(2)}) collective-permute-start(f32[8,128]{1,0:T(8,128)S(1)} %get-tuple-element.58), channel_id=1, source_target_pairs={{192,0},{224,32},{0,64},{32,96},{64,128},{96,160},{128,192},{160,2... | collective-permute-start | bytes 12296 | tf_op jit(solution)/shard_map/ppermute | solution.py:577
  134.0 6.6 %collective-permute-start.9 = (f32[8,128]{1,0:T(8,128)S(1)}, f32[8,128]{1,0:T(8,128)S(1)}, u32[]{:S(2)}, u32[]{:S(2)}) collective-permute-start(f32[8,128]{1,0:T(8,128)S(1)} %get-tuple-element.57.r_5_), channel_id=1, source_target_pairs={{96,0},{128,32},{160,64},{192,96},{224,128},{0,160},{32,192},{64,2... | collective-permute-start | bytes 12296 | tf_op jit(solution)/shard_map/ppermute | solution.py:577
  134.5 6.2 %copy-start.6 = (f32[135,256]{1,0:T(8,128)S(1)}, f32[135,256]{1,0:T(8,128)}, u32[]{:S(2)}) copy-start(f32[135,256]{1,0:T(8,128)} %r_3_.2) | copy-start | bytes 414724

commit v2 on v1

--- a/solution.py
+++ b/solution.py
@@ -138,25 +138,67 @@
     return pltpu.roll(value, lanes_right % value.shape[1], 1)
 
 
-def pack_kernel(forcing_ref, mask_ref, self_ref, out_ref, tall):
-    length = forcing_ref.shape[0]
+def pack_kernel(
+    forcing_ref, mask_ref, self_ref, out_ref, forcing, mask, coupling, tall, arrived
+):
+    copies = [
+        pltpu.make_async_copy(source, target, arrived.at[n])
+        for n, (source, target) in enumerate(
+            ((forcing_ref, forcing), (mask_ref, mask), (self_ref, coupling))
+        )
+    ]
+    for copy in copies:
+        copy.start()
+    for copy in copies:
+        copy.wait()
+    length = forcing.shape[0]
+    wet = mask[...].astype(jnp.float32)
+    tall[:length, :] = wet * forcing[...]
+    tall[length:, :] = (wet * coupling[...])[: WIDE - length]
+    out_ref[...] = tall[...].T
+
+
+def edges_kernel(mask_ref, north_ref, wet_ref, top_ref, tall):
+    length, rows = mask_ref.shape
+    tall[length:, :] = jnp.zeros((WIDE - length, 128), jnp.float32)
+    tall[:length, :] = mask_ref[:, :128].astype(jnp.float32)
+    wet_ref[...] = tall[...].T[:ROWS]
+    tall[:length, :] = mask_ref[:, rows - 128 :].astype(jnp.float32) * north_ref[:, rows - 128 :]
+    top_ref[...] = tall[...].T[128 - ROWS :]
+
+
+def lane_plan(length):
+    cut = WIDE - length
+    north = 2 * length - cut
+    south = north + length
+    east = south + length
+    return cut, north, south, east, 2 * WIDE - east
+
+
+def pack_rest_kernel(
+    mask_ref,
+    self_ref,
+    east_ref,
+    north_ref,
+    wet_above_ref,
+    top_below_ref,
+    out_ref,
+    late_ref,
+    tall,
+    short,
+):
+    length, rows = mask_ref.shape
+    cut, n_at, s_at, e_at, count = lane_plan(length)
+    lane = lanes((length, rows))
     wet = mask_ref[...].astype(jnp.float32)
-    tall[:length, :] = wet * forcing_ref[...]
-    tall[length:, :] = (wet * self_ref[...])[: WIDE - length]
-    out_ref[...] = tall[...].T
-
-
-def pack_rest_kernel(mask_ref, self_ref, east_ref, north_ref, out_ref, late_ref, tall, short):
-    length, rows = mask_ref.shape
-    cut = WIDE - length
-    n_at = 2 * length - cut
-    e_at = n_at + length
-    count = WIDE + 128 - e_at
-    wet = mask_ref[...].astype(jnp.float32)
+    north = wet * north_ref[...]
     east = wet * east_ref[...]
+    wet_above = wet_above_ref[...].T[:length, :1]
+    top_below = top_below_ref[...].T[:length, ROWS - 1 :]
     tall[:length, :] = jnp.zeros((length, rows), jnp.float32)
     tall[length:n_at, :] = (wet * self_ref[...])[cut:]
-    tall[n_at:e_at, :] = wet * north_ref[...]
+    tall[n_at:s_at, :] = north * jnp.where(lane == rows - 1, wet_above, shifted(wet, -1))
+    tall[s_at:e_at, :] = wet * jnp.where(lane == 0, top_below, shifted(north, 1))
     tall[e_at:, :] = east[:count]
     out_ref[...] = tall[...].T
     short[...] = jnp.zeros((128, rows), jnp.float32)
@@ -165,50 +207,27 @@
 
 
 def coefficients_kernel(
-    groups,
-    length,
-    slab_ref,
-    second_ref,
-    diagonal_ref,
-    wet_ref,
-    next_ref,
-    east_ref,
-    north_ref,
-    south_ref,
-    low_row_ref,
-    top_row_ref,
-):
-    cut = WIDE - length
-    n_at = 2 * length - cut
-    e_at = n_at + length
-    count = WIDE + 128 - e_at
-    lane, row = lanes((ROWS, WIDE)), sublanes((ROWS, WIDE))
+    groups, length, slab_ref, second_ref, own_ref, next_ref, east_ref, north_ref, south_ref
+):
+    cut, n_at, s_at, e_at, count = lane_plan(length)
+    lane = lanes((ROWS, WIDE))
     held = lane < length
-
-    def one(p):
+    for p in range(groups):
         at = rows_of(p)
         late = second_ref[at, :]
-        own = jnp.where(
+        own_ref[at, :] = jnp.where(
             lane < cut,
             shifted(slab_ref[at, :], -length),
-            jnp.where(held, shifted(late, cut - length)[:, :WIDE], 0.0),
+            jnp.where(held, shifted(late[:, :WIDE], cut - length), 0.0),
         )
-        return late, own, (own > 0.0).astype(jnp.float32)
-
+        north_ref[at, :] = jnp.where(held, shifted(late, -n_at)[:, :WIDE], 0.0)
+        south_ref[at, :] = jnp.where(held, shifted(late[:, WIDE:], WIDE - s_at), 0.0)
+        east_ref[at, :] = jnp.where(lane < count, shifted(late[:, WIDE:], WIDE - e_at), 0.0)
     for p in range(groups):
-        wet_ref[rows_of(p), :] = one(p)[2]
-    for p in range(groups):
-        at = rows_of(p)
-        late, own, wet = one(p)
-        after = wet_ref[rows_of((p + 1) % groups), 0:1]
-        north = jnp.where(held, shifted(late, -n_at)[:, :WIDE], 0.0)
-        diagonal_ref[at, :] = jnp.where(wet > 0.0, own, 1.0)
-        next_ref[at, :] = shifted(jnp.where(lane == length, after, wet), -1)
-        east_ref[at, :] = jnp.where(lane < count, shifted(late, -e_at)[:, :WIDE], 0.0)
-        north_ref[at, :] = north * jnp.where(row == ROWS - 1, 1.0, pltpu.roll(wet, ROWS - 1, 0))
-        south_ref[at, :] = wet * jnp.where(row == 0, 1.0, pltpu.roll(north, 1, 0))
-        low_row_ref[p : p + 1, :] = wet[:1]
-        top_row_ref[p : p + 1, :] = north[ROWS - 1 :]
+        own = own_ref[rows_of(p), :]
+        after = own_ref[rows_of((p + 1) % groups), 0:1]
+        ocean = jnp.where(lane == length, after, own) > 0.0
+        next_ref[rows_of(p), :] = shifted(ocean.astype(jnp.float32), -1)
 
 
 def transform(chunks, matrix_ref, twiddle_ref, left, right):
@@ -368,7 +387,6 @@
     stag_ref,
     stag_below_ref,
     spec_ref,
-    rhs_ref,
     image_ref,
     weight_ref,
     sums_ref,
@@ -381,9 +399,8 @@
     held = jnp.where(lane < length, full, 0.0)
     weight = weight_ref[0, 0]
     own = jnp.sum(held * spec_ref[...]) * weight
-    cross = jnp.sum(held * rhs_ref[:, :WIDE]) * weight
     out = jnp.where(lane < length, full, shifted(image_ref[...], length))
-    for n, value in enumerate((sums_ref[0, 0], sums_ref[0, 1], own, cross)):
+    for n, value in enumerate((sums_ref[0, 0], sums_ref[0, 1], own)):
         out = jnp.where(lane == SCALARS + n, value, out)
     out_ref[...] = out
 
@@ -393,14 +410,11 @@
     length,
     spec_ref,
     rhs_ref,
-    diagonal_ref,
-    wet_ref,
+    own_ref,
     next_ref,
     east_ref,
     north_ref,
     south_ref,
-    wet_above_ref,
-    north_below_ref,
     matrix_ref,
     twiddle_ref,
     outer_ref,
@@ -440,12 +454,12 @@
 
     cells = transform_back(spec_ref[...], groups, matrix_ref, twiddle_ref)
     for p in range(groups):
-        v = cells[p] * wet_ref[rows_of(p), :]
+        v = jnp.where(own_ref[rows_of(p), :] > 0.0, cells[p], 0.0)
         first_ref[rows_of(p), :] = v
         low[stride * p + ROWS : stride * p + 2 * ROWS, :] = v[:, :128]
         high[stride * p + ROWS : stride * p + 2 * ROWS, :] = v[:, 128:]
-    lane, row = lanes((ROWS, WIDE)), sublanes((ROWS, WIDE))
-    count = WIDE + 128 - (2 * length - (WIDE - length)) - length
+    lane = lanes((ROWS, WIDE))
+    count = lane_plan(length)[-1]
     rz = jnp.zeros((ROWS, WIDE), jnp.float32)
     curvature = jnp.zeros((ROWS, WIDE), jnp.float32)
     images, fluxes = [], []
@@ -461,14 +475,12 @@
         v = first_ref[at, :]
         before = fluxes[(p - 1) % groups][:, length - 1 : length]
         flux = fluxes[p]
-        north, south = north_ref[at, :], south_ref[at, :]
-        north = jnp.where(row == ROWS - 1, north * wet_above_ref[p : p + 1, :], north)
-        south = jnp.where(row == 0, south * north_below_ref[p : p + 1, :], south)
+        own = own_ref[at, :]
         base = stride * p + ROWS
-        image = diagonal_ref[at, :] * v
+        image = jnp.where(own > 0.0, own, 1.0) * v
         image = image + (flux - shifted(jnp.where(lane == WIDE - 1, before, flux), 1))
-        image = image + north * (v - neighbour(base + 1))
-        image = image + south * (v - neighbour(base - 1))
+        image = image + north_ref[at, :] * (v - neighbour(base + 1))
+        image = image + south_ref[at, :] * (v - neighbour(base - 1))
         image = jnp.where(lane < length, image, 0.0)
         image_ref[at, :] = image
         images.append(image)
@@ -490,7 +502,7 @@
 
 
 def last_kernel(
-    groups, length, spec_ref, wet_ref, first_ref, image_ref, matrix_ref, twiddle_ref, out_ref
+    groups, length, spec_ref, own_ref, first_ref, image_ref, matrix_ref, twiddle_ref, out_ref
 ):
     cells = transform_back(spec_ref[...], groups, matrix_ref, twiddle_ref)
     lane = lanes((ROWS, WIDE))
@@ -499,14 +511,19 @@
     image_at = 2 * length - cut
     for p in range(groups):
         at = rows_of(p)
-        out = jnp.where(
-            lane < length, cells[p] * wet_ref[at, :], shifted(first_ref[at, :], length - cut)
-        )
+        cell = jnp.where(own_ref[at, :] > 0.0, cells[p], 0.0)
+        out = jnp.where(lane < length, cell, shifted(first_ref[at, :], length - cut))
         out_ref[at, :] = jnp.where(
             lane < image_at, out, shifted(image_ref[at, :], image_at - image_cut)
         )
 
 
+def insert_kernel(packed_ref, riders_ref, out_ref):
+    out_ref[:, :128] = packed_ref[:, :128]
+    lane = lanes((packed_ref.shape[0], 128))
+    out_ref[:, 128:] = jnp.where(lane < SCALARS - 128, packed_ref[:, 128:], riders_ref[:1, :])
+
+
 def unpack_kernel(length, count, slab_ref, out_ref):
     turned = slab_ref[:, 128:].T
     out_ref[:count, :] = turned[length - 128 : length - 128 + count]
@@ -514,23 +531,21 @@
 
 def finish_kernel(
     length,
+    copies,
     back_ref,
     first_ref,
     image_ref,
     forcing_ref,
     mask_ref,
-    three_ref,
-    others_ref,
-    pair_ref,
     solution_ref,
     residual_ref,
     direction_ref,
 ):
     at = SCALARS - 128
-    totals = three_ref[:1, :] + others_ref[:1, :] + pair_ref[:1, :]
-    rz, curvature, own, cross = [totals[:, at + n : at + n + 1] for n in range(4)]
+    totals = jnp.sum(back_ref[:, 128:], axis=0, keepdims=True) * (1.0 / copies)
+    rz, curvature, own = [totals[:, at + n : at + n + 1] for n in range(3)]
     alpha = rz / curvature
-    rz_next = rz - alpha * curvature - alpha * cross + alpha * alpha * own
+    rz_next = rz - 2.0 * alpha * curvature + alpha * alpha * own
     beta = rz_next / rz
     back = back_ref[...].T
     cut = WIDE - length
@@ -577,10 +592,12 @@
     return lax.ppermute(value, "lat", [(s, d) for s, d in pairs if 0 <= s < count])
 
 
-def from_slab(value, steps):
-    count = lax.axis_size("lat") * lax.axis_size(LON)
-    pairs = [(d + steps, d) for d in range(count)]
-    return lax.ppermute(value, LAT_LON, [(s, d) for s, d in pairs if 0 <= s < count])
+def around_lat(value):
+    lats, lons = lax.axis_size("lat"), lax.axis_size(LON)
+    pairs = [
+        (g * lons + q, (g + q) % lats * lons + q) for g in range(lats) for q in range(lons)
+    ]
+    return lax.ppermute(value, LAT_LON, pairs)
 
 
 def after(value, *others):
@@ -607,19 +624,51 @@
     wide = (rows, WIDE)
     transforms = [wide, wide]
 
-    packed = call(pack_kernel, wide, [wide], name="pack")(
-        surface_forcing, ocean_mask, self_coupling
-    )
+    cells = (length, rows)
+    anywhere = pl.BlockSpec(memory_space=pltpu.HBM)
+    packed = pl.pallas_call(
+        pack_kernel,
+        out_shape=jax.ShapeDtypeStruct(wide, jnp.float32),
+        in_specs=[anywhere] * 3,
+        scratch_shapes=[
+            pltpu.VMEM(cells, jnp.float32),
+            pltpu.VMEM(cells, jnp.int32),
+            pltpu.VMEM(cells, jnp.float32),
+            pltpu.VMEM(wide, jnp.float32),
+            pltpu.SemaphoreType.DMA((3,)),
+        ],
+        compiler_params=pltpu.CompilerParams(vmem_limit_bytes=8 * 2**20),
+        name="pack",
+    )(surface_forcing, ocean_mask, self_coupling)
     slab = exchanged(packed)
+
+    mask, north_cells = lax.optimization_barrier((ocean_mask, north_coupling, packed))[:2]
+    wet_first, top_last = call(
+        edges_kernel, [(ROWS, WIDE)] * 2, [(WIDE, 128)], name="edges"
+    )(mask, north_cells)
     rest, late = call(
         pack_rest_kernel,
-        [(rows, WIDE + 128), (rows, 128)],
-        [(WIDE + 128, rows), (128, rows)],
+        [(rows, 2 * WIDE), (rows, 128)],
+        [(2 * WIDE, rows), (128, rows)],
         name="pack_rest",
-    )(after(ocean_mask, packed), self_coupling, east_coupling, north_coupling)
-    scale = lax.rsqrt(1.0 + zonal_weight[:, None] * lax.dynamic_slice_in_dim(wave, channel, 1, 0))
-    stag_below = from_lat(after(staggered_inverse[count - 1], packed), -1, False)
+    )(
+        mask,
+        self_coupling,
+        east_coupling,
+        north_cells,
+        from_lat(wet_first, 1, False),
+        from_lat(top_last, -1, False),
+    )
+    spectrum = call(
+        lambda *r: forward_kernel(groups, *r), (rows, 2 * WIDE), transforms, name="forward"
+    )(slab, rest, matrices, twiddle)
+    spec_rhs = exchanged(spectrum)
+
+    stag_below = from_lat(after(staggered_inverse[count - 1], spectrum), -1, False)
+    weights = after(zonal_weight, spectrum)
+    scale = lax.rsqrt(1.0 + weights[:, None] * lax.dynamic_slice_in_dim(wave, channel, 1, 0))
     weight = jnp.where(channel < 2, 1.0, 2.0).astype(jnp.float32)
+    spec_rhs = after(spec_rhs, stag_below, scale)
 
     edge = (half + 16, WIDE)
 
@@ -630,19 +679,11 @@
         above, below = from_lat(down, 1, False), from_lat(up, -1, False)
         return scaled, part, scale, above, below, staggered_inverse, stag_below
 
-    spec_rhs = exchanged(
-        call(lambda *r: forward_kernel(groups, *r), (rows, WIDE + 128), transforms, name="forward")(
-            slab, rest, matrices, twiddle
-        )
-    )
     pieces = blocks(spec_rhs)
-    *flat, low_row, top_row = call(
-        lambda *r: coefficients_kernel(groups, length, *r),
-        [wide] * 6 + [(groups, WIDE)] * 2,
-        name="coefficients",
+    flat = call(
+        lambda *r: coefficients_kernel(groups, length, *r), [wide] * 5, name="coefficients"
     )(slab, after(spec_rhs, pieces[0]))
-    wet_slab = flat[1]
-    wet_above, north_below = from_slab(low_row, 1), from_slab(top_row, -1)
+    late = after(late, *flat)
     filtered = exchanged(
         call(lambda *r: halo_kernel(norm, *r), wide, [(rows, 128)] * 2, name="halo")(*pieces, late)
     )
@@ -651,46 +692,36 @@
         [wide, wide, wide, (8, 128)],
         transforms + [(3 * rows, 128)] * 2 + [(rows, 128)],
         name="step",
-    )(filtered, slab, *flat, wet_above, north_below, matrices, twiddle, outer)
+    )(filtered, slab, *flat, matrices, twiddle, outer)
     spec_image = exchanged(spec)
     smem = pl.BlockSpec(memory_space=pltpu.SMEM)
     vmem = pl.BlockSpec(memory_space=pltpu.VMEM)
+    pieces = blocks(spec_image)
+    cut, image_cut = WIDE - length, SCALARS - length
+    first_cells = call(lambda *r: unpack_kernel(length, cut, *r), cells, name="unpack_first")(
+        after(spec_image, pieces[0])
+    )
     summed = pl.pallas_call(
         lambda *r: sums_kernel(norm, length, *r),
         out_shape=jax.ShapeDtypeStruct(wide, jnp.float32),
-        in_specs=[vmem] * 10 + [smem, smem],
+        in_specs=[vmem] * 9 + [smem, smem],
         out_specs=vmem,
         compiler_params=pltpu.CompilerParams(vmem_limit_bytes=16 * 2**20),
         name="sums",
-    )(*blocks(spec_image), spec_image, spec_rhs, image, weight.reshape(1, 1), sums)
-    cut, image_cut = WIDE - length, SCALARS - length
-    first_cells = call(
-        lambda *r: unpack_kernel(length, cut, *r), (length, rows), name="unpack_first"
-    )(after(spec_image, summed))
+    )(*pieces, spec_image, after(image, first_cells), weight.reshape(1, 1), sums)
     filtered = exchanged(summed)
-    lon_sums = call(gather_kernel, (8, 128), name="gather")(filtered)
-    behind, ahead = from_lat(lon_sums, -1, True), from_lat(lon_sums, 1, True)
+    riders = around_lat(call(gather_kernel, (8, 128), name="gather")(filtered))
     packed = call(lambda *r: last_kernel(groups, length, *r), wide, name="last")(
-        filtered, wet_slab, first, image, matrices, twiddle
+        filtered, flat[0], first, image, matrices, twiddle
     )
     image_cells = call(
-        lambda *r: unpack_kernel(length, image_cut, *r), (length, rows), name="unpack_image"
+        lambda *r: unpack_kernel(length, image_cut, *r), cells, name="unpack_image"
     )(after(filtered, packed))
-
-    pair = lon_sums + behind
-    three = pair + ahead
-    others, last_pair = from_lat(three, 3, True), from_lat(pair, -2, True)
-    cells = (length, rows)
+    packed = call(insert_kernel, wide, name="insert")(after(packed, image_cells), riders)
+    copies = ROWS * groups // lax.axis_size("lat")
     return tuple(
-        call(lambda *r: finish_kernel(length, *r), [cells] * 3, name="finish")(
-            exchanged(packed),
-            first_cells,
-            image_cells,
-            surface_forcing,
-            ocean_mask,
-            three,
-            others,
-            last_pair,
+        call(lambda *r: finish_kernel(length, copies, *r), [cells] * 3, name="finish")(
+            exchanged(packed), first_cells, image_cells, surface_forcing, ocean_mask
         )
     )
 

time: 143 us -> 129 us (0.902)
  the two profiles are of different devices: /device:TPU:70 before, /device:TPU:1 now
where the time goes in v2:
time: 129 us
  blocking collectives  54 us (42%)
  starting transfers between devices  40.7 us (32%)
  waiting for transfers between devices  19.3 us (15%)
  Pallas kernels  10.1 us (8%)
  local copies, waits for them, and re-layouts  3.5 us (3%)
    all_to_all x4, blocking collectives, exchanged(): lax.all_to_all(parts, LON, split_axis=0, concat_axis=0, tiled=True)  54 us
    ppermute x7, starting transfers between devices, from_lat(): lax.ppermute(value, 'lat', [(s, d) for s, d in pairs if 0 <= s < count])  21.4 us
    all_to_all x2, starting transfers between devices, exchanged(): lax.all_to_all(parts, LON, split_axis=0, concat_axis=0, tiled=True)  15.3 us
    all_to_all x2, waiting for transfers between devices, exchanged(): lax.all_to_all(parts, LON, split_axis=0, concat_axis=0, tiled=True)  7.57 us
    ppermute x1, waiting for transfers between devices, around_lat(): return lax.ppermute(value, LAT_LON, pairs)  7.04 us
    ppermute x7, waiting for transfers between devices, from_lat(): lax.ppermute(value, 'lat', [(s, d) for s, d in pairs if 0 <= s < count])  4.72 us
    ppermute x1, starting transfers between devices, around_lat(): return lax.ppermute(value, LAT_LON, pairs)  4.03 us
    unnamed x28, local copies, waits for them, and re-layouts  2.78 us
  transfers between devices with their start and end apart: 10, of which 9 were waited for; matrix products, arithmetic and copies ran while one was open for 1% of the time, Pallas kernels for 2%

profile of v2, /device:TPU:1, one launch (start us, length us, event | category | flops | bytes accessed | tf_op | source)
XLA Modules:
  0.0 128.7 jit_solution(6796646800903481897)
XLA Ops:
  0.6 0.0 copy-start.1
  0.6 0.9 copy-done.1
  1.5 0.9 copy-done.5
  2.4 0.9 copy-done.7
  3.4 1.4 %pack.1 = f32[256,256]{1,0:T(8,128)} custom-call(f32[135,256]{1,0:T(8,128)S(1)} %copy-done.5, s32[135,256]{1,0:T(8,128)S(1)} %copy-done.1, f32[135,256]{1,0:T(8,128)S(1)} %copy-done.7), custom_call_target="tpu_custom_call" | custom-call | tf_op jit(solution)/shard_map/pack/pallas_call | solution.py:629
  4.7 0.0 copy-start.2
  4.8 0.0 copy-start.11
  4.8 8.7 %all-to-all-start = ((f32[32,8,256]{2,1,0:T(8,128)}), f32[32,8,256]{2,1,0:T(8,128)S(1)}, u32[]{:S(2)}, u32[]{:S(2)}) async-start(f32[32,8,256]{2,1,0:T(8,128)} %bitcast), calls=%async_computation | async-start | bytes 524288 | tf_op jit(solution)/shard_map/all_to_all | solution.py:584
  13.5 0.0 copy-start
  13.6 0.1 edges.1
  13.7 1.4 %collective-permute-start = (f32[8,256]{1,0:T(8,128)S(1)}, f32[8,256]{1,0:T(8,128)S(1)}, u32[]{:S(2)}, u32[]{:S(2)}) collective-permute-start(f32[8,256]{1,0:T(8,128)S(1)} %get-tuple-element.37), channel_id=1, source_target_pairs={{32,0},{64,32},{96,64},{128,96},{160,128},{192,160},{224,192},{33,... | collective-permute-start | bytes 24584 | tf_op jit(solution)/shard_map/ppermute | solution.py:592
  15.1 4.2 %collective-permute-start.1 = (f32[8,256]{1,0:T(8,128)S(1)}, f32[8,256]{1,0:T(8,128)S(1)}, u32[]{:S(2)}, u32[]{:S(2)}) collective-permute-start(f32[8,256]{1,0:T(8,128)S(1)} %get-tuple-element.38), channel_id=1, source_target_pairs={{0,32},{32,64},{64,96},{96,128},{128,160},{160,192},{192,224},{1,3... | collective-permute-start | bytes 24584 | tf_op jit(solution)/shard_map/ppermute | solution.py:592
  19.3 0.0 copy-start.4
  19.3 0.7 collective-permute-done.1.top_below_ref
  20.1 0.5 pack_rest.1
  20.6 1.9 %all-to-all-done = f32[32,8,256]{2,1,0:T(8,128)S(1)} async-done(((f32[32,8,256]{2,1,0:T(8,128)}), f32[32,8,256]{2,1,0:T(8,128)S(1)}, u32[]{:S(2)}, u32[]{:S(2)}) %all-to-all-start) | async-done | bytes 262176 | tf_op jit(solution)/shard_map/all_to_all | solution.py:584
  22.5 1.2 forward.1
  23.8 6.6 %all-to-all-start.1 = ((f32[32,8,512]{2,1,0:T(8,128)}), f32[32,8,512]{2,1,0:T(8,128)S(1)}, u32[]{:S(2)}, u32[]{:S(2)}) async-start(f32[32,8,512]{2,1,0:T(8,128)} %bitcast.2), calls=%async_computation.1 | async-start | bytes 1048576 | tf_op jit(solution)/shard_map/all_to_all | solution.py:584
  30.4 0.7 constant_dynamic-slice_fusion
  31.1 3.9 %collective-permute-start.2 = (f32[128,128]{1,0:T(8,128)S(1)}, f32[128,128]{1,0:T(8,128)S(1)}, u32[]{:S(2)}, u32[]{:S(2)}) collective-permute-start(f32[128,128]{1,0:T(8,128)S(1)} %slice_bitcast_fusion), channel_id=1, source_target_pairs={{0,32},{32,64},{64,96},{96,128},{128,160},{160,192},{192,224},{1,3... | collective-permute-start | bytes 196616 | tf_op jit(solution)/shard_map/ppermute | solution.py:592
  35.0 0.1 add_rsqrt_fusion.scale_ref.r_2_
  35.1 1.2 collective-permute-done.2.r_6_
  36.3 5.7 %all-to-all-done.1 = f32[32,8,512]{2,1,0:T(8,128)S(1)} async-done(((f32[32,8,512]{2,1,0:T(8,128)}), f32[32,8,512]{2,1,0:T(8,128)S(1)}, u32[]{:S(2)}, u32[]{:S(2)}) %all-to-all-start.1) | async-done | bytes 524320 | tf_op jit(solution)/shard_map/all_to_all | solution.py:584
  42.0 0.3 blocks.2
  42.3 1.3 %collective-permute-start.3 = (f32[80,256]{1,0:T(8,128)S(1)}, f32[80,256]{1,0:T(8,128)S(1)}, u32[]{:S(2)}, u32[]{:S(2)}) collective-permute-start(f32[80,256]{1,0:T(8,128)S(1)} %get-tuple-element.45), channel_id=1, source_target_pairs={{32,0},{64,32},{96,64},{128,96},{160,128},{192,160},{224,192},{33,... | collective-permute-start | bytes 245768 | tf_op jit(solution)/shard_map/ppermute | solution.py:592
  43.6 4.5 %collective-permute-start.4 = (f32[80,256]{1,0:T(8,128)S(1)}, f32[80,256]{1,0:T(8,128)S(1)}, u32[]{:S(2)}, u32[]{:S(2)}) collective-permute-start(f32[80,256]{1,0:T(8,128)S(1)} %get-tuple-element.46), channel_id=1, source_target_pairs={{0,32},{32,64},{64,96},{96,128},{128,160},{160,192},{192,224},{1,3... | collective-permute-start | bytes 245768 | tf_op jit(solution)/shard_map/ppermute | solution.py:592
  48.1 0.7 coefficients.1
  48.8 0.3 collective-permute-done.3.r_3_
  49.1 1.0 collective-permute-done.4.r_4_
  50.1 0.4 halo.1
  50.5 0.0 copy-start.12
  50.5 12.8 %all_to_all.30 = f32[32,8,256]{2,1,0:T(8,128)S(1)} all-to-all(f32[32,8,256]{2,1,0:T(8,128)S(1)} %bitcast.31), channel_id=1, replica_groups=mesh['lat'=8,'lon_0'=4,'lon_1'=4,'lon_2'=2] {'lon_0','lon_1','lon_2'}, dimensions={0} | all-to-all | bytes 524288 | tf_op jit(solution)/shard_map/all_to_all | solution.py:584
  63.3 2.3 %step.1 = (f32[256,256]{1,0:T(8,128)S(1)}, f32[256,256]{1,0:T(8,128)S(1)}, f32[256,256]{1,0:T(8,128)S(1)}, f32[8,128]{1,0:T(8,128)S(1)}) custom-call(f32[256,256]{1,0:T(8,128)S(1)} %bitcast.27, f32[256,256]{1,0:T(8,128)S(1)} %bitcast.23, f32[256,256]{1,0:T(8,128)S(1)} %get-tuple-element.49.r_2_.r_1_, f32[256,256]{1,0:T(8,128)S(1)} %get-tuple-element.50.r_3_, ...), custom_call_target="tpu_custom_call" | custom-call | tf_op jit(solution)/shard_map/step/pallas_call | solution.py:690
  65.7 12.5 %all_to_all.31 = f32[32,8,256]{2,1,0:T(8,128)S(1)} all-to-all(f32[32,8,256]{2,1,0:T(8,128)S(1)} %bitcast.32), channel_id=1, replica_groups=mesh['lat'=8,'lon_0'=4,'lon_1'=4,'lon_2'=2] {'lon_0','lon_1','lon_2'}, dimensions={0} | all-to-all | bytes 524288 | tf_op jit(solution)/shard_map/all_to_all | solution.py:584
  78.2 0.3 blocks.3
  78.4 1.3 %collective-permute-start.5 = (f32[80,256]{1,0:T(8,128)S(1)}, f32[80,256]{1,0:T(8,128)S(1)}, u32[]{:S(2)}, u32[]{:S(2)}) collective-permute-start(f32[80,256]{1,0:T(8,128)S(1)} %get-tuple-element.58), channel_id=1, source_target_pairs={{32,0},{64,32},{96,64},{128,96},{160,128},{192,160},{224,192},{33,... | collective-permute-start | bytes 245768 | tf_op jit(solution)/shard_map/ppermute | solution.py:592
  79.7 4.7 %collective-permute-start.6 = (f32[80,256]{1,0:T(8,128)S(1)}, f32[80,256]{1,0:T(8,128)S(1)}, u32[]{:S(2)}, u32[]{:S(2)}) collective-permute-start(f32[80,256]{1,0:T(8,128)S(1)} %get-tuple-element.59), channel_id=1, source_target_pairs={{0,32},{32,64},{64,96},{96,128},{128,160},{160,192},{192,224},{1,3... | collective-permute-start | bytes 245768 | tf_op jit(solution)/shard_map/ppermute | solution.py:592
  84.5 0.1 unpack_first.1.r_1_
  84.6 0.7 collective-permute-done.5.r_3_
  85.3 0.9 collective-permute-done.6.r_4_
  86.1 1.1 sums.1
  87.2 13.1 %all_to_all.32 = f32[32,8,256]{2,1,0:T(8,128)S(1)} all-to-all(f32[32,8,256]{2,1,0:T(8,128)S(1)} %bitcast.28), channel_id=1, replica_groups=mesh['lat'=8,'lon_0'=4,'lon_1'=4,'lon_2'=2] {'lon_0','lon_1','lon_2'}, dimensions={0} | all-to-all | bytes 524288 | tf_op jit(solution)/shard_map/all_to_all | solution.py:584
  100.4 4.0 %collective-permute-start.7 = (f32[8,128]{1,0:T(8,128)S(1)}, f32[8,128]{1,0:T(8,128)S(1)}, u32[]{:S(2)}, u32[]{:S(2)}) collective-permute-start(f32[8,128]{1,0:T(8,128)S(1)} %gather.1), channel_id=1, source_target_pairs={{0,0},{1,33},{2,66},{3,99},{4,132},{5,165},{6,198},{7,231},{8,8},{... | collective-permute-start | bytes 12296 | tf_op jit(solution)/shard_map/ppermute | solution.py:600
  104.4 0.5 last.1.packed_ref
  104.9 0.1 unpack_image.1.r_2_
  105.0 7.0 %collective-permute-done.7.riders_ref = f32[8,128]{1,0:T(8,128)S(1)} collective-permute-done((f32[8,128]{1,0:T(8,128)S(1)}, f32[8,128]{1,0:T(8,128)S(1)}, u32[]{:S(2)}, u32[]{:S(2)}) %collective-permute-start.7) | collective-permute-done | bytes 4128 | tf_op jit(solution)/shard_map/ppermute | solution.py:600
  112.1 15.6 %all_to_all.33 = f32[32,8,256]{2,1,0:T(8,128)S(1)} all-to-all(f32[32,8,256]{2,1,0:T(8,128)S(1)} %bitcast.30), channel_id=1, replica_groups=mesh['lat'=8,'lon_0'=4,'lon_1'=4,'lon_2'=2] {'lon_0','lon_1','lon_2'}, dimensions={0} | all-to-all | bytes 524288 | tf_op jit(solution)/shard_map/all_to_all | solution.py:584
  127.7 1.0 finish.1
  (23 shorter events, 0.1 us)
Async XLA Ops:
  0.6 0.9 copy-start.1
  1.5 0.9 copy-start.5
  2.4 0.9 copy-start.7
  4.7 8.8 %copy-start.2 = (s32[135,256]{1,0:T(8,128)S(1)}, s32[135,256]{1,0:T(8,128)}, u32[]{:S(2)}) copy-start(s32[135,256]{1,0:T(8,128)} %r_4_.2) | copy-start | bytes 414724
  4.7 8.8 %copy-start.9 = (f32[135,256]{1,0:T(8,128)S(1)}, f32[135,256]{1,0:T(8,128)}, u32[]{:S(2)}) copy-start(f32[135,256]{1,0:T(8,128)} %north_ref.1) | copy-start | bytes 414724
  4.8 15.3 %copy-start.8 = (f32[135,256]{1,0:T(8,128)S(1)}, f32[135,256]{1,0:T(8,128)}, u32[]{:S(2)}) copy-start(f32[135,256]{1,0:T(8,128)} %self_ref.3) | copy-start | bytes 414724
  4.8 15.3 %copy-start.11 = (f32[135,256]{1,0:T(8,128)S(1)}, f32[135,256]{1,0:T(8,128)}, u32[]{:S(2)}) copy-start(f32[135,256]{1,0:T(8,128)} %east_ref.1) | copy-start | bytes 414724
  4.8 17.7 %all-to-all-start = ((f32[32,8,256]{2,1,0:T(8,128)}), f32[32,8,256]{2,1,0:T(8,128)S(1)}, u32[]{:S(2)}, u32[]{:S(2)}) async-start(f32[32,8,256]{2,1,0:T(8,128)} %bitcast), calls=%async_computation | async-start | bytes 524288 | tf_op jit(solution)/shard_map/all_to_all | solution.py:584
  13.5 9.0 %copy-start = (bf16[2,2,256,256]{3,2,1,0:T(8,128)(2,1)S(1)}, bf16[2,2,256,256]{3,2,1,0:T(8,128)(2,1)}, u32[]{:S(2)}) copy-start(bf16[2,2,256,256]{3,2,1,0:T(8,128)(2,1)} %constant.32.clone.r_2_.r_7_.r_4_) | copy-start | bytes 1572868
  13.7 5.6 %collective-permute-start = (f32[8,256]{1,0:T(8,128)S(1)}, f32[8,256]{1,0:T(8,128)S(1)}, u32[]{:S(2)}, u32[]{:S(2)}) collective-permute-start(f32[8,256]{1,0:T(8,128)S(1)} %get-tuple-element.37), channel_id=1, source_target_pairs={{32,0},{64,32},{96,64},{128,96},{160,128},{192,160},{224,192},{33,... | collective-permute-start | bytes 24584 | tf_op jit(solution)/shard_map/ppermute | solution.py:592
  15.1 5.0 %collective-permute-start.1 = (f32[8,256]{1,0:T(8,128)S(1)}, f32[8,256]{1,0:T(8,128)S(1)}, u32[]{:S(2)}, u32[]{:S(2)}) collective-permute-start(f32[8,256]{1,0:T(8,128)S(1)} %get-tuple-element.38), channel_id=1, source_target_pairs={{0,32},{32,64},{64,96},{96,128},{128,160},{160,192},{192,224},{1,3... | collective-permute-start | bytes 24584 | tf_op jit(solution)/shard_map/ppermute | solution.py:592
  19.3 3.2 %copy-start.4 = (f32[2,32,256]{2,1,0:T(8,128)S(1)}, f32[2,32,256]{2,1,0:T(8,128)}, u32[]{:S(2)}) copy-start(f32[2,32,256]{2,1,0:T(8,128)} %constant.33.clone.r_3_.r_8_.r_5_) | copy-start | bytes 196612
  23.8 7.3 %copy-start.3 = (f32[2,128,128]{2,1,0:T(8,128)S(1)}, f32[2,128,128]{2,1,0:T(8,128)}, u32[]{:S(2)}) copy-start(f32[2,128,128]{2,1,0:T(8,128)} %r_5_.4) | copy-start | bytes 393220
  23.8 18.2 %all-to-all-start.1 = ((f32[32,8,512]{2,1,0:T(8,128)}), f32[32,8,512]{2,1,0:T(8,128)S(1)}, u32[]{:S(2)}, u32[]{:S(2)}) async-start(f32[32,8,512]{2,1,0:T(8,128)} %bitcast.2), calls=%async_computation.1 | async-start | bytes 1048576 | tf_op jit(solution)/shard_map/all_to_all | solution.py:584
  31.1 3.9 %copy-start.13 = (f32[256]{0:T(256)S(1)}, f32[256]{0:T(256)}, u32[]{:S(2)}) copy-start(f32[256]{0:T(256)} %param.17) | copy-start | bytes 3076
  31.1 5.2 %collective-permute-start.2 = (f32[128,128]{1,0:T(8,128)S(1)}, f32[128,128]{1,0:T(8,128)S(1)}, u32[]{:S(2)}, u32[]{:S(2)}) collective-permute-start(f32[128,128]{1,0:T(8,128)S(1)} %slice_bitcast_fusion), channel_id=1, source_target_pairs={{0,32},{32,64},{64,96},{96,128},{128,160},{160,192},{192,224},{1,3... | collective-permute-start | bytes 196616 | tf_op jit(solution)/shard_map/ppermute | solution.py:592
  35.0 7.0 %copy-start.10 = (f32[2,128,128]{2,1,0:T(8,128)S(1)}, f32[2,128,128]{2,1,0:T(8,128)}, u32[]{:S(2)}) copy-start(f32[2,128,128]{2,1,0:T(8,128)} %aligned_ref.3) | copy-start | bytes 393220
  42.3 6.9 %collective-permute-start.3 = (f32[80,256]{1,0:T(8,128)S(1)}, f32[80,256]{1,0:T(8,128)S(1)}, u32[]{:S(2)}, u32[]{:S(2)}) collective-permute-start(f32[80,256]{1,0:T(8,128)S(1)} %get-tuple-element.45), channel_id=1, source_target_pairs={{32,0},{64,32},{96,64},{128,96},{160,128},{192,160},{224,192},{33,... | collective-permute-start | bytes 245768 | tf_op jit(solution)/shard_map/ppermute | solution.py:592
  43.6 6.5 %collective-permute-start.4 = (f32[80,256]{1,0:T(8,128)S(1)}, f32[80,256]{1,0:T(8,128)S(1)}, u32[]{:S(2)}, u32[]{:S(2)}) collective-permute-start(f32[80,256]{1,0:T(8,128)S(1)} %get-tuple-element.46), channel_id=1, source_target_pairs={{0,32},{32,64},{64,96},{96,128},{128,160},{160,192},{192,224},{1,3... | collective-permute-start | bytes 245768 | tf_op jit(solution)/shard_map/ppermute | solution.py:592
  50.5 12.8 %copy-start.12 = (f32[2,32,32]{2,1,0:T(8,128)S(1)}, f32[2,32,32]{2,1,0:T(8,128)}, u32[]{:S(2)}) copy-start(f32[2,32,32]{2,1,0:T(8,128)} %constant.35.clone.r_9_) | copy-start | bytes 24580
  78.4 6.8 %collective-permute-start.5 = (f32[80,256]{1,0:T(8,128)S(1)}, f32[80,256]{1,0:T(8,128)S(1)}, u32[]{:S(2)}, u32[]{:S(2)}) collective-permute-start(f32[80,256]{1,0:T(8,128)S(1)} %get-tuple-element.58), channel_id=1, source_target_pairs={{32,0},{64,32},{96,64},{128,96},{160,128},{192,160},{224,192},{33,... | collective-permute-start | bytes 245768 | tf_op jit(solution)/shard_map/ppermute | solution.py:592
  79.7 6.4 %collective-permute-start.6 = (f32[80,256]{1,0:T(8,128)S(1)}, f32[80,256]{1,0:T(8,128)S(1)}, u32[]{:S(2)}, u32[]{:S(2)}) collective-permute-start(f32[80,256]{1,0:T(8,128)S(1)} %get-tuple-element.59), channel_id=1, source_target_pairs={{0,32},{32,64},{64,96},{96,128},{128,160},{160,192},{192,224},{1,3... | collective-permute-start | bytes 245768 | tf_op jit(solution)/shard_map/ppermute | solution.py:592
  100.4 11.7 %collective-permute-start.7 = (f32[8,128]{1,0:T(8,128)S(1)}, f32[8,128]{1,0:T(8,128)S(1)}, u32[]{:S(2)}, u32[]{:S(2)}) collective-permute-start(f32[8,128]{1,0:T(8,128)S(1)} %gather.1), channel_id=1, source_target_pairs={{0,0},{1,33},{2,66},{3,99},{4,132},{5,165},{6,198},{7,231},{8,8},{... | collective-permute-start | bytes 12296 | tf_op jit(solution)/shard_map/ppermute | solution.py:600
  112.1 15.6 %copy-start.6 = (f32[135,256]{1,0:T(8,128)S(1)}, f32[135,256]{1,0:T(8,128)}, u32[]{:S(2)}) copy-start(f32[135,256]{1,0:T(8,128)} %r_3_.2) | copy-start | bytes 414724

commit v3 on v2

--- a/solution.py
+++ b/solution.py
@@ -8,7 +8,6 @@
 from jax.sharding import PartitionSpec as P
 
 LON = ("lon_0", "lon_1", "lon_2")
-LAT_LON = ("lat", "lon_0", "lon_1", "lon_2")
 TURN = 2.0 * np.pi
 ROWS = 8
 WIDE = 256
@@ -138,23 +137,10 @@
     return pltpu.roll(value, lanes_right % value.shape[1], 1)
 
 
-def pack_kernel(
-    forcing_ref, mask_ref, self_ref, out_ref, forcing, mask, coupling, tall, arrived
-):
-    copies = [
-        pltpu.make_async_copy(source, target, arrived.at[n])
-        for n, (source, target) in enumerate(
-            ((forcing_ref, forcing), (mask_ref, mask), (self_ref, coupling))
-        )
-    ]
-    for copy in copies:
-        copy.start()
-    for copy in copies:
-        copy.wait()
-    length = forcing.shape[0]
-    wet = mask[...].astype(jnp.float32)
-    tall[:length, :] = wet * forcing[...]
-    tall[length:, :] = (wet * coupling[...])[: WIDE - length]
+def pack_kernel(rhs_ref, own_ref, out_ref, tall):
+    length = rhs_ref.shape[0]
+    tall[:length, :] = rhs_ref[...]
+    tall[length:, :] = own_ref[: WIDE - length, :]
     out_ref[...] = tall[...].T
 
 
@@ -180,6 +166,7 @@
     self_ref,
     east_ref,
     north_ref,
+    flags_ref,
     wet_above_ref,
     top_below_ref,
     out_ref,
@@ -193,8 +180,8 @@
     wet = mask_ref[...].astype(jnp.float32)
     north = wet * north_ref[...]
     east = wet * east_ref[...]
-    wet_above = wet_above_ref[...].T[:length, :1]
-    top_below = top_below_ref[...].T[:length, ROWS - 1 :]
+    wet_above = wet_above_ref[...].T[:length, :1] * flags_ref[:1, :1]
+    top_below = top_below_ref[...].T[:length, ROWS - 1 :] * flags_ref[1:2, :1]
     tall[:length, :] = jnp.zeros((length, rows), jnp.float32)
     tall[length:n_at, :] = (wet * self_ref[...])[cut:]
     tall[n_at:s_at, :] = north * jnp.where(lane == rows - 1, wet_above, shifted(wet, -1))
@@ -305,19 +292,22 @@
     up_ref[half + 8 :, :] = scale_ref[rows - 8 :, :]
 
 
-def combine(norm, scaled_ref, part_ref, scale_ref, above_ref, below_ref, stag_ref, stag_below_ref):
+def combine(
+    norm, scaled_ref, part_ref, scale_ref, above_ref, below_ref, stag_ref, stag_below_ref, flags_ref
+):
     count, block = stag_ref.shape[0], stag_ref.shape[1]
     half, rows = block // 2, count * block
-    before = dot(
+    before = flags_ref[1:2, :] * dot(
         stag_below_ref[...],
         jnp.concatenate([below_ref[:half, :], scaled_ref[:half, :]], axis=0),
     )
+    upper = above_ref[:half, :] * flags_ref[:1, :]
     pieces = [before[half:]]
     for b in range(count - 1):
         pieces.append(dot(stag_ref[b], scaled_ref[half + b * block : half + (b + 1) * block, :]))
     after = dot(
         stag_ref[count - 1],
-        jnp.concatenate([scaled_ref[rows - half :, :], above_ref[:half, :]], axis=0),
+        jnp.concatenate([scaled_ref[rows - half :, :], upper], axis=0),
     )
     pieces.append(after[:half])
     full = (part_ref[...] + jnp.concatenate(pieces, axis=0)) * (scale_ref[...] * norm)
@@ -333,6 +323,7 @@
     below_ref,
     stag_ref,
     stag_below_ref,
+    flags_ref,
     late_ref,
     out_ref,
     low,
@@ -340,7 +331,15 @@
 ):
     half = stag_ref.shape[1] // 2
     full, before, after = combine(
-        norm, scaled_ref, part_ref, scale_ref, above_ref, below_ref, stag_ref, stag_below_ref
+        norm,
+        scaled_ref,
+        part_ref,
+        scale_ref,
+        above_ref,
+        below_ref,
+        stag_ref,
+        stag_below_ref,
+        flags_ref,
     )
     row_below = (before[half - 1 : half] + below_ref[half + 7 : half + 8, :]) * (
         below_ref[half + 15 : half + 16, :] * norm
@@ -386,23 +385,31 @@
     below_ref,
     stag_ref,
     stag_below_ref,
+    flags_ref,
     spec_ref,
-    image_ref,
-    weight_ref,
+    aside_ref,
     sums_ref,
     out_ref,
+    sums_out_ref,
 ):
     full, _, _ = combine(
-        norm, scaled_ref, part_ref, scale_ref, above_ref, below_ref, stag_ref, stag_below_ref
+        norm,
+        scaled_ref,
+        part_ref,
+        scale_ref,
+        above_ref,
+        below_ref,
+        stag_ref,
+        stag_below_ref,
+        flags_ref,
     )
     lane = lanes(full.shape)
     held = jnp.where(lane < length, full, 0.0)
-    weight = weight_ref[0, 0]
-    own = jnp.sum(held * spec_ref[...]) * weight
-    out = jnp.where(lane < length, full, shifted(image_ref[...], length))
-    for n, value in enumerate((sums_ref[0, 0], sums_ref[0, 1], own)):
-        out = jnp.where(lane == SCALARS + n, value, out)
-    out_ref[...] = out
+    own = jnp.sum(held * spec_ref[...], axis=0, keepdims=True)
+    own = jnp.sum(own[:, :128] + own[:, 128:], axis=1, keepdims=True) * flags_ref[2:3, :1]
+    small = lanes((8, 128))
+    sums_out_ref[...] = jnp.where(small == SCALARS - 128 + 2, own, sums_ref[...])
+    out_ref[...] = held + aside_ref[...]
 
 
 def step_kernel(
@@ -487,8 +494,9 @@
         rz = rz + rhs_ref[at, :] * v
         curvature = curvature + v * image
     small = lanes((8, 128))
+    at = SCALARS - 128
     sums_ref[...] = jnp.where(
-        small == 0, jnp.sum(rz), jnp.where(small == 1, jnp.sum(curvature), 0.0)
+        small == at, jnp.sum(rz), jnp.where(small == at + 1, jnp.sum(curvature), 0.0)
     )
     spectrum = transform(images, matrix_ref, twiddle_ref, left, right)
     out_ref[...] = jnp.where(
@@ -496,32 +504,33 @@
     )
 
 
-def gather_kernel(spec_ref, sums_ref):
-    riders = jnp.sum(spec_ref[:, 128:], axis=0, keepdims=True) * (1.0 / ROWS)
-    sums_ref[...] = jnp.broadcast_to(riders, (8, 128))
-
-
 def last_kernel(
-    groups, length, spec_ref, own_ref, first_ref, image_ref, matrix_ref, twiddle_ref, out_ref
+    groups,
+    length,
+    spec_ref,
+    own_ref,
+    first_ref,
+    image_ref,
+    three_ref,
+    others_ref,
+    pair_ref,
+    matrix_ref,
+    twiddle_ref,
+    out_ref,
 ):
     cells = transform_back(spec_ref[...], groups, matrix_ref, twiddle_ref)
     lane = lanes((ROWS, WIDE))
     cut = WIDE - length
     image_cut = SCALARS - length
     image_at = 2 * length - cut
+    totals = three_ref[...] + others_ref[...] + pair_ref[...]
+    riders = jnp.concatenate([totals, totals], axis=1)
     for p in range(groups):
         at = rows_of(p)
         cell = jnp.where(own_ref[at, :] > 0.0, cells[p], 0.0)
         out = jnp.where(lane < length, cell, shifted(first_ref[at, :], length - cut))
-        out_ref[at, :] = jnp.where(
-            lane < image_at, out, shifted(image_ref[at, :], image_at - image_cut)
-        )
-
-
-def insert_kernel(packed_ref, riders_ref, out_ref):
-    out_ref[:, :128] = packed_ref[:, :128]
-    lane = lanes((packed_ref.shape[0], 128))
-    out_ref[:, 128:] = jnp.where(lane < SCALARS - 128, packed_ref[:, 128:], riders_ref[:1, :])
+        out = jnp.where(lane < image_at, out, shifted(image_ref[at, :], image_at - image_cut))
+        out_ref[at, :] = jnp.where(lane < SCALARS, out, riders)
 
 
 def unpack_kernel(length, count, slab_ref, out_ref):
@@ -529,9 +538,14 @@
     out_ref[:count, :] = turned[length - 128 : length - 128 + count]
 
 
+def unpack_first_kernel(length, count, slab_ref, image_ref, out_ref, aside_ref):
+    unpack_kernel(length, count, slab_ref, out_ref)
+    lane = lanes(image_ref.shape)
+    aside_ref[...] = jnp.where(lane < length, 0.0, shifted(image_ref[...], length))
+
+
 def finish_kernel(
     length,
-    copies,
     back_ref,
     first_ref,
     image_ref,
@@ -542,7 +556,7 @@
     direction_ref,
 ):
     at = SCALARS - 128
-    totals = jnp.sum(back_ref[:, 128:], axis=0, keepdims=True) * (1.0 / copies)
+    totals = jnp.sum(back_ref[:, 128:], axis=0, keepdims=True) * (1.0 / ROWS)
     rz, curvature, own = [totals[:, at + n : at + n + 1] for n in range(3)]
     alpha = rz / curvature
     rz_next = rz - 2.0 * alpha * curvature + alpha * alpha * own
@@ -584,20 +598,9 @@
     return lax.all_to_all(parts, LON, split_axis=0, concat_axis=0, tiled=True).reshape(value.shape)
 
 
-def from_lat(value, steps, ring):
+def from_lat(value, steps):
     count = lax.axis_size("lat")
-    pairs = [(d + steps, d) for d in range(count)]
-    if ring:
-        pairs = [(s % count, d) for s, d in pairs]
-    return lax.ppermute(value, "lat", [(s, d) for s, d in pairs if 0 <= s < count])
-
-
-def around_lat(value):
-    lats, lons = lax.axis_size("lat"), lax.axis_size(LON)
-    pairs = [
-        (g * lons + q, (g + q) % lats * lons + q) for g in range(lats) for q in range(lons)
-    ]
-    return lax.ppermute(value, LAT_LON, pairs)
+    return lax.ppermute(value, "lat", [((d + steps) % count, d) for d in range(count)])
 
 
 def after(value, *others):
@@ -625,24 +628,24 @@
     transforms = [wide, wide]
 
     cells = (length, rows)
-    anywhere = pl.BlockSpec(memory_space=pltpu.HBM)
-    packed = pl.pallas_call(
-        pack_kernel,
-        out_shape=jax.ShapeDtypeStruct(wide, jnp.float32),
-        in_specs=[anywhere] * 3,
-        scratch_shapes=[
-            pltpu.VMEM(cells, jnp.float32),
-            pltpu.VMEM(cells, jnp.int32),
-            pltpu.VMEM(cells, jnp.float32),
-            pltpu.VMEM(wide, jnp.float32),
-            pltpu.SemaphoreType.DMA((3,)),
-        ],
-        compiler_params=pltpu.CompilerParams(vmem_limit_bytes=8 * 2**20),
-        name="pack",
-    )(surface_forcing, ocean_mask, self_coupling)
+    wet_cells = ocean_mask.astype(jnp.float32)
+    packed = call(pack_kernel, wide, [wide], name="pack")(
+        wet_cells * surface_forcing, wet_cells * self_coupling
+    )
     slab = exchanged(packed)
 
     mask, north_cells = lax.optimization_barrier((ocean_mask, north_coupling, packed))[:2]
+    lat = lax.axis_index("lat")
+    flag_row = lax.broadcasted_iota(jnp.int32, (8, WIDE), 0)
+    north_of, south_of, weight = (
+        jnp.where(condition, yes, no).astype(jnp.float32)
+        for condition, yes, no in (
+            (lat < lax.axis_size("lat") - 1, 1.0, 0.0),
+            (lat > 0, 1.0, 0.0),
+            (channel < 2, 1.0, 2.0),
+        )
+    )
+    flags = jnp.where(flag_row == 0, north_of, jnp.where(flag_row == 1, south_of, weight))
     wet_first, top_last = call(
         edges_kernel, [(ROWS, WIDE)] * 2, [(WIDE, 128)], name="edges"
     )(mask, north_cells)
@@ -656,18 +659,18 @@
         self_coupling,
         east_coupling,
         north_cells,
-        from_lat(wet_first, 1, False),
-        from_lat(top_last, -1, False),
+        flags,
+        from_lat(wet_first, 1),
+        from_lat(top_last, -1),
     )
     spectrum = call(
         lambda *r: forward_kernel(groups, *r), (rows, 2 * WIDE), transforms, name="forward"
     )(slab, rest, matrices, twiddle)
     spec_rhs = exchanged(spectrum)
 
-    stag_below = from_lat(after(staggered_inverse[count - 1], spectrum), -1, False)
+    stag_below = from_lat(after(staggered_inverse[count - 1], spectrum), -1)
     weights = after(zonal_weight, spectrum)
     scale = lax.rsqrt(1.0 + weights[:, None] * lax.dynamic_slice_in_dim(wave, channel, 1, 0))
-    weight = jnp.where(channel < 2, 1.0, 2.0).astype(jnp.float32)
     spec_rhs = after(spec_rhs, stag_below, scale)
 
     edge = (half + 16, WIDE)
@@ -676,8 +679,8 @@
         scaled, part, down, up = call(blocks_kernel, [wide, wide, edge, edge], name="blocks")(
             spectrum, scale, aligned_inverse
         )
-        above, below = from_lat(down, 1, False), from_lat(up, -1, False)
-        return scaled, part, scale, above, below, staggered_inverse, stag_below
+        above, below = from_lat(down, 1), from_lat(up, -1)
+        return scaled, part, scale, above, below, staggered_inverse, stag_below, flags
 
     pieces = blocks(spec_rhs)
     flat = call(
@@ -694,33 +697,27 @@
         name="step",
     )(filtered, slab, *flat, matrices, twiddle, outer)
     spec_image = exchanged(spec)
-    smem = pl.BlockSpec(memory_space=pltpu.SMEM)
-    vmem = pl.BlockSpec(memory_space=pltpu.VMEM)
     pieces = blocks(spec_image)
     cut, image_cut = WIDE - length, SCALARS - length
-    first_cells = call(lambda *r: unpack_kernel(length, cut, *r), cells, name="unpack_first")(
-        after(spec_image, pieces[0])
-    )
-    summed = pl.pallas_call(
-        lambda *r: sums_kernel(norm, length, *r),
-        out_shape=jax.ShapeDtypeStruct(wide, jnp.float32),
-        in_specs=[vmem] * 9 + [smem, smem],
-        out_specs=vmem,
-        compiler_params=pltpu.CompilerParams(vmem_limit_bytes=16 * 2**20),
-        name="sums",
-    )(*pieces, spec_image, after(image, first_cells), weight.reshape(1, 1), sums)
+    first_cells, aside = call(
+        lambda *r: unpack_first_kernel(length, cut, *r), [cells, wide], name="unpack_first"
+    )(after(spec_image, pieces[0]), image)
+    summed, sums = call(
+        lambda *r: sums_kernel(norm, length, *r), [wide, (8, 128)], name="sums"
+    )(*pieces, spec_image, aside, sums)
+
+    pair = sums + from_lat(sums, -1)
+    three = pair + from_lat(sums, 1)
+    others, last_pair = from_lat(three, 3), from_lat(pair, -2)
     filtered = exchanged(summed)
-    riders = around_lat(call(gather_kernel, (8, 128), name="gather")(filtered))
-    packed = call(lambda *r: last_kernel(groups, length, *r), wide, name="last")(
-        filtered, flat[0], first, image, matrices, twiddle
-    )
     image_cells = call(
         lambda *r: unpack_kernel(length, image_cut, *r), cells, name="unpack_image"
-    )(after(filtered, packed))
-    packed = call(insert_kernel, wide, name="insert")(after(packed, image_cells), riders)
-    copies = ROWS * groups // lax.axis_size("lat")
+    )(filtered)
+    packed = call(lambda *r: last_kernel(groups, length, *r), wide, name="last")(
+        filtered, flat[0], first, image, three, others, last_pair, matrices, twiddle
+    )
     return tuple(
-        call(lambda *r: finish_kernel(length, copies, *r), [cells] * 3, name="finish")(
+        call(lambda *r: finish_kernel(length, *r), [cells] * 3, name="finish")(
             exchanged(packed), first_cells, image_cells, surface_forcing, ocean_mask
         )
     )

time: 129 us -> 119 us (0.922)
  blocking collectives: 54 us -> 25.3 us
  waiting for transfers between devices: 19.3 us -> 34.7 us
  starting transfers between devices: 40.7 us -> 44.5 us
  local copies, waits for them, and re-layouts: 3.5 us -> 1.34 us
    all_to_all x4 -> x2, blocking collectives: 54 us -> 25.3 us  [exchanged(): lax.all_to_all(parts, LON, split_axis=0, concat_axis=0, tiled=True)]
    all_to_all x2 -> x4, starting transfers between devices: 15.3 us -> 31.9 us  [exchanged(): lax.all_to_all(parts, LON, split_axis=0, concat_axis=0, tiled=True)]
    ppermute x8 -> x11, starting transfers between devices: 25.4 us -> 12.5 us  [from_lat(): lax.ppermute(value, 'lat', [((d + steps) % count, d) for d in range(count)])]
    ppermute x8 -> x11, waiting for transfers between devices: 11.8 us -> 19.5 us  [from_lat(): lax.ppermute(value, 'lat', [((d + steps) % count, d) for d in range(count)])]
    all_to_all x2 -> x4, waiting for transfers between devices: 7.57 us -> 15.2 us  [exchanged(): lax.all_to_all(parts, LON, split_axis=0, concat_axis=0, tiled=True)]
    unnamed x28 -> x22, local copies, waits for them, and re-layouts: 2.78 us -> 0.63 us
    pallas_call x6 -> x4, Pallas kernels: 3.6 us -> 3.05 us  [the longest x1 1.03 us: local(): call(lambda *r: sums_kernel(norm, length, *r), [wide, (8, 128)], name='su...]
  transfers between devices with their start and end apart: 10 -> 15, of which waited for: 9 -> 13; matrix products, arithmetic and copies ran while one was open for 1% -> 1% of each run, Pallas kernels for 2% -> 1%
where the time goes in v3:
time: 119 us; the launch traced here: 118 us
  starting transfers between devices  44.5 us (37%)
  waiting for transfers between devices  34.7 us (29%)
  blocking collectives  25.3 us (21%)
  Pallas kernels  10.1 us (8%)
  local copies, waits for them, and re-layouts  1.34 us (1%)
  other arithmetic  1.26 us (1%)
    all_to_all x4, starting transfers between devices, exchanged(): lax.all_to_all(parts, LON, split_axis=0, concat_axis=0, tiled=True)  31.9 us
    all_to_all x2, blocking collectives, exchanged(): lax.all_to_all(parts, LON, split_axis=0, concat_axis=0, tiled=True)  25.3 us
    ppermute x11, waiting for transfers between devices, from_lat(): lax.ppermute(value, 'lat', [((d + steps) % count, d) for d in range(count)])  19.5 us
    all_to_all x4, waiting for transfers between devices, exchanged(): lax.all_to_all(parts, LON, split_axis=0, concat_axis=0, tiled=True)  15.2 us
    ppermute x11, starting transfers between devices, from_lat(): lax.ppermute(value, 'lat', [((d + steps) % count, d) for d in range(count)])  12.5 us
  transfers between devices with their start and end apart: 15, of which 13 were waited for; matrix products, arithmetic and copies ran while one was open for 1% of the time, Pallas kernels for 1%

profile of v3, /device:TPU:1, one launch (start us, length us, event | category | flops | bytes accessed | tf_op | source)
XLA Modules:
  0.0 118.0 jit_solution(15165389311379240986)
XLA Ops:
  0.6 1.1 convert_multiply_fusion
  1.7 0.8 pack.1
  2.5 8.7 %all-to-all-start = ((f32[32,8,256]{2,1,0:T(8,128)}), f32[32,8,256]{2,1,0:T(8,128)S(1)}, u32[]{:S(2)}, u32[]{:S(2)}) async-start(f32[32,8,256]{2,1,0:T(8,128)} %bitcast), calls=%async_computation | async-start | bytes 524288 | tf_op jit(solution)/shard_map/all_to_all | solution.py:598
  11.3 0.1 edges.1
  11.4 5.7 %collective-permute-start = (f32[8,256]{1,0:T(8,128)S(1)}, f32[8,256]{1,0:T(8,128)S(1)}, u32[]{:S(2)}, u32[]{:S(2)}) collective-permute-start(f32[8,256]{1,0:T(8,128)S(1)} %get-tuple-element.38), channel_id=1, source_target_pairs={{32,0},{64,32},{96,64},{128,96},{160,128},{192,160},{224,192},{0,2... | collective-permute-start | bytes 24584 | tf_op jit(solution)/shard_map/ppermute | solution.py:603
  17.1 0.1 broadcast_select_fusion.flags_ref.r_7_
  17.2 0.7 collective-permute-done.wet_above_ref
  17.9 2.9 %collective-permute-done.1.top_below_ref = f32[8,256]{1,0:T(8,128)S(1)} collective-permute-done((f32[8,256]{1,0:T(8,128)S(1)}, f32[8,256]{1,0:T(8,128)S(1)}, u32[]{:S(2)}, u32[]{:S(2)}) %collective-permute-start.1) | collective-permute-done | bytes 8224 | tf_op jit(solution)/shard_map/ppermute | solution.py:603
  20.8 0.4 pack_rest.1
  21.3 1.2 %forward.1 = f32[256,512]{1,0:T(8,128)} custom-call(f32[256,256]{1,0:T(8,128)S(1)} %bitcast.20, f32[256,512]{1,0:T(8,128)S(1)} %get-tuple-element.40.r_1_, bf16[2,2,256,256]{3,2,1,0:T(8,128)(2,1)S(1)} %copy-done, f32[2,32,256]{2,1,0:T(8,128)S(1)} %copy-done.3), custom_call_target="tpu_custom_call" | custom-call | tf_op jit(solution)/shard_map/forward/pallas_call | solution.py:666
  22.5 8.9 %all-to-all-start.1 = ((f32[32,8,512]{2,1,0:T(8,128)}), f32[32,8,512]{2,1,0:T(8,128)S(1)}, u32[]{:S(2)}, u32[]{:S(2)}) async-start(f32[32,8,512]{2,1,0:T(8,128)} %bitcast.2), calls=%async_computation.1 | async-start | bytes 1048576 | tf_op jit(solution)/shard_map/all_to_all | solution.py:598
  31.4 0.7 constant_dynamic-slice_fusion
  32.2 0.1 collective-permute-start.2
  32.3 0.6 copy-done.10
  32.8 0.1 add_rsqrt_fusion.scale_ref.r_2_
  33.0 4.0 %collective-permute-done.2.r_6_ = f32[128,128]{1,0:T(8,128)S(1)} collective-permute-done((f32[128,128]{1,0:T(8,128)S(1)}, f32[128,128]{1,0:T(8,128)S(1)}, u32[]{:S(2)}, u32[]{:S(2)}) %collective-permute-start.2) | collective-permute-done | bytes 65568 | tf_op jit(solution)/shard_map/ppermute | solution.py:603
  36.9 6.1 %all-to-all-done.1 = f32[32,8,512]{2,1,0:T(8,128)S(1)} async-done(((f32[32,8,512]{2,1,0:T(8,128)}), f32[32,8,512]{2,1,0:T(8,128)S(1)}, u32[]{:S(2)}, u32[]{:S(2)}) %all-to-all-start.1) | async-done | bytes 524320 | tf_op jit(solution)/shard_map/all_to_all | solution.py:598
  43.1 0.3 blocks.2
  43.3 0.1 collective-permute-start.3
  43.4 1.5 %collective-permute-start.4 = (f32[80,256]{1,0:T(8,128)S(1)}, f32[80,256]{1,0:T(8,128)S(1)}, u32[]{:S(2)}, u32[]{:S(2)}) collective-permute-start(f32[80,256]{1,0:T(8,128)S(1)} %get-tuple-element.47), channel_id=1, source_target_pairs={{224,0},{0,32},{32,64},{64,96},{96,128},{128,160},{160,192},{192,2... | collective-permute-start | bytes 245768 | tf_op jit(solution)/shard_map/ppermute | solution.py:603
  44.9 0.7 coefficients.1
  45.6 2.0 %collective-permute-done.3.r_3_ = f32[80,256]{1,0:T(8,128)S(1)} collective-permute-done((f32[80,256]{1,0:T(8,128)S(1)}, f32[80,256]{1,0:T(8,128)S(1)}, u32[]{:S(2)}, u32[]{:S(2)}) %collective-permute-start.3) | collective-permute-done | bytes 81952 | tf_op jit(solution)/shard_map/ppermute | solution.py:603
  47.6 1.3 %collective-permute-done.4.r_4_ = f32[80,256]{1,0:T(8,128)S(1)} collective-permute-done((f32[80,256]{1,0:T(8,128)S(1)}, f32[80,256]{1,0:T(8,128)S(1)}, u32[]{:S(2)}, u32[]{:S(2)}) %collective-permute-start.4) | collective-permute-done | bytes 81952 | tf_op jit(solution)/shard_map/ppermute | solution.py:603
  48.9 0.4 halo.1
  49.4 12.8 %all_to_all.30 = f32[32,8,256]{2,1,0:T(8,128)S(1)} all-to-all(f32[32,8,256]{2,1,0:T(8,128)S(1)} %bitcast.27), channel_id=1, replica_groups=mesh['lat'=8,'lon_0'=4,'lon_1'=4,'lon_2'=2] {'lon_0','lon_1','lon_2'}, dimensions={0} | all-to-all | bytes 524288 | tf_op jit(solution)/shard_map/all_to_all | solution.py:598
  62.2 2.4 %step.1 = (f32[256,256]{1,0:T(8,128)S(1)}, f32[256,256]{1,0:T(8,128)S(1)}, f32[256,256]{1,0:T(8,128)S(1)}, f32[8,128]{1,0:T(8,128)S(1)}) custom-call(f32[256,256]{1,0:T(8,128)S(1)} %bitcast.26, f32[256,256]{1,0:T(8,128)S(1)} %bitcast.22, f32[256,256]{1,0:T(8,128)S(1)} %get-tuple-element.50.r_2_.r_1_, f32[256,256]{1,0:T(8,128)S(1)} %get-tuple-element.51.r_3_, ...), custom_call_target="tpu_custom_call" | custom-call | tf_op jit(solution)/shard_map/step/pallas_call | solution.py:693
  64.5 12.5 %all_to_all.31 = f32[32,8,256]{2,1,0:T(8,128)S(1)} all-to-all(f32[32,8,256]{2,1,0:T(8,128)S(1)} %bitcast.28), channel_id=1, replica_groups=mesh['lat'=8,'lon_0'=4,'lon_1'=4,'lon_2'=2] {'lon_0','lon_1','lon_2'}, dimensions={0} | all-to-all | bytes 524288 | tf_op jit(solution)/shard_map/all_to_all | solution.py:598
  77.0 0.3 blocks.3
  77.3 0.1 collective-permute-start.5
  77.4 1.5 %collective-permute-start.6 = (f32[80,256]{1,0:T(8,128)S(1)}, f32[80,256]{1,0:T(8,128)S(1)}, u32[]{:S(2)}, u32[]{:S(2)}) collective-permute-start(f32[80,256]{1,0:T(8,128)S(1)} %get-tuple-element.60), channel_id=1, source_target_pairs={{224,0},{0,32},{32,64},{64,96},{96,128},{128,160},{160,192},{192,2... | collective-permute-start | bytes 245768 | tf_op jit(solution)/shard_map/ppermute | solution.py:603
  78.8 0.2 unpack_first.1
  79.0 2.2 %collective-permute-done.5.r_3_ = f32[80,256]{1,0:T(8,128)S(1)} collective-permute-done((f32[80,256]{1,0:T(8,128)S(1)}, f32[80,256]{1,0:T(8,128)S(1)}, u32[]{:S(2)}, u32[]{:S(2)}) %collective-permute-start.5) | collective-permute-done | bytes 81952 | tf_op jit(solution)/shard_map/ppermute | solution.py:603
  81.2 1.2 %collective-permute-done.6.r_4_ = f32[80,256]{1,0:T(8,128)S(1)} collective-permute-done((f32[80,256]{1,0:T(8,128)S(1)}, f32[80,256]{1,0:T(8,128)S(1)}, u32[]{:S(2)}, u32[]{:S(2)}) %collective-permute-start.6) | collective-permute-done | bytes 81952 | tf_op jit(solution)/shard_map/ppermute | solution.py:603
  82.4 1.0 sums.1
  83.5 4.6 %all-to-all-start.4 = ((f32[32,8,256]{2,1,0:T(8,128)}), f32[32,8,256]{2,1,0:T(8,128)S(1)}, u32[]{:S(2)}, u32[]{:S(2)}) async-start(f32[32,8,256]{2,1,0:T(8,128)} %bitcast.10), calls=%async_computation.4 | async-start | bytes 524288 | tf_op jit(solution)/shard_map/all_to_all | solution.py:598
  88.1 0.3 collective-permute-start.8
  88.4 1.5 %collective-permute-start.7 = (f32[8,128]{1,0:T(8,128)S(1)}, f32[8,128]{1,0:T(8,128)S(1)}, u32[]{:S(2)}, u32[]{:S(2)}) collective-permute-start(f32[8,128]{1,0:T(8,128)S(1)} %get-tuple-element.67), channel_id=1, source_target_pairs={{224,0},{0,32},{32,64},{64,96},{96,128},{128,160},{160,192},{192,2... | collective-permute-start | bytes 12296 | tf_op jit(solution)/shard_map/ppermute | solution.py:603
  89.8 1.1 collective-permute-done.8
  90.9 1.5 %collective-permute-done.7 = f32[8,128]{1,0:T(8,128)S(1)} collective-permute-done((f32[8,128]{1,0:T(8,128)S(1)}, f32[8,128]{1,0:T(8,128)S(1)}, u32[]{:S(2)}, u32[]{:S(2)}) %collective-permute-start.7) | collective-permute-done | bytes 4128 | tf_op jit(solution)/shard_map/ppermute | solution.py:603
  92.4 0.1 collective-permute-start.10
  92.5 1.9 %collective-permute-start.9 = (f32[8,128]{1,0:T(8,128)S(1)}, f32[8,128]{1,0:T(8,128)S(1)}, u32[]{:S(2)}, u32[]{:S(2)}) collective-permute-start(f32[8,128]{1,0:T(8,128)S(1)} %get-tuple-element.69.r_4_), channel_id=1, source_target_pairs={{96,0},{128,32},{160,64},{192,96},{224,128},{0,160},{32,192},{64,2... | collective-permute-start | bytes 12296 | tf_op jit(solution)/shard_map/ppermute | solution.py:603
  94.4 2.6 %collective-permute-done.10.r_6_ = f32[8,128]{1,0:T(8,128)S(1)} collective-permute-done((f32[8,128]{1,0:T(8,128)S(1)}, f32[8,128]{1,0:T(8,128)S(1)}, u32[]{:S(2)}, u32[]{:S(2)}) %collective-permute-start.10) | collective-permute-done | bytes 4128 | tf_op jit(solution)/shard_map/ppermute | solution.py:603
  97.0 0.2 all-to-all-done.4
  97.2 1.2 last.1
  98.4 9.6 %all-to-all-start.5 = ((f32[32,8,256]{2,1,0:T(8,128)}), f32[32,8,256]{2,1,0:T(8,128)S(1)}, u32[]{:S(2)}, u32[]{:S(2)}) async-start(f32[32,8,256]{2,1,0:T(8,128)} %bitcast.12), calls=%async_computation.5 | async-start | bytes 524288 | tf_op jit(solution)/shard_map/all_to_all | solution.py:598
  108.0 0.1 unpack_image.1.r_2_
  108.1 8.9 %all-to-all-done.5 = f32[32,8,256]{2,1,0:T(8,128)S(1)} async-done(((f32[32,8,256]{2,1,0:T(8,128)}), f32[32,8,256]{2,1,0:T(8,128)S(1)}, u32[]{:S(2)}, u32[]{:S(2)}) %all-to-all-start.5) | async-done | bytes 262176 | tf_op jit(solution)/shard_map/all_to_all | solution.py:598
  117.0 1.0 finish.1
  (28 shorter events, 0.1 us)
Async XLA Ops:
  2.5 8.8 %copy-start.1 = (s32[135,256]{1,0:T(8,128)S(1)}, s32[135,256]{1,0:T(8,128)}, u32[]{:S(2)}) copy-start(s32[135,256]{1,0:T(8,128)} %r_4_.1) | copy-start | bytes 414724
  2.5 8.8 %copy-start.6 = (f32[135,256]{1,0:T(8,128)S(1)}, f32[135,256]{1,0:T(8,128)}, u32[]{:S(2)}) copy-start(f32[135,256]{1,0:T(8,128)} %north_ref.1) | copy-start | bytes 414724
  2.5 18.3 %copy-start.5 = (f32[135,256]{1,0:T(8,128)S(1)}, f32[135,256]{1,0:T(8,128)}, u32[]{:S(2)}) copy-start(f32[135,256]{1,0:T(8,128)} %self_ref.1) | copy-start | bytes 414724
  2.5 18.3 %copy-start.8 = (f32[135,256]{1,0:T(8,128)S(1)}, f32[135,256]{1,0:T(8,128)}, u32[]{:S(2)}) copy-start(f32[135,256]{1,0:T(8,128)} %east_ref.1) | copy-start | bytes 414724
  2.5 18.7 %all-to-all-start = ((f32[32,8,256]{2,1,0:T(8,128)}), f32[32,8,256]{2,1,0:T(8,128)S(1)}, u32[]{:S(2)}, u32[]{:S(2)}) async-start(f32[32,8,256]{2,1,0:T(8,128)} %bitcast), calls=%async_computation | async-start | bytes 524288 | tf_op jit(solution)/shard_map/all_to_all | solution.py:598
  11.3 9.9 %copy-start = (bf16[2,2,256,256]{3,2,1,0:T(8,128)(2,1)S(1)}, bf16[2,2,256,256]{3,2,1,0:T(8,128)(2,1)}, u32[]{:S(2)}) copy-start(bf16[2,2,256,256]{3,2,1,0:T(8,128)(2,1)} %constant.44.clone.r_2_.r_7_) | copy-start | bytes 1572868
  11.4 6.4 %collective-permute-start = (f32[8,256]{1,0:T(8,128)S(1)}, f32[8,256]{1,0:T(8,128)S(1)}, u32[]{:S(2)}, u32[]{:S(2)}) collective-permute-start(f32[8,256]{1,0:T(8,128)S(1)} %get-tuple-element.38), channel_id=1, source_target_pairs={{32,0},{64,32},{96,64},{128,96},{160,128},{192,160},{224,192},{0,2... | collective-permute-start | bytes 24584 | tf_op jit(solution)/shard_map/ppermute | solution.py:603
  17.1 3.7 %collective-permute-start.1 = (f32[8,256]{1,0:T(8,128)S(1)}, f32[8,256]{1,0:T(8,128)S(1)}, u32[]{:S(2)}, u32[]{:S(2)}) collective-permute-start(f32[8,256]{1,0:T(8,128)S(1)} %get-tuple-element.39), channel_id=1, source_target_pairs={{224,0},{0,32},{32,64},{64,96},{96,128},{128,160},{160,192},{192,2... | collective-permute-start | bytes 24584 | tf_op jit(solution)/shard_map/ppermute | solution.py:603
  17.2 4.1 %copy-start.3 = (f32[2,32,256]{2,1,0:T(8,128)S(1)}, f32[2,32,256]{2,1,0:T(8,128)}, u32[]{:S(2)}) copy-start(f32[2,32,256]{2,1,0:T(8,128)} %constant.45.clone.r_3_.r_8_) | copy-start | bytes 196612
  22.5 9.7 %copy-start.2 = (f32[2,128,128]{2,1,0:T(8,128)S(1)}, f32[2,128,128]{2,1,0:T(8,128)}, u32[]{:S(2)}) copy-start(f32[2,128,128]{2,1,0:T(8,128)} %r_5_.3) | copy-start | bytes 393220
  22.5 20.6 %all-to-all-start.1 = ((f32[32,8,512]{2,1,0:T(8,128)}), f32[32,8,512]{2,1,0:T(8,128)S(1)}, u32[]{:S(2)}, u32[]{:S(2)}) async-start(f32[32,8,512]{2,1,0:T(8,128)} %bitcast.2), calls=%async_computation.1 | async-start | bytes 1048576 | tf_op jit(solution)/shard_map/all_to_all | solution.py:598
  32.2 0.7 copy-start.10
  32.2 4.7 %collective-permute-start.2 = (f32[128,128]{1,0:T(8,128)S(1)}, f32[128,128]{1,0:T(8,128)S(1)}, u32[]{:S(2)}, u32[]{:S(2)}) collective-permute-start(f32[128,128]{1,0:T(8,128)S(1)} %slice_bitcast_fusion), channel_id=1, source_target_pairs={{224,0},{0,32},{32,64},{64,96},{96,128},{128,160},{160,192},{192,2... | collective-permute-start | bytes 196616 | tf_op jit(solution)/shard_map/ppermute | solution.py:603
  32.8 10.2 %copy-start.7 = (f32[2,128,128]{2,1,0:T(8,128)S(1)}, f32[2,128,128]{2,1,0:T(8,128)}, u32[]{:S(2)}) copy-start(f32[2,128,128]{2,1,0:T(8,128)} %aligned_ref.3) | copy-start | bytes 393220
  43.3 4.3 %collective-permute-start.3 = (f32[80,256]{1,0:T(8,128)S(1)}, f32[80,256]{1,0:T(8,128)S(1)}, u32[]{:S(2)}, u32[]{:S(2)}) collective-permute-start(f32[80,256]{1,0:T(8,128)S(1)} %get-tuple-element.46), channel_id=1, source_target_pairs={{32,0},{64,32},{96,64},{128,96},{160,128},{192,160},{224,192},{0,2... | collective-permute-start | bytes 245768 | tf_op jit(solution)/shard_map/ppermute | solution.py:603
  43.4 5.5 %collective-permute-start.4 = (f32[80,256]{1,0:T(8,128)S(1)}, f32[80,256]{1,0:T(8,128)S(1)}, u32[]{:S(2)}, u32[]{:S(2)}) collective-permute-start(f32[80,256]{1,0:T(8,128)S(1)} %get-tuple-element.47), channel_id=1, source_target_pairs={{224,0},{0,32},{32,64},{64,96},{96,128},{128,160},{160,192},{192,2... | collective-permute-start | bytes 245768 | tf_op jit(solution)/shard_map/ppermute | solution.py:603
  49.4 12.8 %copy-start.9 = (f32[2,32,32]{2,1,0:T(8,128)S(1)}, f32[2,32,32]{2,1,0:T(8,128)}, u32[]{:S(2)}) copy-start(f32[2,32,32]{2,1,0:T(8,128)} %constant.47.clone.r_9_) | copy-start | bytes 24580
  77.3 3.9 %collective-permute-start.5 = (f32[80,256]{1,0:T(8,128)S(1)}, f32[80,256]{1,0:T(8,128)S(1)}, u32[]{:S(2)}, u32[]{:S(2)}) collective-permute-start(f32[80,256]{1,0:T(8,128)S(1)} %get-tuple-element.59), channel_id=1, source_target_pairs={{32,0},{64,32},{96,64},{128,96},{160,128},{192,160},{224,192},{0,2... | collective-permute-start | bytes 245768 | tf_op jit(solution)/shard_map/ppermute | solution.py:603
  77.4 5.0 %collective-permute-start.6 = (f32[80,256]{1,0:T(8,128)S(1)}, f32[80,256]{1,0:T(8,128)S(1)}, u32[]{:S(2)}, u32[]{:S(2)}) collective-permute-start(f32[80,256]{1,0:T(8,128)S(1)} %get-tuple-element.60), channel_id=1, source_target_pairs={{224,0},{0,32},{32,64},{64,96},{96,128},{128,160},{160,192},{192,2... | collective-permute-start | bytes 245768 | tf_op jit(solution)/shard_map/ppermute | solution.py:603
  83.5 13.7 %all-to-all-start.4 = ((f32[32,8,256]{2,1,0:T(8,128)}), f32[32,8,256]{2,1,0:T(8,128)S(1)}, u32[]{:S(2)}, u32[]{:S(2)}) async-start(f32[32,8,256]{2,1,0:T(8,128)} %bitcast.10), calls=%async_computation.4 | async-start | bytes 524288 | tf_op jit(solution)/shard_map/all_to_all | solution.py:598
  88.1 2.8 %collective-permute-start.8 = (f32[8,128]{1,0:T(8,128)S(1)}, f32[8,128]{1,0:T(8,128)S(1)}, u32[]{:S(2)}, u32[]{:S(2)}) collective-permute-start(f32[8,128]{1,0:T(8,128)S(1)} %get-tuple-element.67), channel_id=1, source_target_pairs={{32,0},{64,32},{96,64},{128,96},{160,128},{192,160},{224,192},{0,2... | collective-permute-start | bytes 12296 | tf_op jit(solution)/shard_map/ppermute | solution.py:603
  88.4 4.0 %collective-permute-start.7 = (f32[8,128]{1,0:T(8,128)S(1)}, f32[8,128]{1,0:T(8,128)S(1)}, u32[]{:S(2)}, u32[]{:S(2)}) collective-permute-start(f32[8,128]{1,0:T(8,128)S(1)} %get-tuple-element.67), channel_id=1, source_target_pairs={{224,0},{0,32},{32,64},{64,96},{96,128},{128,160},{160,192},{192,2... | collective-permute-start | bytes 12296 | tf_op jit(solution)/shard_map/ppermute | solution.py:603
  92.4 4.6 %collective-permute-start.10 = (f32[8,128]{1,0:T(8,128)S(1)}, f32[8,128]{1,0:T(8,128)S(1)}, u32[]{:S(2)}, u32[]{:S(2)}) collective-permute-start(f32[8,128]{1,0:T(8,128)S(1)} %get-tuple-element.70), channel_id=1, source_target_pairs={{192,0},{224,32},{0,64},{32,96},{64,128},{96,160},{128,192},{160,2... | collective-permute-start | bytes 12296 | tf_op jit(solution)/shard_map/ppermute | solution.py:603
  92.5 4.5 %collective-permute-start.9 = (f32[8,128]{1,0:T(8,128)S(1)}, f32[8,128]{1,0:T(8,128)S(1)}, u32[]{:S(2)}, u32[]{:S(2)}) collective-permute-start(f32[8,128]{1,0:T(8,128)S(1)} %get-tuple-element.69.r_4_), channel_id=1, source_target_pairs={{96,0},{128,32},{160,64},{192,96},{224,128},{0,160},{32,192},{64,2... | collective-permute-start | bytes 12296 | tf_op jit(solution)/shard_map/ppermute | solution.py:603
  98.4 18.6 %all-to-all-start.5 = ((f32[32,8,256]{2,1,0:T(8,128)}), f32[32,8,256]{2,1,0:T(8,128)S(1)}, u32[]{:S(2)}, u32[]{:S(2)}) async-start(f32[32,8,256]{2,1,0:T(8,128)} %bitcast.12), calls=%async_computation.5 | async-start | bytes 524288 | tf_op jit(solution)/shard_map/all_to_all | solution.py:598
  108.0 9.0 %copy-start.4 = (f32[135,256]{1,0:T(8,128)S(1)}, f32[135,256]{1,0:T(8,128)}, u32[]{:S(2)}) copy-start(f32[135,256]{1,0:T(8,128)} %r_3_.2) | copy-start | bytes 414724

commit v4 on v3

--- a/solution.py
+++ b/solution.py
@@ -155,61 +155,52 @@
 
 def lane_plan(length):
     cut = WIDE - length
-    north = 2 * length - cut
+    north = LATE
     south = north + length
     east = south + length
-    return cut, north, south, east, 2 * WIDE - east
+    return cut, 2 * cut - length, north, south, east
+
+
+def pack_more_kernel(own_ref, mask_ref, east_ref, out_ref, tall):
+    length, rows = mask_ref.shape
+    cut, count = lane_plan(length)[:2]
+    tall[:length, :] = jnp.zeros((length, rows), jnp.float32)
+    tall[length : WIDE - count, :] = own_ref[cut:, :]
+    tall[WIDE - count :, :] = (mask_ref[...].astype(jnp.float32) * east_ref[...])[:count]
+    out_ref[...] = tall[...].T
 
 
 def pack_rest_kernel(
-    mask_ref,
-    self_ref,
-    east_ref,
-    north_ref,
-    flags_ref,
-    wet_above_ref,
-    top_below_ref,
-    out_ref,
-    late_ref,
-    tall,
-    short,
+    mask_ref, east_ref, north_ref, flags_ref, wet_above_ref, top_below_ref, out_ref, tall
 ):
     length, rows = mask_ref.shape
-    cut, n_at, s_at, e_at, count = lane_plan(length)
+    _, count, n_at, s_at, e_at = lane_plan(length)
     lane = lanes((length, rows))
     wet = mask_ref[...].astype(jnp.float32)
     north = wet * north_ref[...]
-    east = wet * east_ref[...]
     wet_above = wet_above_ref[...].T[:length, :1] * flags_ref[:1, :1]
     top_below = top_below_ref[...].T[:length, ROWS - 1 :] * flags_ref[1:2, :1]
-    tall[:length, :] = jnp.zeros((length, rows), jnp.float32)
-    tall[length:n_at, :] = (wet * self_ref[...])[cut:]
+    tall[128:n_at, :] = jnp.zeros((n_at - 128, rows), jnp.float32)
     tall[n_at:s_at, :] = north * jnp.where(lane == rows - 1, wet_above, shifted(wet, -1))
     tall[s_at:e_at, :] = wet * jnp.where(lane == 0, top_below, shifted(north, 1))
-    tall[e_at:, :] = east[:count]
-    out_ref[...] = tall[...].T
-    short[...] = jnp.zeros((128, rows), jnp.float32)
-    short[LATE - 128 : LATE - 128 + length - count, :] = east[count:]
-    late_ref[...] = short[...].T
-
-
-def coefficients_kernel(
-    groups, length, slab_ref, second_ref, own_ref, next_ref, east_ref, north_ref, south_ref
-):
-    cut, n_at, s_at, e_at, count = lane_plan(length)
+    tall[e_at : e_at + length - count, :] = (wet * east_ref[...])[count:]
+    unused = 2 * WIDE - (e_at + length - count)
+    tall[2 * WIDE - unused :, :] = jnp.zeros((unused, rows), jnp.float32)
+    out_ref[...] = tall[128:, :].T
+
+
+def coefficients_kernel(groups, length, slab_ref, second_ref, own_ref, next_ref, east_ref):
+    cut, count = lane_plan(length)[:2]
     lane = lanes((ROWS, WIDE))
-    held = lane < length
     for p in range(groups):
         at = rows_of(p)
-        late = second_ref[at, :]
+        more = second_ref[at, :]
         own_ref[at, :] = jnp.where(
             lane < cut,
             shifted(slab_ref[at, :], -length),
-            jnp.where(held, shifted(late[:, :WIDE], cut - length), 0.0),
-        )
-        north_ref[at, :] = jnp.where(held, shifted(late, -n_at)[:, :WIDE], 0.0)
-        south_ref[at, :] = jnp.where(held, shifted(late[:, WIDE:], WIDE - s_at), 0.0)
-        east_ref[at, :] = jnp.where(lane < count, shifted(late[:, WIDE:], WIDE - e_at), 0.0)
+            jnp.where(lane < length, shifted(more, cut - length), 0.0),
+        )
+        east_ref[at, :] = jnp.where(lane < count, shifted(more, count), 0.0)
     for p in range(groups):
         own = own_ref[rows_of(p), :]
         after = own_ref[rows_of((p + 1) % groups), 0:1]
@@ -271,14 +262,13 @@
 def forward_kernel(groups, field_ref, rest_ref, matrix_ref, twiddle_ref, out_ref, left, right):
     chunks = [field_ref[rows_of(p), :] for p in range(groups)]
     spectrum = transform(chunks, matrix_ref, twiddle_ref, left, right)
-    out_ref[:, :WIDE] = spectrum + rest_ref[:, :WIDE]
-    out_ref[:, WIDE:] = rest_ref[:, WIDE:]
+    out_ref[...] = spectrum + rest_ref[...]
 
 
 def blocks_kernel(spec_ref, scale_ref, aligned_ref, scaled_ref, part_ref, down_ref, up_ref):
     count, block = aligned_ref.shape[0], aligned_ref.shape[1]
     half, rows = block // 2, count * block
-    scaled = spec_ref[:, :WIDE] * scale_ref[...]
+    scaled = spec_ref[...] * scale_ref[...]
     scaled_ref[...] = scaled
     for b in range(count):
         part_ref[b * block : (b + 1) * block, :] = dot(
@@ -370,9 +360,10 @@
     ):
         at = pl.ds(s, groups, stride=ROWS)
         high[at, :] = jnp.where(lane >= HALO, part[:, 128:], high[at, :])
-    out_ref[:, 128:] = jnp.where(
-        lanes(high.shape) < LATE - 128, high[...], late_ref[...]
-    )
+    out_ref[:, 128:WIDE] = jnp.where(
+        lanes(high.shape) < LATE - 128, high[...], late_ref[:, :128]
+    )
+    out_ref[:, WIDE:] = late_ref[:, 128:]
 
 
 def sums_kernel(
@@ -390,7 +381,6 @@
     aside_ref,
     sums_ref,
     out_ref,
-    sums_out_ref,
 ):
     full, _, _ = combine(
         norm,
@@ -407,9 +397,17 @@
     held = jnp.where(lane < length, full, 0.0)
     own = jnp.sum(held * spec_ref[...], axis=0, keepdims=True)
     own = jnp.sum(own[:, :128] + own[:, 128:], axis=1, keepdims=True) * flags_ref[2:3, :1]
-    small = lanes((8, 128))
-    sums_out_ref[...] = jnp.where(small == SCALARS - 128 + 2, own, sums_ref[...])
-    out_ref[...] = held + aside_ref[...]
+    full = held + aside_ref[...]
+    full = jnp.where(lane == SCALARS + 2, own, full)
+    out_ref[:, :128] = full[:, :128]
+    out_ref[:, 128:] = jnp.where(
+        (lane[:, 128:] == SCALARS) | (lane[:, 128:] == SCALARS + 1), sums_ref[:1, :], full[:, 128:]
+    )
+
+
+def gather_kernel(spec_ref, sums_ref):
+    riders = jnp.sum(spec_ref[:, 128:], axis=0, keepdims=True) * (1.0 / ROWS)
+    sums_ref[...] = jnp.broadcast_to(riders, (8, 128))
 
 
 def step_kernel(
@@ -420,8 +418,6 @@
     own_ref,
     next_ref,
     east_ref,
-    north_ref,
-    south_ref,
     matrix_ref,
     twiddle_ref,
     outer_ref,
@@ -437,7 +433,7 @@
 ):
     lane_row = lanes((groups, WIDE))
     stride = 3 * ROWS
-    tail[...] = spec_ref[:, 128:]
+    tail[...] = spec_ref[:, 128:WIDE]
 
     def halo_row(s):
         blank = jnp.zeros((groups, 128), jnp.float32)
@@ -459,14 +455,14 @@
         at = slice(start, start + ROWS)
         return jnp.concatenate([low[at, :], high[at, :]], axis=1)
 
-    cells = transform_back(spec_ref[...], groups, matrix_ref, twiddle_ref)
+    cells = transform_back(spec_ref[:, :WIDE], groups, matrix_ref, twiddle_ref)
     for p in range(groups):
         v = jnp.where(own_ref[rows_of(p), :] > 0.0, cells[p], 0.0)
         first_ref[rows_of(p), :] = v
         low[stride * p + ROWS : stride * p + 2 * ROWS, :] = v[:, :128]
         high[stride * p + ROWS : stride * p + 2 * ROWS, :] = v[:, 128:]
     lane = lanes((ROWS, WIDE))
-    count = lane_plan(length)[-1]
+    _, count, n_at, s_at, e_at = lane_plan(length)
     rz = jnp.zeros((ROWS, WIDE), jnp.float32)
     curvature = jnp.zeros((ROWS, WIDE), jnp.float32)
     images, fluxes = [], []
@@ -474,7 +470,9 @@
         at = rows_of(p)
         v = first_ref[at, :]
         after = first_ref[rows_of((p + 1) % groups), 0:1]
-        east = jnp.where(lane < count, east_ref[at, :], shifted(spec_ref[at, :], count - LATE))
+        east = jnp.where(
+            lane < count, east_ref[at, :], shifted(spec_ref[at, WIDE:], count - (e_at - WIDE))
+        )
         flux = v - shifted(jnp.where(lane == length, after, v), -1)
         fluxes.append(jnp.where(lane < length, east * next_ref[at, :] * flux, 0.0))
     for p in range(groups):
@@ -484,10 +482,12 @@
         flux = fluxes[p]
         own = own_ref[at, :]
         base = stride * p + ROWS
+        north = shifted(spec_ref[at, 128 : 128 + WIDE], 128 - n_at)
+        south = shifted(spec_ref[at, WIDE:], WIDE - s_at)
         image = jnp.where(own > 0.0, own, 1.0) * v
         image = image + (flux - shifted(jnp.where(lane == WIDE - 1, before, flux), 1))
-        image = image + north_ref[at, :] * (v - neighbour(base + 1))
-        image = image + south_ref[at, :] * (v - neighbour(base - 1))
+        image = image + north * (v - neighbour(base + 1))
+        image = image + south * (v - neighbour(base - 1))
         image = jnp.where(lane < length, image, 0.0)
         image_ref[at, :] = image
         images.append(image)
@@ -511,9 +511,6 @@
     own_ref,
     first_ref,
     image_ref,
-    three_ref,
-    others_ref,
-    pair_ref,
     matrix_ref,
     twiddle_ref,
     out_ref,
@@ -523,14 +520,13 @@
     cut = WIDE - length
     image_cut = SCALARS - length
     image_at = 2 * length - cut
-    totals = three_ref[...] + others_ref[...] + pair_ref[...]
-    riders = jnp.concatenate([totals, totals], axis=1)
     for p in range(groups):
         at = rows_of(p)
         cell = jnp.where(own_ref[at, :] > 0.0, cells[p], 0.0)
         out = jnp.where(lane < length, cell, shifted(first_ref[at, :], length - cut))
-        out = jnp.where(lane < image_at, out, shifted(image_ref[at, :], image_at - image_cut))
-        out_ref[at, :] = jnp.where(lane < SCALARS, out, riders)
+        out_ref[at, :] = jnp.where(
+            lane < image_at, out, shifted(image_ref[at, :], image_at - image_cut)
+        )
 
 
 def unpack_kernel(length, count, slab_ref, out_ref):
@@ -551,12 +547,15 @@
     image_ref,
     forcing_ref,
     mask_ref,
+    three_ref,
+    others_ref,
+    pair_ref,
     solution_ref,
     residual_ref,
     direction_ref,
 ):
     at = SCALARS - 128
-    totals = jnp.sum(back_ref[:, 128:], axis=0, keepdims=True) * (1.0 / ROWS)
+    totals = three_ref[:1, :] + others_ref[:1, :] + pair_ref[:1, :]
     rz, curvature, own = [totals[:, at + n : at + n + 1] for n in range(3)]
     alpha = rz / curvature
     rz_next = rz - 2.0 * alpha * curvature + alpha * alpha * own
@@ -629,12 +628,19 @@
 
     cells = (length, rows)
     wet_cells = ocean_mask.astype(jnp.float32)
-    packed = call(pack_kernel, wide, [wide], name="pack")(
-        wet_cells * surface_forcing, wet_cells * self_coupling
-    )
+    own_cells = wet_cells * self_coupling
+    packed = call(pack_kernel, wide, [wide], name="pack")(wet_cells * surface_forcing, own_cells)
     slab = exchanged(packed)
 
-    mask, north_cells = lax.optimization_barrier((ocean_mask, north_coupling, packed))[:2]
+    mask, east_cells, north_cells, weights, stag = lax.optimization_barrier(
+        (ocean_mask, east_coupling, north_coupling, zonal_weight, staggered_inverse, packed)
+    )[:-1]
+    stag_below = from_lat(stag[count - 1], -1)
+    more = call(pack_more_kernel, wide, [wide], name="pack_more")(own_cells, mask, east_cells)
+    wet_first, top_last = call(
+        edges_kernel, [(ROWS, WIDE)] * 2, [(WIDE, 128)], name="edges"
+    )(mask, north_cells)
+    scale = lax.rsqrt(1.0 + weights[:, None] * lax.dynamic_slice_in_dim(wave, channel, 1, 0))
     lat = lax.axis_index("lat")
     flag_row = lax.broadcasted_iota(jnp.int32, (8, WIDE), 0)
     north_of, south_of, weight = (
@@ -646,32 +652,17 @@
         )
     )
     flags = jnp.where(flag_row == 0, north_of, jnp.where(flag_row == 1, south_of, weight))
-    wet_first, top_last = call(
-        edges_kernel, [(ROWS, WIDE)] * 2, [(WIDE, 128)], name="edges"
-    )(mask, north_cells)
-    rest, late = call(
-        pack_rest_kernel,
-        [(rows, 2 * WIDE), (rows, 128)],
-        [(2 * WIDE, rows), (128, rows)],
-        name="pack_rest",
-    )(
-        mask,
-        self_coupling,
-        east_coupling,
-        north_cells,
-        flags,
-        from_lat(wet_first, 1),
-        from_lat(top_last, -1),
-    )
-    spectrum = call(
-        lambda *r: forward_kernel(groups, *r), (rows, 2 * WIDE), transforms, name="forward"
-    )(slab, rest, matrices, twiddle)
+    slab = after(slab, stag_below, scale, flags, wet_first)
+    spectrum = call(lambda *r: forward_kernel(groups, *r), wide, transforms, name="forward")(
+        slab, more, matrices, twiddle
+    )
     spec_rhs = exchanged(spectrum)
 
-    stag_below = from_lat(after(staggered_inverse[count - 1], spectrum), -1)
-    weights = after(zonal_weight, spectrum)
-    scale = lax.rsqrt(1.0 + weights[:, None] * lax.dynamic_slice_in_dim(wave, channel, 1, 0))
-    spec_rhs = after(spec_rhs, stag_below, scale)
+    wet_first, top_last = lax.optimization_barrier((wet_first, top_last, spectrum))[:2]
+    late = call(pack_rest_kernel, (rows, WIDE + 128), [(2 * WIDE, rows)], name="pack_rest")(
+        mask, east_cells, north_cells, flags, from_lat(wet_first, 1), from_lat(top_last, -1)
+    )
+    spec_rhs = after(spec_rhs, late)
 
     edge = (half + 16, WIDE)
 
@@ -680,15 +671,17 @@
             spectrum, scale, aligned_inverse
         )
         above, below = from_lat(down, 1), from_lat(up, -1)
-        return scaled, part, scale, above, below, staggered_inverse, stag_below, flags
+        return scaled, part, scale, above, below, stag, stag_below, flags
 
     pieces = blocks(spec_rhs)
     flat = call(
-        lambda *r: coefficients_kernel(groups, length, *r), [wide] * 5, name="coefficients"
+        lambda *r: coefficients_kernel(groups, length, *r), [wide] * 3, name="coefficients"
     )(slab, after(spec_rhs, pieces[0]))
     late = after(late, *flat)
     filtered = exchanged(
-        call(lambda *r: halo_kernel(norm, *r), wide, [(rows, 128)] * 2, name="halo")(*pieces, late)
+        call(
+            lambda *r: halo_kernel(norm, *r), (rows, 2 * WIDE), [(rows, 128)] * 2, name="halo"
+        )(*pieces, late)
     )
     spec, first, image, sums = call(
         lambda *r: step_kernel(groups, length, *r),
@@ -702,23 +695,32 @@
     first_cells, aside = call(
         lambda *r: unpack_first_kernel(length, cut, *r), [cells, wide], name="unpack_first"
     )(after(spec_image, pieces[0]), image)
-    summed, sums = call(
-        lambda *r: sums_kernel(norm, length, *r), [wide, (8, 128)], name="sums"
-    )(*pieces, spec_image, aside, sums)
-
+    filtered = exchanged(
+        call(lambda *r: sums_kernel(norm, length, *r), wide, name="sums")(
+            *pieces, spec_image, aside, sums
+        )
+    )
+
+    sums = call(gather_kernel, (8, 128), name="gather")(filtered)
     pair = sums + from_lat(sums, -1)
     three = pair + from_lat(sums, 1)
-    others, last_pair = from_lat(three, 3), from_lat(pair, -2)
-    filtered = exchanged(summed)
     image_cells = call(
         lambda *r: unpack_kernel(length, image_cut, *r), cells, name="unpack_image"
     )(filtered)
     packed = call(lambda *r: last_kernel(groups, length, *r), wide, name="last")(
-        filtered, flat[0], first, image, three, others, last_pair, matrices, twiddle
-    )
+        filtered, flat[0], first, image, matrices, twiddle
+    )
+    packed, three, pair = lax.optimization_barrier((packed, three, pair, image_cells))[:3]
     return tuple(
         call(lambda *r: finish_kernel(length, *r), [cells] * 3, name="finish")(
-            exchanged(packed), first_cells, image_cells, surface_forcing, ocean_mask
+            exchanged(packed),
+            first_cells,
+            image_cells,
+            surface_forcing,
+            ocean_mask,
+            three,
+            from_lat(three, 3),
+            from_lat(pair, -2),
         )
     )
 

time: 119 us -> 116 us (0.975)
  blocking collectives: 25.3 us -> 42.1 us
  starting transfers between devices: 44.5 us -> 32.7 us
  waiting for transfers between devices: 34.7 us -> 26.9 us
    all_to_all x2 -> x3, blocking collectives: 25.3 us -> 42.1 us  [exchanged(): lax.all_to_all(parts, LON, split_axis=0, concat_axis=0, tiled=True)]
    all_to_all x4 -> x3, starting transfers between devices: 31.9 us -> 20.6 us  [exchanged(): lax.all_to_all(parts, LON, split_axis=0, concat_axis=0, tiled=True)]
    all_to_all x4 -> x3, waiting for transfers between devices: 15.2 us -> 7.01 us  [exchanged(): lax.all_to_all(parts, LON, split_axis=0, concat_axis=0, tiled=True)]
    pallas_call x5 -> x7, Pallas kernels: 3.79 us -> 3.12 us  [the longest x1 1.13 us: local(): call(lambda *r: forward_kernel(groups, *r), wide, transforms, name='forwa...]
  transfers between devices with their start and end apart: 15 -> 14, of which waited for: 13 -> 13; matrix products, arithmetic and copies ran while one was open for 1% -> 1% of each run, Pallas kernels for 1% -> 2%
where the time goes in v4:
time: 116 us; the launch traced here: 115 us
  blocking collectives  42.1 us (36%)
  starting transfers between devices  32.7 us (28%)
  waiting for transfers between devices  26.9 us (23%)
  Pallas kernels  9.46 us (8%)
  local copies, waits for them, and re-layouts  1.5 us (1%)
  other arithmetic  1.27 us (1%)
    all_to_all x3, blocking collectives, exchanged(): lax.all_to_all(parts, LON, split_axis=0, concat_axis=0, tiled=True)  42.1 us
    all_to_all x3, starting transfers between devices, exchanged(): lax.all_to_all(parts, LON, split_axis=0, concat_axis=0, tiled=True)  20.6 us
    ppermute x11, waiting for transfers between devices, from_lat(): lax.ppermute(value, 'lat', [((d + steps) % count, d) for d in range(count)])  19.9 us
    ppermute x11, starting transfers between devices, from_lat(): lax.ppermute(value, 'lat', [((d + steps) % count, d) for d in range(count)])  12.2 us
    all_to_all x3, waiting for transfers between devices, exchanged(): lax.all_to_all(parts, LON, split_axis=0, concat_axis=0, tiled=True)  7.01 us
    pallas_call x1, Pallas kernels, local(): call(lambda *r: step_kernel(groups, length, *r), [wide, wide, wide, (8, 1...  2.41 us
  transfers between devices with their start and end apart: 14, of which 13 were waited for; matrix products, arithmetic and copies ran while one was open for 1% of the time, Pallas kernels for 2%

profile of v4, /device:TPU:1, one launch (start us, length us, event | category | flops | bytes accessed | tf_op | source)
XLA Modules:
  0.0 114.9 jit_solution(14542918637853161755)
XLA Ops:
  0.6 1.1 convert_multiply_fusion
  1.7 0.8 pack.1
  2.5 8.7 %all-to-all-start = ((f32[32,8,256]{2,1,0:T(8,128)}), f32[32,8,256]{2,1,0:T(8,128)S(1)}, u32[]{:S(2)}, u32[]{:S(2)}) async-start(f32[32,8,256]{2,1,0:T(8,128)} %bitcast), calls=%async_computation | async-start | bytes 524288 | tf_op jit(solution)/shard_map/all_to_all | solution.py:597
  11.3 1.7 %collective-permute-start = (f32[128,128]{1,0:T(8,128)S(1)}, f32[128,128]{1,0:T(8,128)S(1)}, u32[]{:S(2)}, u32[]{:S(2)}) collective-permute-start(f32[128,128]{1,0:T(8,128)S(1)} %slice_bitcast_fusion), channel_id=1, source_target_pairs={{224,0},{0,32},{32,64},{64,96},{96,128},{128,160},{160,192},{192,2... | collective-permute-start | bytes 196616 | tf_op jit(solution)/shard_map/ppermute | solution.py:602
  13.0 0.8 constant_dynamic-slice_fusion
  13.8 0.1 add_rsqrt_fusion.scale_ref.r_2_
  13.9 0.1 broadcast_select_fusion.flags_ref.r_7_
  14.0 0.7 copy-done.1
  14.7 0.1 edges.1
  14.9 0.1 pack_more.1.r_1_
  15.0 4.3 %collective-permute-done.r_6_ = f32[128,128]{1,0:T(8,128)S(1)} collective-permute-done((f32[128,128]{1,0:T(8,128)S(1)}, f32[128,128]{1,0:T(8,128)S(1)}, u32[]{:S(2)}, u32[]{:S(2)}) %collective-permute-start) | collective-permute-done | bytes 65568 | tf_op jit(solution)/shard_map/ppermute | solution.py:602
  19.3 1.0 all-to-all-done
  20.3 1.1 forward.1
  21.4 6.8 %all-to-all-start.1 = ((f32[32,8,256]{2,1,0:T(8,128)}), f32[32,8,256]{2,1,0:T(8,128)S(1)}, u32[]{:S(2)}, u32[]{:S(2)}) async-start(f32[32,8,256]{2,1,0:T(8,128)} %bitcast.4), calls=%async_computation.1 | async-start | bytes 524288 | tf_op jit(solution)/shard_map/all_to_all | solution.py:597
  28.2 2.6 %collective-permute-start.1 = (f32[8,256]{1,0:T(8,128)S(1)}, f32[8,256]{1,0:T(8,128)S(1)}, u32[]{:S(2)}, u32[]{:S(2)}) collective-permute-start(f32[8,256]{1,0:T(8,128)S(1)} %get-tuple-element.45), channel_id=1, source_target_pairs={{32,0},{64,32},{96,64},{128,96},{160,128},{192,160},{224,192},{0,2... | collective-permute-start | bytes 24584 | tf_op jit(solution)/shard_map/ppermute | solution.py:602
  30.8 0.8 collective-permute-done.1.wet_above_ref
  31.6 3.2 %collective-permute-done.2.top_below_ref = f32[8,256]{1,0:T(8,128)S(1)} collective-permute-done((f32[8,256]{1,0:T(8,128)S(1)}, f32[8,256]{1,0:T(8,128)S(1)}, u32[]{:S(2)}, u32[]{:S(2)}) %collective-permute-start.2) | collective-permute-done | bytes 8224 | tf_op jit(solution)/shard_map/ppermute | solution.py:602
  34.8 0.4 pack_rest.1.r_8_
  35.1 2.0 %all-to-all-done.1 = f32[32,8,256]{2,1,0:T(8,128)S(1)} async-done(((f32[32,8,256]{2,1,0:T(8,128)}), f32[32,8,256]{2,1,0:T(8,128)S(1)}, u32[]{:S(2)}, u32[]{:S(2)}) %all-to-all-start.1) | async-done | bytes 262176 | tf_op jit(solution)/shard_map/all_to_all | solution.py:597
  37.1 0.3 blocks.2
  37.4 2.7 %collective-permute-start.3 = (f32[80,256]{1,0:T(8,128)S(1)}, f32[80,256]{1,0:T(8,128)S(1)}, u32[]{:S(2)}, u32[]{:S(2)}) collective-permute-start(f32[80,256]{1,0:T(8,128)S(1)} %get-tuple-element.50), channel_id=1, source_target_pairs={{32,0},{64,32},{96,64},{128,96},{160,128},{192,160},{224,192},{0,2... | collective-permute-start | bytes 245768 | tf_op jit(solution)/shard_map/ppermute | solution.py:602
  40.1 0.5 coefficients.1
  40.7 1.1 collective-permute-done.3.r_3_
  41.8 2.8 %collective-permute-done.4.r_4_ = f32[80,256]{1,0:T(8,128)S(1)} collective-permute-done((f32[80,256]{1,0:T(8,128)S(1)}, f32[80,256]{1,0:T(8,128)S(1)}, u32[]{:S(2)}, u32[]{:S(2)}) %collective-permute-start.4) | collective-permute-done | bytes 81952 | tf_op jit(solution)/shard_map/ppermute | solution.py:602
  44.6 0.4 halo.1
  45.1 16.7 %all_to_all.30 = f32[32,8,512]{2,1,0:T(8,128)S(1)} all-to-all(f32[32,8,512]{2,1,0:T(8,128)S(1)} %bitcast.27), channel_id=1, replica_groups=mesh['lat'=8,'lon_0'=4,'lon_1'=4,'lon_2'=2] {'lon_0','lon_1','lon_2'}, dimensions={0} | all-to-all | bytes 1048576 | tf_op jit(solution)/shard_map/all_to_all | solution.py:597
  61.8 2.4 %step.1 = (f32[256,256]{1,0:T(8,128)S(1)}, f32[256,256]{1,0:T(8,128)S(1)}, f32[256,256]{1,0:T(8,128)S(1)}, f32[8,128]{1,0:T(8,128)S(1)}) custom-call(f32[256,512]{1,0:T(8,128)S(1)} %bitcast.26, f32[256,256]{1,0:T(8,128)S(1)} %bitcast.17, f32[256,256]{1,0:T(8,128)S(1)} %get-tuple-element.53.r_2_.r_1_, f32[256,256]{1,0:T(8,128)S(1)} %get-tuple-element.54.r_3_, ...), custom_call_target="tpu_custom_call" | custom-call | tf_op jit(solution)/shard_map/step/pallas_call | solution.py:686
  64.2 12.4 %all_to_all.31 = f32[32,8,256]{2,1,0:T(8,128)S(1)} all-to-all(f32[32,8,256]{2,1,0:T(8,128)S(1)} %bitcast.30), channel_id=1, replica_groups=mesh['lat'=8,'lon_0'=4,'lon_1'=4,'lon_2'=2] {'lon_0','lon_1','lon_2'}, dimensions={0} | all-to-all | bytes 524288 | tf_op jit(solution)/shard_map/all_to_all | solution.py:597
  76.6 0.3 blocks.3
  76.9 0.1 collective-permute-start.5
  77.0 1.5 %collective-permute-start.6 = (f32[80,256]{1,0:T(8,128)S(1)}, f32[80,256]{1,0:T(8,128)S(1)}, u32[]{:S(2)}, u32[]{:S(2)}) collective-permute-start(f32[80,256]{1,0:T(8,128)S(1)} %get-tuple-element.61), channel_id=1, source_target_pairs={{224,0},{0,32},{32,64},{64,96},{96,128},{128,160},{160,192},{192,2... | collective-permute-start | bytes 245768 | tf_op jit(solution)/shard_map/ppermute | solution.py:602
  78.4 0.2 unpack_first.1
  78.6 2.2 %collective-permute-done.5.r_3_ = f32[80,256]{1,0:T(8,128)S(1)} collective-permute-done((f32[80,256]{1,0:T(8,128)S(1)}, f32[80,256]{1,0:T(8,128)S(1)}, u32[]{:S(2)}, u32[]{:S(2)}) %collective-permute-start.5) | collective-permute-done | bytes 81952 | tf_op jit(solution)/shard_map/ppermute | solution.py:602
  80.8 1.3 %collective-permute-done.6.r_4_ = f32[80,256]{1,0:T(8,128)S(1)} collective-permute-done((f32[80,256]{1,0:T(8,128)S(1)}, f32[80,256]{1,0:T(8,128)S(1)}, u32[]{:S(2)}, u32[]{:S(2)}) %collective-permute-start.6) | collective-permute-done | bytes 81952 | tf_op jit(solution)/shard_map/ppermute | solution.py:602
  82.1 0.5 sums.1
  82.6 13.1 %all_to_all.32 = f32[32,8,256]{2,1,0:T(8,128)S(1)} all-to-all(f32[32,8,256]{2,1,0:T(8,128)S(1)} %bitcast.29), channel_id=1, replica_groups=mesh['lat'=8,'lon_0'=4,'lon_1'=4,'lon_2'=2] {'lon_0','lon_1','lon_2'}, dimensions={0} | all-to-all | bytes 524288 | tf_op jit(solution)/shard_map/all_to_all | solution.py:597
  95.7 0.3 collective-permute-start.8
  96.0 1.5 %collective-permute-start.7 = (f32[8,128]{1,0:T(8,128)S(1)}, f32[8,128]{1,0:T(8,128)S(1)}, u32[]{:S(2)}, u32[]{:S(2)}) collective-permute-start(f32[8,128]{1,0:T(8,128)S(1)} %gather.1), channel_id=1, source_target_pairs={{224,0},{0,32},{32,64},{64,96},{96,128},{128,160},{160,192},{192,2... | collective-permute-start | bytes 12296 | tf_op jit(solution)/shard_map/ppermute | solution.py:602
  97.5 0.1 unpack_image.1.r_2_
  97.6 1.2 %last.1 = f32[256,256]{1,0:T(8,128)} custom-call(f32[256,256]{1,0:T(8,128)S(1)} %bitcast.23, f32[256,256]{1,0:T(8,128)S(1)} %get-tuple-element.53.r_2_.r_1_, f32[256,256]{1,0:T(8,128)S(1)} %get-tuple-element.66.r_2_, f32[256,256]{1,0:T(8,128)S(1)} %get-tuple-element.63.r_1_.r_3_, bf16[2,2,256,256]{3,2,1,0:T(8,128)(2,1)S(1)} %copy-done, ...), custom_call_target="tpu_custom_call" | custom-call | tf_op jit(solution)/shard_map/last/pallas_call | solution.py:710
  98.8 1.0 collective-permute-done.7
  99.8 5.1 %all-to-all-start.5 = ((f32[32,8,256]{2,1,0:T(8,128)}), f32[32,8,256]{2,1,0:T(8,128)S(1)}, u32[]{:S(2)}, u32[]{:S(2)}) async-start(f32[32,8,256]{2,1,0:T(8,128)} %bitcast.12), calls=%async_computation.5 | async-start | bytes 524288 | tf_op jit(solution)/shard_map/all_to_all | solution.py:597
  104.9 0.5 collective-permute-start.10
  105.4 1.3 %collective-permute-start.9 = (f32[8,128]{1,0:T(8,128)S(1)}, f32[8,128]{1,0:T(8,128)S(1)}, u32[]{:S(2)}, u32[]{:S(2)}) collective-permute-start(f32[8,128]{1,0:T(8,128)S(1)} %get-tuple-element.69.r_5_), channel_id=1, source_target_pairs={{96,0},{128,32},{160,64},{192,96},{224,128},{0,160},{32,192},{64,2... | collective-permute-start | bytes 12296 | tf_op jit(solution)/shard_map/ppermute | solution.py:602
  106.8 2.8 %collective-permute-done.10.r_7_ = f32[8,128]{1,0:T(8,128)S(1)} collective-permute-done((f32[8,128]{1,0:T(8,128)S(1)}, f32[8,128]{1,0:T(8,128)S(1)}, u32[]{:S(2)}, u32[]{:S(2)}) %collective-permute-start.10) | collective-permute-done | bytes 4128 | tf_op jit(solution)/shard_map/ppermute | solution.py:602
  109.5 0.4 collective-permute-done.9.r_6_
  110.0 4.0 %all-to-all-done.5 = f32[32,8,256]{2,1,0:T(8,128)S(1)} async-done(((f32[32,8,256]{2,1,0:T(8,128)}), f32[32,8,256]{2,1,0:T(8,128)S(1)}, u32[]{:S(2)}, u32[]{:S(2)}) %all-to-all-start.5) | async-done | bytes 262176 | tf_op jit(solution)/shard_map/all_to_all | solution.py:597
  114.0 1.0 finish.1
  (27 shorter events, 0.1 us)
Async XLA Ops:
  2.5 8.7 %copy-start.2 = (f32[2,128,128]{2,1,0:T(8,128)S(1)}, f32[2,128,128]{2,1,0:T(8,128)}, u32[]{:S(2)}) copy-start(f32[2,128,128]{2,1,0:T(8,128)} %r_5_.3) | copy-start | bytes 393220
  2.5 17.7 %all-to-all-start = ((f32[32,8,256]{2,1,0:T(8,128)}), f32[32,8,256]{2,1,0:T(8,128)S(1)}, u32[]{:S(2)}, u32[]{:S(2)}) async-start(f32[32,8,256]{2,1,0:T(8,128)} %bitcast), calls=%async_computation | async-start | bytes 524288 | tf_op jit(solution)/shard_map/all_to_all | solution.py:597
  11.3 8.0 %collective-permute-start = (f32[128,128]{1,0:T(8,128)S(1)}, f32[128,128]{1,0:T(8,128)S(1)}, u32[]{:S(2)}, u32[]{:S(2)}) collective-permute-start(f32[128,128]{1,0:T(8,128)S(1)} %slice_bitcast_fusion), channel_id=1, source_target_pairs={{224,0},{0,32},{32,64},{64,96},{96,128},{128,160},{160,192},{192,2... | collective-permute-start | bytes 196616 | tf_op jit(solution)/shard_map/ppermute | solution.py:602
  13.0 0.8 copy-start.9
  13.0 1.0 copy-start.5
  13.8 0.9 copy-start.1
  13.8 1.0 copy-start.4
  13.9 6.3 %copy-start = (bf16[2,2,256,256]{3,2,1,0:T(8,128)(2,1)S(1)}, bf16[2,2,256,256]{3,2,1,0:T(8,128)(2,1)}, u32[]{:S(2)}) copy-start(bf16[2,2,256,256]{3,2,1,0:T(8,128)(2,1)} %constant.45.clone.r_2_.r_5_.r_4_) | copy-start | bytes 1572868
  14.8 5.4 %copy-start.3 = (f32[2,32,256]{2,1,0:T(8,128)S(1)}, f32[2,32,256]{2,1,0:T(8,128)}, u32[]{:S(2)}) copy-start(f32[2,32,256]{2,1,0:T(8,128)} %constant.46.clone.r_3_.r_6_.r_5_) | copy-start | bytes 196612
  21.4 15.8 %all-to-all-start.1 = ((f32[32,8,256]{2,1,0:T(8,128)}), f32[32,8,256]{2,1,0:T(8,128)S(1)}, u32[]{:S(2)}, u32[]{:S(2)}) async-start(f32[32,8,256]{2,1,0:T(8,128)} %bitcast.4), calls=%async_computation.1 | async-start | bytes 524288 | tf_op jit(solution)/shard_map/all_to_all | solution.py:597
  28.2 9.0 %copy-start.7 = (f32[2,128,128]{2,1,0:T(8,128)S(1)}, f32[2,128,128]{2,1,0:T(8,128)}, u32[]{:S(2)}) copy-start(f32[2,128,128]{2,1,0:T(8,128)} %aligned_ref.3) | copy-start | bytes 393220
  28.2 3.4 %collective-permute-start.1 = (f32[8,256]{1,0:T(8,128)S(1)}, f32[8,256]{1,0:T(8,128)S(1)}, u32[]{:S(2)}, u32[]{:S(2)}) collective-permute-start(f32[8,256]{1,0:T(8,128)S(1)} %get-tuple-element.45), channel_id=1, source_target_pairs={{32,0},{64,32},{96,64},{128,96},{160,128},{192,160},{224,192},{0,2... | collective-permute-start | bytes 24584 | tf_op jit(solution)/shard_map/ppermute | solution.py:602
  30.8 4.0 %collective-permute-start.2 = (f32[8,256]{1,0:T(8,128)S(1)}, f32[8,256]{1,0:T(8,128)S(1)}, u32[]{:S(2)}, u32[]{:S(2)}) collective-permute-start(f32[8,256]{1,0:T(8,128)S(1)} %get-tuple-element.46), channel_id=1, source_target_pairs={{224,0},{0,32},{32,64},{64,96},{96,128},{128,160},{160,192},{192,2... | collective-permute-start | bytes 24584 | tf_op jit(solution)/shard_map/ppermute | solution.py:602
  37.4 4.4 %collective-permute-start.3 = (f32[80,256]{1,0:T(8,128)S(1)}, f32[80,256]{1,0:T(8,128)S(1)}, u32[]{:S(2)}, u32[]{:S(2)}) collective-permute-start(f32[80,256]{1,0:T(8,128)S(1)} %get-tuple-element.50), channel_id=1, source_target_pairs={{32,0},{64,32},{96,64},{128,96},{160,128},{192,160},{224,192},{0,2... | collective-permute-start | bytes 245768 | tf_op jit(solution)/shard_map/ppermute | solution.py:602
  40.1 4.5 %collective-permute-start.4 = (f32[80,256]{1,0:T(8,128)S(1)}, f32[80,256]{1,0:T(8,128)S(1)}, u32[]{:S(2)}, u32[]{:S(2)}) collective-permute-start(f32[80,256]{1,0:T(8,128)S(1)} %get-tuple-element.51), channel_id=1, source_target_pairs={{224,0},{0,32},{32,64},{64,96},{96,128},{128,160},{160,192},{192,2... | collective-permute-start | bytes 245768 | tf_op jit(solution)/shard_map/ppermute | solution.py:602
  45.1 16.7 %copy-start.8 = (f32[2,32,32]{2,1,0:T(8,128)S(1)}, f32[2,32,32]{2,1,0:T(8,128)}, u32[]{:S(2)}) copy-start(f32[2,32,32]{2,1,0:T(8,128)} %constant.47.clone.r_7_) | copy-start | bytes 24580
  76.9 3.9 %collective-permute-start.5 = (f32[80,256]{1,0:T(8,128)S(1)}, f32[80,256]{1,0:T(8,128)S(1)}, u32[]{:S(2)}, u32[]{:S(2)}) collective-permute-start(f32[80,256]{1,0:T(8,128)S(1)} %get-tuple-element.60), channel_id=1, source_target_pairs={{32,0},{64,32},{96,64},{128,96},{160,128},{192,160},{224,192},{0,2... | collective-permute-start | bytes 245768 | tf_op jit(solution)/shard_map/ppermute | solution.py:602
  77.0 5.2 %collective-permute-start.6 = (f32[80,256]{1,0:T(8,128)S(1)}, f32[80,256]{1,0:T(8,128)S(1)}, u32[]{:S(2)}, u32[]{:S(2)}) collective-permute-start(f32[80,256]{1,0:T(8,128)S(1)} %get-tuple-element.61), channel_id=1, source_target_pairs={{224,0},{0,32},{32,64},{64,96},{96,128},{128,160},{160,192},{192,2... | collective-permute-start | bytes 245768 | tf_op jit(solution)/shard_map/ppermute | solution.py:602
  95.7 3.0 %collective-permute-start.8 = (f32[8,128]{1,0:T(8,128)S(1)}, f32[8,128]{1,0:T(8,128)S(1)}, u32[]{:S(2)}, u32[]{:S(2)}) collective-permute-start(f32[8,128]{1,0:T(8,128)S(1)} %gather.1), channel_id=1, source_target_pairs={{32,0},{64,32},{96,64},{128,96},{160,128},{192,160},{224,192},{0,2... | collective-permute-start | bytes 12296 | tf_op jit(solution)/shard_map/ppermute | solution.py:602
  96.0 3.7 %collective-permute-start.7 = (f32[8,128]{1,0:T(8,128)S(1)}, f32[8,128]{1,0:T(8,128)S(1)}, u32[]{:S(2)}, u32[]{:S(2)}) collective-permute-start(f32[8,128]{1,0:T(8,128)S(1)} %gather.1), channel_id=1, source_target_pairs={{224,0},{0,32},{32,64},{64,96},{96,128},{128,160},{160,192},{192,2... | collective-permute-start | bytes 12296 | tf_op jit(solution)/shard_map/ppermute | solution.py:602
  99.8 14.2 %copy-start.6 = (f32[135,256]{1,0:T(8,128)S(1)}, f32[135,256]{1,0:T(8,128)}, u32[]{:S(2)}) copy-start(f32[135,256]{1,0:T(8,128)} %r_3_.2) | copy-start | bytes 414724
  99.8 14.2 %all-to-all-start.5 = ((f32[32,8,256]{2,1,0:T(8,128)}), f32[32,8,256]{2,1,0:T(8,128)S(1)}, u32[]{:S(2)}, u32[]{:S(2)}) async-start(f32[32,8,256]{2,1,0:T(8,128)} %bitcast.12), calls=%async_computation.5 | async-start | bytes 524288 | tf_op jit(solution)/shard_map/all_to_all | solution.py:597
  104.9 4.7 %collective-permute-start.10 = (f32[8,128]{1,0:T(8,128)S(1)}, f32[8,128]{1,0:T(8,128)S(1)}, u32[]{:S(2)}, u32[]{:S(2)}) collective-permute-start(f32[8,128]{1,0:T(8,128)S(1)} %get-tuple-element.70), channel_id=1, source_target_pairs={{192,0},{224,32},{0,64},{32,96},{64,128},{96,160},{128,192},{160,2... | collective-permute-start | bytes 12296 | tf_op jit(solution)/shard_map/ppermute | solution.py:602
  105.4 4.6 %collective-permute-start.9 = (f32[8,128]{1,0:T(8,128)S(1)}, f32[8,128]{1,0:T(8,128)S(1)}, u32[]{:S(2)}, u32[]{:S(2)}) collective-permute-start(f32[8,128]{1,0:T(8,128)S(1)} %get-tuple-element.69.r_5_), channel_id=1, source_target_pairs={{96,0},{128,32},{160,64},{192,96},{224,128},{0,160},{32,192},{64,2... | collective-permute-start | bytes 12296 | tf_op jit(solution)/shard_map/ppermute | solution.py:602

commit v5 on v4

--- a/solution.py
+++ b/solution.py
@@ -144,21 +144,25 @@
     out_ref[...] = tall[...].T
 
 
-def edges_kernel(mask_ref, north_ref, wet_ref, top_ref, tall):
+def edges_kernel(mask_ref, north_ref, stag_ref, wet_ref, low_ref, tall):
     length, rows = mask_ref.shape
+    count, block = stag_ref.shape[0], stag_ref.shape[1]
     tall[length:, :] = jnp.zeros((WIDE - length, 128), jnp.float32)
     tall[:length, :] = mask_ref[:, :128].astype(jnp.float32)
     wet_ref[...] = tall[...].T[:ROWS]
     tall[:length, :] = mask_ref[:, rows - 128 :].astype(jnp.float32) * north_ref[:, rows - 128 :]
-    top_ref[...] = tall[...].T[128 - ROWS :]
+    top = tall[...].T[127:]
+    low_ref[:block, :] = stag_ref[count - 1]
+    row = sublanes((ROWS, 128))
+    low_ref[block:, :] = jnp.where(row == 0, top[:, :128], top[:, 128:])
 
 
 def lane_plan(length):
     cut = WIDE - length
+    count = 2 * cut - length
     north = LATE
-    south = north + length
-    east = south + length
-    return cut, 2 * cut - length, north, south, east
+    east = north + length
+    return cut, count, north, east, east + length - count
 
 
 def pack_more_kernel(own_ref, mask_ref, east_ref, out_ref, tall):
@@ -171,22 +175,48 @@
 
 
 def pack_rest_kernel(
-    mask_ref, east_ref, north_ref, flags_ref, wet_above_ref, top_below_ref, out_ref, tall
+    mask_ref,
+    east_ref,
+    north_ref,
+    flags_ref,
+    wet_above_ref,
+    from_below_ref,
+    out_ref,
+    tall,
+    aside,
+    low,
+    high,
+    last,
 ):
     length, rows = mask_ref.shape
-    _, count, n_at, s_at, e_at = lane_plan(length)
+    _, count, n_at, e_at, f_at = lane_plan(length)
+    block = from_below_ref.shape[0] - ROWS
     lane = lanes((length, rows))
     wet = mask_ref[...].astype(jnp.float32)
     north = wet * north_ref[...]
     wet_above = wet_above_ref[...].T[:length, :1] * flags_ref[:1, :1]
-    top_below = top_below_ref[...].T[:length, ROWS - 1 :] * flags_ref[1:2, :1]
+    top = from_below_ref[block:, :].T
+    top_below = jnp.concatenate([top[:, :1], top[: length - 128, 1:2]], axis=0) * flags_ref[1:2, :1]
     tall[128:n_at, :] = jnp.zeros((n_at - 128, rows), jnp.float32)
-    tall[n_at:s_at, :] = north * jnp.where(lane == rows - 1, wet_above, shifted(wet, -1))
-    tall[s_at:e_at, :] = wet * jnp.where(lane == 0, top_below, shifted(north, 1))
-    tall[e_at : e_at + length - count, :] = (wet * east_ref[...])[count:]
-    unused = 2 * WIDE - (e_at + length - count)
-    tall[2 * WIDE - unused :, :] = jnp.zeros((unused, rows), jnp.float32)
-    out_ref[...] = tall[128:, :].T
+    tall[n_at:e_at, :] = north * jnp.where(lane == rows - 1, wet_above, shifted(wet, -1))
+    tall[e_at:f_at, :] = (wet * east_ref[...])[count:]
+    tall[f_at:, :] = jnp.zeros((WIDE + 128 - f_at, rows), jnp.float32)
+    out_ref[:, :128] = tall[128:WIDE, :].T
+    last[...] = tall[WIDE:, :].T
+    aside[length:, :] = jnp.zeros((WIDE - length, rows), jnp.float32)
+    aside[:length, :] = wet * jnp.where(lane == 0, top_below, shifted(north, 1))
+    low[...] = aside[:128, :].T
+    high[...] = aside[128:, :].T
+    groups = rows // ROWS
+    at = pl.ds(0, groups, stride=ROWS)
+    before = jnp.concatenate([low[at, :], high[at, :]], axis=1)
+    fold = f_at - WIDE
+    lane = lanes((groups, 128))
+    for n in range(ROWS):
+        at = pl.ds(n, groups, stride=ROWS)
+        piece = shifted(before, fold - n * (128 - fold))[:, :128]
+        last[at, :] = jnp.where(lane >= fold, piece, last[at, :])
+    out_ref[:, 128:] = last[...]
 
 
 def coefficients_kernel(groups, length, slab_ref, second_ref, own_ref, next_ref, east_ref):
@@ -288,7 +318,7 @@
     count, block = stag_ref.shape[0], stag_ref.shape[1]
     half, rows = block // 2, count * block
     before = flags_ref[1:2, :] * dot(
-        stag_below_ref[...],
+        stag_below_ref[:block, :],
         jnp.concatenate([below_ref[:half, :], scaled_ref[:half, :]], axis=0),
     )
     upper = above_ref[:half, :] * flags_ref[:1, :]
@@ -430,6 +460,7 @@
     low,
     high,
     tail,
+    folded,
 ):
     lane_row = lanes((groups, WIDE))
     stride = 3 * ROWS
@@ -461,8 +492,17 @@
         first_ref[rows_of(p), :] = v
         low[stride * p + ROWS : stride * p + 2 * ROWS, :] = v[:, :128]
         high[stride * p + ROWS : stride * p + 2 * ROWS, :] = v[:, 128:]
-    lane = lanes((ROWS, WIDE))
-    _, count, n_at, s_at, e_at = lane_plan(length)
+    lane, row = lanes((ROWS, WIDE)), sublanes((ROWS, WIDE))
+    _, count, n_at, e_at, f_at = lane_plan(length)
+    tail[...] = spec_ref[:, WIDE:]
+    fold, blank = f_at - WIDE, jnp.zeros((groups, 128), jnp.float32)
+    width = 128 - fold
+    before = jnp.zeros((groups, WIDE), jnp.float32)
+    for n in range(ROWS):
+        piece = jnp.concatenate([tail[pl.ds(n, groups, stride=ROWS), :], blank], axis=1)
+        inside = (lane_row >= n * width) & (lane_row < (n + 1) * width)
+        before = jnp.where(inside, shifted(piece, n * width - fold), before)
+    folded[...] = before
     rz = jnp.zeros((ROWS, WIDE), jnp.float32)
     curvature = jnp.zeros((ROWS, WIDE), jnp.float32)
     images, fluxes = [], []
@@ -471,7 +511,7 @@
         v = first_ref[at, :]
         after = first_ref[rows_of((p + 1) % groups), 0:1]
         east = jnp.where(
-            lane < count, east_ref[at, :], shifted(spec_ref[at, WIDE:], count - (e_at - WIDE))
+            lane < count, east_ref[at, :], shifted(spec_ref[at, 128:], count - (e_at - 128))
         )
         flux = v - shifted(jnp.where(lane == length, after, v), -1)
         fluxes.append(jnp.where(lane < length, east * next_ref[at, :] * flux, 0.0))
@@ -482,8 +522,8 @@
         flux = fluxes[p]
         own = own_ref[at, :]
         base = stride * p + ROWS
-        north = shifted(spec_ref[at, 128 : 128 + WIDE], 128 - n_at)
-        south = shifted(spec_ref[at, WIDE:], WIDE - s_at)
+        north = shifted(spec_ref[at, 128:], 128 - n_at)
+        south = jnp.where(row == 0, folded[p : p + 1, :], pltpu.roll(north, 1, 0))
         image = jnp.where(own > 0.0, own, 1.0) * v
         image = image + (flux - shifted(jnp.where(lane == WIDE - 1, before, flux), 1))
         image = image + north * (v - neighbour(base + 1))
@@ -635,11 +675,10 @@
     mask, east_cells, north_cells, weights, stag = lax.optimization_barrier(
         (ocean_mask, east_coupling, north_coupling, zonal_weight, staggered_inverse, packed)
     )[:-1]
-    stag_below = from_lat(stag[count - 1], -1)
     more = call(pack_more_kernel, wide, [wide], name="pack_more")(own_cells, mask, east_cells)
-    wet_first, top_last = call(
-        edges_kernel, [(ROWS, WIDE)] * 2, [(WIDE, 128)], name="edges"
-    )(mask, north_cells)
+    wet_first, low_last = call(
+        edges_kernel, [(ROWS, WIDE), (block + ROWS, 128)], [(WIDE, 128)], name="edges"
+    )(mask, north_cells, stag)
     scale = lax.rsqrt(1.0 + weights[:, None] * lax.dynamic_slice_in_dim(wave, channel, 1, 0))
     lat = lax.axis_index("lat")
     flag_row = lax.broadcasted_iota(jnp.int32, (8, WIDE), 0)
@@ -652,16 +691,20 @@
         )
     )
     flags = jnp.where(flag_row == 0, north_of, jnp.where(flag_row == 1, south_of, weight))
-    slab = after(slab, stag_below, scale, flags, wet_first)
+    slab = after(slab, scale, flags, wet_first)
     spectrum = call(lambda *r: forward_kernel(groups, *r), wide, transforms, name="forward")(
         slab, more, matrices, twiddle
     )
     spec_rhs = exchanged(spectrum)
 
-    wet_first, top_last = lax.optimization_barrier((wet_first, top_last, spectrum))[:2]
-    late = call(pack_rest_kernel, (rows, WIDE + 128), [(2 * WIDE, rows)], name="pack_rest")(
-        mask, east_cells, north_cells, flags, from_lat(wet_first, 1), from_lat(top_last, -1)
-    )
+    wet_first, low_last = lax.optimization_barrier((wet_first, low_last, spectrum))[:2]
+    stag_below = from_lat(low_last, -1)
+    late = call(
+        pack_rest_kernel,
+        wide,
+        [(WIDE + 128, rows), wide, (rows, 128), (rows, 128), (rows, 128)],
+        name="pack_rest",
+    )(mask, east_cells, north_cells, flags, from_lat(wet_first, 1), stag_below)
     spec_rhs = after(spec_rhs, late)
 
     edge = (half + 16, WIDE)
@@ -680,13 +723,13 @@
     late = after(late, *flat)
     filtered = exchanged(
         call(
-            lambda *r: halo_kernel(norm, *r), (rows, 2 * WIDE), [(rows, 128)] * 2, name="halo"
+            lambda *r: halo_kernel(norm, *r), (rows, WIDE + 128), [(rows, 128)] * 2, name="halo"
         )(*pieces, late)
     )
     spec, first, image, sums = call(
         lambda *r: step_kernel(groups, length, *r),
         [wide, wide, wide, (8, 128)],
-        transforms + [(3 * rows, 128)] * 2 + [(rows, 128)],
+        transforms + [(3 * rows, 128)] * 2 + [(rows, 128), (groups, WIDE)],
         name="step",
     )(filtered, slab, *flat, matrices, twiddle, outer)
     spec_image = exchanged(spec)

time: 116 us -> 114 us (0.983)
  waiting for transfers between devices: 26.9 us -> 23.4 us
  starting transfers between devices: 32.7 us -> 35.3 us
    ppermute x11 -> x10, waiting for transfers between devices: 19.9 us -> 13.2 us  [from_lat(): lax.ppermute(value, 'lat', [((d + steps) % count, d) for d in range(count)])]
    ppermute x11 -> x10, starting transfers between devices: 12.2 us -> 17.9 us  [from_lat(): lax.ppermute(value, 'lat', [((d + steps) % count, d) for d in range(count)])]
    all_to_all x3, starting transfers between devices: 20.6 us -> 17.4 us  [exchanged(): lax.all_to_all(parts, LON, split_axis=0, concat_axis=0, tiled=True)]
    all_to_all x3, waiting for transfers between devices: 7.01 us -> 10.2 us  [exchanged(): lax.all_to_all(parts, LON, split_axis=0, concat_axis=0, tiled=True)]
    all_to_all x3, blocking collectives: 42.1 us -> 41 us  [exchanged(): lax.all_to_all(parts, LON, split_axis=0, concat_axis=0, tiled=True)]
  transfers between devices with their start and end apart: 14 -> 13, of which waited for: 13 -> 12; matrix products, arithmetic and copies ran while one was open for 1% -> 1% of each run, Pallas kernels for 2% -> 2%
where the time goes in v5:
time: 114 us
  blocking collectives  41 us (36%)
  starting transfers between devices  35.3 us (31%)
  waiting for transfers between devices  23.4 us (21%)
  Pallas kernels  9.63 us (8%)
  local copies, waits for them, and re-layouts  2.18 us (2%)
  other arithmetic  1.27 us (1%)
    all_to_all x3, blocking collectives, exchanged(): lax.all_to_all(parts, LON, split_axis=0, concat_axis=0, tiled=True)  41 us
    ppermute x10, starting transfers between devices, from_lat(): lax.ppermute(value, 'lat', [((d + steps) % count, d) for d in range(count)])  17.9 us
    all_to_all x3, starting transfers between devices, exchanged(): lax.all_to_all(parts, LON, split_axis=0, concat_axis=0, tiled=True)  17.4 us
    ppermute x10, waiting for transfers between devices, from_lat(): lax.ppermute(value, 'lat', [((d + steps) % count, d) for d in range(count)])  13.2 us
    all_to_all x3, waiting for transfers between devices, exchanged(): lax.all_to_all(parts, LON, split_axis=0, concat_axis=0, tiled=True)  10.2 us
    pallas_call x1, Pallas kernels, local(): call(lambda *r: step_kernel(groups, length, *r), [wide, wide, wide, (8, 1...  2.39 us
  transfers between devices with their start and end apart: 13, of which 12 were waited for; matrix products, arithmetic and copies ran while one was open for 1% of the time, Pallas kernels for 2%

profile of v5, /device:TPU:1, one launch (start us, length us, event | category | flops | bytes accessed | tf_op | source)
XLA Modules:
  0.0 113.6 jit_solution(10931121234362030026)
XLA Ops:
  0.6 1.1 convert_multiply_fusion
  1.7 0.8 pack.1
  2.5 8.7 %all-to-all-start = ((f32[32,8,256]{2,1,0:T(8,128)}), f32[32,8,256]{2,1,0:T(8,128)S(1)}, u32[]{:S(2)}, u32[]{:S(2)}) async-start(f32[32,8,256]{2,1,0:T(8,128)} %bitcast), calls=%async_computation | async-start | bytes 524288 | tf_op jit(solution)/shard_map/all_to_all | solution.py:637
  11.3 0.1 broadcast_select_fusion.flags_ref.r_7_
  11.4 0.7 constant_dynamic-slice_fusion
  12.1 0.1 pack_more.1.r_1_
  12.3 0.7 copy-done.2
  13.0 0.1 edges.1
  13.1 0.7 copy-done.9
  13.8 0.1 add_rsqrt_fusion.scale_ref.r_2_
  13.9 6.3 %all-to-all-done = f32[32,8,256]{2,1,0:T(8,128)S(1)} async-done(((f32[32,8,256]{2,1,0:T(8,128)}), f32[32,8,256]{2,1,0:T(8,128)S(1)}, u32[]{:S(2)}, u32[]{:S(2)}) %all-to-all-start) | async-done | bytes 262176 | tf_op jit(solution)/shard_map/all_to_all | solution.py:637
  20.3 1.1 forward.1
  21.4 3.7 %all-to-all-start.1 = ((f32[32,8,256]{2,1,0:T(8,128)}), f32[32,8,256]{2,1,0:T(8,128)S(1)}, u32[]{:S(2)}, u32[]{:S(2)}) async-start(f32[32,8,256]{2,1,0:T(8,128)} %bitcast.3), calls=%async_computation.1 | async-start | bytes 524288 | tf_op jit(solution)/shard_map/all_to_all | solution.py:637
  25.1 1.7 %collective-permute-start.1 = (f32[136,128]{1,0:T(8,128)S(1)}, f32[136,128]{1,0:T(8,128)S(1)}, u32[]{:S(2)}, u32[]{:S(2)}) collective-permute-start(f32[136,128]{1,0:T(8,128)S(1)} %get-tuple-element.46), channel_id=1, source_target_pairs={{224,0},{0,32},{32,64},{64,96},{96,128},{128,160},{160,192},{192,2... | collective-permute-start | bytes 208904 | tf_op jit(solution)/shard_map/ppermute | solution.py:642
  26.8 4.0 %collective-permute-start = (f32[8,256]{1,0:T(8,128)S(1)}, f32[8,256]{1,0:T(8,128)S(1)}, u32[]{:S(2)}, u32[]{:S(2)}) collective-permute-start(f32[8,256]{1,0:T(8,128)S(1)} %get-tuple-element.45), channel_id=1, source_target_pairs={{32,0},{64,32},{96,64},{128,96},{160,128},{192,160},{224,192},{0,2... | collective-permute-start | bytes 24584 | tf_op jit(solution)/shard_map/ppermute | solution.py:642
  30.9 0.8 collective-permute-done.wet_above_ref
  31.6 1.4 %collective-permute-done.1.from_below_ref.r_6_ = f32[136,128]{1,0:T(8,128)S(1)} collective-permute-done((f32[136,128]{1,0:T(8,128)S(1)}, f32[136,128]{1,0:T(8,128)S(1)}, u32[]{:S(2)}, u32[]{:S(2)}) %collective-permute-start.1) | collective-permute-done | bytes 69664 | tf_op jit(solution)/shard_map/ppermute | solution.py:642
  33.0 0.6 pack_rest.1.r_8_
  33.6 0.6 all-to-all-done.1
  34.2 0.3 blocks.2
  34.5 5.7 %collective-permute-start.2 = (f32[80,256]{1,0:T(8,128)S(1)}, f32[80,256]{1,0:T(8,128)S(1)}, u32[]{:S(2)}, u32[]{:S(2)}) collective-permute-start(f32[80,256]{1,0:T(8,128)S(1)} %get-tuple-element.50), channel_id=1, source_target_pairs={{32,0},{64,32},{96,64},{128,96},{160,128},{192,160},{224,192},{0,2... | collective-permute-start | bytes 245768 | tf_op jit(solution)/shard_map/ppermute | solution.py:642
  40.1 0.5 coefficients.1
  40.7 1.1 collective-permute-done.2.r_3_
  41.8 2.8 %collective-permute-done.3.r_4_ = f32[80,256]{1,0:T(8,128)S(1)} collective-permute-done((f32[80,256]{1,0:T(8,128)S(1)}, f32[80,256]{1,0:T(8,128)S(1)}, u32[]{:S(2)}, u32[]{:S(2)}) %collective-permute-start.3) | collective-permute-done | bytes 81952 | tf_op jit(solution)/shard_map/ppermute | solution.py:642
  44.6 0.4 halo.1
  45.1 15.6 %all_to_all.30 = f32[32,8,384]{2,1,0:T(8,128)S(1)} all-to-all(f32[32,8,384]{2,1,0:T(8,128)S(1)} %bitcast.24), channel_id=1, replica_groups=mesh['lat'=8,'lon_0'=4,'lon_1'=4,'lon_2'=2] {'lon_0','lon_1','lon_2'}, dimensions={0} | all-to-all | bytes 786432 | tf_op jit(solution)/shard_map/all_to_all | solution.py:637
  60.7 2.4 %step.1 = (f32[256,256]{1,0:T(8,128)S(1)}, f32[256,256]{1,0:T(8,128)S(1)}, f32[256,256]{1,0:T(8,128)S(1)}, f32[8,128]{1,0:T(8,128)S(1)}) custom-call(f32[256,384]{1,0:T(8,128)S(1)} %bitcast.25, f32[256,256]{1,0:T(8,128)S(1)} %bitcast.21, f32[256,256]{1,0:T(8,128)S(1)} %get-tuple-element.53.r_2_.r_1_, f32[256,256]{1,0:T(8,128)S(1)} %get-tuple-element.54.r_3_, ...), custom_call_target="tpu_custom_call" | custom-call | tf_op jit(solution)/shard_map/step/pallas_call | solution.py:729
  63.1 12.3 %all_to_all.31 = f32[32,8,256]{2,1,0:T(8,128)S(1)} all-to-all(f32[32,8,256]{2,1,0:T(8,128)S(1)} %bitcast.28), channel_id=1, replica_groups=mesh['lat'=8,'lon_0'=4,'lon_1'=4,'lon_2'=2] {'lon_0','lon_1','lon_2'}, dimensions={0} | all-to-all | bytes 524288 | tf_op jit(solution)/shard_map/all_to_all | solution.py:637
  75.4 0.3 blocks.3
  75.7 0.1 collective-permute-start.4
  75.8 1.5 %collective-permute-start.5 = (f32[80,256]{1,0:T(8,128)S(1)}, f32[80,256]{1,0:T(8,128)S(1)}, u32[]{:S(2)}, u32[]{:S(2)}) collective-permute-start(f32[80,256]{1,0:T(8,128)S(1)} %get-tuple-element.61), channel_id=1, source_target_pairs={{224,0},{0,32},{32,64},{64,96},{96,128},{128,160},{160,192},{192,2... | collective-permute-start | bytes 245768 | tf_op jit(solution)/shard_map/ppermute | solution.py:642
  77.2 0.2 unpack_first.1
  77.4 2.2 %collective-permute-done.4.r_3_ = f32[80,256]{1,0:T(8,128)S(1)} collective-permute-done((f32[80,256]{1,0:T(8,128)S(1)}, f32[80,256]{1,0:T(8,128)S(1)}, u32[]{:S(2)}, u32[]{:S(2)}) %collective-permute-start.4) | collective-permute-done | bytes 81952 | tf_op jit(solution)/shard_map/ppermute | solution.py:642
  79.6 1.3 %collective-permute-done.5.r_4_ = f32[80,256]{1,0:T(8,128)S(1)} collective-permute-done((f32[80,256]{1,0:T(8,128)S(1)}, f32[80,256]{1,0:T(8,128)S(1)}, u32[]{:S(2)}, u32[]{:S(2)}) %collective-permute-start.5) | collective-permute-done | bytes 81952 | tf_op jit(solution)/shard_map/ppermute | solution.py:642
  80.9 0.5 sums.1
  81.4 13.1 %all_to_all.32 = f32[32,8,256]{2,1,0:T(8,128)S(1)} all-to-all(f32[32,8,256]{2,1,0:T(8,128)S(1)} %bitcast.27), channel_id=1, replica_groups=mesh['lat'=8,'lon_0'=4,'lon_1'=4,'lon_2'=2] {'lon_0','lon_1','lon_2'}, dimensions={0} | all-to-all | bytes 524288 | tf_op jit(solution)/shard_map/all_to_all | solution.py:637
  94.5 0.1 collective-permute-start.7
  94.6 1.5 %collective-permute-start.6 = (f32[8,128]{1,0:T(8,128)S(1)}, f32[8,128]{1,0:T(8,128)S(1)}, u32[]{:S(2)}, u32[]{:S(2)}) collective-permute-start(f32[8,128]{1,0:T(8,128)S(1)} %gather.1), channel_id=1, source_target_pairs={{224,0},{0,32},{32,64},{64,96},{96,128},{128,160},{160,192},{192,2... | collective-permute-start | bytes 12296 | tf_op jit(solution)/shard_map/ppermute | solution.py:642
  96.1 0.1 unpack_image.1.r_2_
  96.2 1.2 %last.1 = f32[256,256]{1,0:T(8,128)} custom-call(f32[256,256]{1,0:T(8,128)S(1)} %bitcast.18, f32[256,256]{1,0:T(8,128)S(1)} %get-tuple-element.53.r_2_.r_1_, f32[256,256]{1,0:T(8,128)S(1)} %get-tuple-element.66.r_2_, f32[256,256]{1,0:T(8,128)S(1)} %get-tuple-element.63.r_1_.r_3_, bf16[2,2,256,256]{3,2,1,0:T(8,128)(2,1)S(1)} %copy-done, ...), custom_call_target="tpu_custom_call" | custom-call | tf_op jit(solution)/shard_map/last/pallas_call | solution.py:753
  97.3 1.2 %collective-permute-done.6 = f32[8,128]{1,0:T(8,128)S(1)} collective-permute-done((f32[8,128]{1,0:T(8,128)S(1)}, f32[8,128]{1,0:T(8,128)S(1)}, u32[]{:S(2)}, u32[]{:S(2)}) %collective-permute-start.6) | collective-permute-done | bytes 4128 | tf_op jit(solution)/shard_map/ppermute | solution.py:642
  98.5 5.0 %all-to-all-start.5 = ((f32[32,8,256]{2,1,0:T(8,128)}), f32[32,8,256]{2,1,0:T(8,128)S(1)}, u32[]{:S(2)}, u32[]{:S(2)}) async-start(f32[32,8,256]{2,1,0:T(8,128)} %bitcast.11), calls=%async_computation.5 | async-start | bytes 524288 | tf_op jit(solution)/shard_map/all_to_all | solution.py:637
  103.5 0.5 collective-permute-start.9
  104.0 3.0 %collective-permute-start.8 = (f32[8,128]{1,0:T(8,128)S(1)}, f32[8,128]{1,0:T(8,128)S(1)}, u32[]{:S(2)}, u32[]{:S(2)}) collective-permute-start(f32[8,128]{1,0:T(8,128)S(1)} %get-tuple-element.69.r_5_), channel_id=1, source_target_pairs={{96,0},{128,32},{160,64},{192,96},{224,128},{0,160},{32,192},{64,2... | collective-permute-start | bytes 12296 | tf_op jit(solution)/shard_map/ppermute | solution.py:642
  107.0 1.2 %collective-permute-done.9.r_7_ = f32[8,128]{1,0:T(8,128)S(1)} collective-permute-done((f32[8,128]{1,0:T(8,128)S(1)}, f32[8,128]{1,0:T(8,128)S(1)}, u32[]{:S(2)}, u32[]{:S(2)}) %collective-permute-start.9) | collective-permute-done | bytes 4128 | tf_op jit(solution)/shard_map/ppermute | solution.py:642
  108.2 1.2 %collective-permute-done.8.r_6_ = f32[8,128]{1,0:T(8,128)S(1)} collective-permute-done((f32[8,128]{1,0:T(8,128)S(1)}, f32[8,128]{1,0:T(8,128)S(1)}, u32[]{:S(2)}, u32[]{:S(2)}) %collective-permute-start.8) | collective-permute-done | bytes 4128 | tf_op jit(solution)/shard_map/ppermute | solution.py:642
  109.4 3.3 %all-to-all-done.5 = f32[32,8,256]{2,1,0:T(8,128)S(1)} async-done(((f32[32,8,256]{2,1,0:T(8,128)}), f32[32,8,256]{2,1,0:T(8,128)S(1)}, u32[]{:S(2)}, u32[]{:S(2)}) %all-to-all-start.5) | async-done | bytes 262176 | tf_op jit(solution)/shard_map/all_to_all | solution.py:637
  112.6 1.0 finish.1
  (24 shorter events, 0.1 us)
Async XLA Ops:
  2.5 9.6 %copy-start.1 = (s32[135,256]{1,0:T(8,128)S(1)}, s32[135,256]{1,0:T(8,128)}, u32[]{:S(2)}) copy-start(s32[135,256]{1,0:T(8,128)} %r_4_.2) | copy-start | bytes 414724
  2.5 9.6 %copy-start.5 = (f32[135,256]{1,0:T(8,128)S(1)}, f32[135,256]{1,0:T(8,128)}, u32[]{:S(2)}) copy-start(f32[135,256]{1,0:T(8,128)} %east_ref.1) | copy-start | bytes 414724
  2.5 9.7 %copy-start.6 = (f32[135,256]{1,0:T(8,128)S(1)}, f32[135,256]{1,0:T(8,128)}, u32[]{:S(2)}) copy-start(f32[135,256]{1,0:T(8,128)} %north_ref.1) | copy-start | bytes 414724
  2.5 17.7 %all-to-all-start = ((f32[32,8,256]{2,1,0:T(8,128)}), f32[32,8,256]{2,1,0:T(8,128)S(1)}, u32[]{:S(2)}, u32[]{:S(2)}) async-start(f32[32,8,256]{2,1,0:T(8,128)} %bitcast), calls=%async_computation | async-start | bytes 524288 | tf_op jit(solution)/shard_map/all_to_all | solution.py:637
  12.1 0.9 copy-start.2
  12.1 8.2 %copy-start = (bf16[2,2,256,256]{3,2,1,0:T(8,128)(2,1)S(1)}, bf16[2,2,256,256]{3,2,1,0:T(8,128)(2,1)}, u32[]{:S(2)}) copy-start(bf16[2,2,256,256]{3,2,1,0:T(8,128)(2,1)} %constant.45.clone.r_2_.r_5_.r_4_) | copy-start | bytes 1572868
  13.1 0.7 copy-start.9
  13.8 6.4 %copy-start.3 = (f32[2,32,256]{2,1,0:T(8,128)S(1)}, f32[2,32,256]{2,1,0:T(8,128)}, u32[]{:S(2)}) copy-start(f32[2,32,256]{2,1,0:T(8,128)} %constant.46.clone.r_3_.r_6_.r_5_) | copy-start | bytes 196612
  21.4 12.8 %all-to-all-start.1 = ((f32[32,8,256]{2,1,0:T(8,128)}), f32[32,8,256]{2,1,0:T(8,128)S(1)}, u32[]{:S(2)}, u32[]{:S(2)}) async-start(f32[32,8,256]{2,1,0:T(8,128)} %bitcast.3), calls=%async_computation.1 | async-start | bytes 524288 | tf_op jit(solution)/shard_map/all_to_all | solution.py:637
  25.1 9.1 %copy-start.7 = (f32[2,128,128]{2,1,0:T(8,128)S(1)}, f32[2,128,128]{2,1,0:T(8,128)}, u32[]{:S(2)}) copy-start(f32[2,128,128]{2,1,0:T(8,128)} %aligned_ref.3) | copy-start | bytes 393220
  25.1 7.9 %collective-permute-start.1 = (f32[136,128]{1,0:T(8,128)S(1)}, f32[136,128]{1,0:T(8,128)S(1)}, u32[]{:S(2)}, u32[]{:S(2)}) collective-permute-start(f32[136,128]{1,0:T(8,128)S(1)} %get-tuple-element.46), channel_id=1, source_target_pairs={{224,0},{0,32},{32,64},{64,96},{96,128},{128,160},{160,192},{192,2... | collective-permute-start | bytes 208904 | tf_op jit(solution)/shard_map/ppermute | solution.py:642
  26.8 4.8 %collective-permute-start = (f32[8,256]{1,0:T(8,128)S(1)}, f32[8,256]{1,0:T(8,128)S(1)}, u32[]{:S(2)}, u32[]{:S(2)}) collective-permute-start(f32[8,256]{1,0:T(8,128)S(1)} %get-tuple-element.45), channel_id=1, source_target_pairs={{32,0},{64,32},{96,64},{128,96},{160,128},{192,160},{224,192},{0,2... | collective-permute-start | bytes 24584 | tf_op jit(solution)/shard_map/ppermute | solution.py:642
  34.5 7.3 %collective-permute-start.2 = (f32[80,256]{1,0:T(8,128)S(1)}, f32[80,256]{1,0:T(8,128)S(1)}, u32[]{:S(2)}, u32[]{:S(2)}) collective-permute-start(f32[80,256]{1,0:T(8,128)S(1)} %get-tuple-element.50), channel_id=1, source_target_pairs={{32,0},{64,32},{96,64},{128,96},{160,128},{192,160},{224,192},{0,2... | collective-permute-start | bytes 245768 | tf_op jit(solution)/shard_map/ppermute | solution.py:642
  40.1 4.5 %collective-permute-start.3 = (f32[80,256]{1,0:T(8,128)S(1)}, f32[80,256]{1,0:T(8,128)S(1)}, u32[]{:S(2)}, u32[]{:S(2)}) collective-permute-start(f32[80,256]{1,0:T(8,128)S(1)} %get-tuple-element.51), channel_id=1, source_target_pairs={{224,0},{0,32},{32,64},{64,96},{96,128},{128,160},{160,192},{192,2... | collective-permute-start | bytes 245768 | tf_op jit(solution)/shard_map/ppermute | solution.py:642
  45.1 15.6 %copy-start.8 = (f32[2,32,32]{2,1,0:T(8,128)S(1)}, f32[2,32,32]{2,1,0:T(8,128)}, u32[]{:S(2)}) copy-start(f32[2,32,32]{2,1,0:T(8,128)} %constant.47.clone.r_7_) | copy-start | bytes 24580
  75.7 3.9 %collective-permute-start.4 = (f32[80,256]{1,0:T(8,128)S(1)}, f32[80,256]{1,0:T(8,128)S(1)}, u32[]{:S(2)}, u32[]{:S(2)}) collective-permute-start(f32[80,256]{1,0:T(8,128)S(1)} %get-tuple-element.60), channel_id=1, source_target_pairs={{32,0},{64,32},{96,64},{128,96},{160,128},{192,160},{224,192},{0,2... | collective-permute-start | bytes 245768 | tf_op jit(solution)/shard_map/ppermute | solution.py:642
  75.8 5.1 %collective-permute-start.5 = (f32[80,256]{1,0:T(8,128)S(1)}, f32[80,256]{1,0:T(8,128)S(1)}, u32[]{:S(2)}, u32[]{:S(2)}) collective-permute-start(f32[80,256]{1,0:T(8,128)S(1)} %get-tuple-element.61), channel_id=1, source_target_pairs={{224,0},{0,32},{32,64},{64,96},{96,128},{128,160},{160,192},{192,2... | collective-permute-start | bytes 245768 | tf_op jit(solution)/shard_map/ppermute | solution.py:642
  94.5 2.8 %collective-permute-start.7 = (f32[8,128]{1,0:T(8,128)S(1)}, f32[8,128]{1,0:T(8,128)S(1)}, u32[]{:S(2)}, u32[]{:S(2)}) collective-permute-start(f32[8,128]{1,0:T(8,128)S(1)} %gather.1), channel_id=1, source_target_pairs={{32,0},{64,32},{96,64},{128,96},{160,128},{192,160},{224,192},{0,2... | collective-permute-start | bytes 12296 | tf_op jit(solution)/shard_map/ppermute | solution.py:642
  94.6 3.9 %collective-permute-start.6 = (f32[8,128]{1,0:T(8,128)S(1)}, f32[8,128]{1,0:T(8,128)S(1)}, u32[]{:S(2)}, u32[]{:S(2)}) collective-permute-start(f32[8,128]{1,0:T(8,128)S(1)} %gather.1), channel_id=1, source_target_pairs={{224,0},{0,32},{32,64},{64,96},{96,128},{128,160},{160,192},{192,2... | collective-permute-start | bytes 12296 | tf_op jit(solution)/shard_map/ppermute | solution.py:642
  98.5 14.1 %copy-start.4 = (f32[135,256]{1,0:T(8,128)S(1)}, f32[135,256]{1,0:T(8,128)}, u32[]{:S(2)}) copy-start(f32[135,256]{1,0:T(8,128)} %r_3_.2) | copy-start | bytes 414724
  98.5 14.1 %all-to-all-start.5 = ((f32[32,8,256]{2,1,0:T(8,128)}), f32[32,8,256]{2,1,0:T(8,128)S(1)}, u32[]{:S(2)}, u32[]{:S(2)}) async-start(f32[32,8,256]{2,1,0:T(8,128)} %bitcast.11), calls=%async_computation.5 | async-start | bytes 524288 | tf_op jit(solution)/shard_map/all_to_all | solution.py:637
  103.5 4.6 %collective-permute-start.9 = (f32[8,128]{1,0:T(8,128)S(1)}, f32[8,128]{1,0:T(8,128)S(1)}, u32[]{:S(2)}, u32[]{:S(2)}) collective-permute-start(f32[8,128]{1,0:T(8,128)S(1)} %get-tuple-element.70), channel_id=1, source_target_pairs={{192,0},{224,32},{0,64},{32,96},{64,128},{96,160},{128,192},{160,2... | collective-permute-start | bytes 12296 | tf_op jit(solution)/shard_map/ppermute | solution.py:642
  104.0 5.4 %collective-permute-start.8 = (f32[8,128]{1,0:T(8,128)S(1)}, f32[8,128]{1,0:T(8,128)S(1)}, u32[]{:S(2)}, u32[]{:S(2)}) collective-permute-start(f32[8,128]{1,0:T(8,128)S(1)} %get-tuple-element.69.r_5_), channel_id=1, source_target_pairs={{96,0},{128,32},{160,64},{192,96},{224,128},{0,160},{32,192},{64,2... | collective-permute-start | bytes 12296 | tf_op jit(solution)/shard_map/ppermute | solution.py:642

commit v6 on v5

--- a/solution.py
+++ b/solution.py
@@ -399,6 +399,54 @@
 def sums_kernel(
     norm,
     length,
+    spec_ref,
+    scale_ref,
+    aligned_ref,
+    stag_ref,
+    stag_below_ref,
+    flags_ref,
+    sums_ref,
+    scaled_ref,
+    part_ref,
+    down_ref,
+    up_ref,
+    own_ref,
+):
+    count, block = aligned_ref.shape[0], aligned_ref.shape[1]
+    half, rows = block // 2, count * block
+    scaled = spec_ref[...] * scale_ref[...]
+    scaled_ref[...] = scaled
+    for b in range(count):
+        at = slice(b * block, (b + 1) * block)
+        part_ref[at, :] = dot(aligned_ref[b], scaled[at])
+    for b in range(count - 1):
+        at = slice(half + b * block, half + (b + 1) * block)
+        part_ref[at, :] = part_ref[at, :] + dot(stag_ref[b], scaled[at])
+    first, last = slice(0, half), slice(rows - half, rows)
+    part_ref[first, :] = part_ref[first, :] + flags_ref[1:2, :] * dot(
+        stag_below_ref[half:block, half:], scaled[first]
+    )
+    part_ref[last, :] = part_ref[last, :] + dot(stag_ref[count - 1, :half, :half], scaled[last])
+    total = total_of(scaled * part_ref[...], length) * (flags_ref[2:3, :1] * norm)
+    small = lanes((8, 128))
+    own = jnp.where(small == SCALARS - 128 + 2, total, sums_ref[...])
+    own_ref[...] = own
+    down_ref[:half, :] = scaled[first]
+    up_ref[:half, :] = scaled[last]
+    for ref in (down_ref, up_ref):
+        ref[half:, :128] = own
+        ref[half:, 128:] = own
+
+
+def total_of(value, length):
+    columns = jnp.sum(value, axis=0, keepdims=True)
+    columns = jnp.where(lanes(columns.shape) < length, columns, 0.0)
+    return jnp.sum(columns[:, :128] + columns[:, 128:], axis=1, keepdims=True)
+
+
+def ends_kernel(
+    norm,
+    length,
     scaled_ref,
     part_ref,
     scale_ref,
@@ -407,32 +455,27 @@
     stag_ref,
     stag_below_ref,
     flags_ref,
-    spec_ref,
     aside_ref,
-    sums_ref,
+    own_ref,
     out_ref,
 ):
-    full, _, _ = combine(
-        norm,
-        scaled_ref,
-        part_ref,
-        scale_ref,
-        above_ref,
-        below_ref,
-        stag_ref,
-        stag_below_ref,
-        flags_ref,
-    )
-    lane = lanes(full.shape)
-    held = jnp.where(lane < length, full, 0.0)
-    own = jnp.sum(held * spec_ref[...], axis=0, keepdims=True)
-    own = jnp.sum(own[:, :128] + own[:, 128:], axis=1, keepdims=True) * flags_ref[2:3, :1]
-    full = held + aside_ref[...]
-    full = jnp.where(lane == SCALARS + 2, own, full)
-    out_ref[:, :128] = full[:, :128]
-    out_ref[:, 128:] = jnp.where(
-        (lane[:, 128:] == SCALARS) | (lane[:, 128:] == SCALARS + 1), sums_ref[:1, :], full[:, 128:]
-    )
+    count, block = stag_ref.shape[0], stag_ref.shape[1]
+    half, rows = block // 2, count * block
+    first, last = slice(0, half), slice(rows - half, rows)
+    low = dot(stag_below_ref[half:block, :half], below_ref[:half, :]) * flags_ref[1:2, :]
+    high = dot(stag_ref[count - 1, :half, half:], above_ref[:half, :]) * flags_ref[:1, :]
+    both = total_of(low * scaled_ref[first, :] + high * scaled_ref[last, :], length)
+    both = both * (flags_ref[2:3, :1] * (2.0 * norm))
+    pair = own_ref[:1, :] + below_ref[half : half + 1, 128:]
+    pair = jnp.where(lanes(pair.shape) == SCALARS - 128 + 2, pair + both, pair)
+    middle = slice(half, rows - half)
+    for at, more in ((first, low), (middle, None), (last, high)):
+        full = part_ref[at, :] if more is None else part_ref[at, :] + more
+        full = full * (scale_ref[at, :] * norm)
+        full = jnp.where(lanes(full.shape) < length, full, aside_ref[at, :])
+        out_ref[at, :128] = full[:, :128]
+        inside = lanes((full.shape[0], 128)) < SCALARS - 128
+        out_ref[at, 128:] = jnp.where(inside, full[:, 128:], pair)
 
 
 def gather_kernel(spec_ref, sums_ref):
@@ -587,15 +630,16 @@
     image_ref,
     forcing_ref,
     mask_ref,
-    three_ref,
-    others_ref,
     pair_ref,
+    ahead_ref,
+    behind_ref,
+    across_ref,
     solution_ref,
     residual_ref,
     direction_ref,
 ):
     at = SCALARS - 128
-    totals = three_ref[:1, :] + others_ref[:1, :] + pair_ref[:1, :]
+    totals = (pair_ref[:1, :] + across_ref[:1, :]) + (ahead_ref[:1, :] + behind_ref[:1, :])
     rz, curvature, own = [totals[:, at + n : at + n + 1] for n in range(3)]
     alpha = rz / curvature
     rz_next = rz - 2.0 * alpha * curvature + alpha * alpha * own
@@ -733,27 +777,28 @@
         name="step",
     )(filtered, slab, *flat, matrices, twiddle, outer)
     spec_image = exchanged(spec)
-    pieces = blocks(spec_image)
+    edge = (half + ROWS, WIDE)
+    scaled, part, down, up, own = call(
+        lambda *r: sums_kernel(norm, length, *r), [wide, wide, edge, edge, (8, 128)], name="sums"
+    )(spec_image, scale, aligned_inverse, stag, stag_below, flags, sums)
+    above, below = from_lat(down, 1), from_lat(up, -1)
     cut, image_cut = WIDE - length, SCALARS - length
     first_cells, aside = call(
         lambda *r: unpack_first_kernel(length, cut, *r), [cells, wide], name="unpack_first"
-    )(after(spec_image, pieces[0]), image)
+    )(after(spec_image, scaled), image)
     filtered = exchanged(
-        call(lambda *r: sums_kernel(norm, length, *r), wide, name="sums")(
-            *pieces, spec_image, aside, sums
-        )
-    )
-
-    sums = call(gather_kernel, (8, 128), name="gather")(filtered)
-    pair = sums + from_lat(sums, -1)
-    three = pair + from_lat(sums, 1)
+        call(lambda *r: ends_kernel(norm, length, *r), wide, name="ends")(
+            scaled, part, scale, above, below, stag, stag_below, flags, aside, own
+        )
+    )
+
+    pair = call(gather_kernel, (8, 128), name="gather")(filtered)
     image_cells = call(
         lambda *r: unpack_kernel(length, image_cut, *r), cells, name="unpack_image"
     )(filtered)
     packed = call(lambda *r: last_kernel(groups, length, *r), wide, name="last")(
         filtered, flat[0], first, image, matrices, twiddle
     )
-    packed, three, pair = lax.optimization_barrier((packed, three, pair, image_cells))[:3]
     return tuple(
         call(lambda *r: finish_kernel(length, *r), [cells] * 3, name="finish")(
             exchanged(packed),
@@ -761,9 +806,10 @@
             image_cells,
             surface_forcing,
             ocean_mask,
-            three,
-            from_lat(three, 3),
+            pair,
+            from_lat(pair, 2),
             from_lat(pair, -2),
+            from_lat(pair, 4),
         )
     )
 

time: 114 us -> 110 us (0.965)
  waiting for transfers between devices: 23.4 us -> 17.4 us
  starting transfers between devices: 35.3 us -> 36.9 us
    all_to_all x3, waiting for transfers between devices: 10.2 us -> 7.08 us  [exchanged(): lax.all_to_all(parts, LON, split_axis=0, concat_axis=0, tiled=True)]
    ppermute x10 -> x9, waiting for transfers between devices: 13.2 us -> 10.3 us  [from_lat(): lax.ppermute(value, 'lat', [((d + steps) % count, d) for d in range(count)])]
    ppermute x10 -> x9, starting transfers between devices: 17.9 us -> 20.7 us  [from_lat(): lax.ppermute(value, 'lat', [((d + steps) % count, d) for d in range(count)])]
    all_to_all x3, starting transfers between devices: 17.4 us -> 16.1 us  [exchanged(): lax.all_to_all(parts, LON, split_axis=0, concat_axis=0, tiled=True)]
  transfers between devices with their start and end apart: 13 -> 12, of which waited for: 12 -> 10; matrix products, arithmetic and copies ran while one was open for 1% -> 1% of each run, Pallas kernels for 2% -> 2%
where the time goes in v6:
time: 110 us; the launch traced here: 109 us
  blocking collectives  41 us (37%)
  starting transfers between devices  36.9 us (34%)
  waiting for transfers between devices  17.4 us (16%)
  Pallas kernels  9.81 us (9%)
  local copies, waits for them, and re-layouts  2.18 us (2%)
  other arithmetic  1.26 us (1%)
    all_to_all x3, blocking collectives, exchanged(): lax.all_to_all(parts, LON, split_axis=0, concat_axis=0, tiled=True)  41 us
    ppermute x9, starting transfers between devices, from_lat(): lax.ppermute(value, 'lat', [((d + steps) % count, d) for d in range(count)])  20.7 us
    all_to_all x3, starting transfers between devices, exchanged(): lax.all_to_all(parts, LON, split_axis=0, concat_axis=0, tiled=True)  16.1 us
    ppermute x9, waiting for transfers between devices, from_lat(): lax.ppermute(value, 'lat', [((d + steps) % count, d) for d in range(count)])  10.3 us
    all_to_all x3, waiting for transfers between devices, exchanged(): lax.all_to_all(parts, LON, split_axis=0, concat_axis=0, tiled=True)  7.08 us
    pallas_call x1, Pallas kernels, local(): call(lambda *r: step_kernel(groups, length, *r), [wide, wide, wide, (8, 1...  2.34 us
  transfers between devices with their start and end apart: 12, of which 10 were waited for; matrix products, arithmetic and copies ran while one was open for 1% of the time, Pallas kernels for 2%

profile of v6, /device:TPU:1, one launch (start us, length us, event | category | flops | bytes accessed | tf_op | source)
XLA Modules:
  0.0 109.4 jit_solution(18101947835923895697)
XLA Ops:
  0.6 1.1 convert_multiply_fusion
  1.7 0.8 pack.1
  2.5 8.7 %all-to-all-start = ((f32[32,8,256]{2,1,0:T(8,128)}), f32[32,8,256]{2,1,0:T(8,128)S(1)}, u32[]{:S(2)}, u32[]{:S(2)}) async-start(f32[32,8,256]{2,1,0:T(8,128)} %bitcast), calls=%async_computation | async-start | bytes 524288 | tf_op jit(solution)/shard_map/all_to_all | solution.py:681
  11.3 0.1 broadcast_select_fusion.flags_ref.r_7_.r_5_
  11.4 0.7 constant_dynamic-slice_fusion
  12.1 0.0 copy-start
  12.1 0.1 pack_more.1.r_1_
  12.3 0.7 copy-done.2
  13.0 0.1 edges.1
  13.1 0.0 copy-start.9
  13.2 0.7 copy-done.9
  13.8 0.1 add_rsqrt_fusion.scale_ref.r_2_.r_1_
  14.0 6.3 %all-to-all-done = f32[32,8,256]{2,1,0:T(8,128)S(1)} async-done(((f32[32,8,256]{2,1,0:T(8,128)}), f32[32,8,256]{2,1,0:T(8,128)S(1)}, u32[]{:S(2)}, u32[]{:S(2)}) %all-to-all-start) | async-done | bytes 262176 | tf_op jit(solution)/shard_map/all_to_all | solution.py:681
  20.3 1.1 %forward.1 = f32[256,256]{1,0:T(8,128)} custom-call(f32[256,256]{1,0:T(8,128)S(1)} %bitcast.16, f32[256,256]{1,0:T(8,128)S(1)} %pack_more.1.r_1_, bf16[2,2,256,256]{3,2,1,0:T(8,128)(2,1)S(1)} %copy-done, f32[2,32,256]{2,1,0:T(8,128)S(1)} %copy-done.3), custom_call_target="tpu_custom_call" | custom-call | tf_op jit(solution)/shard_map/forward/pallas_call | solution.py:739
  21.4 3.7 %all-to-all-start.1 = ((f32[32,8,256]{2,1,0:T(8,128)}), f32[32,8,256]{2,1,0:T(8,128)S(1)}, u32[]{:S(2)}, u32[]{:S(2)}) async-start(f32[32,8,256]{2,1,0:T(8,128)} %bitcast.3), calls=%async_computation.1 | async-start | bytes 524288 | tf_op jit(solution)/shard_map/all_to_all | solution.py:681
  25.1 0.0 copy-start.7
  25.1 1.7 %collective-permute-start.1 = (f32[136,128]{1,0:T(8,128)S(1)}, f32[136,128]{1,0:T(8,128)S(1)}, u32[]{:S(2)}, u32[]{:S(2)}) collective-permute-start(f32[136,128]{1,0:T(8,128)S(1)} %get-tuple-element.44), channel_id=1, source_target_pairs={{224,0},{0,32},{32,64},{64,96},{96,128},{128,160},{160,192},{192,2... | collective-permute-start | bytes 208904 | tf_op jit(solution)/shard_map/ppermute | solution.py:686
  26.9 4.0 %collective-permute-start = (f32[8,256]{1,0:T(8,128)S(1)}, f32[8,256]{1,0:T(8,128)S(1)}, u32[]{:S(2)}, u32[]{:S(2)}) collective-permute-start(f32[8,256]{1,0:T(8,128)S(1)} %get-tuple-element.43), channel_id=1, source_target_pairs={{32,0},{64,32},{96,64},{128,96},{160,128},{192,160},{224,192},{0,2... | collective-permute-start | bytes 24584 | tf_op jit(solution)/shard_map/ppermute | solution.py:686
  30.9 0.8 collective-permute-done.wet_above_ref
  31.7 1.4 %collective-permute-done.1.from_below_ref.r_6_.r_4_ = f32[136,128]{1,0:T(8,128)S(1)} collective-permute-done((f32[136,128]{1,0:T(8,128)S(1)}, f32[136,128]{1,0:T(8,128)S(1)}, u32[]{:S(2)}, u32[]{:S(2)}) %collective-permute-start.1) | collective-permute-done | bytes 69664 | tf_op jit(solution)/shard_map/ppermute | solution.py:686
  33.1 0.6 pack_rest.1.r_8_
  33.6 0.6 all-to-all-done.1
  34.2 0.3 blocks.1
  34.5 5.7 %collective-permute-start.2 = (f32[80,256]{1,0:T(8,128)S(1)}, f32[80,256]{1,0:T(8,128)S(1)}, u32[]{:S(2)}, u32[]{:S(2)}) collective-permute-start(f32[80,256]{1,0:T(8,128)S(1)} %get-tuple-element.48), channel_id=1, source_target_pairs={{32,0},{64,32},{96,64},{128,96},{160,128},{192,160},{224,192},{0,2... | collective-permute-start | bytes 245768 | tf_op jit(solution)/shard_map/ppermute | solution.py:686
  40.2 0.5 coefficients.1
  40.7 1.1 %collective-permute-done.2.r_3_ = f32[80,256]{1,0:T(8,128)S(1)} collective-permute-done((f32[80,256]{1,0:T(8,128)S(1)}, f32[80,256]{1,0:T(8,128)S(1)}, u32[]{:S(2)}, u32[]{:S(2)}) %collective-permute-start.2) | collective-permute-done | bytes 81952 | tf_op jit(solution)/shard_map/ppermute | solution.py:686
  41.8 2.8 %collective-permute-done.3.r_4_ = f32[80,256]{1,0:T(8,128)S(1)} collective-permute-done((f32[80,256]{1,0:T(8,128)S(1)}, f32[80,256]{1,0:T(8,128)S(1)}, u32[]{:S(2)}, u32[]{:S(2)}) %collective-permute-start.3) | collective-permute-done | bytes 81952 | tf_op jit(solution)/shard_map/ppermute | solution.py:686
  44.7 0.4 halo.1
  45.1 0.0 copy-start.8
  45.1 15.6 %all_to_all.30 = f32[32,8,384]{2,1,0:T(8,128)S(1)} all-to-all(f32[32,8,384]{2,1,0:T(8,128)S(1)} %bitcast.23), channel_id=1, replica_groups=mesh['lat'=8,'lon_0'=4,'lon_1'=4,'lon_2'=2] {'lon_0','lon_1','lon_2'}, dimensions={0} | all-to-all | bytes 786432 | tf_op jit(solution)/shard_map/all_to_all | solution.py:681
  60.7 2.3 %step.1 = (f32[256,256]{1,0:T(8,128)S(1)}, f32[256,256]{1,0:T(8,128)S(1)}, f32[256,256]{1,0:T(8,128)S(1)}, f32[8,128]{1,0:T(8,128)S(1)}) custom-call(f32[256,384]{1,0:T(8,128)S(1)} %bitcast.24, f32[256,256]{1,0:T(8,128)S(1)} %bitcast.18, f32[256,256]{1,0:T(8,128)S(1)} %get-tuple-element.51.r_2_.r_1_, f32[256,256]{1,0:T(8,128)S(1)} %get-tuple-element.52.r_3_, ...), custom_call_target="tpu_custom_call" | custom-call | tf_op jit(solution)/shard_map/step/pallas_call | solution.py:773
  63.0 12.3 %all_to_all.31 = f32[32,8,256]{2,1,0:T(8,128)S(1)} all-to-all(f32[32,8,256]{2,1,0:T(8,128)S(1)} %bitcast.27), channel_id=1, replica_groups=mesh['lat'=8,'lon_0'=4,'lon_1'=4,'lon_2'=2] {'lon_0','lon_1','lon_2'}, dimensions={0} | all-to-all | bytes 524288 | tf_op jit(solution)/shard_map/all_to_all | solution.py:681
  75.4 0.6 sums.1
  75.9 0.0 collective-permute-start.4
  75.9 1.5 %collective-permute-start.5 = (f32[72,256]{1,0:T(8,128)S(1)}, f32[72,256]{1,0:T(8,128)S(1)}, u32[]{:S(2)}, u32[]{:S(2)}) collective-permute-start(f32[72,256]{1,0:T(8,128)S(1)} %get-tuple-element.60), channel_id=1, source_target_pairs={{224,0},{0,32},{32,64},{64,96},{96,128},{128,160},{160,192},{192,2... | collective-permute-start | bytes 221192 | tf_op jit(solution)/shard_map/ppermute | solution.py:686
  77.4 0.2 unpack_first.1
  77.6 2.0 %collective-permute-done.4.r_3_ = f32[72,256]{1,0:T(8,128)S(1)} collective-permute-done((f32[72,256]{1,0:T(8,128)S(1)}, f32[72,256]{1,0:T(8,128)S(1)}, u32[]{:S(2)}, u32[]{:S(2)}) %collective-permute-start.4) | collective-permute-done | bytes 73760 | tf_op jit(solution)/shard_map/ppermute | solution.py:686
  79.6 1.2 %collective-permute-done.5.r_4_ = f32[72,256]{1,0:T(8,128)S(1)} collective-permute-done((f32[72,256]{1,0:T(8,128)S(1)}, f32[72,256]{1,0:T(8,128)S(1)}, u32[]{:S(2)}, u32[]{:S(2)}) %collective-permute-start.5) | collective-permute-done | bytes 73760 | tf_op jit(solution)/shard_map/ppermute | solution.py:686
  80.8 0.4 ends.1
  81.3 13.1 %all_to_all.32 = f32[32,8,256]{2,1,0:T(8,128)S(1)} all-to-all(f32[32,8,256]{2,1,0:T(8,128)S(1)} %bitcast.26), channel_id=1, replica_groups=mesh['lat'=8,'lon_0'=4,'lon_1'=4,'lon_2'=2] {'lon_0','lon_1','lon_2'}, dimensions={0} | all-to-all | bytes 524288 | tf_op jit(solution)/shard_map/all_to_all | solution.py:681
  94.4 1.2 %last.1 = f32[256,256]{1,0:T(8,128)} custom-call(f32[256,256]{1,0:T(8,128)S(1)} %bitcast.13, f32[256,256]{1,0:T(8,128)S(1)} %get-tuple-element.51.r_2_.r_1_, f32[256,256]{1,0:T(8,128)S(1)} %get-tuple-element.65.r_2_, f32[256,256]{1,0:T(8,128)S(1)} %get-tuple-element.62.r_1_.r_3_, bf16[2,2,256,256]{3,2,1,0:T(8,128)(2,1)S(1)} %copy-done, ...), custom_call_target="tpu_custom_call" | custom-call | tf_op jit(solution)/shard_map/last/pallas_call | solution.py:799
  95.6 3.7 %all-to-all-start.5 = ((f32[32,8,256]{2,1,0:T(8,128)}), f32[32,8,256]{2,1,0:T(8,128)S(1)}, u32[]{:S(2)}, u32[]{:S(2)}) async-start(f32[32,8,256]{2,1,0:T(8,128)} %bitcast.11), calls=%async_computation.5 | async-start | bytes 524288 | tf_op jit(solution)/shard_map/all_to_all | solution.py:681
  99.3 4.3 %collective-permute-start.8 = (f32[8,128]{1,0:T(8,128)S(1)}, f32[8,128]{1,0:T(8,128)S(1)}, u32[]{:S(2)}, u32[]{:S(2)}) collective-permute-start(f32[8,128]{1,0:T(8,128)S(1)} %gather.1.r_5_), channel_id=1, source_target_pairs={{128,0},{160,32},{192,64},{224,96},{0,128},{32,160},{64,192},{96,2... | collective-permute-start | bytes 12296 | tf_op jit(solution)/shard_map/ppermute | solution.py:686
  103.6 3.6 %collective-permute-start.6 = (f32[8,128]{1,0:T(8,128)S(1)}, f32[8,128]{1,0:T(8,128)S(1)}, u32[]{:S(2)}, u32[]{:S(2)}) collective-permute-start(f32[8,128]{1,0:T(8,128)S(1)} %gather.1.r_5_), channel_id=1, source_target_pairs={{64,0},{96,32},{128,64},{160,96},{192,128},{224,160},{0,192},{32,2... | collective-permute-start | bytes 12296 | tf_op jit(solution)/shard_map/ppermute | solution.py:686
  107.2 0.1 unpack_image.1.r_2_
  107.3 0.9 collective-permute-done.7.r_7_
  108.2 0.2 all-to-all-done.5
  108.4 1.0 finish.1
  (21 shorter events, 0.1 us)
Async XLA Ops:
  2.5 9.6 %copy-start.1 = (s32[135,256]{1,0:T(8,128)S(1)}, s32[135,256]{1,0:T(8,128)}, u32[]{:S(2)}) copy-start(s32[135,256]{1,0:T(8,128)} %r_4_.2) | copy-start | bytes 414724
  2.5 9.6 %copy-start.5 = (f32[135,256]{1,0:T(8,128)S(1)}, f32[135,256]{1,0:T(8,128)}, u32[]{:S(2)}) copy-start(f32[135,256]{1,0:T(8,128)} %east_ref.1) | copy-start | bytes 414724
  2.5 9.7 %copy-start.6 = (f32[135,256]{1,0:T(8,128)S(1)}, f32[135,256]{1,0:T(8,128)}, u32[]{:S(2)}) copy-start(f32[135,256]{1,0:T(8,128)} %north_ref.1) | copy-start | bytes 414724
  2.5 17.7 %all-to-all-start = ((f32[32,8,256]{2,1,0:T(8,128)}), f32[32,8,256]{2,1,0:T(8,128)S(1)}, u32[]{:S(2)}, u32[]{:S(2)}) async-start(f32[32,8,256]{2,1,0:T(8,128)} %bitcast), calls=%async_computation | async-start | bytes 524288 | tf_op jit(solution)/shard_map/all_to_all | solution.py:681
  12.1 0.9 copy-start.2
  12.1 8.2 %copy-start = (bf16[2,2,256,256]{3,2,1,0:T(8,128)(2,1)S(1)}, bf16[2,2,256,256]{3,2,1,0:T(8,128)(2,1)}, u32[]{:S(2)}) copy-start(bf16[2,2,256,256]{3,2,1,0:T(8,128)(2,1)} %constant.45.clone.r_2_.r_5_.r_4_) | copy-start | bytes 1572868
  13.1 0.7 copy-start.9
  13.8 6.4 %copy-start.3 = (f32[2,32,256]{2,1,0:T(8,128)S(1)}, f32[2,32,256]{2,1,0:T(8,128)}, u32[]{:S(2)}) copy-start(f32[2,32,256]{2,1,0:T(8,128)} %constant.46.clone.r_3_.r_6_.r_5_) | copy-start | bytes 196612
  21.4 12.8 %all-to-all-start.1 = ((f32[32,8,256]{2,1,0:T(8,128)}), f32[32,8,256]{2,1,0:T(8,128)S(1)}, u32[]{:S(2)}, u32[]{:S(2)}) async-start(f32[32,8,256]{2,1,0:T(8,128)} %bitcast.3), calls=%async_computation.1 | async-start | bytes 524288 | tf_op jit(solution)/shard_map/all_to_all | solution.py:681
  25.1 9.1 %copy-start.7 = (f32[2,128,128]{2,1,0:T(8,128)S(1)}, f32[2,128,128]{2,1,0:T(8,128)}, u32[]{:S(2)}) copy-start(f32[2,128,128]{2,1,0:T(8,128)} %r_2_.2) | copy-start | bytes 393220
  25.1 7.9 %collective-permute-start.1 = (f32[136,128]{1,0:T(8,128)S(1)}, f32[136,128]{1,0:T(8,128)S(1)}, u32[]{:S(2)}, u32[]{:S(2)}) collective-permute-start(f32[136,128]{1,0:T(8,128)S(1)} %get-tuple-element.44), channel_id=1, source_target_pairs={{224,0},{0,32},{32,64},{64,96},{96,128},{128,160},{160,192},{192,2... | collective-permute-start | bytes 208904 | tf_op jit(solution)/shard_map/ppermute | solution.py:686
  26.9 4.8 %collective-permute-start = (f32[8,256]{1,0:T(8,128)S(1)}, f32[8,256]{1,0:T(8,128)S(1)}, u32[]{:S(2)}, u32[]{:S(2)}) collective-permute-start(f32[8,256]{1,0:T(8,128)S(1)} %get-tuple-element.43), channel_id=1, source_target_pairs={{32,0},{64,32},{96,64},{128,96},{160,128},{192,160},{224,192},{0,2... | collective-permute-start | bytes 24584 | tf_op jit(solution)/shard_map/ppermute | solution.py:686
  34.5 7.3 %collective-permute-start.2 = (f32[80,256]{1,0:T(8,128)S(1)}, f32[80,256]{1,0:T(8,128)S(1)}, u32[]{:S(2)}, u32[]{:S(2)}) collective-permute-start(f32[80,256]{1,0:T(8,128)S(1)} %get-tuple-element.48), channel_id=1, source_target_pairs={{32,0},{64,32},{96,64},{128,96},{160,128},{192,160},{224,192},{0,2... | collective-permute-start | bytes 245768 | tf_op jit(solution)/shard_map/ppermute | solution.py:686
  40.2 4.5 %collective-permute-start.3 = (f32[80,256]{1,0:T(8,128)S(1)}, f32[80,256]{1,0:T(8,128)S(1)}, u32[]{:S(2)}, u32[]{:S(2)}) collective-permute-start(f32[80,256]{1,0:T(8,128)S(1)} %get-tuple-element.49), channel_id=1, source_target_pairs={{224,0},{0,32},{32,64},{64,96},{96,128},{128,160},{160,192},{192,2... | collective-permute-start | bytes 245768 | tf_op jit(solution)/shard_map/ppermute | solution.py:686
  45.1 15.6 %copy-start.8 = (f32[2,32,32]{2,1,0:T(8,128)S(1)}, f32[2,32,32]{2,1,0:T(8,128)}, u32[]{:S(2)}) copy-start(f32[2,32,32]{2,1,0:T(8,128)} %constant.47.clone.r_7_) | copy-start | bytes 24580
  75.9 3.7 %collective-permute-start.4 = (f32[72,256]{1,0:T(8,128)S(1)}, f32[72,256]{1,0:T(8,128)S(1)}, u32[]{:S(2)}, u32[]{:S(2)}) collective-permute-start(f32[72,256]{1,0:T(8,128)S(1)} %get-tuple-element.59), channel_id=1, source_target_pairs={{32,0},{64,32},{96,64},{128,96},{160,128},{192,160},{224,192},{0,2... | collective-permute-start | bytes 221192 | tf_op jit(solution)/shard_map/ppermute | solution.py:686
  75.9 4.9 %collective-permute-start.5 = (f32[72,256]{1,0:T(8,128)S(1)}, f32[72,256]{1,0:T(8,128)S(1)}, u32[]{:S(2)}, u32[]{:S(2)}) collective-permute-start(f32[72,256]{1,0:T(8,128)S(1)} %get-tuple-element.60), channel_id=1, source_target_pairs={{224,0},{0,32},{32,64},{64,96},{96,128},{128,160},{160,192},{192,2... | collective-permute-start | bytes 221192 | tf_op jit(solution)/shard_map/ppermute | solution.py:686
  95.6 12.8 %all-to-all-start.5 = ((f32[32,8,256]{2,1,0:T(8,128)}), f32[32,8,256]{2,1,0:T(8,128)S(1)}, u32[]{:S(2)}, u32[]{:S(2)}) async-start(f32[32,8,256]{2,1,0:T(8,128)} %bitcast.11), calls=%async_computation.5 | async-start | bytes 524288 | tf_op jit(solution)/shard_map/all_to_all | solution.py:681
  99.3 9.1 %copy-start.4 = (f32[135,256]{1,0:T(8,128)S(1)}, f32[135,256]{1,0:T(8,128)}, u32[]{:S(2)}) copy-start(f32[135,256]{1,0:T(8,128)} %r_3_.3) | copy-start | bytes 414724
  99.3 8.0 %collective-permute-start.8 = (f32[8,128]{1,0:T(8,128)S(1)}, f32[8,128]{1,0:T(8,128)S(1)}, u32[]{:S(2)}, u32[]{:S(2)}) collective-permute-start(f32[8,128]{1,0:T(8,128)S(1)} %gather.1.r_5_), channel_id=1, source_target_pairs={{128,0},{160,32},{192,64},{224,96},{0,128},{32,160},{64,192},{96,2... | collective-permute-start | bytes 12296 | tf_op jit(solution)/shard_map/ppermute | solution.py:686
  103.6 4.6 %collective-permute-start.7 = (f32[8,128]{1,0:T(8,128)S(1)}, f32[8,128]{1,0:T(8,128)S(1)}, u32[]{:S(2)}, u32[]{:S(2)}) collective-permute-start(f32[8,128]{1,0:T(8,128)S(1)} %gather.1.r_5_), channel_id=1, source_target_pairs={{192,0},{224,32},{0,64},{32,96},{64,128},{96,160},{128,192},{160,2... | collective-permute-start | bytes 12296 | tf_op jit(solution)/shard_map/ppermute | solution.py:686
  103.6 4.6 %collective-permute-start.6 = (f32[8,128]{1,0:T(8,128)S(1)}, f32[8,128]{1,0:T(8,128)S(1)}, u32[]{:S(2)}, u32[]{:S(2)}) collective-permute-start(f32[8,128]{1,0:T(8,128)S(1)} %gather.1.r_5_), channel_id=1, source_target_pairs={{64,0},{96,32},{128,64},{160,96},{192,128},{224,160},{0,192},{32,2... | collective-permute-start | bytes 12296 | tf_op jit(solution)/shard_map/ppermute | solution.py:686

commit v7 on v6

--- a/solution.py
+++ b/solution.py
@@ -50,7 +50,7 @@
     return (
         np.stack([coarse, rest]),
         twiddle.astype(np.float32),
-        outer.astype(np.float32),
+        np.concatenate([outer[0], outer[1]], axis=1).astype(np.float32),
         wave.astype(np.float32),
     )
 
@@ -263,9 +263,13 @@
     )
 
 
-def transform_back(spectrum, groups, matrix_ref, twiddle_ref):
+def both_products(spectrum, matrix_ref):
     parts = split(spectrum)
-    pc, ps = product(parts, table(matrix_ref, 0)), product(parts, table(matrix_ref, 1))
+    return product(parts, table(matrix_ref, 0)), product(parts, table(matrix_ref, 1))
+
+
+def transform_back(products, groups, twiddle_ref):
+    pc, ps = products
     mixed = []
     for m in range(groups // 2 + 1):
         if m == 0:
@@ -282,17 +286,55 @@
     return real_ifft(mixed)
 
 
-def row_back(spectrum, matrix_ref, twiddle_ref, outer_ref):
-    parts = split(spectrum)
-    pc, ps = product(parts, table(matrix_ref, 0)), product(parts, table(matrix_ref, 1))
+def rows_back(products, start, twiddle_ref, outer_ref):
+    groups = outer_ref.shape[0]
     cos, sin = twiddle_ref[0], twiddle_ref[1]
-    return dot(outer_ref[0], pc * cos - ps * sin) + dot(outer_ref[1], ps * cos + pc * sin)
+    turned = [[], []]
+    for n in range(2):
+        pc, ps = (v[start + n * groups : start + (n + 1) * groups] for v in products)
+        turned[0].append(pc * cos - ps * sin)
+        turned[1].append(ps * cos + pc * sin)
+    both = jnp.concatenate([jnp.concatenate(v, axis=1) for v in turned], axis=0)
+    both = dot(outer_ref[...], both)
+    return both[:, :WIDE], both[:, WIDE:]
 
 
 def forward_kernel(groups, field_ref, rest_ref, matrix_ref, twiddle_ref, out_ref, left, right):
     chunks = [field_ref[rows_of(p), :] for p in range(groups)]
     spectrum = transform(chunks, matrix_ref, twiddle_ref, left, right)
     out_ref[...] = spectrum + rest_ref[...]
+
+
+def store_edge(ref, value, extra):
+    half = value.shape[0]
+    ref[:half, :] = value[:, :128]
+    ref[half : half + ROWS, :] = jnp.concatenate(
+        [value[:, 128:].T[:ROWS], jnp.zeros((ROWS, 128 - half), jnp.float32)], axis=1
+    )
+    ref[half + ROWS :, :] = extra
+
+
+def load_edge(ref):
+    half = ref.shape[0] - 2 * ROWS
+    turned = ref[half : half + ROWS, :].T[:half]
+    blank = jnp.zeros((half, 128 - ROWS), jnp.float32)
+    return jnp.concatenate([ref[:half, :], turned, blank], axis=1)
+
+
+def store_rows(ref, value, part, scale):
+    row = sublanes((ROWS, 128))
+    extra = jnp.where(row == 0, part[:, :128], part[:, 128:])
+    store_edge(
+        ref,
+        value,
+        jnp.where(row < 2, extra, jnp.where(row == 2, scale[:, :128], scale[:, 128:])),
+    )
+
+
+def load_rows(ref):
+    at = ref.shape[0] - ROWS
+    lines = [ref[at + n : at + n + 1, :] for n in range(4)]
+    return jnp.concatenate(lines[:2], axis=1), jnp.concatenate(lines[2:], axis=1)
 
 
 def blocks_kernel(spec_ref, scale_ref, aligned_ref, scaled_ref, part_ref, down_ref, up_ref):
@@ -304,12 +346,8 @@
         part_ref[b * block : (b + 1) * block, :] = dot(
             aligned_ref[b], scaled[b * block : (b + 1) * block]
         )
-    down_ref[:half, :] = scaled[:half]
-    down_ref[half : half + 8, :] = part_ref[:8, :]
-    down_ref[half + 8 :, :] = scale_ref[:8, :]
-    up_ref[:half, :] = scaled[rows - half :]
-    up_ref[half : half + 8, :] = part_ref[rows - 8 :, :]
-    up_ref[half + 8 :, :] = scale_ref[rows - 8 :, :]
+    store_rows(down_ref, scaled[:half], part_ref[:1, :], scale_ref[:1, :])
+    store_rows(up_ref, scaled[rows - half :], part_ref[rows - 1 :, :], scale_ref[rows - 1 :, :])
 
 
 def combine(
@@ -319,9 +357,9 @@
     half, rows = block // 2, count * block
     before = flags_ref[1:2, :] * dot(
         stag_below_ref[:block, :],
-        jnp.concatenate([below_ref[:half, :], scaled_ref[:half, :]], axis=0),
-    )
-    upper = above_ref[:half, :] * flags_ref[:1, :]
+        jnp.concatenate([load_edge(below_ref), scaled_ref[:half, :]], axis=0),
+    )
+    upper = load_edge(above_ref) * flags_ref[:1, :]
     pieces = [before[half:]]
     for b in range(count - 1):
         pieces.append(dot(stag_ref[b], scaled_ref[half + b * block : half + (b + 1) * block, :]))
@@ -361,12 +399,10 @@
         stag_below_ref,
         flags_ref,
     )
-    row_below = (before[half - 1 : half] + below_ref[half + 7 : half + 8, :]) * (
-        below_ref[half + 15 : half + 16, :] * norm
-    )
-    row_above = (after[half : half + 1] + above_ref[half : half + 1, :]) * (
-        above_ref[half + 8 : half + 9, :] * norm
-    )
+    part, scale = load_rows(below_ref)
+    row_below = (before[half - 1 : half] + part) * (scale * norm)
+    part, scale = load_rows(above_ref)
+    row_above = (after[half : half + 1] + part) * (scale * norm)
     out_ref[:, :128] = full[:, :128]
     low[...] = full[:, :128]
     high[...] = full[:, 128:]
@@ -431,11 +467,8 @@
     small = lanes((8, 128))
     own = jnp.where(small == SCALARS - 128 + 2, total, sums_ref[...])
     own_ref[...] = own
-    down_ref[:half, :] = scaled[first]
-    up_ref[:half, :] = scaled[last]
-    for ref in (down_ref, up_ref):
-        ref[half:, :128] = own
-        ref[half:, 128:] = own
+    store_edge(down_ref, scaled[first], own)
+    store_edge(up_ref, scaled[last], own)
 
 
 def total_of(value, length):
@@ -462,11 +495,11 @@
     count, block = stag_ref.shape[0], stag_ref.shape[1]
     half, rows = block // 2, count * block
     first, last = slice(0, half), slice(rows - half, rows)
-    low = dot(stag_below_ref[half:block, :half], below_ref[:half, :]) * flags_ref[1:2, :]
-    high = dot(stag_ref[count - 1, :half, half:], above_ref[:half, :]) * flags_ref[:1, :]
+    low = dot(stag_below_ref[half:block, :half], load_edge(below_ref)) * flags_ref[1:2, :]
+    high = dot(stag_ref[count - 1, :half, half:], load_edge(above_ref)) * flags_ref[:1, :]
     both = total_of(low * scaled_ref[first, :] + high * scaled_ref[last, :], length)
     both = both * (flags_ref[2:3, :1] * (2.0 * norm))
-    pair = own_ref[:1, :] + below_ref[half : half + 1, 128:]
+    pair = own_ref[:1, :] + below_ref[half + ROWS : half + ROWS + 1, :]
     pair = jnp.where(lanes(pair.shape) == SCALARS - 128 + 2, pair + both, pair)
     middle = slice(half, rows - half)
     for at, more in ((first, low), (middle, None), (last, high)):
@@ -515,13 +548,14 @@
             jnp.concatenate([tail[pl.ds(s + n, groups, stride=ROWS), :], blank], axis=1)
             for n in range(2)
         ]
-        row = jnp.where(
+        return jnp.where(
             lane_row < FOLD, shifted(parts[0], 128 - HALO), shifted(parts[1], FOLD + 128 - HALO)
         )
-        return row_back(row, matrix_ref, twiddle_ref, outer_ref)
-
-    for start, s in ((ROWS - 1, 0), (2 * ROWS, 2)):
-        row = halo_row(s)
+
+    stacked = jnp.concatenate([spec_ref[:, :WIDE], halo_row(0), halo_row(2)], axis=0)
+    products = both_products(stacked, matrix_ref)
+    halos = rows_back(products, groups * ROWS, twiddle_ref, outer_ref)
+    for start, row in zip((ROWS - 1, 2 * ROWS), halos, strict=True):
         low[pl.ds(start, groups, stride=stride), :] = row[:, :128]
         high[pl.ds(start, groups, stride=stride), :] = row[:, 128:]
 
@@ -529,7 +563,7 @@
         at = slice(start, start + ROWS)
         return jnp.concatenate([low[at, :], high[at, :]], axis=1)
 
-    cells = transform_back(spec_ref[:, :WIDE], groups, matrix_ref, twiddle_ref)
+    cells = transform_back(products, groups, twiddle_ref)
     for p in range(groups):
         v = jnp.where(own_ref[rows_of(p), :] > 0.0, cells[p], 0.0)
         first_ref[rows_of(p), :] = v
@@ -598,7 +632,7 @@
     twiddle_ref,
     out_ref,
 ):
-    cells = transform_back(spec_ref[...], groups, matrix_ref, twiddle_ref)
+    cells = transform_back(both_products(spec_ref[...], matrix_ref), groups, twiddle_ref)
     lane = lanes((ROWS, WIDE))
     cut = WIDE - length
     image_cut = SCALARS - length
@@ -751,7 +785,7 @@
     )(mask, east_cells, north_cells, flags, from_lat(wet_first, 1), stag_below)
     spec_rhs = after(spec_rhs, late)
 
-    edge = (half + 16, WIDE)
+    edge = (half + 2 * ROWS, 128)
 
     def blocks(spectrum):
         scaled, part, down, up = call(blocks_kernel, [wide, wide, edge, edge], name="blocks")(
@@ -777,7 +811,6 @@
         name="step",
     )(filtered, slab, *flat, matrices, twiddle, outer)
     spec_image = exchanged(spec)
-    edge = (half + ROWS, WIDE)
     scaled, part, down, up, own = call(
         lambda *r: sums_kernel(norm, length, *r), [wide, wide, edge, edge, (8, 128)], name="sums"
     )(spec_image, scale, aligned_inverse, stag, stag_below, flags, sums)

time: 110 us -> 109 us (level)
  waiting for transfers between devices: 17.4 us -> 16.2 us
    ppermute x9, waiting for transfers between devices: 10.3 us -> 9.08 us  [from_lat(): lax.ppermute(value, 'lat', [((d + steps) % count, d) for d in range(count)])]
where the time goes in v7:
time: 109 us; the launch traced here: 108 us
  blocking collectives  41.5 us (38%)
  starting transfers between devices  36.9 us (34%)
  waiting for transfers between devices  16.2 us (15%)
  Pallas kernels  9.41 us (9%)
  local copies, waits for them, and re-layouts  2.18 us (2%)
  other arithmetic  1.26 us (1%)
    all_to_all x3, blocking collectives, exchanged(): lax.all_to_all(parts, LON, split_axis=0, concat_axis=0, tiled=True)  41.5 us
    ppermute x9, starting transfers between devices, from_lat(): lax.ppermute(value, 'lat', [((d + steps) % count, d) for d in range(count)])  20.8 us
    all_to_all x3, starting transfers between devices, exchanged(): lax.all_to_all(parts, LON, split_axis=0, concat_axis=0, tiled=True)  16.1 us
    ppermute x9, waiting for transfers between devices, from_lat(): lax.ppermute(value, 'lat', [((d + steps) % count, d) for d in range(count)])  9.08 us
    all_to_all x3, waiting for transfers between devices, exchanged(): lax.all_to_all(parts, LON, split_axis=0, concat_axis=0, tiled=True)  7.08 us
  transfers between devices with their start and end apart: 12, of which 10 were waited for; matrix products, arithmetic and copies ran while one was open for 1% of the time, Pallas kernels for 2%

profile of v7, /device:TPU:1, one launch (start us, length us, event | category | flops | bytes accessed | tf_op | source)
XLA Modules:
  0.0 108.3 jit_solution(4372962480336874447)
XLA Ops:
  0.6 1.1 convert_multiply_fusion
  1.7 0.8 pack.1
  2.5 8.7 %all-to-all-start = ((f32[32,8,256]{2,1,0:T(8,128)}), f32[32,8,256]{2,1,0:T(8,128)S(1)}, u32[]{:S(2)}, u32[]{:S(2)}) async-start(f32[32,8,256]{2,1,0:T(8,128)} %bitcast), calls=%async_computation | async-start | bytes 524288 | tf_op jit(solution)/shard_map/all_to_all | solution.py:715
  11.3 0.1 broadcast_select_fusion.flags_ref.r_7_.r_5_
  11.4 0.7 constant_dynamic-slice_fusion
  12.1 0.0 copy-start
  12.1 0.1 pack_more.1.r_1_
  12.3 0.7 copy-done.2
  13.0 0.1 edges.1
  13.1 0.0 copy-start.9
  13.2 0.7 copy-done.9
  13.8 0.1 add_rsqrt_fusion.scale_ref.r_2_.r_1_
  14.0 6.3 %all-to-all-done = f32[32,8,256]{2,1,0:T(8,128)S(1)} async-done(((f32[32,8,256]{2,1,0:T(8,128)}), f32[32,8,256]{2,1,0:T(8,128)S(1)}, u32[]{:S(2)}, u32[]{:S(2)}) %all-to-all-start) | async-done | bytes 262176 | tf_op jit(solution)/shard_map/all_to_all | solution.py:715
  20.3 1.1 %forward.1 = f32[256,256]{1,0:T(8,128)} custom-call(f32[256,256]{1,0:T(8,128)S(1)} %bitcast.16, f32[256,256]{1,0:T(8,128)S(1)} %pack_more.1.r_1_, bf16[2,2,256,256]{3,2,1,0:T(8,128)(2,1)S(1)} %copy-done, f32[2,32,256]{2,1,0:T(8,128)S(1)} %copy-done.3), custom_call_target="tpu_custom_call" | custom-call | tf_op jit(solution)/shard_map/forward/pallas_call | solution.py:773
  21.4 3.7 %all-to-all-start.1 = ((f32[32,8,256]{2,1,0:T(8,128)}), f32[32,8,256]{2,1,0:T(8,128)S(1)}, u32[]{:S(2)}, u32[]{:S(2)}) async-start(f32[32,8,256]{2,1,0:T(8,128)} %bitcast.3), calls=%async_computation.1 | async-start | bytes 524288 | tf_op jit(solution)/shard_map/all_to_all | solution.py:715
  25.1 0.0 copy-start.7
  25.1 1.7 %collective-permute-start.1 = (f32[136,128]{1,0:T(8,128)S(1)}, f32[136,128]{1,0:T(8,128)S(1)}, u32[]{:S(2)}, u32[]{:S(2)}) collective-permute-start(f32[136,128]{1,0:T(8,128)S(1)} %get-tuple-element.44), channel_id=1, source_target_pairs={{224,0},{0,32},{32,64},{64,96},{96,128},{128,160},{160,192},{192,2... | collective-permute-start | bytes 208904 | tf_op jit(solution)/shard_map/ppermute | solution.py:720
  26.9 4.0 %collective-permute-start = (f32[8,256]{1,0:T(8,128)S(1)}, f32[8,256]{1,0:T(8,128)S(1)}, u32[]{:S(2)}, u32[]{:S(2)}) collective-permute-start(f32[8,256]{1,0:T(8,128)S(1)} %get-tuple-element.43), channel_id=1, source_target_pairs={{32,0},{64,32},{96,64},{128,96},{160,128},{192,160},{224,192},{0,2... | collective-permute-start | bytes 24584 | tf_op jit(solution)/shard_map/ppermute | solution.py:720
  30.9 0.8 collective-permute-done.wet_above_ref
  31.7 1.4 %collective-permute-done.1.from_below_ref.r_6_.r_4_ = f32[136,128]{1,0:T(8,128)S(1)} collective-permute-done((f32[136,128]{1,0:T(8,128)S(1)}, f32[136,128]{1,0:T(8,128)S(1)}, u32[]{:S(2)}, u32[]{:S(2)}) %collective-permute-start.1) | collective-permute-done | bytes 69664 | tf_op jit(solution)/shard_map/ppermute | solution.py:720
  33.1 0.6 pack_rest.1.r_8_
  33.6 0.6 all-to-all-done.1
  34.2 0.3 blocks.1
  34.5 5.7 %collective-permute-start.2 = (f32[80,128]{1,0:T(8,128)S(1)}, f32[80,128]{1,0:T(8,128)S(1)}, u32[]{:S(2)}, u32[]{:S(2)}) collective-permute-start(f32[80,128]{1,0:T(8,128)S(1)} %get-tuple-element.48), channel_id=1, source_target_pairs={{32,0},{64,32},{96,64},{128,96},{160,128},{192,160},{224,192},{0,2... | collective-permute-start | bytes 122888 | tf_op jit(solution)/shard_map/ppermute | solution.py:720
  40.2 0.5 coefficients.1
  40.7 0.6 collective-permute-done.2.r_3_
  41.3 3.0 %collective-permute-done.3.r_4_ = f32[80,128]{1,0:T(8,128)S(1)} collective-permute-done((f32[80,128]{1,0:T(8,128)S(1)}, f32[80,128]{1,0:T(8,128)S(1)}, u32[]{:S(2)}, u32[]{:S(2)}) %collective-permute-start.3) | collective-permute-done | bytes 40992 | tf_op jit(solution)/shard_map/ppermute | solution.py:720
  44.2 0.5 halo.1
  44.8 0.0 copy-start.8
  44.8 15.6 %all_to_all.30 = f32[32,8,384]{2,1,0:T(8,128)S(1)} all-to-all(f32[32,8,384]{2,1,0:T(8,128)S(1)} %bitcast.23), channel_id=1, replica_groups=mesh['lat'=8,'lon_0'=4,'lon_1'=4,'lon_2'=2] {'lon_0','lon_1','lon_2'}, dimensions={0} | all-to-all | bytes 786432 | tf_op jit(solution)/shard_map/all_to_all | solution.py:715
  60.4 1.8 %step.1 = (f32[256,256]{1,0:T(8,128)S(1)}, f32[256,256]{1,0:T(8,128)S(1)}, f32[256,256]{1,0:T(8,128)S(1)}, f32[8,128]{1,0:T(8,128)S(1)}) custom-call(f32[256,384]{1,0:T(8,128)S(1)} %bitcast.24, f32[256,256]{1,0:T(8,128)S(1)} %bitcast.18, f32[256,256]{1,0:T(8,128)S(1)} %get-tuple-element.51.r_2_.r_1_, f32[256,256]{1,0:T(8,128)S(1)} %get-tuple-element.52.r_3_, ...), custom_call_target="tpu_custom_call" | custom-call | tf_op jit(solution)/shard_map/step/pallas_call | solution.py:807
  62.2 12.3 %all_to_all.31 = f32[32,8,256]{2,1,0:T(8,128)S(1)} all-to-all(f32[32,8,256]{2,1,0:T(8,128)S(1)} %bitcast.27), channel_id=1, replica_groups=mesh['lat'=8,'lon_0'=4,'lon_1'=4,'lon_2'=2] {'lon_0','lon_1','lon_2'}, dimensions={0} | all-to-all | bytes 524288 | tf_op jit(solution)/shard_map/all_to_all | solution.py:715
  74.5 0.5 sums.1
  75.1 0.1 collective-permute-start.4
  75.1 1.5 %collective-permute-start.5 = (f32[80,128]{1,0:T(8,128)S(1)}, f32[80,128]{1,0:T(8,128)S(1)}, u32[]{:S(2)}, u32[]{:S(2)}) collective-permute-start(f32[80,128]{1,0:T(8,128)S(1)} %get-tuple-element.60), channel_id=1, source_target_pairs={{224,0},{0,32},{32,64},{64,96},{96,128},{128,160},{160,192},{192,2... | collective-permute-start | bytes 122888 | tf_op jit(solution)/shard_map/ppermute | solution.py:720
  76.6 0.2 unpack_first.1
  76.8 1.2 %collective-permute-done.4.r_3_ = f32[80,128]{1,0:T(8,128)S(1)} collective-permute-done((f32[80,128]{1,0:T(8,128)S(1)}, f32[80,128]{1,0:T(8,128)S(1)}, u32[]{:S(2)}, u32[]{:S(2)}) %collective-permute-start.4) | collective-permute-done | bytes 40992 | tf_op jit(solution)/shard_map/ppermute | solution.py:720
  78.0 1.3 %collective-permute-done.5.r_4_ = f32[80,128]{1,0:T(8,128)S(1)} collective-permute-done((f32[80,128]{1,0:T(8,128)S(1)}, f32[80,128]{1,0:T(8,128)S(1)}, u32[]{:S(2)}, u32[]{:S(2)}) %collective-permute-start.5) | collective-permute-done | bytes 40992 | tf_op jit(solution)/shard_map/ppermute | solution.py:720
  79.3 0.4 ends.1
  79.7 13.6 %all_to_all.32 = f32[32,8,256]{2,1,0:T(8,128)S(1)} all-to-all(f32[32,8,256]{2,1,0:T(8,128)S(1)} %bitcast.26), channel_id=1, replica_groups=mesh['lat'=8,'lon_0'=4,'lon_1'=4,'lon_2'=2] {'lon_0','lon_1','lon_2'}, dimensions={0} | all-to-all | bytes 524288 | tf_op jit(solution)/shard_map/all_to_all | solution.py:715
  93.3 1.2 %last.1 = f32[256,256]{1,0:T(8,128)} custom-call(f32[256,256]{1,0:T(8,128)S(1)} %bitcast.13, f32[256,256]{1,0:T(8,128)S(1)} %get-tuple-element.51.r_2_.r_1_, f32[256,256]{1,0:T(8,128)S(1)} %get-tuple-element.65.r_2_, f32[256,256]{1,0:T(8,128)S(1)} %get-tuple-element.62.r_1_.r_3_, bf16[2,2,256,256]{3,2,1,0:T(8,128)(2,1)S(1)} %copy-done, ...), custom_call_target="tpu_custom_call" | custom-call | tf_op jit(solution)/shard_map/last/pallas_call | solution.py:832
  94.5 3.7 %all-to-all-start.5 = ((f32[32,8,256]{2,1,0:T(8,128)}), f32[32,8,256]{2,1,0:T(8,128)S(1)}, u32[]{:S(2)}, u32[]{:S(2)}) async-start(f32[32,8,256]{2,1,0:T(8,128)} %bitcast.11), calls=%async_computation.5 | async-start | bytes 524288 | tf_op jit(solution)/shard_map/all_to_all | solution.py:715
  98.3 4.3 %collective-permute-start.8 = (f32[8,128]{1,0:T(8,128)S(1)}, f32[8,128]{1,0:T(8,128)S(1)}, u32[]{:S(2)}, u32[]{:S(2)}) collective-permute-start(f32[8,128]{1,0:T(8,128)S(1)} %gather.1.r_5_), channel_id=1, source_target_pairs={{128,0},{160,32},{192,64},{224,96},{0,128},{32,160},{64,192},{96,2... | collective-permute-start | bytes 12296 | tf_op jit(solution)/shard_map/ppermute | solution.py:720
  102.6 3.6 %collective-permute-start.6 = (f32[8,128]{1,0:T(8,128)S(1)}, f32[8,128]{1,0:T(8,128)S(1)}, u32[]{:S(2)}, u32[]{:S(2)}) collective-permute-start(f32[8,128]{1,0:T(8,128)S(1)} %gather.1.r_5_), channel_id=1, source_target_pairs={{64,0},{96,32},{128,64},{160,96},{192,128},{224,160},{0,192},{32,2... | collective-permute-start | bytes 12296 | tf_op jit(solution)/shard_map/ppermute | solution.py:720
  106.2 0.1 unpack_image.1.r_2_
  106.3 0.9 collective-permute-done.7.r_7_
  107.2 0.2 all-to-all-done.5
  107.4 1.0 finish.1
  (21 shorter events, 0.1 us)
Async XLA Ops:
  2.5 9.6 %copy-start.1 = (s32[135,256]{1,0:T(8,128)S(1)}, s32[135,256]{1,0:T(8,128)}, u32[]{:S(2)}) copy-start(s32[135,256]{1,0:T(8,128)} %r_4_.2) | copy-start | bytes 414724
  2.5 9.6 %copy-start.5 = (f32[135,256]{1,0:T(8,128)S(1)}, f32[135,256]{1,0:T(8,128)}, u32[]{:S(2)}) copy-start(f32[135,256]{1,0:T(8,128)} %east_ref.1) | copy-start | bytes 414724
  2.5 9.7 %copy-start.6 = (f32[135,256]{1,0:T(8,128)S(1)}, f32[135,256]{1,0:T(8,128)}, u32[]{:S(2)}) copy-start(f32[135,256]{1,0:T(8,128)} %north_ref.1) | copy-start | bytes 414724
  2.5 17.7 %all-to-all-start = ((f32[32,8,256]{2,1,0:T(8,128)}), f32[32,8,256]{2,1,0:T(8,128)S(1)}, u32[]{:S(2)}, u32[]{:S(2)}) async-start(f32[32,8,256]{2,1,0:T(8,128)} %bitcast), calls=%async_computation | async-start | bytes 524288 | tf_op jit(solution)/shard_map/all_to_all | solution.py:715
  12.1 0.9 copy-start.2
  12.1 8.2 %copy-start = (bf16[2,2,256,256]{3,2,1,0:T(8,128)(2,1)S(1)}, bf16[2,2,256,256]{3,2,1,0:T(8,128)(2,1)}, u32[]{:S(2)}) copy-start(bf16[2,2,256,256]{3,2,1,0:T(8,128)(2,1)} %constant.45.clone.r_2_.r_5_.r_4_) | copy-start | bytes 1572868
  13.1 0.7 copy-start.9
  13.8 6.4 %copy-start.3 = (f32[2,32,256]{2,1,0:T(8,128)S(1)}, f32[2,32,256]{2,1,0:T(8,128)}, u32[]{:S(2)}) copy-start(f32[2,32,256]{2,1,0:T(8,128)} %constant.46.clone.r_3_.r_6_.r_5_) | copy-start | bytes 196612
  21.4 12.8 %all-to-all-start.1 = ((f32[32,8,256]{2,1,0:T(8,128)}), f32[32,8,256]{2,1,0:T(8,128)S(1)}, u32[]{:S(2)}, u32[]{:S(2)}) async-start(f32[32,8,256]{2,1,0:T(8,128)} %bitcast.3), calls=%async_computation.1 | async-start | bytes 524288 | tf_op jit(solution)/shard_map/all_to_all | solution.py:715
  25.1 9.1 %copy-start.7 = (f32[2,128,128]{2,1,0:T(8,128)S(1)}, f32[2,128,128]{2,1,0:T(8,128)}, u32[]{:S(2)}) copy-start(f32[2,128,128]{2,1,0:T(8,128)} %r_2_.2) | copy-start | bytes 393220
  25.1 7.9 %collective-permute-start.1 = (f32[136,128]{1,0:T(8,128)S(1)}, f32[136,128]{1,0:T(8,128)S(1)}, u32[]{:S(2)}, u32[]{:S(2)}) collective-permute-start(f32[136,128]{1,0:T(8,128)S(1)} %get-tuple-element.44), channel_id=1, source_target_pairs={{224,0},{0,32},{32,64},{64,96},{96,128},{128,160},{160,192},{192,2... | collective-permute-start | bytes 208904 | tf_op jit(solution)/shard_map/ppermute | solution.py:720
  26.9 4.8 %collective-permute-start = (f32[8,256]{1,0:T(8,128)S(1)}, f32[8,256]{1,0:T(8,128)S(1)}, u32[]{:S(2)}, u32[]{:S(2)}) collective-permute-start(f32[8,256]{1,0:T(8,128)S(1)} %get-tuple-element.43), channel_id=1, source_target_pairs={{32,0},{64,32},{96,64},{128,96},{160,128},{192,160},{224,192},{0,2... | collective-permute-start | bytes 24584 | tf_op jit(solution)/shard_map/ppermute | solution.py:720
  34.5 6.8 %collective-permute-start.2 = (f32[80,128]{1,0:T(8,128)S(1)}, f32[80,128]{1,0:T(8,128)S(1)}, u32[]{:S(2)}, u32[]{:S(2)}) collective-permute-start(f32[80,128]{1,0:T(8,128)S(1)} %get-tuple-element.48), channel_id=1, source_target_pairs={{32,0},{64,32},{96,64},{128,96},{160,128},{192,160},{224,192},{0,2... | collective-permute-start | bytes 122888 | tf_op jit(solution)/shard_map/ppermute | solution.py:720
  40.2 4.1 %collective-permute-start.3 = (f32[80,128]{1,0:T(8,128)S(1)}, f32[80,128]{1,0:T(8,128)S(1)}, u32[]{:S(2)}, u32[]{:S(2)}) collective-permute-start(f32[80,128]{1,0:T(8,128)S(1)} %get-tuple-element.49), channel_id=1, source_target_pairs={{224,0},{0,32},{32,64},{64,96},{96,128},{128,160},{160,192},{192,2... | collective-permute-start | bytes 122888 | tf_op jit(solution)/shard_map/ppermute | solution.py:720
  44.8 15.6 %copy-start.8 = (f32[32,64]{1,0:T(8,128)S(1)}, f32[32,64]{1,0:T(8,128)}, u32[]{:S(2)}) copy-start(f32[32,64]{1,0:T(8,128)} %constant.47.clone.r_7_) | copy-start | bytes 24580
  75.1 2.9 %collective-permute-start.4 = (f32[80,128]{1,0:T(8,128)S(1)}, f32[80,128]{1,0:T(8,128)S(1)}, u32[]{:S(2)}, u32[]{:S(2)}) collective-permute-start(f32[80,128]{1,0:T(8,128)S(1)} %get-tuple-element.59), channel_id=1, source_target_pairs={{32,0},{64,32},{96,64},{128,96},{160,128},{192,160},{224,192},{0,2... | collective-permute-start | bytes 122888 | tf_op jit(solution)/shard_map/ppermute | solution.py:720
  75.1 4.1 %collective-permute-start.5 = (f32[80,128]{1,0:T(8,128)S(1)}, f32[80,128]{1,0:T(8,128)S(1)}, u32[]{:S(2)}, u32[]{:S(2)}) collective-permute-start(f32[80,128]{1,0:T(8,128)S(1)} %get-tuple-element.60), channel_id=1, source_target_pairs={{224,0},{0,32},{32,64},{64,96},{96,128},{128,160},{160,192},{192,2... | collective-permute-start | bytes 122888 | tf_op jit(solution)/shard_map/ppermute | solution.py:720
  94.5 12.8 %all-to-all-start.5 = ((f32[32,8,256]{2,1,0:T(8,128)}), f32[32,8,256]{2,1,0:T(8,128)S(1)}, u32[]{:S(2)}, u32[]{:S(2)}) async-start(f32[32,8,256]{2,1,0:T(8,128)} %bitcast.11), calls=%async_computation.5 | async-start | bytes 524288 | tf_op jit(solution)/shard_map/all_to_all | solution.py:715
  98.3 9.1 %copy-start.4 = (f32[135,256]{1,0:T(8,128)S(1)}, f32[135,256]{1,0:T(8,128)}, u32[]{:S(2)}) copy-start(f32[135,256]{1,0:T(8,128)} %r_3_.3) | copy-start | bytes 414724
  98.3 8.0 %collective-permute-start.8 = (f32[8,128]{1,0:T(8,128)S(1)}, f32[8,128]{1,0:T(8,128)S(1)}, u32[]{:S(2)}, u32[]{:S(2)}) collective-permute-start(f32[8,128]{1,0:T(8,128)S(1)} %gather.1.r_5_), channel_id=1, source_target_pairs={{128,0},{160,32},{192,64},{224,96},{0,128},{32,160},{64,192},{96,2... | collective-permute-start | bytes 12296 | tf_op jit(solution)/shard_map/ppermute | solution.py:720
  102.6 4.6 %collective-permute-start.7 = (f32[8,128]{1,0:T(8,128)S(1)}, f32[8,128]{1,0:T(8,128)S(1)}, u32[]{:S(2)}, u32[]{:S(2)}) collective-permute-start(f32[8,128]{1,0:T(8,128)S(1)} %gather.1.r_5_), channel_id=1, source_target_pairs={{192,0},{224,32},{0,64},{32,96},{64,128},{96,160},{128,192},{160,2... | collective-permute-start | bytes 12296 | tf_op jit(solution)/shard_map/ppermute | solution.py:720
  102.6 4.6 %collective-permute-start.6 = (f32[8,128]{1,0:T(8,128)S(1)}, f32[8,128]{1,0:T(8,128)S(1)}, u32[]{:S(2)}, u32[]{:S(2)}) collective-permute-start(f32[8,128]{1,0:T(8,128)S(1)} %gather.1.r_5_), channel_id=1, source_target_pairs={{64,0},{96,32},{128,64},{160,96},{192,128},{224,160},{0,192},{32,2... | collective-permute-start | bytes 12296 | tf_op jit(solution)/shard_map/ppermute | solution.py:720

commit v8 on v7

--- a/solution.py
+++ b/solution.py
@@ -738,28 +738,41 @@
     length, rows = surface_forcing.shape
     norm = 1.0 / (groups * length)
     matrices, twiddle, outer, wave = tables(groups, length)
-    channel = lax.axis_index(LON)
     count, block = aligned_inverse.shape[0], aligned_inverse.shape[1]
     half = block // 2
     wide = (rows, WIDE)
     transforms = [wide, wide]
 
     cells = (length, rows)
+    places = (lax.axis_index(LON), lax.axis_index("lat"))
+    flag_row = lax.broadcasted_iota(jnp.int32, (8, WIDE), 0)
+    surface_forcing, channel, lat = lax.optimization_barrier((surface_forcing, *places))
     wet_cells = ocean_mask.astype(jnp.float32)
     own_cells = wet_cells * self_coupling
     packed = call(pack_kernel, wide, [wide], name="pack")(wet_cells * surface_forcing, own_cells)
     slab = exchanged(packed)
 
-    mask, east_cells, north_cells, weights, stag = lax.optimization_barrier(
-        (ocean_mask, east_coupling, north_coupling, zonal_weight, staggered_inverse, packed)
-    )[:-1]
+    mask, east_cells = lax.optimization_barrier((ocean_mask, east_coupling, slab))[:2]
     more = call(pack_more_kernel, wide, [wide], name="pack_more")(own_cells, mask, east_cells)
+    spectrum = call(lambda *r: forward_kernel(groups, *r), wide, transforms, name="forward")(
+        slab, more, matrices, twiddle
+    )
+    spec_rhs = exchanged(spectrum)
+
+    north_cells, stag = lax.optimization_barrier((north_coupling, staggered_inverse, spectrum))[:-1]
     wet_first, low_last = call(
         edges_kernel, [(ROWS, WIDE), (block + ROWS, 128)], [(WIDE, 128)], name="edges"
     )(mask, north_cells, stag)
+    weights, channel, lat, flag_row = lax.optimization_barrier(
+        (
+            zonal_weight,
+            channel,
+            lat,
+            flag_row,
+            wet_first,
+        )
+    )[:-1]
     scale = lax.rsqrt(1.0 + weights[:, None] * lax.dynamic_slice_in_dim(wave, channel, 1, 0))
-    lat = lax.axis_index("lat")
-    flag_row = lax.broadcasted_iota(jnp.int32, (8, WIDE), 0)
     north_of, south_of, weight = (
         jnp.where(condition, yes, no).astype(jnp.float32)
         for condition, yes, no in (
@@ -769,13 +782,6 @@
         )
     )
     flags = jnp.where(flag_row == 0, north_of, jnp.where(flag_row == 1, south_of, weight))
-    slab = after(slab, scale, flags, wet_first)
-    spectrum = call(lambda *r: forward_kernel(groups, *r), wide, transforms, name="forward")(
-        slab, more, matrices, twiddle
-    )
-    spec_rhs = exchanged(spectrum)
-
-    wet_first, low_last = lax.optimization_barrier((wet_first, low_last, spectrum))[:2]
     stag_below = from_lat(low_last, -1)
     late = call(
         pack_rest_kernel,
@@ -783,7 +789,7 @@
         [(WIDE + 128, rows), wide, (rows, 128), (rows, 128), (rows, 128)],
         name="pack_rest",
     )(mask, east_cells, north_cells, flags, from_lat(wet_first, 1), stag_below)
-    spec_rhs = after(spec_rhs, late)
+    spec_rhs = after(spec_rhs, late, scale, flags)
 
     edge = (half + 2 * ROWS, 128)
 

time: 109 us -> 110 us (level)
  blocking collectives: 41.5 us -> 59.8 us
  starting transfers between devices: 36.9 us -> 23.5 us
  waiting for transfers between devices: 16.2 us -> 13 us
    all_to_all x3 -> x4, blocking collectives: 41.5 us -> 59.8 us  [exchanged(): lax.all_to_all(parts, LON, split_axis=0, concat_axis=0, tiled=True)]
    all_to_all x3 -> x2, starting transfers between devices: 16.1 us -> 7.55 us  [exchanged(): lax.all_to_all(parts, LON, split_axis=0, concat_axis=0, tiled=True)]
    all_to_all x3 -> x2, waiting for transfers between devices: 7.08 us -> 2.02 us  [exchanged(): lax.all_to_all(parts, LON, split_axis=0, concat_axis=0, tiled=True)]
    ppermute x9, starting transfers between devices: 20.8 us -> 16 us  [from_lat(): lax.ppermute(value, 'lat', [((d + steps) % count, d) for d in range(count)])]
    ppermute x9, waiting for transfers between devices: 9.08 us -> 11 us  [from_lat(): lax.ppermute(value, 'lat', [((d + steps) % count, d) for d in range(count)])]
  transfers between devices with their start and end apart: 12 -> 11, of which waited for: 10 -> 8; matrix products, arithmetic and copies ran while one was open for 1% -> 1% of each run, Pallas kernels for 2% -> 1%
where the time goes in v8:
time: 110 us; the launch traced here: 109 us
  blocking collectives  59.8 us (54%)
  starting transfers between devices  23.5 us (21%)
  waiting for transfers between devices  13 us (12%)
  Pallas kernels  8.7 us (8%)
  local copies, waits for them, and re-layouts  2.12 us (2%)
  other arithmetic  1.18 us (1%)
    all_to_all x4, blocking collectives, exchanged(): lax.all_to_all(parts, LON, split_axis=0, concat_axis=0, tiled=True)  59.8 us
    ppermute x9, starting transfers between devices, from_lat(): lax.ppermute(value, 'lat', [((d + steps) % count, d) for d in range(count)])  16 us
    ppermute x9, waiting for transfers between devices, from_lat(): lax.ppermute(value, 'lat', [((d + steps) % count, d) for d in range(count)])  11 us
    all_to_all x2, starting transfers between devices, exchanged(): lax.all_to_all(parts, LON, split_axis=0, concat_axis=0, tiled=True)  7.55 us
  transfers between devices with their start and end apart: 11, of which 8 were waited for; matrix products, arithmetic and copies ran while one was open for 1% of the time, Pallas kernels for 1%

profile of v8, /device:TPU:1, one launch (start us, length us, event | category | flops | bytes accessed | tf_op | source)
XLA Modules:
  0.0 109.2 jit_solution(17917544144180983795)
XLA Ops:
  0.6 1.1 convert_multiply_fusion
  1.7 0.0 copy-start.1
  1.7 0.0 copy-start.5
  1.7 0.1 pack.1
  1.9 0.0 copy-start
  1.9 17.5 %all_to_all.30 = f32[32,8,256]{2,1,0:T(8,128)S(1)} all-to-all(f32[32,8,256]{2,1,0:T(8,128)S(1)} %bitcast.27), channel_id=1, replica_groups=mesh['lat'=8,'lon_0'=4,'lon_1'=4,'lon_2'=2] {'lon_0','lon_1','lon_2'}, dimensions={0} | all-to-all | bytes 524288 | tf_op jit(solution)/shard_map/all_to_all | solution.py:715
  19.4 0.1 pack_more.1.r_1_
  19.5 0.7 copy-done.3
  20.2 1.1 %forward.1 = f32[256,256]{1,0:T(8,128)} custom-call(f32[256,256]{1,0:T(8,128)S(1)} %bitcast.16, f32[256,256]{1,0:T(8,128)S(1)} %pack_more.1.r_1_, bf16[2,2,256,256]{3,2,1,0:T(8,128)(2,1)S(1)} %copy-done, f32[2,32,256]{2,1,0:T(8,128)S(1)} %copy-done.3), custom_call_target="tpu_custom_call" | custom-call | tf_op jit(solution)/shard_map/forward/pallas_call | solution.py:757
  21.4 3.8 %all-to-all-start.1 = ((f32[32,8,256]{2,1,0:T(8,128)}), f32[32,8,256]{2,1,0:T(8,128)S(1)}, u32[]{:S(2)}, u32[]{:S(2)}) async-start(f32[32,8,256]{2,1,0:T(8,128)} %bitcast.2), calls=%async_computation.1 | async-start | bytes 524288 | tf_op jit(solution)/shard_map/all_to_all | solution.py:715
  25.2 0.1 edges.1
  25.4 5.7 %collective-permute-start = (f32[8,256]{1,0:T(8,128)S(1)}, f32[8,256]{1,0:T(8,128)S(1)}, u32[]{:S(2)}, u32[]{:S(2)}) collective-permute-start(f32[8,256]{1,0:T(8,128)S(1)} %get-tuple-element.45), channel_id=1, source_target_pairs={{32,0},{64,32},{96,64},{128,96},{160,128},{192,160},{224,192},{0,2... | collective-permute-start | bytes 24584 | tf_op jit(solution)/shard_map/ppermute | solution.py:720
  31.0 0.0 collective-permute-start.1
  31.0 0.7 constant_dynamic-slice_fusion
  31.7 0.7 copy-done.9
  32.4 0.1 add_rsqrt_fusion.scale_ref.r_2_.r_1_
  32.6 0.0 copy-start.7
  32.6 2.8 %collective-permute-done.1.from_below_ref.r_6_.r_4_ = f32[136,128]{1,0:T(8,128)S(1)} collective-permute-done((f32[136,128]{1,0:T(8,128)S(1)}, f32[136,128]{1,0:T(8,128)S(1)}, u32[]{:S(2)}, u32[]{:S(2)}) %collective-permute-start.1) | collective-permute-done | bytes 69664 | tf_op jit(solution)/shard_map/ppermute | solution.py:720
  35.4 0.6 pack_rest.1.r_8_
  36.0 0.3 blocks.1
  36.3 4.0 %collective-permute-start.2 = (f32[80,128]{1,0:T(8,128)S(1)}, f32[80,128]{1,0:T(8,128)S(1)}, u32[]{:S(2)}, u32[]{:S(2)}) collective-permute-start(f32[80,128]{1,0:T(8,128)S(1)} %get-tuple-element.54), channel_id=1, source_target_pairs={{32,0},{64,32},{96,64},{128,96},{160,128},{192,160},{224,192},{0,2... | collective-permute-start | bytes 122888 | tf_op jit(solution)/shard_map/ppermute | solution.py:720
  40.3 0.5 coefficients.1
  40.8 0.6 collective-permute-done.2.r_3_
  41.4 3.0 %collective-permute-done.3.r_4_ = f32[80,128]{1,0:T(8,128)S(1)} collective-permute-done((f32[80,128]{1,0:T(8,128)S(1)}, f32[80,128]{1,0:T(8,128)S(1)}, u32[]{:S(2)}, u32[]{:S(2)}) %collective-permute-start.3) | collective-permute-done | bytes 40992 | tf_op jit(solution)/shard_map/ppermute | solution.py:720
  44.3 0.5 halo.1
  44.9 0.0 copy-start.8
  44.9 16.4 %all_to_all.31 = f32[32,8,384]{2,1,0:T(8,128)S(1)} all-to-all(f32[32,8,384]{2,1,0:T(8,128)S(1)} %bitcast.23), channel_id=1, replica_groups=mesh['lat'=8,'lon_0'=4,'lon_1'=4,'lon_2'=2] {'lon_0','lon_1','lon_2'}, dimensions={0} | all-to-all | bytes 786432 | tf_op jit(solution)/shard_map/all_to_all | solution.py:715
  61.2 1.8 %step.1 = (f32[256,256]{1,0:T(8,128)S(1)}, f32[256,256]{1,0:T(8,128)S(1)}, f32[256,256]{1,0:T(8,128)S(1)}, f32[8,128]{1,0:T(8,128)S(1)}) custom-call(f32[256,384]{1,0:T(8,128)S(1)} %bitcast.24, f32[256,256]{1,0:T(8,128)S(1)} %bitcast.18, f32[256,256]{1,0:T(8,128)S(1)} %get-tuple-element.57.r_2_.r_1_, f32[256,256]{1,0:T(8,128)S(1)} %get-tuple-element.58.r_3_, ...), custom_call_target="tpu_custom_call" | custom-call | tf_op jit(solution)/shard_map/step/pallas_call | solution.py:813
  63.1 12.3 %all_to_all.32 = f32[32,8,256]{2,1,0:T(8,128)S(1)} all-to-all(f32[32,8,256]{2,1,0:T(8,128)S(1)} %bitcast.28), channel_id=1, replica_groups=mesh['lat'=8,'lon_0'=4,'lon_1'=4,'lon_2'=2] {'lon_0','lon_1','lon_2'}, dimensions={0} | all-to-all | bytes 524288 | tf_op jit(solution)/shard_map/all_to_all | solution.py:715
  75.4 0.5 sums.1
  76.0 0.1 collective-permute-start.4
  76.0 1.5 %collective-permute-start.5 = (f32[80,128]{1,0:T(8,128)S(1)}, f32[80,128]{1,0:T(8,128)S(1)}, u32[]{:S(2)}, u32[]{:S(2)}) collective-permute-start(f32[80,128]{1,0:T(8,128)S(1)} %get-tuple-element.66), channel_id=1, source_target_pairs={{224,0},{0,32},{32,64},{64,96},{96,128},{128,160},{160,192},{192,2... | collective-permute-start | bytes 122888 | tf_op jit(solution)/shard_map/ppermute | solution.py:720
  77.5 0.2 unpack_first.1
  77.7 1.2 %collective-permute-done.4.r_3_ = f32[80,128]{1,0:T(8,128)S(1)} collective-permute-done((f32[80,128]{1,0:T(8,128)S(1)}, f32[80,128]{1,0:T(8,128)S(1)}, u32[]{:S(2)}, u32[]{:S(2)}) %collective-permute-start.4) | collective-permute-done | bytes 40992 | tf_op jit(solution)/shard_map/ppermute | solution.py:720
  78.9 1.3 %collective-permute-done.5.r_4_ = f32[80,128]{1,0:T(8,128)S(1)} collective-permute-done((f32[80,128]{1,0:T(8,128)S(1)}, f32[80,128]{1,0:T(8,128)S(1)}, u32[]{:S(2)}, u32[]{:S(2)}) %collective-permute-start.5) | collective-permute-done | bytes 40992 | tf_op jit(solution)/shard_map/ppermute | solution.py:720
  80.2 0.4 ends.1
  80.6 13.6 %all_to_all.33 = f32[32,8,256]{2,1,0:T(8,128)S(1)} all-to-all(f32[32,8,256]{2,1,0:T(8,128)S(1)} %bitcast.26), channel_id=1, replica_groups=mesh['lat'=8,'lon_0'=4,'lon_1'=4,'lon_2'=2] {'lon_0','lon_1','lon_2'}, dimensions={0} | all-to-all | bytes 524288 | tf_op jit(solution)/shard_map/all_to_all | solution.py:715
  94.2 1.2 %last.1 = f32[256,256]{1,0:T(8,128)} custom-call(f32[256,256]{1,0:T(8,128)S(1)} %bitcast.13, f32[256,256]{1,0:T(8,128)S(1)} %get-tuple-element.57.r_2_.r_1_, f32[256,256]{1,0:T(8,128)S(1)} %get-tuple-element.71.r_2_, f32[256,256]{1,0:T(8,128)S(1)} %get-tuple-element.68.r_1_.r_3_, bf16[2,2,256,256]{3,2,1,0:T(8,128)(2,1)S(1)} %copy-done, ...), custom_call_target="tpu_custom_call" | custom-call | tf_op jit(solution)/shard_map/last/pallas_call | solution.py:838
  95.4 3.7 %all-to-all-start.5 = ((f32[32,8,256]{2,1,0:T(8,128)}), f32[32,8,256]{2,1,0:T(8,128)S(1)}, u32[]{:S(2)}, u32[]{:S(2)}) async-start(f32[32,8,256]{2,1,0:T(8,128)} %bitcast.11), calls=%async_computation.5 | async-start | bytes 524288 | tf_op jit(solution)/shard_map/all_to_all | solution.py:715
  99.2 1.2 %collective-permute-start.8 = (f32[8,128]{1,0:T(8,128)S(1)}, f32[8,128]{1,0:T(8,128)S(1)}, u32[]{:S(2)}, u32[]{:S(2)}) collective-permute-start(f32[8,128]{1,0:T(8,128)S(1)} %gather.1.r_5_), channel_id=1, source_target_pairs={{128,0},{160,32},{192,64},{224,96},{0,128},{32,160},{64,192},{96,2... | collective-permute-start | bytes 12296 | tf_op jit(solution)/shard_map/ppermute | solution.py:720
  100.4 0.6 collective-permute-start.7
  101.0 3.0 %collective-permute-start.6 = (f32[8,128]{1,0:T(8,128)S(1)}, f32[8,128]{1,0:T(8,128)S(1)}, u32[]{:S(2)}, u32[]{:S(2)}) collective-permute-start(f32[8,128]{1,0:T(8,128)S(1)} %gather.1.r_5_), channel_id=1, source_target_pairs={{64,0},{96,32},{128,64},{160,96},{192,128},{224,160},{0,192},{32,2... | collective-permute-start | bytes 12296 | tf_op jit(solution)/shard_map/ppermute | solution.py:720
  104.0 0.1 unpack_image.1.r_2_
  104.1 1.8 %collective-permute-done.8.r_8_ = f32[8,128]{1,0:T(8,128)S(1)} collective-permute-done((f32[8,128]{1,0:T(8,128)S(1)}, f32[8,128]{1,0:T(8,128)S(1)}, u32[]{:S(2)}, u32[]{:S(2)}) %collective-permute-start.8) | collective-permute-done | bytes 4128 | tf_op jit(solution)/shard_map/ppermute | solution.py:720
  105.9 0.0 collective-permute-done.7.r_7_
  105.9 0.3 collective-permute-done.6.r_6_
  106.2 2.0 %all-to-all-done.5 = f32[32,8,256]{2,1,0:T(8,128)S(1)} async-done(((f32[32,8,256]{2,1,0:T(8,128)}), f32[32,8,256]{2,1,0:T(8,128)S(1)}, u32[]{:S(2)}, u32[]{:S(2)}) %all-to-all-start.5) | async-done | bytes 262176 | tf_op jit(solution)/shard_map/all_to_all | solution.py:715
  108.2 1.0 finish.1
  (19 shorter events, 0.1 us)
Async XLA Ops:
  1.7 17.7 %copy-start.1 = (s32[135,256]{1,0:T(8,128)S(1)}, s32[135,256]{1,0:T(8,128)}, u32[]{:S(2)}) copy-start(s32[135,256]{1,0:T(8,128)} %r_4_.2) | copy-start | bytes 414724
  1.7 17.7 %copy-start.5 = (f32[135,256]{1,0:T(8,128)S(1)}, f32[135,256]{1,0:T(8,128)}, u32[]{:S(2)}) copy-start(f32[135,256]{1,0:T(8,128)} %east_ref.1) | copy-start | bytes 414724
  1.9 17.7 %copy-start = (bf16[2,2,256,256]{3,2,1,0:T(8,128)(2,1)S(1)}, bf16[2,2,256,256]{3,2,1,0:T(8,128)(2,1)}, u32[]{:S(2)}) copy-start(bf16[2,2,256,256]{3,2,1,0:T(8,128)(2,1)} %constant.44.clone.r_2_.r_5_.r_4_) | copy-start | bytes 1572868
  19.4 0.8 copy-start.3
  21.4 3.9 %copy-start.2 = (f32[2,128,128]{2,1,0:T(8,128)S(1)}, f32[2,128,128]{2,1,0:T(8,128)}, u32[]{:S(2)}) copy-start(f32[2,128,128]{2,1,0:T(8,128)} %r_5_.3) | copy-start | bytes 393220
  21.4 3.9 %copy-start.6 = (f32[135,256]{1,0:T(8,128)S(1)}, f32[135,256]{1,0:T(8,128)}, u32[]{:S(2)}) copy-start(f32[135,256]{1,0:T(8,128)} %north_ref.1) | copy-start | bytes 414724
  21.4 14.6 %all-to-all-start.1 = ((f32[32,8,256]{2,1,0:T(8,128)}), f32[32,8,256]{2,1,0:T(8,128)S(1)}, u32[]{:S(2)}, u32[]{:S(2)}) async-start(f32[32,8,256]{2,1,0:T(8,128)} %bitcast.2), calls=%async_computation.1 | async-start | bytes 524288 | tf_op jit(solution)/shard_map/all_to_all | solution.py:715
  25.4 7.2 %collective-permute-start = (f32[8,256]{1,0:T(8,128)S(1)}, f32[8,256]{1,0:T(8,128)S(1)}, u32[]{:S(2)}, u32[]{:S(2)}) collective-permute-start(f32[8,256]{1,0:T(8,128)S(1)} %get-tuple-element.45), channel_id=1, source_target_pairs={{32,0},{64,32},{96,64},{128,96},{160,128},{192,160},{224,192},{0,2... | collective-permute-start | bytes 24584 | tf_op jit(solution)/shard_map/ppermute | solution.py:720
  31.0 4.4 %collective-permute-start.1 = (f32[136,128]{1,0:T(8,128)S(1)}, f32[136,128]{1,0:T(8,128)S(1)}, u32[]{:S(2)}, u32[]{:S(2)}) collective-permute-start(f32[136,128]{1,0:T(8,128)S(1)} %get-tuple-element.49), channel_id=1, source_target_pairs={{224,0},{0,32},{32,64},{64,96},{96,128},{128,160},{160,192},{192,2... | collective-permute-start | bytes 208904 | tf_op jit(solution)/shard_map/ppermute | solution.py:720
  31.7 0.7 copy-start.9
  32.6 3.4 %copy-start.7 = (f32[2,128,128]{2,1,0:T(8,128)S(1)}, f32[2,128,128]{2,1,0:T(8,128)}, u32[]{:S(2)}) copy-start(f32[2,128,128]{2,1,0:T(8,128)} %r_2_.2) | copy-start | bytes 393220
  36.3 5.1 %collective-permute-start.2 = (f32[80,128]{1,0:T(8,128)S(1)}, f32[80,128]{1,0:T(8,128)S(1)}, u32[]{:S(2)}, u32[]{:S(2)}) collective-permute-start(f32[80,128]{1,0:T(8,128)S(1)} %get-tuple-element.54), channel_id=1, source_target_pairs={{32,0},{64,32},{96,64},{128,96},{160,128},{192,160},{224,192},{0,2... | collective-permute-start | bytes 122888 | tf_op jit(solution)/shard_map/ppermute | solution.py:720
  40.3 4.1 %collective-permute-start.3 = (f32[80,128]{1,0:T(8,128)S(1)}, f32[80,128]{1,0:T(8,128)S(1)}, u32[]{:S(2)}, u32[]{:S(2)}) collective-permute-start(f32[80,128]{1,0:T(8,128)S(1)} %get-tuple-element.55), channel_id=1, source_target_pairs={{224,0},{0,32},{32,64},{64,96},{96,128},{128,160},{160,192},{192,2... | collective-permute-start | bytes 122888 | tf_op jit(solution)/shard_map/ppermute | solution.py:720
  44.9 16.4 %copy-start.8 = (f32[32,64]{1,0:T(8,128)S(1)}, f32[32,64]{1,0:T(8,128)}, u32[]{:S(2)}) copy-start(f32[32,64]{1,0:T(8,128)} %constant.47.clone.r_7_) | copy-start | bytes 24580
  76.0 2.9 %collective-permute-start.4 = (f32[80,128]{1,0:T(8,128)S(1)}, f32[80,128]{1,0:T(8,128)S(1)}, u32[]{:S(2)}, u32[]{:S(2)}) collective-permute-start(f32[80,128]{1,0:T(8,128)S(1)} %get-tuple-element.65), channel_id=1, source_target_pairs={{32,0},{64,32},{96,64},{128,96},{160,128},{192,160},{224,192},{0,2... | collective-permute-start | bytes 122888 | tf_op jit(solution)/shard_map/ppermute | solution.py:720
  76.0 4.1 %collective-permute-start.5 = (f32[80,128]{1,0:T(8,128)S(1)}, f32[80,128]{1,0:T(8,128)S(1)}, u32[]{:S(2)}, u32[]{:S(2)}) collective-permute-start(f32[80,128]{1,0:T(8,128)S(1)} %get-tuple-element.66), channel_id=1, source_target_pairs={{224,0},{0,32},{32,64},{64,96},{96,128},{128,160},{160,192},{192,2... | collective-permute-start | bytes 122888 | tf_op jit(solution)/shard_map/ppermute | solution.py:720
  95.4 12.8 %all-to-all-start.5 = ((f32[32,8,256]{2,1,0:T(8,128)}), f32[32,8,256]{2,1,0:T(8,128)S(1)}, u32[]{:S(2)}, u32[]{:S(2)}) async-start(f32[32,8,256]{2,1,0:T(8,128)} %bitcast.11), calls=%async_computation.5 | async-start | bytes 524288 | tf_op jit(solution)/shard_map/all_to_all | solution.py:715
  99.2 9.1 %copy-start.4 = (f32[135,256]{1,0:T(8,128)S(1)}, f32[135,256]{1,0:T(8,128)}, u32[]{:S(2)}) copy-start(f32[135,256]{1,0:T(8,128)} %r_3_.2) | copy-start | bytes 414724
  99.2 6.7 %collective-permute-start.8 = (f32[8,128]{1,0:T(8,128)S(1)}, f32[8,128]{1,0:T(8,128)S(1)}, u32[]{:S(2)}, u32[]{:S(2)}) collective-permute-start(f32[8,128]{1,0:T(8,128)S(1)} %gather.1.r_5_), channel_id=1, source_target_pairs={{128,0},{160,32},{192,64},{224,96},{0,128},{32,160},{64,192},{96,2... | collective-permute-start | bytes 12296 | tf_op jit(solution)/shard_map/ppermute | solution.py:720
  100.4 5.5 %collective-permute-start.7 = (f32[8,128]{1,0:T(8,128)S(1)}, f32[8,128]{1,0:T(8,128)S(1)}, u32[]{:S(2)}, u32[]{:S(2)}) collective-permute-start(f32[8,128]{1,0:T(8,128)S(1)} %gather.1.r_5_), channel_id=1, source_target_pairs={{192,0},{224,32},{0,64},{32,96},{64,128},{96,160},{128,192},{160,2... | collective-permute-start | bytes 12296 | tf_op jit(solution)/shard_map/ppermute | solution.py:720
  101.0 5.2 %collective-permute-start.6 = (f32[8,128]{1,0:T(8,128)S(1)}, f32[8,128]{1,0:T(8,128)S(1)}, u32[]{:S(2)}, u32[]{:S(2)}) collective-permute-start(f32[8,128]{1,0:T(8,128)S(1)} %gather.1.r_5_), channel_id=1, source_target_pairs={{64,0},{96,32},{128,64},{160,96},{192,128},{224,160},{0,192},{32,2... | collective-permute-start | bytes 12296 | tf_op jit(solution)/shard_map/ppermute | solution.py:720

commit v9 on v8

--- a/solution.py
+++ b/solution.py
@@ -26,14 +26,13 @@
     for m in range(1, groups // 2):
         wave_of[2 * m] = wave_of[2 * m + 1] = m
     turn = TURN * (np.outer(wave_of, index) % period) / period
-    matrices = np.zeros((2, WIDE, WIDE), np.float32)
-    matrices[0, :length, :length] = np.cos(inner)
-    matrices[1, :length, :length] = np.sin(inner)
-    coarse = matrices.astype(jnp.bfloat16)
-    rest = (matrices - coarse.astype(np.float32)).astype(jnp.bfloat16)
-    twiddle = np.zeros((2, groups, WIDE))
-    twiddle[0, :, :length] = np.cos(turn)
-    twiddle[1, :, :length] = np.sin(turn)
+    rows = np.zeros((2 * WIDE + 2 * groups, WIDE), np.float32)
+    rows[:length, :length] = np.cos(inner)
+    rows[WIDE : WIDE + length, :length] = np.sin(inner)
+    rows[2 * WIDE : 2 * WIDE + groups, :length] = np.cos(turn)
+    rows[2 * WIDE + groups :, :length] = np.sin(turn)
+    coarse = rows.astype(jnp.bfloat16)
+    rest = (rows - coarse.astype(np.float32)).astype(jnp.bfloat16)
     chunk = np.arange(groups)
     outer = np.zeros((2, groups, groups))
     for c in range(groups):
@@ -49,7 +48,6 @@
     wave[:, :length] = 4.0 * np.sin(np.pi * modes / period) ** 2
     return (
         np.stack([coarse, rest]),
-        twiddle.astype(np.float32),
         np.concatenate([outer[0], outer[1]], axis=1).astype(np.float32),
         wave.astype(np.float32),
     )
@@ -118,7 +116,17 @@
 
 
 def table(matrix_ref, n):
-    return matrix_ref[0, n], matrix_ref[1, n]
+    at = slice(n * WIDE, (n + 1) * WIDE)
+    return matrix_ref[0, at, :], matrix_ref[1, at, :]
+
+
+def load_twiddle(matrix_ref, twiddle):
+    groups = twiddle.shape[1]
+    for n in range(2):
+        at = slice(2 * WIDE + n * groups, 2 * WIDE + (n + 1) * groups)
+        twiddle[n] = matrix_ref[0, at, :].astype(jnp.float32) + matrix_ref[1, at, :].astype(
+            jnp.float32
+        )
 
 
 def rows_of(p):
@@ -299,7 +307,8 @@
     return both[:, :WIDE], both[:, WIDE:]
 
 
-def forward_kernel(groups, field_ref, rest_ref, matrix_ref, twiddle_ref, out_ref, left, right):
+def forward_kernel(groups, field_ref, rest_ref, matrix_ref, out_ref, left, right, twiddle_ref):
+    load_twiddle(matrix_ref, twiddle_ref)
     chunks = [field_ref[rows_of(p), :] for p in range(groups)]
     spectrum = transform(chunks, matrix_ref, twiddle_ref, left, right)
     out_ref[...] = spectrum + rest_ref[...]
@@ -525,7 +534,6 @@
     next_ref,
     east_ref,
     matrix_ref,
-    twiddle_ref,
     outer_ref,
     out_ref,
     first_ref,
@@ -537,7 +545,9 @@
     high,
     tail,
     folded,
+    twiddle_ref,
 ):
+    load_twiddle(matrix_ref, twiddle_ref)
     lane_row = lanes((groups, WIDE))
     stride = 3 * ROWS
     tail[...] = spec_ref[:, 128:WIDE]
@@ -629,9 +639,10 @@
     first_ref,
     image_ref,
     matrix_ref,
+    out_ref,
     twiddle_ref,
-    out_ref,
 ):
+    load_twiddle(matrix_ref, twiddle_ref)
     cells = transform_back(both_products(spec_ref[...], matrix_ref), groups, twiddle_ref)
     lane = lanes((ROWS, WIDE))
     cut = WIDE - length
@@ -737,10 +748,11 @@
     groups = lax.axis_size(LON)
     length, rows = surface_forcing.shape
     norm = 1.0 / (groups * length)
-    matrices, twiddle, outer, wave = tables(groups, length)
+    matrices, outer, wave = tables(groups, length)
     count, block = aligned_inverse.shape[0], aligned_inverse.shape[1]
     half = block // 2
     wide = (rows, WIDE)
+    turns = [(2, groups, WIDE)]
     transforms = [wide, wide]
 
     cells = (length, rows)
@@ -754,8 +766,8 @@
 
     mask, east_cells = lax.optimization_barrier((ocean_mask, east_coupling, slab))[:2]
     more = call(pack_more_kernel, wide, [wide], name="pack_more")(own_cells, mask, east_cells)
-    spectrum = call(lambda *r: forward_kernel(groups, *r), wide, transforms, name="forward")(
-        slab, more, matrices, twiddle
+    spectrum = call(lambda *r: forward_kernel(groups, *r), wide, transforms + turns, name="forward")(
+        slab, more, matrices
     )
     spec_rhs = exchanged(spectrum)
 
@@ -813,9 +825,9 @@
     spec, first, image, sums = call(
         lambda *r: step_kernel(groups, length, *r),
         [wide, wide, wide, (8, 128)],
-        transforms + [(3 * rows, 128)] * 2 + [(rows, 128), (groups, WIDE)],
+        transforms + [(3 * rows, 128)] * 2 + [(rows, 128), (groups, WIDE)] + turns,
         name="step",
-    )(filtered, slab, *flat, matrices, twiddle, outer)
+    )(filtered, slab, *flat, matrices, outer)
     spec_image = exchanged(spec)
     scaled, part, down, up, own = call(
         lambda *r: sums_kernel(norm, length, *r), [wide, wide, edge, edge, (8, 128)], name="sums"
@@ -835,8 +847,8 @@
     image_cells = call(
         lambda *r: unpack_kernel(length, image_cut, *r), cells, name="unpack_image"
     )(filtered)
-    packed = call(lambda *r: last_kernel(groups, length, *r), wide, name="last")(
-        filtered, flat[0], first, image, matrices, twiddle
+    packed = call(lambda *r: last_kernel(groups, length, *r), wide, turns, name="last")(
+        filtered, flat[0], first, image, matrices
     )
     return tuple(
         call(lambda *r: finish_kernel(length, *r), [cells] * 3, name="finish")(

time: 110 us -> 109 us (level)
  no operation moved by 1% of the time
where the time goes in v9:
time: 109 us
  blocking collectives  59.8 us (55%)
  starting transfers between devices  23.5 us (22%)
  waiting for transfers between devices  13 us (12%)
  Pallas kernels  8.72 us (8%)
  local copies, waits for them, and re-layouts  1.43 us (1%)
  other arithmetic  1.18 us (1%)
    all_to_all x4, blocking collectives, exchanged(): lax.all_to_all(parts, LON, split_axis=0, concat_axis=0, tiled=True)  59.8 us
    ppermute x9, starting transfers between devices, from_lat(): lax.ppermute(value, 'lat', [((d + steps) % count, d) for d in range(count)])  16 us
    ppermute x9, waiting for transfers between devices, from_lat(): lax.ppermute(value, 'lat', [((d + steps) % count, d) for d in range(count)])  11 us
    all_to_all x2, starting transfers between devices, exchanged(): lax.all_to_all(parts, LON, split_axis=0, concat_axis=0, tiled=True)  7.55 us
  transfers between devices with their start and end apart: 11, of which 8 were waited for; matrix products, arithmetic and copies ran while one was open for 1% of the time, Pallas kernels for 1%

profile of v9, /device:TPU:1, one launch (start us, length us, event | category | flops | bytes accessed | tf_op | source)
XLA Modules:
  0.0 108.5 jit_solution(2477949945114040827)
XLA Ops:
  0.6 1.1 convert_multiply_fusion
  1.7 0.0 copy-start.1
  1.7 0.0 copy-start.4
  1.7 0.1 pack.1
  1.9 0.0 copy-start
  1.9 17.5 %all_to_all.30 = f32[32,8,256]{2,1,0:T(8,128)S(1)} all-to-all(f32[32,8,256]{2,1,0:T(8,128)S(1)} %bitcast.27), channel_id=1, replica_groups=mesh['lat'=8,'lon_0'=4,'lon_1'=4,'lon_2'=2] {'lon_0','lon_1','lon_2'}, dimensions={0} | all-to-all | bytes 524288 | tf_op jit(solution)/shard_map/all_to_all | solution.py:726
  19.4 0.1 pack_more.1.r_1_
  19.5 1.2 %forward.1 = f32[256,256]{1,0:T(8,128)} custom-call(f32[256,256]{1,0:T(8,128)S(1)} %bitcast.16, f32[256,256]{1,0:T(8,128)S(1)} %pack_more.1.r_1_, bf16[2,576,256]{2,1,0:T(8,128)(2,1)S(1)} %copy-done), custom_call_target="tpu_custom_call" | custom-call | tf_op jit(solution)/shard_map/forward/pallas_call | solution.py:769
  20.7 3.8 %all-to-all-start.1 = ((f32[32,8,256]{2,1,0:T(8,128)}), f32[32,8,256]{2,1,0:T(8,128)S(1)}, u32[]{:S(2)}, u32[]{:S(2)}) async-start(f32[32,8,256]{2,1,0:T(8,128)} %bitcast.2), calls=%async_computation.1 | async-start | bytes 524288 | tf_op jit(solution)/shard_map/all_to_all | solution.py:726
  24.6 0.1 edges.1
  24.7 5.7 %collective-permute-start = (f32[8,256]{1,0:T(8,128)S(1)}, f32[8,256]{1,0:T(8,128)S(1)}, u32[]{:S(2)}, u32[]{:S(2)}) collective-permute-start(f32[8,256]{1,0:T(8,128)S(1)} %get-tuple-element.45), channel_id=1, source_target_pairs={{32,0},{64,32},{96,64},{128,96},{160,128},{192,160},{224,192},{0,2... | collective-permute-start | bytes 24584 | tf_op jit(solution)/shard_map/ppermute | solution.py:731
  30.4 0.0 collective-permute-start.1
  30.4 0.7 constant_dynamic-slice_fusion
  31.1 0.7 copy-done.8
  31.7 0.1 add_rsqrt_fusion.scale_ref.r_2_.r_1_
  31.9 0.0 copy-start.6
  31.9 2.8 %collective-permute-done.1.from_below_ref.r_6_.r_4_ = f32[136,128]{1,0:T(8,128)S(1)} collective-permute-done((f32[136,128]{1,0:T(8,128)S(1)}, f32[136,128]{1,0:T(8,128)S(1)}, u32[]{:S(2)}, u32[]{:S(2)}) %collective-permute-start.1) | collective-permute-done | bytes 69664 | tf_op jit(solution)/shard_map/ppermute | solution.py:731
  34.7 0.6 pack_rest.1.r_8_
  35.3 0.0 all-to-all-done.1
  35.3 0.3 blocks.1
  35.6 4.0 %collective-permute-start.2 = (f32[80,128]{1,0:T(8,128)S(1)}, f32[80,128]{1,0:T(8,128)S(1)}, u32[]{:S(2)}, u32[]{:S(2)}) collective-permute-start(f32[80,128]{1,0:T(8,128)S(1)} %get-tuple-element.54), channel_id=1, source_target_pairs={{32,0},{64,32},{96,64},{128,96},{160,128},{192,160},{224,192},{0,2... | collective-permute-start | bytes 122888 | tf_op jit(solution)/shard_map/ppermute | solution.py:731
  39.6 0.0 collective-permute-start.3
  39.6 0.5 coefficients.1
  40.1 0.6 collective-permute-done.2.r_3_
  40.7 3.0 %collective-permute-done.3.r_4_ = f32[80,128]{1,0:T(8,128)S(1)} collective-permute-done((f32[80,128]{1,0:T(8,128)S(1)}, f32[80,128]{1,0:T(8,128)S(1)}, u32[]{:S(2)}, u32[]{:S(2)}) %collective-permute-start.3) | collective-permute-done | bytes 40992 | tf_op jit(solution)/shard_map/ppermute | solution.py:731
  43.7 0.5 halo.1
  44.2 0.0 copy-start.7
  44.2 16.4 %all_to_all.31 = f32[32,8,384]{2,1,0:T(8,128)S(1)} all-to-all(f32[32,8,384]{2,1,0:T(8,128)S(1)} %bitcast.23), channel_id=1, replica_groups=mesh['lat'=8,'lon_0'=4,'lon_1'=4,'lon_2'=2] {'lon_0','lon_1','lon_2'}, dimensions={0} | all-to-all | bytes 786432 | tf_op jit(solution)/shard_map/all_to_all | solution.py:726
  60.6 1.8 %step.1 = (f32[256,256]{1,0:T(8,128)S(1)}, f32[256,256]{1,0:T(8,128)S(1)}, f32[256,256]{1,0:T(8,128)S(1)}, f32[8,128]{1,0:T(8,128)S(1)}) custom-call(f32[256,384]{1,0:T(8,128)S(1)} %bitcast.24, f32[256,256]{1,0:T(8,128)S(1)} %bitcast.18, f32[256,256]{1,0:T(8,128)S(1)} %get-tuple-element.57.r_2_.r_1_, f32[256,256]{1,0:T(8,128)S(1)} %get-tuple-element.58.r_3_, ...), custom_call_target="tpu_custom_call" | custom-call | tf_op jit(solution)/shard_map/step/pallas_call | solution.py:825
  62.4 12.3 %all_to_all.32 = f32[32,8,256]{2,1,0:T(8,128)S(1)} all-to-all(f32[32,8,256]{2,1,0:T(8,128)S(1)} %bitcast.28), channel_id=1, replica_groups=mesh['lat'=8,'lon_0'=4,'lon_1'=4,'lon_2'=2] {'lon_0','lon_1','lon_2'}, dimensions={0} | all-to-all | bytes 524288 | tf_op jit(solution)/shard_map/all_to_all | solution.py:726
  74.8 0.5 sums.1
  75.3 0.1 collective-permute-start.4
  75.4 1.5 %collective-permute-start.5 = (f32[80,128]{1,0:T(8,128)S(1)}, f32[80,128]{1,0:T(8,128)S(1)}, u32[]{:S(2)}, u32[]{:S(2)}) collective-permute-start(f32[80,128]{1,0:T(8,128)S(1)} %get-tuple-element.66), channel_id=1, source_target_pairs={{224,0},{0,32},{32,64},{64,96},{96,128},{128,160},{160,192},{192,2... | collective-permute-start | bytes 122888 | tf_op jit(solution)/shard_map/ppermute | solution.py:731
  76.8 0.2 unpack_first.1
  77.0 1.2 %collective-permute-done.4.r_3_ = f32[80,128]{1,0:T(8,128)S(1)} collective-permute-done((f32[80,128]{1,0:T(8,128)S(1)}, f32[80,128]{1,0:T(8,128)S(1)}, u32[]{:S(2)}, u32[]{:S(2)}) %collective-permute-start.4) | collective-permute-done | bytes 40992 | tf_op jit(solution)/shard_map/ppermute | solution.py:731
  78.2 1.3 %collective-permute-done.5.r_4_ = f32[80,128]{1,0:T(8,128)S(1)} collective-permute-done((f32[80,128]{1,0:T(8,128)S(1)}, f32[80,128]{1,0:T(8,128)S(1)}, u32[]{:S(2)}, u32[]{:S(2)}) %collective-permute-start.5) | collective-permute-done | bytes 40992 | tf_op jit(solution)/shard_map/ppermute | solution.py:731
  79.5 0.4 ends.1
  79.9 13.6 %all_to_all.33 = f32[32,8,256]{2,1,0:T(8,128)S(1)} all-to-all(f32[32,8,256]{2,1,0:T(8,128)S(1)} %bitcast.26), channel_id=1, replica_groups=mesh['lat'=8,'lon_0'=4,'lon_1'=4,'lon_2'=2] {'lon_0','lon_1','lon_2'}, dimensions={0} | all-to-all | bytes 524288 | tf_op jit(solution)/shard_map/all_to_all | solution.py:726
  93.6 1.2 %last.1 = f32[256,256]{1,0:T(8,128)} custom-call(f32[256,256]{1,0:T(8,128)S(1)} %bitcast.13, f32[256,256]{1,0:T(8,128)S(1)} %get-tuple-element.57.r_2_.r_1_, f32[256,256]{1,0:T(8,128)S(1)} %get-tuple-element.71.r_2_, f32[256,256]{1,0:T(8,128)S(1)} %get-tuple-element.68.r_1_.r_3_, bf16[2,576,256]{2,1,0:T(8,128)(2,1)S(1)} %copy-done), custom_call_target="tpu_custom_call" | custom-call | tf_op jit(solution)/shard_map/last/pallas_call | solution.py:850
  94.8 3.7 %all-to-all-start.5 = ((f32[32,8,256]{2,1,0:T(8,128)}), f32[32,8,256]{2,1,0:T(8,128)S(1)}, u32[]{:S(2)}, u32[]{:S(2)}) async-start(f32[32,8,256]{2,1,0:T(8,128)} %bitcast.11), calls=%async_computation.5 | async-start | bytes 524288 | tf_op jit(solution)/shard_map/all_to_all | solution.py:726
  98.5 1.2 %collective-permute-start.8 = (f32[8,128]{1,0:T(8,128)S(1)}, f32[8,128]{1,0:T(8,128)S(1)}, u32[]{:S(2)}, u32[]{:S(2)}) collective-permute-start(f32[8,128]{1,0:T(8,128)S(1)} %gather.1.r_5_), channel_id=1, source_target_pairs={{128,0},{160,32},{192,64},{224,96},{0,128},{32,160},{64,192},{96,2... | collective-permute-start | bytes 12296 | tf_op jit(solution)/shard_map/ppermute | solution.py:731
  99.8 0.6 collective-permute-start.7
  100.4 3.0 %collective-permute-start.6 = (f32[8,128]{1,0:T(8,128)S(1)}, f32[8,128]{1,0:T(8,128)S(1)}, u32[]{:S(2)}, u32[]{:S(2)}) collective-permute-start(f32[8,128]{1,0:T(8,128)S(1)} %gather.1.r_5_), channel_id=1, source_target_pairs={{64,0},{96,32},{128,64},{160,96},{192,128},{224,160},{0,192},{32,2... | collective-permute-start | bytes 12296 | tf_op jit(solution)/shard_map/ppermute | solution.py:731
  103.3 0.1 unpack_image.1.r_2_
  103.4 1.8 %collective-permute-done.8.r_8_ = f32[8,128]{1,0:T(8,128)S(1)} collective-permute-done((f32[8,128]{1,0:T(8,128)S(1)}, f32[8,128]{1,0:T(8,128)S(1)}, u32[]{:S(2)}, u32[]{:S(2)}) %collective-permute-start.8) | collective-permute-done | bytes 4128 | tf_op jit(solution)/shard_map/ppermute | solution.py:731
  105.3 0.3 collective-permute-done.6.r_6_
  105.6 2.0 %all-to-all-done.5 = f32[32,8,256]{2,1,0:T(8,128)S(1)} async-done(((f32[32,8,256]{2,1,0:T(8,128)}), f32[32,8,256]{2,1,0:T(8,128)S(1)}, u32[]{:S(2)}, u32[]{:S(2)}) %all-to-all-start.5) | async-done | bytes 262176 | tf_op jit(solution)/shard_map/all_to_all | solution.py:726
  107.6 1.0 finish.1
  (17 shorter events, 0.1 us)
Async XLA Ops:
  1.7 17.7 %copy-start.1 = (s32[135,256]{1,0:T(8,128)S(1)}, s32[135,256]{1,0:T(8,128)}, u32[]{:S(2)}) copy-start(s32[135,256]{1,0:T(8,128)} %r_4_.2) | copy-start | bytes 414724
  1.7 17.7 %copy-start.4 = (f32[135,256]{1,0:T(8,128)S(1)}, f32[135,256]{1,0:T(8,128)}, u32[]{:S(2)}) copy-start(f32[135,256]{1,0:T(8,128)} %east_ref.1) | copy-start | bytes 414724
  1.9 17.7 %copy-start = (bf16[2,576,256]{2,1,0:T(8,128)(2,1)S(1)}, bf16[2,576,256]{2,1,0:T(8,128)(2,1)}, u32[]{:S(2)}) copy-start(bf16[2,576,256]{2,1,0:T(8,128)(2,1)} %constant.42.clone.r_2_.r_5_.r_4_) | copy-start | bytes 1769476
  20.7 3.9 %copy-start.2 = (f32[2,128,128]{2,1,0:T(8,128)S(1)}, f32[2,128,128]{2,1,0:T(8,128)}, u32[]{:S(2)}) copy-start(f32[2,128,128]{2,1,0:T(8,128)} %r_5_.2) | copy-start | bytes 393220
  20.7 3.9 %copy-start.5 = (f32[135,256]{1,0:T(8,128)S(1)}, f32[135,256]{1,0:T(8,128)}, u32[]{:S(2)}) copy-start(f32[135,256]{1,0:T(8,128)} %north_ref.1) | copy-start | bytes 414724
  20.7 14.6 %all-to-all-start.1 = ((f32[32,8,256]{2,1,0:T(8,128)}), f32[32,8,256]{2,1,0:T(8,128)S(1)}, u32[]{:S(2)}, u32[]{:S(2)}) async-start(f32[32,8,256]{2,1,0:T(8,128)} %bitcast.2), calls=%async_computation.1 | async-start | bytes 524288 | tf_op jit(solution)/shard_map/all_to_all | solution.py:726
  24.7 7.2 %collective-permute-start = (f32[8,256]{1,0:T(8,128)S(1)}, f32[8,256]{1,0:T(8,128)S(1)}, u32[]{:S(2)}, u32[]{:S(2)}) collective-permute-start(f32[8,256]{1,0:T(8,128)S(1)} %get-tuple-element.45), channel_id=1, source_target_pairs={{32,0},{64,32},{96,64},{128,96},{160,128},{192,160},{224,192},{0,2... | collective-permute-start | bytes 24584 | tf_op jit(solution)/shard_map/ppermute | solution.py:731
  30.4 4.4 %collective-permute-start.1 = (f32[136,128]{1,0:T(8,128)S(1)}, f32[136,128]{1,0:T(8,128)S(1)}, u32[]{:S(2)}, u32[]{:S(2)}) collective-permute-start(f32[136,128]{1,0:T(8,128)S(1)} %get-tuple-element.49), channel_id=1, source_target_pairs={{224,0},{0,32},{32,64},{64,96},{96,128},{128,160},{160,192},{192,2... | collective-permute-start | bytes 208904 | tf_op jit(solution)/shard_map/ppermute | solution.py:731
  31.1 0.7 copy-start.8
  31.9 3.4 %copy-start.6 = (f32[2,128,128]{2,1,0:T(8,128)S(1)}, f32[2,128,128]{2,1,0:T(8,128)}, u32[]{:S(2)}) copy-start(f32[2,128,128]{2,1,0:T(8,128)} %r_2_.2) | copy-start | bytes 393220
  35.6 5.1 %collective-permute-start.2 = (f32[80,128]{1,0:T(8,128)S(1)}, f32[80,128]{1,0:T(8,128)S(1)}, u32[]{:S(2)}, u32[]{:S(2)}) collective-permute-start(f32[80,128]{1,0:T(8,128)S(1)} %get-tuple-element.54), channel_id=1, source_target_pairs={{32,0},{64,32},{96,64},{128,96},{160,128},{192,160},{224,192},{0,2... | collective-permute-start | bytes 122888 | tf_op jit(solution)/shard_map/ppermute | solution.py:731
  39.6 4.1 %collective-permute-start.3 = (f32[80,128]{1,0:T(8,128)S(1)}, f32[80,128]{1,0:T(8,128)S(1)}, u32[]{:S(2)}, u32[]{:S(2)}) collective-permute-start(f32[80,128]{1,0:T(8,128)S(1)} %get-tuple-element.55), channel_id=1, source_target_pairs={{224,0},{0,32},{32,64},{64,96},{96,128},{128,160},{160,192},{192,2... | collective-permute-start | bytes 122888 | tf_op jit(solution)/shard_map/ppermute | solution.py:731
  44.2 16.4 %copy-start.7 = (f32[32,64]{1,0:T(8,128)S(1)}, f32[32,64]{1,0:T(8,128)}, u32[]{:S(2)}) copy-start(f32[32,64]{1,0:T(8,128)} %constant.44.clone.r_6_) | copy-start | bytes 24580
  75.3 2.9 %collective-permute-start.4 = (f32[80,128]{1,0:T(8,128)S(1)}, f32[80,128]{1,0:T(8,128)S(1)}, u32[]{:S(2)}, u32[]{:S(2)}) collective-permute-start(f32[80,128]{1,0:T(8,128)S(1)} %get-tuple-element.65), channel_id=1, source_target_pairs={{32,0},{64,32},{96,64},{128,96},{160,128},{192,160},{224,192},{0,2... | collective-permute-start | bytes 122888 | tf_op jit(solution)/shard_map/ppermute | solution.py:731
  75.4 4.1 %collective-permute-start.5 = (f32[80,128]{1,0:T(8,128)S(1)}, f32[80,128]{1,0:T(8,128)S(1)}, u32[]{:S(2)}, u32[]{:S(2)}) collective-permute-start(f32[80,128]{1,0:T(8,128)S(1)} %get-tuple-element.66), channel_id=1, source_target_pairs={{224,0},{0,32},{32,64},{64,96},{96,128},{128,160},{160,192},{192,2... | collective-permute-start | bytes 122888 | tf_op jit(solution)/shard_map/ppermute | solution.py:731
  94.8 12.8 %all-to-all-start.5 = ((f32[32,8,256]{2,1,0:T(8,128)}), f32[32,8,256]{2,1,0:T(8,128)S(1)}, u32[]{:S(2)}, u32[]{:S(2)}) async-start(f32[32,8,256]{2,1,0:T(8,128)} %bitcast.11), calls=%async_computation.5 | async-start | bytes 524288 | tf_op jit(solution)/shard_map/all_to_all | solution.py:726
  98.5 9.1 %copy-start.3 = (f32[135,256]{1,0:T(8,128)S(1)}, f32[135,256]{1,0:T(8,128)}, u32[]{:S(2)}) copy-start(f32[135,256]{1,0:T(8,128)} %r_3_.1) | copy-start | bytes 414724
  98.5 6.7 %collective-permute-start.8 = (f32[8,128]{1,0:T(8,128)S(1)}, f32[8,128]{1,0:T(8,128)S(1)}, u32[]{:S(2)}, u32[]{:S(2)}) collective-permute-start(f32[8,128]{1,0:T(8,128)S(1)} %gather.1.r_5_), channel_id=1, source_target_pairs={{128,0},{160,32},{192,64},{224,96},{0,128},{32,160},{64,192},{96,2... | collective-permute-start | bytes 12296 | tf_op jit(solution)/shard_map/ppermute | solution.py:731
  99.8 5.5 %collective-permute-start.7 = (f32[8,128]{1,0:T(8,128)S(1)}, f32[8,128]{1,0:T(8,128)S(1)}, u32[]{:S(2)}, u32[]{:S(2)}) collective-permute-start(f32[8,128]{1,0:T(8,128)S(1)} %gather.1.r_5_), channel_id=1, source_target_pairs={{192,0},{224,32},{0,64},{32,96},{64,128},{96,160},{128,192},{160,2... | collective-permute-start | bytes 12296 | tf_op jit(solution)/shard_map/ppermute | solution.py:731
  100.4 5.2 %collective-permute-start.6 = (f32[8,128]{1,0:T(8,128)S(1)}, f32[8,128]{1,0:T(8,128)S(1)}, u32[]{:S(2)}, u32[]{:S(2)}) collective-permute-start(f32[8,128]{1,0:T(8,128)S(1)} %gather.1.r_5_), channel_id=1, source_target_pairs={{64,0},{96,32},{128,64},{160,96},{192,128},{224,160},{0,192},{32,2... | collective-permute-start | bytes 12296 | tf_op jit(solution)/shard_map/ppermute | solution.py:731

commit v10 on v9

--- a/solution.py
+++ b/solution.py
@@ -160,9 +160,10 @@
     wet_ref[...] = tall[...].T[:ROWS]
     tall[:length, :] = mask_ref[:, rows - 128 :].astype(jnp.float32) * north_ref[:, rows - 128 :]
     top = tall[...].T[127:]
-    low_ref[:block, :] = stag_ref[count - 1]
+    keep = block // 2 + ROWS
+    low_ref[:keep, :] = stag_ref[count - 1, block - keep :, :]
     row = sublanes((ROWS, 128))
-    low_ref[block:, :] = jnp.where(row == 0, top[:, :128], top[:, 128:])
+    low_ref[keep:, :] = jnp.where(row == 0, top[:, :128], top[:, 128:])
 
 
 def lane_plan(length):
@@ -365,15 +366,15 @@
     count, block = stag_ref.shape[0], stag_ref.shape[1]
     half, rows = block // 2, count * block
     before = flags_ref[1:2, :] * dot(
-        stag_below_ref[:block, :],
+        stag_below_ref[: ROWS + half, :],
         jnp.concatenate([load_edge(below_ref), scaled_ref[:half, :]], axis=0),
     )
     upper = load_edge(above_ref) * flags_ref[:1, :]
-    pieces = [before[half:]]
+    pieces = [before[ROWS:]]
     for b in range(count - 1):
         pieces.append(dot(stag_ref[b], scaled_ref[half + b * block : half + (b + 1) * block, :]))
     after = dot(
-        stag_ref[count - 1],
+        stag_ref[count - 1, : half + ROWS, :],
         jnp.concatenate([scaled_ref[rows - half :, :], upper], axis=0),
     )
     pieces.append(after[:half])
@@ -409,7 +410,7 @@
         flags_ref,
     )
     part, scale = load_rows(below_ref)
-    row_below = (before[half - 1 : half] + part) * (scale * norm)
+    row_below = (before[ROWS - 1 : ROWS] + part) * (scale * norm)
     part, scale = load_rows(above_ref)
     row_above = (after[half : half + 1] + part) * (scale * norm)
     out_ref[:, :128] = full[:, :128]
@@ -469,7 +470,7 @@
         part_ref[at, :] = part_ref[at, :] + dot(stag_ref[b], scaled[at])
     first, last = slice(0, half), slice(rows - half, rows)
     part_ref[first, :] = part_ref[first, :] + flags_ref[1:2, :] * dot(
-        stag_below_ref[half:block, half:], scaled[first]
+        stag_below_ref[ROWS : ROWS + half, half:], scaled[first]
     )
     part_ref[last, :] = part_ref[last, :] + dot(stag_ref[count - 1, :half, :half], scaled[last])
     total = total_of(scaled * part_ref[...], length) * (flags_ref[2:3, :1] * norm)
@@ -504,7 +505,7 @@
     count, block = stag_ref.shape[0], stag_ref.shape[1]
     half, rows = block // 2, count * block
     first, last = slice(0, half), slice(rows - half, rows)
-    low = dot(stag_below_ref[half:block, :half], load_edge(below_ref)) * flags_ref[1:2, :]
+    low = dot(stag_below_ref[ROWS : ROWS + half, :half], load_edge(below_ref)) * flags_ref[1:2, :]
     high = dot(stag_ref[count - 1, :half, half:], load_edge(above_ref)) * flags_ref[:1, :]
     both = total_of(low * scaled_ref[first, :] + high * scaled_ref[last, :], length)
     both = both * (flags_ref[2:3, :1] * (2.0 * norm))
@@ -773,7 +774,7 @@
 
     north_cells, stag = lax.optimization_barrier((north_coupling, staggered_inverse, spectrum))[:-1]
     wet_first, low_last = call(
-        edges_kernel, [(ROWS, WIDE), (block + ROWS, 128)], [(WIDE, 128)], name="edges"
+        edges_kernel, [(ROWS, WIDE), (half + 2 * ROWS, 128)], [(WIDE, 128)], name="edges"
     )(mask, north_cells, stag)
     weights, channel, lat, flag_row = lax.optimization_barrier(
         (

time: 109 us -> 109 us (level)
  no operation moved by 1% of the time
where the time goes in v10:
time: 109 us; the launch traced here: 108 us
  blocking collectives  59.5 us (55%)
  starting transfers between devices  23.8 us (22%)
  waiting for transfers between devices  12.7 us (12%)
  Pallas kernels  8.62 us (8%)
  local copies, waits for them, and re-layouts  1.43 us (1%)
  other arithmetic  1.18 us (1%)
    all_to_all x4, blocking collectives, exchanged(): lax.all_to_all(parts, LON, split_axis=0, concat_axis=0, tiled=True)  59.5 us
    ppermute x9, starting transfers between devices, from_lat(): lax.ppermute(value, 'lat', [((d + steps) % count, d) for d in range(count)])  16.3 us
    ppermute x9, waiting for transfers between devices, from_lat(): lax.ppermute(value, 'lat', [((d + steps) % count, d) for d in range(count)])  10.6 us
    all_to_all x2, starting transfers between devices, exchanged(): lax.all_to_all(parts, LON, split_axis=0, concat_axis=0, tiled=True)  7.55 us
  transfers between devices with their start and end apart: 11, of which 8 were waited for; matrix products, arithmetic and copies ran while one was open for 1% of the time, Pallas kernels for 1%

profile of v10, /device:TPU:1, one launch (start us, length us, event | category | flops | bytes accessed | tf_op | source)
XLA Modules:
  0.0 108.1 jit_solution(7214452758037555836)
XLA Ops:
  0.6 1.1 convert_multiply_fusion
  1.7 0.0 copy-start.1
  1.7 0.0 copy-start.4
  1.7 0.1 pack.1
  1.9 0.0 copy-start
  1.9 17.5 %all_to_all.30 = f32[32,8,256]{2,1,0:T(8,128)S(1)} all-to-all(f32[32,8,256]{2,1,0:T(8,128)S(1)} %bitcast.26), channel_id=1, replica_groups=mesh['lat'=8,'lon_0'=4,'lon_1'=4,'lon_2'=2] {'lon_0','lon_1','lon_2'}, dimensions={0} | all-to-all | bytes 524288 | tf_op jit(solution)/shard_map/all_to_all | solution.py:727
  19.4 0.1 pack_more.1.r_1_
  19.5 1.2 %forward.1 = f32[256,256]{1,0:T(8,128)} custom-call(f32[256,256]{1,0:T(8,128)S(1)} %bitcast.16, f32[256,256]{1,0:T(8,128)S(1)} %pack_more.1.r_1_, bf16[2,576,256]{2,1,0:T(8,128)(2,1)S(1)} %copy-done), custom_call_target="tpu_custom_call" | custom-call | tf_op jit(solution)/shard_map/forward/pallas_call | solution.py:770
  20.7 3.8 %all-to-all-start.1 = ((f32[32,8,256]{2,1,0:T(8,128)}), f32[32,8,256]{2,1,0:T(8,128)S(1)}, u32[]{:S(2)}, u32[]{:S(2)}) async-start(f32[32,8,256]{2,1,0:T(8,128)} %bitcast.2), calls=%async_computation.1 | async-start | bytes 524288 | tf_op jit(solution)/shard_map/all_to_all | solution.py:727
  24.6 0.1 edges.1
  24.7 5.7 %collective-permute-start = (f32[8,256]{1,0:T(8,128)S(1)}, f32[8,256]{1,0:T(8,128)S(1)}, u32[]{:S(2)}, u32[]{:S(2)}) collective-permute-start(f32[8,256]{1,0:T(8,128)S(1)} %get-tuple-element.45), channel_id=1, source_target_pairs={{32,0},{64,32},{96,64},{128,96},{160,128},{192,160},{224,192},{0,2... | collective-permute-start | bytes 24584 | tf_op jit(solution)/shard_map/ppermute | solution.py:732
  30.4 0.0 collective-permute-start.1
  30.4 0.7 constant_dynamic-slice_fusion
  31.1 0.7 copy-done.8
  31.7 0.1 add_rsqrt_fusion.scale_ref.r_2_.r_1_
  31.9 0.0 copy-start.6
  31.9 0.0 collective-permute-done.wet_above_ref
  31.9 2.5 %collective-permute-done.1.from_below_ref.r_6_.r_4_ = f32[80,128]{1,0:T(8,128)S(1)} collective-permute-done((f32[80,128]{1,0:T(8,128)S(1)}, f32[80,128]{1,0:T(8,128)S(1)}, u32[]{:S(2)}, u32[]{:S(2)}) %collective-permute-start.1) | collective-permute-done | bytes 40992 | tf_op jit(solution)/shard_map/ppermute | solution.py:732
  34.4 0.6 pack_rest.1.r_8_
  35.0 0.0 all-to-all-done.1
  35.0 0.3 blocks.1
  35.3 4.3 %collective-permute-start.2 = (f32[80,128]{1,0:T(8,128)S(1)}, f32[80,128]{1,0:T(8,128)S(1)}, u32[]{:S(2)}, u32[]{:S(2)}) collective-permute-start(f32[80,128]{1,0:T(8,128)S(1)} %get-tuple-element.54), channel_id=1, source_target_pairs={{32,0},{64,32},{96,64},{128,96},{160,128},{192,160},{224,192},{0,2... | collective-permute-start | bytes 122888 | tf_op jit(solution)/shard_map/ppermute | solution.py:732
  39.6 0.5 coefficients.1
  40.1 0.6 collective-permute-done.2.r_3_
  40.7 3.0 %collective-permute-done.3.r_4_ = f32[80,128]{1,0:T(8,128)S(1)} collective-permute-done((f32[80,128]{1,0:T(8,128)S(1)}, f32[80,128]{1,0:T(8,128)S(1)}, u32[]{:S(2)}, u32[]{:S(2)}) %collective-permute-start.3) | collective-permute-done | bytes 40992 | tf_op jit(solution)/shard_map/ppermute | solution.py:732
  43.7 0.4 halo.1
  44.1 0.0 copy-start.7
  44.1 16.1 %all_to_all.31 = f32[32,8,384]{2,1,0:T(8,128)S(1)} all-to-all(f32[32,8,384]{2,1,0:T(8,128)S(1)} %bitcast.24), channel_id=1, replica_groups=mesh['lat'=8,'lon_0'=4,'lon_1'=4,'lon_2'=2] {'lon_0','lon_1','lon_2'}, dimensions={0} | all-to-all | bytes 786432 | tf_op jit(solution)/shard_map/all_to_all | solution.py:727
  60.2 1.8 %step.1 = (f32[256,256]{1,0:T(8,128)S(1)}, f32[256,256]{1,0:T(8,128)S(1)}, f32[256,256]{1,0:T(8,128)S(1)}, f32[8,128]{1,0:T(8,128)S(1)}) custom-call(f32[256,384]{1,0:T(8,128)S(1)} %bitcast.23, f32[256,256]{1,0:T(8,128)S(1)} %bitcast.18, f32[256,256]{1,0:T(8,128)S(1)} %get-tuple-element.57.r_2_.r_1_, f32[256,256]{1,0:T(8,128)S(1)} %get-tuple-element.58.r_3_, ...), custom_call_target="tpu_custom_call" | custom-call | tf_op jit(solution)/shard_map/step/pallas_call | solution.py:826
  62.0 12.3 %all_to_all.32 = f32[32,8,256]{2,1,0:T(8,128)S(1)} all-to-all(f32[32,8,256]{2,1,0:T(8,128)S(1)} %bitcast.28), channel_id=1, replica_groups=mesh['lat'=8,'lon_0'=4,'lon_1'=4,'lon_2'=2] {'lon_0','lon_1','lon_2'}, dimensions={0} | all-to-all | bytes 524288 | tf_op jit(solution)/shard_map/all_to_all | solution.py:727
  74.3 0.5 sums.1
  74.9 0.1 collective-permute-start.4
  74.9 1.5 %collective-permute-start.5 = (f32[80,128]{1,0:T(8,128)S(1)}, f32[80,128]{1,0:T(8,128)S(1)}, u32[]{:S(2)}, u32[]{:S(2)}) collective-permute-start(f32[80,128]{1,0:T(8,128)S(1)} %get-tuple-element.66), channel_id=1, source_target_pairs={{224,0},{0,32},{32,64},{64,96},{96,128},{128,160},{160,192},{192,2... | collective-permute-start | bytes 122888 | tf_op jit(solution)/shard_map/ppermute | solution.py:732
  76.4 0.2 unpack_first.1
  76.6 1.2 %collective-permute-done.4.r_3_ = f32[80,128]{1,0:T(8,128)S(1)} collective-permute-done((f32[80,128]{1,0:T(8,128)S(1)}, f32[80,128]{1,0:T(8,128)S(1)}, u32[]{:S(2)}, u32[]{:S(2)}) %collective-permute-start.4) | collective-permute-done | bytes 40992 | tf_op jit(solution)/shard_map/ppermute | solution.py:732
  77.8 1.3 %collective-permute-done.5.r_4_ = f32[80,128]{1,0:T(8,128)S(1)} collective-permute-done((f32[80,128]{1,0:T(8,128)S(1)}, f32[80,128]{1,0:T(8,128)S(1)}, u32[]{:S(2)}, u32[]{:S(2)}) %collective-permute-start.5) | collective-permute-done | bytes 40992 | tf_op jit(solution)/shard_map/ppermute | solution.py:732
  79.1 0.4 ends.1
  79.5 13.6 %all_to_all.33 = f32[32,8,256]{2,1,0:T(8,128)S(1)} all-to-all(f32[32,8,256]{2,1,0:T(8,128)S(1)} %bitcast.27), channel_id=1, replica_groups=mesh['lat'=8,'lon_0'=4,'lon_1'=4,'lon_2'=2] {'lon_0','lon_1','lon_2'}, dimensions={0} | all-to-all | bytes 524288 | tf_op jit(solution)/shard_map/all_to_all | solution.py:727
  93.1 1.2 %last.1 = f32[256,256]{1,0:T(8,128)} custom-call(f32[256,256]{1,0:T(8,128)S(1)} %bitcast.13, f32[256,256]{1,0:T(8,128)S(1)} %get-tuple-element.57.r_2_.r_1_, f32[256,256]{1,0:T(8,128)S(1)} %get-tuple-element.71.r_2_, f32[256,256]{1,0:T(8,128)S(1)} %get-tuple-element.68.r_1_.r_3_, bf16[2,576,256]{2,1,0:T(8,128)(2,1)S(1)} %copy-done), custom_call_target="tpu_custom_call" | custom-call | tf_op jit(solution)/shard_map/last/pallas_call | solution.py:851
  94.3 3.7 %all-to-all-start.5 = ((f32[32,8,256]{2,1,0:T(8,128)}), f32[32,8,256]{2,1,0:T(8,128)S(1)}, u32[]{:S(2)}, u32[]{:S(2)}) async-start(f32[32,8,256]{2,1,0:T(8,128)} %bitcast.11), calls=%async_computation.5 | async-start | bytes 524288 | tf_op jit(solution)/shard_map/all_to_all | solution.py:727
  98.1 1.2 %collective-permute-start.8 = (f32[8,128]{1,0:T(8,128)S(1)}, f32[8,128]{1,0:T(8,128)S(1)}, u32[]{:S(2)}, u32[]{:S(2)}) collective-permute-start(f32[8,128]{1,0:T(8,128)S(1)} %gather.1.r_5_), channel_id=1, source_target_pairs={{128,0},{160,32},{192,64},{224,96},{0,128},{32,160},{64,192},{96,2... | collective-permute-start | bytes 12296 | tf_op jit(solution)/shard_map/ppermute | solution.py:732
  99.3 0.6 collective-permute-start.7
  100.0 3.0 %collective-permute-start.6 = (f32[8,128]{1,0:T(8,128)S(1)}, f32[8,128]{1,0:T(8,128)S(1)}, u32[]{:S(2)}, u32[]{:S(2)}) collective-permute-start(f32[8,128]{1,0:T(8,128)S(1)} %gather.1.r_5_), channel_id=1, source_target_pairs={{64,0},{96,32},{128,64},{160,96},{192,128},{224,160},{0,192},{32,2... | collective-permute-start | bytes 12296 | tf_op jit(solution)/shard_map/ppermute | solution.py:732
  102.9 0.1 unpack_image.1.r_2_
  103.0 1.8 %collective-permute-done.8.r_8_ = f32[8,128]{1,0:T(8,128)S(1)} collective-permute-done((f32[8,128]{1,0:T(8,128)S(1)}, f32[8,128]{1,0:T(8,128)S(1)}, u32[]{:S(2)}, u32[]{:S(2)}) %collective-permute-start.8) | collective-permute-done | bytes 4128 | tf_op jit(solution)/shard_map/ppermute | solution.py:732
  104.9 0.3 collective-permute-done.6.r_6_
  105.1 2.0 %all-to-all-done.5 = f32[32,8,256]{2,1,0:T(8,128)S(1)} async-done(((f32[32,8,256]{2,1,0:T(8,128)}), f32[32,8,256]{2,1,0:T(8,128)S(1)}, u32[]{:S(2)}, u32[]{:S(2)}) %all-to-all-start.5) | async-done | bytes 262176 | tf_op jit(solution)/shard_map/all_to_all | solution.py:727
  107.2 1.0 finish.1
  (17 shorter events, 0.1 us)
Async XLA Ops:
  1.7 17.7 %copy-start.1 = (s32[135,256]{1,0:T(8,128)S(1)}, s32[135,256]{1,0:T(8,128)}, u32[]{:S(2)}) copy-start(s32[135,256]{1,0:T(8,128)} %r_4_.2) | copy-start | bytes 414724
  1.7 17.7 %copy-start.4 = (f32[135,256]{1,0:T(8,128)S(1)}, f32[135,256]{1,0:T(8,128)}, u32[]{:S(2)}) copy-start(f32[135,256]{1,0:T(8,128)} %east_ref.1) | copy-start | bytes 414724
  1.9 17.7 %copy-start = (bf16[2,576,256]{2,1,0:T(8,128)(2,1)S(1)}, bf16[2,576,256]{2,1,0:T(8,128)(2,1)}, u32[]{:S(2)}) copy-start(bf16[2,576,256]{2,1,0:T(8,128)(2,1)} %constant.42.clone.r_2_.r_5_.r_4_) | copy-start | bytes 1769476
  20.7 3.9 %copy-start.2 = (f32[2,128,128]{2,1,0:T(8,128)S(1)}, f32[2,128,128]{2,1,0:T(8,128)}, u32[]{:S(2)}) copy-start(f32[2,128,128]{2,1,0:T(8,128)} %r_5_.2) | copy-start | bytes 393220
  20.7 3.9 %copy-start.5 = (f32[135,256]{1,0:T(8,128)S(1)}, f32[135,256]{1,0:T(8,128)}, u32[]{:S(2)}) copy-start(f32[135,256]{1,0:T(8,128)} %north_ref.1) | copy-start | bytes 414724
  20.7 14.3 %all-to-all-start.1 = ((f32[32,8,256]{2,1,0:T(8,128)}), f32[32,8,256]{2,1,0:T(8,128)S(1)}, u32[]{:S(2)}, u32[]{:S(2)}) async-start(f32[32,8,256]{2,1,0:T(8,128)} %bitcast.2), calls=%async_computation.1 | async-start | bytes 524288 | tf_op jit(solution)/shard_map/all_to_all | solution.py:727
  24.7 7.2 %collective-permute-start = (f32[8,256]{1,0:T(8,128)S(1)}, f32[8,256]{1,0:T(8,128)S(1)}, u32[]{:S(2)}, u32[]{:S(2)}) collective-permute-start(f32[8,256]{1,0:T(8,128)S(1)} %get-tuple-element.45), channel_id=1, source_target_pairs={{32,0},{64,32},{96,64},{128,96},{160,128},{192,160},{224,192},{0,2... | collective-permute-start | bytes 24584 | tf_op jit(solution)/shard_map/ppermute | solution.py:732
  30.4 4.1 %collective-permute-start.1 = (f32[80,128]{1,0:T(8,128)S(1)}, f32[80,128]{1,0:T(8,128)S(1)}, u32[]{:S(2)}, u32[]{:S(2)}) collective-permute-start(f32[80,128]{1,0:T(8,128)S(1)} %get-tuple-element.49), channel_id=1, source_target_pairs={{224,0},{0,32},{32,64},{64,96},{96,128},{128,160},{160,192},{192,2... | collective-permute-start | bytes 122888 | tf_op jit(solution)/shard_map/ppermute | solution.py:732
  31.1 0.7 copy-start.8
  31.9 3.1 %copy-start.6 = (f32[2,128,128]{2,1,0:T(8,128)S(1)}, f32[2,128,128]{2,1,0:T(8,128)}, u32[]{:S(2)}) copy-start(f32[2,128,128]{2,1,0:T(8,128)} %r_2_.2) | copy-start | bytes 393220
  35.3 5.4 %collective-permute-start.2 = (f32[80,128]{1,0:T(8,128)S(1)}, f32[80,128]{1,0:T(8,128)S(1)}, u32[]{:S(2)}, u32[]{:S(2)}) collective-permute-start(f32[80,128]{1,0:T(8,128)S(1)} %get-tuple-element.54), channel_id=1, source_target_pairs={{32,0},{64,32},{96,64},{128,96},{160,128},{192,160},{224,192},{0,2... | collective-permute-start | bytes 122888 | tf_op jit(solution)/shard_map/ppermute | solution.py:732
  39.6 4.1 %collective-permute-start.3 = (f32[80,128]{1,0:T(8,128)S(1)}, f32[80,128]{1,0:T(8,128)S(1)}, u32[]{:S(2)}, u32[]{:S(2)}) collective-permute-start(f32[80,128]{1,0:T(8,128)S(1)} %get-tuple-element.55), channel_id=1, source_target_pairs={{224,0},{0,32},{32,64},{64,96},{96,128},{128,160},{160,192},{192,2... | collective-permute-start | bytes 122888 | tf_op jit(solution)/shard_map/ppermute | solution.py:732
  44.1 16.1 %copy-start.7 = (f32[32,64]{1,0:T(8,128)S(1)}, f32[32,64]{1,0:T(8,128)}, u32[]{:S(2)}) copy-start(f32[32,64]{1,0:T(8,128)} %constant.44.clone.r_6_) | copy-start | bytes 24580
  74.9 2.9 %collective-permute-start.4 = (f32[80,128]{1,0:T(8,128)S(1)}, f32[80,128]{1,0:T(8,128)S(1)}, u32[]{:S(2)}, u32[]{:S(2)}) collective-permute-start(f32[80,128]{1,0:T(8,128)S(1)} %get-tuple-element.65), channel_id=1, source_target_pairs={{32,0},{64,32},{96,64},{128,96},{160,128},{192,160},{224,192},{0,2... | collective-permute-start | bytes 122888 | tf_op jit(solution)/shard_map/ppermute | solution.py:732
  74.9 4.1 %collective-permute-start.5 = (f32[80,128]{1,0:T(8,128)S(1)}, f32[80,128]{1,0:T(8,128)S(1)}, u32[]{:S(2)}, u32[]{:S(2)}) collective-permute-start(f32[80,128]{1,0:T(8,128)S(1)} %get-tuple-element.66), channel_id=1, source_target_pairs={{224,0},{0,32},{32,64},{64,96},{96,128},{128,160},{160,192},{192,2... | collective-permute-start | bytes 122888 | tf_op jit(solution)/shard_map/ppermute | solution.py:732
  94.3 12.8 %all-to-all-start.5 = ((f32[32,8,256]{2,1,0:T(8,128)}), f32[32,8,256]{2,1,0:T(8,128)S(1)}, u32[]{:S(2)}, u32[]{:S(2)}) async-start(f32[32,8,256]{2,1,0:T(8,128)} %bitcast.11), calls=%async_computation.5 | async-start | bytes 524288 | tf_op jit(solution)/shard_map/all_to_all | solution.py:727
  98.1 9.1 %copy-start.3 = (f32[135,256]{1,0:T(8,128)S(1)}, f32[135,256]{1,0:T(8,128)}, u32[]{:S(2)}) copy-start(f32[135,256]{1,0:T(8,128)} %r_3_.1) | copy-start | bytes 414724
  98.1 6.7 %collective-permute-start.8 = (f32[8,128]{1,0:T(8,128)S(1)}, f32[8,128]{1,0:T(8,128)S(1)}, u32[]{:S(2)}, u32[]{:S(2)}) collective-permute-start(f32[8,128]{1,0:T(8,128)S(1)} %gather.1.r_5_), channel_id=1, source_target_pairs={{128,0},{160,32},{192,64},{224,96},{0,128},{32,160},{64,192},{96,2... | collective-permute-start | bytes 12296 | tf_op jit(solution)/shard_map/ppermute | solution.py:732
  99.3 5.5 %collective-permute-start.7 = (f32[8,128]{1,0:T(8,128)S(1)}, f32[8,128]{1,0:T(8,128)S(1)}, u32[]{:S(2)}, u32[]{:S(2)}) collective-permute-start(f32[8,128]{1,0:T(8,128)S(1)} %gather.1.r_5_), channel_id=1, source_target_pairs={{192,0},{224,32},{0,64},{32,96},{64,128},{96,160},{128,192},{160,2... | collective-permute-start | bytes 12296 | tf_op jit(solution)/shard_map/ppermute | solution.py:732
  100.0 5.2 %collective-permute-start.6 = (f32[8,128]{1,0:T(8,128)S(1)}, f32[8,128]{1,0:T(8,128)S(1)}, u32[]{:S(2)}, u32[]{:S(2)}) collective-permute-start(f32[8,128]{1,0:T(8,128)S(1)} %gather.1.r_5_), channel_id=1, source_target_pairs={{64,0},{96,32},{128,64},{160,96},{192,128},{224,160},{0,192},{32,2... | collective-permute-start | bytes 12296 | tf_op jit(solution)/shard_map/ppermute | solution.py:732

commit v11 on v10

--- a/solution.py
+++ b/solution.py
@@ -347,17 +347,26 @@
     return jnp.concatenate(lines[:2], axis=1), jnp.concatenate(lines[2:], axis=1)
 
 
-def blocks_kernel(spec_ref, scale_ref, aligned_ref, scaled_ref, part_ref, down_ref, up_ref):
+def blocks_kernel(spec_ref, scale_ref, aligned_ref, scaled_ref, down_ref, up_ref):
     count, block = aligned_ref.shape[0], aligned_ref.shape[1]
     half, rows = block // 2, count * block
     scaled = spec_ref[...] * scale_ref[...]
     scaled_ref[...] = scaled
+    first = dot(aligned_ref[0, :ROWS, :], scaled[:block])
+    last = dot(aligned_ref[count - 1, block - ROWS :, :], scaled[rows - block :])
+    store_rows(down_ref, scaled[:half], first[:1], scale_ref[:1, :])
+    store_rows(up_ref, scaled[rows - half :], last[ROWS - 1 :], scale_ref[rows - 1 :, :])
+
+
+def inner_kernel(scaled_ref, aligned_ref, stag_ref, part_ref):
+    count, block = aligned_ref.shape[0], aligned_ref.shape[1]
+    half = block // 2
     for b in range(count):
-        part_ref[b * block : (b + 1) * block, :] = dot(
-            aligned_ref[b], scaled[b * block : (b + 1) * block]
-        )
-    store_rows(down_ref, scaled[:half], part_ref[:1, :], scale_ref[:1, :])
-    store_rows(up_ref, scaled[rows - half :], part_ref[rows - 1 :, :], scale_ref[rows - 1 :, :])
+        at = slice(b * block, (b + 1) * block)
+        part_ref[at, :] = dot(aligned_ref[b], scaled_ref[at, :])
+    for b in range(count - 1):
+        at = slice(half + b * block, half + (b + 1) * block)
+        part_ref[at, :] = part_ref[at, :] + dot(stag_ref[b], scaled_ref[at, :])
 
 
 def combine(
@@ -370,15 +379,16 @@
         jnp.concatenate([load_edge(below_ref), scaled_ref[:half, :]], axis=0),
     )
     upper = load_edge(above_ref) * flags_ref[:1, :]
-    pieces = [before[ROWS:]]
-    for b in range(count - 1):
-        pieces.append(dot(stag_ref[b], scaled_ref[half + b * block : half + (b + 1) * block, :]))
     after = dot(
         stag_ref[count - 1, : half + ROWS, :],
         jnp.concatenate([scaled_ref[rows - half :, :], upper], axis=0),
     )
-    pieces.append(after[:half])
-    full = (part_ref[...] + jnp.concatenate(pieces, axis=0)) * (scale_ref[...] * norm)
+    pieces = [
+        part_ref[:half, :] + before[ROWS:],
+        part_ref[half : rows - half, :],
+        part_ref[rows - half :, :] + after[:half],
+    ]
+    full = jnp.concatenate(pieces, axis=0) * (scale_ref[...] * norm)
     return full, before, after
 
 
@@ -806,17 +816,15 @@
 
     edge = (half + 2 * ROWS, 128)
 
-    def blocks(spectrum):
-        scaled, part, down, up = call(blocks_kernel, [wide, wide, edge, edge], name="blocks")(
-            spectrum, scale, aligned_inverse
-        )
-        above, below = from_lat(down, 1), from_lat(up, -1)
-        return scaled, part, scale, above, below, stag, stag_below, flags
-
-    pieces = blocks(spec_rhs)
+    scaled, down, up = call(blocks_kernel, [wide, edge, edge], name="blocks")(
+        spec_rhs, scale, aligned_inverse
+    )
+    above, below = from_lat(down, 1), from_lat(up, -1)
+    part = call(inner_kernel, wide, name="inner")(scaled, aligned_inverse, stag)
+    pieces = (scaled, part, scale, above, below, stag, stag_below, flags)
     flat = call(
         lambda *r: coefficients_kernel(groups, length, *r), [wide] * 3, name="coefficients"
-    )(slab, after(spec_rhs, pieces[0]))
+    )(slab, after(spec_rhs, scaled))
     late = after(late, *flat)
     filtered = exchanged(
         call(

time: 109 us -> 108 us (level)
  transfers between devices with their start and end apart: 11 -> 11, of which waited for: 8 -> 8; matrix products, arithmetic and copies ran while one was open for 1% -> 1% of each run, Pallas kernels for 1% -> 2%
where the time goes in v11:
time: 108 us
  blocking collectives  59.5 us (55%)
  starting transfers between devices  23.8 us (22%)
  waiting for transfers between devices  12.3 us (11%)
  Pallas kernels  8.84 us (8%)
  local copies, waits for them, and re-layouts  1.43 us (1%)
  other arithmetic  1.18 us (1%)
    all_to_all x4, blocking collectives, exchanged(): lax.all_to_all(parts, LON, split_axis=0, concat_axis=0, tiled=True)  59.5 us
    ppermute x9, starting transfers between devices, from_lat(): lax.ppermute(value, 'lat', [((d + steps) % count, d) for d in range(count)])  16.2 us
    ppermute x9, waiting for transfers between devices, from_lat(): lax.ppermute(value, 'lat', [((d + steps) % count, d) for d in range(count)])  10.3 us
    all_to_all x2, starting transfers between devices, exchanged(): lax.all_to_all(parts, LON, split_axis=0, concat_axis=0, tiled=True)  7.55 us
  transfers between devices with their start and end apart: 11, of which 8 were waited for; matrix products, arithmetic and copies ran while one was open for 1% of the time, Pallas kernels for 2%

profile of v11, /device:TPU:1, one launch (start us, length us, event | category | flops | bytes accessed | tf_op | source)
XLA Modules:
  0.0 107.9 jit_solution(6299149198825181130)
XLA Ops:
  0.6 1.1 convert_multiply_fusion
  1.7 0.0 copy-start.1
  1.7 0.0 copy-start.5
  1.7 0.1 pack.1
  1.9 0.0 copy-start
  1.9 17.5 %all_to_all.30 = f32[32,8,256]{2,1,0:T(8,128)S(1)} all-to-all(f32[32,8,256]{2,1,0:T(8,128)S(1)} %bitcast.26), channel_id=1, replica_groups=mesh['lat'=8,'lon_0'=4,'lon_1'=4,'lon_2'=2] {'lon_0','lon_1','lon_2'}, dimensions={0} | all-to-all | bytes 524288 | tf_op jit(solution)/shard_map/all_to_all | solution.py:737
  19.4 0.1 pack_more.1.r_1_
  19.5 1.2 %forward.1 = f32[256,256]{1,0:T(8,128)} custom-call(f32[256,256]{1,0:T(8,128)S(1)} %bitcast.16, f32[256,256]{1,0:T(8,128)S(1)} %pack_more.1.r_1_, bf16[2,576,256]{2,1,0:T(8,128)(2,1)S(1)} %copy-done), custom_call_target="tpu_custom_call" | custom-call | tf_op jit(solution)/shard_map/forward/pallas_call | solution.py:780
  20.7 3.8 %all-to-all-start.1 = ((f32[32,8,256]{2,1,0:T(8,128)}), f32[32,8,256]{2,1,0:T(8,128)S(1)}, u32[]{:S(2)}, u32[]{:S(2)}) async-start(f32[32,8,256]{2,1,0:T(8,128)} %bitcast.2), calls=%async_computation.1 | async-start | bytes 524288 | tf_op jit(solution)/shard_map/all_to_all | solution.py:737
  24.6 0.1 edges.1
  24.7 5.7 %collective-permute-start = (f32[8,256]{1,0:T(8,128)S(1)}, f32[8,256]{1,0:T(8,128)S(1)}, u32[]{:S(2)}, u32[]{:S(2)}) collective-permute-start(f32[8,256]{1,0:T(8,128)S(1)} %get-tuple-element.44), channel_id=1, source_target_pairs={{32,0},{64,32},{96,64},{128,96},{160,128},{192,160},{224,192},{0,2... | collective-permute-start | bytes 24584 | tf_op jit(solution)/shard_map/ppermute | solution.py:742
  30.4 0.0 collective-permute-start.1
  30.4 0.7 constant_dynamic-slice_fusion
  31.1 0.7 copy-done.8
  31.7 0.1 add_rsqrt_fusion.scale_ref.r_2_.r_1_
  31.9 0.0 copy-start.3
  31.9 0.0 collective-permute-done.wet_above_ref
  31.9 2.5 %collective-permute-done.1.from_below_ref.r_6_.r_4_ = f32[80,128]{1,0:T(8,128)S(1)} collective-permute-done((f32[80,128]{1,0:T(8,128)S(1)}, f32[80,128]{1,0:T(8,128)S(1)}, u32[]{:S(2)}, u32[]{:S(2)}) %collective-permute-start.1) | collective-permute-done | bytes 40992 | tf_op jit(solution)/shard_map/ppermute | solution.py:742
  34.4 0.6 pack_rest.1.r_8_
  35.0 0.2 blocks.1
  35.2 4.2 %collective-permute-start.2 = (f32[80,128]{1,0:T(8,128)S(1)}, f32[80,128]{1,0:T(8,128)S(1)}, u32[]{:S(2)}, u32[]{:S(2)}) collective-permute-start(f32[80,128]{1,0:T(8,128)S(1)} %get-tuple-element.52), channel_id=1, source_target_pairs={{32,0},{64,32},{96,64},{128,96},{160,128},{192,160},{224,192},{0,2... | collective-permute-start | bytes 122888 | tf_op jit(solution)/shard_map/ppermute | solution.py:742
  39.4 0.3 inner.1.r_1_
  39.8 0.5 coefficients.1
  40.3 0.2 collective-permute-done.2.r_3_
  40.5 3.0 %collective-permute-done.3.r_4_ = f32[80,128]{1,0:T(8,128)S(1)} collective-permute-done((f32[80,128]{1,0:T(8,128)S(1)}, f32[80,128]{1,0:T(8,128)S(1)}, u32[]{:S(2)}, u32[]{:S(2)}) %collective-permute-start.3) | collective-permute-done | bytes 40992 | tf_op jit(solution)/shard_map/ppermute | solution.py:742
  43.5 0.4 halo.1
  43.9 0.0 copy-start.7
  43.9 16.0 %all_to_all.31 = f32[32,8,384]{2,1,0:T(8,128)S(1)} all-to-all(f32[32,8,384]{2,1,0:T(8,128)S(1)} %bitcast.24), channel_id=1, replica_groups=mesh['lat'=8,'lon_0'=4,'lon_1'=4,'lon_2'=2] {'lon_0','lon_1','lon_2'}, dimensions={0} | all-to-all | bytes 786432 | tf_op jit(solution)/shard_map/all_to_all | solution.py:737
  60.0 1.8 %step.1 = (f32[256,256]{1,0:T(8,128)S(1)}, f32[256,256]{1,0:T(8,128)S(1)}, f32[256,256]{1,0:T(8,128)S(1)}, f32[8,128]{1,0:T(8,128)S(1)}) custom-call(f32[256,384]{1,0:T(8,128)S(1)} %bitcast.23, f32[256,256]{1,0:T(8,128)S(1)} %bitcast.18, f32[256,256]{1,0:T(8,128)S(1)} %get-tuple-element.55.r_2_.r_1_, f32[256,256]{1,0:T(8,128)S(1)} %get-tuple-element.56.r_3_, ...), custom_call_target="tpu_custom_call" | custom-call | tf_op jit(solution)/shard_map/step/pallas_call | solution.py:834
  61.8 12.3 %all_to_all.32 = f32[32,8,256]{2,1,0:T(8,128)S(1)} all-to-all(f32[32,8,256]{2,1,0:T(8,128)S(1)} %bitcast.28), channel_id=1, replica_groups=mesh['lat'=8,'lon_0'=4,'lon_1'=4,'lon_2'=2] {'lon_0','lon_1','lon_2'}, dimensions={0} | all-to-all | bytes 524288 | tf_op jit(solution)/shard_map/all_to_all | solution.py:737
  74.1 0.5 sums.1
  74.6 0.1 collective-permute-start.4
  74.7 1.5 %collective-permute-start.5 = (f32[80,128]{1,0:T(8,128)S(1)}, f32[80,128]{1,0:T(8,128)S(1)}, u32[]{:S(2)}, u32[]{:S(2)}) collective-permute-start(f32[80,128]{1,0:T(8,128)S(1)} %get-tuple-element.64), channel_id=1, source_target_pairs={{224,0},{0,32},{32,64},{64,96},{96,128},{128,160},{160,192},{192,2... | collective-permute-start | bytes 122888 | tf_op jit(solution)/shard_map/ppermute | solution.py:742
  76.2 0.2 unpack_first.1
  76.4 1.2 %collective-permute-done.4.r_3_ = f32[80,128]{1,0:T(8,128)S(1)} collective-permute-done((f32[80,128]{1,0:T(8,128)S(1)}, f32[80,128]{1,0:T(8,128)S(1)}, u32[]{:S(2)}, u32[]{:S(2)}) %collective-permute-start.4) | collective-permute-done | bytes 40992 | tf_op jit(solution)/shard_map/ppermute | solution.py:742
  77.6 1.3 %collective-permute-done.5.r_4_ = f32[80,128]{1,0:T(8,128)S(1)} collective-permute-done((f32[80,128]{1,0:T(8,128)S(1)}, f32[80,128]{1,0:T(8,128)S(1)}, u32[]{:S(2)}, u32[]{:S(2)}) %collective-permute-start.5) | collective-permute-done | bytes 40992 | tf_op jit(solution)/shard_map/ppermute | solution.py:742
  78.9 0.4 ends.1
  79.3 13.6 %all_to_all.33 = f32[32,8,256]{2,1,0:T(8,128)S(1)} all-to-all(f32[32,8,256]{2,1,0:T(8,128)S(1)} %bitcast.27), channel_id=1, replica_groups=mesh['lat'=8,'lon_0'=4,'lon_1'=4,'lon_2'=2] {'lon_0','lon_1','lon_2'}, dimensions={0} | all-to-all | bytes 524288 | tf_op jit(solution)/shard_map/all_to_all | solution.py:737
  92.9 1.2 %last.1 = f32[256,256]{1,0:T(8,128)} custom-call(f32[256,256]{1,0:T(8,128)S(1)} %bitcast.13, f32[256,256]{1,0:T(8,128)S(1)} %get-tuple-element.55.r_2_.r_1_, f32[256,256]{1,0:T(8,128)S(1)} %get-tuple-element.69.r_2_, f32[256,256]{1,0:T(8,128)S(1)} %get-tuple-element.66.r_1_.r_3_, bf16[2,576,256]{2,1,0:T(8,128)(2,1)S(1)} %copy-done), custom_call_target="tpu_custom_call" | custom-call | tf_op jit(solution)/shard_map/last/pallas_call | solution.py:859
  94.1 3.7 %all-to-all-start.5 = ((f32[32,8,256]{2,1,0:T(8,128)}), f32[32,8,256]{2,1,0:T(8,128)S(1)}, u32[]{:S(2)}, u32[]{:S(2)}) async-start(f32[32,8,256]{2,1,0:T(8,128)} %bitcast.11), calls=%async_computation.5 | async-start | bytes 524288 | tf_op jit(solution)/shard_map/all_to_all | solution.py:737
  97.9 1.2 %collective-permute-start.8 = (f32[8,128]{1,0:T(8,128)S(1)}, f32[8,128]{1,0:T(8,128)S(1)}, u32[]{:S(2)}, u32[]{:S(2)}) collective-permute-start(f32[8,128]{1,0:T(8,128)S(1)} %gather.1.r_5_), channel_id=1, source_target_pairs={{128,0},{160,32},{192,64},{224,96},{0,128},{32,160},{64,192},{96,2... | collective-permute-start | bytes 12296 | tf_op jit(solution)/shard_map/ppermute | solution.py:742
  99.1 0.6 collective-permute-start.7
  99.8 2.9 %collective-permute-start.6 = (f32[8,128]{1,0:T(8,128)S(1)}, f32[8,128]{1,0:T(8,128)S(1)}, u32[]{:S(2)}, u32[]{:S(2)}) collective-permute-start(f32[8,128]{1,0:T(8,128)S(1)} %gather.1.r_5_), channel_id=1, source_target_pairs={{64,0},{96,32},{128,64},{160,96},{192,128},{224,160},{0,192},{32,2... | collective-permute-start | bytes 12296 | tf_op jit(solution)/shard_map/ppermute | solution.py:742
  102.7 0.1 unpack_image.1.r_2_
  102.8 1.8 %collective-permute-done.8.r_8_ = f32[8,128]{1,0:T(8,128)S(1)} collective-permute-done((f32[8,128]{1,0:T(8,128)S(1)}, f32[8,128]{1,0:T(8,128)S(1)}, u32[]{:S(2)}, u32[]{:S(2)}) %collective-permute-start.8) | collective-permute-done | bytes 4128 | tf_op jit(solution)/shard_map/ppermute | solution.py:742
  104.6 0.3 collective-permute-done.6.r_6_
  104.9 2.0 %all-to-all-done.5 = f32[32,8,256]{2,1,0:T(8,128)S(1)} async-done(((f32[32,8,256]{2,1,0:T(8,128)}), f32[32,8,256]{2,1,0:T(8,128)S(1)}, u32[]{:S(2)}, u32[]{:S(2)}) %all-to-all-start.5) | async-done | bytes 262176 | tf_op jit(solution)/shard_map/all_to_all | solution.py:737
  107.0 1.0 finish.1
  (18 shorter events, 0.1 us)
Async XLA Ops:
  1.7 17.7 %copy-start.1 = (s32[135,256]{1,0:T(8,128)S(1)}, s32[135,256]{1,0:T(8,128)}, u32[]{:S(2)}) copy-start(s32[135,256]{1,0:T(8,128)} %r_4_.2) | copy-start | bytes 414724
  1.7 17.7 %copy-start.5 = (f32[135,256]{1,0:T(8,128)S(1)}, f32[135,256]{1,0:T(8,128)}, u32[]{:S(2)}) copy-start(f32[135,256]{1,0:T(8,128)} %east_ref.1) | copy-start | bytes 414724
  1.9 17.7 %copy-start = (bf16[2,576,256]{2,1,0:T(8,128)(2,1)S(1)}, bf16[2,576,256]{2,1,0:T(8,128)(2,1)}, u32[]{:S(2)}) copy-start(bf16[2,576,256]{2,1,0:T(8,128)(2,1)} %constant.42.clone.r_2_.r_5_.r_4_) | copy-start | bytes 1769476
  20.7 3.9 %copy-start.2 = (f32[2,128,128]{2,1,0:T(8,128)S(1)}, f32[2,128,128]{2,1,0:T(8,128)}, u32[]{:S(2)}) copy-start(f32[2,128,128]{2,1,0:T(8,128)} %r_5_.2) | copy-start | bytes 393220
  20.7 3.9 %copy-start.6 = (f32[135,256]{1,0:T(8,128)S(1)}, f32[135,256]{1,0:T(8,128)}, u32[]{:S(2)}) copy-start(f32[135,256]{1,0:T(8,128)} %north_ref.1) | copy-start | bytes 414724
  20.7 14.3 %all-to-all-start.1 = ((f32[32,8,256]{2,1,0:T(8,128)}), f32[32,8,256]{2,1,0:T(8,128)S(1)}, u32[]{:S(2)}, u32[]{:S(2)}) async-start(f32[32,8,256]{2,1,0:T(8,128)} %bitcast.2), calls=%async_computation.1 | async-start | bytes 524288 | tf_op jit(solution)/shard_map/all_to_all | solution.py:737
  24.7 7.2 %collective-permute-start = (f32[8,256]{1,0:T(8,128)S(1)}, f32[8,256]{1,0:T(8,128)S(1)}, u32[]{:S(2)}, u32[]{:S(2)}) collective-permute-start(f32[8,256]{1,0:T(8,128)S(1)} %get-tuple-element.44), channel_id=1, source_target_pairs={{32,0},{64,32},{96,64},{128,96},{160,128},{192,160},{224,192},{0,2... | collective-permute-start | bytes 24584 | tf_op jit(solution)/shard_map/ppermute | solution.py:742
  30.4 4.1 %collective-permute-start.1 = (f32[80,128]{1,0:T(8,128)S(1)}, f32[80,128]{1,0:T(8,128)S(1)}, u32[]{:S(2)}, u32[]{:S(2)}) collective-permute-start(f32[80,128]{1,0:T(8,128)S(1)} %get-tuple-element.48), channel_id=1, source_target_pairs={{224,0},{0,32},{32,64},{64,96},{96,128},{128,160},{160,192},{192,2... | collective-permute-start | bytes 122888 | tf_op jit(solution)/shard_map/ppermute | solution.py:742
  31.1 0.7 copy-start.8
  31.9 3.1 %copy-start.3 = (f32[2,128,128]{2,1,0:T(8,128)S(1)}, f32[2,128,128]{2,1,0:T(8,128)}, u32[]{:S(2)}) copy-start(f32[2,128,128]{2,1,0:T(8,128)} %r_2_.2) | copy-start | bytes 393220
  35.2 5.3 %collective-permute-start.2 = (f32[80,128]{1,0:T(8,128)S(1)}, f32[80,128]{1,0:T(8,128)S(1)}, u32[]{:S(2)}, u32[]{:S(2)}) collective-permute-start(f32[80,128]{1,0:T(8,128)S(1)} %get-tuple-element.52), channel_id=1, source_target_pairs={{32,0},{64,32},{96,64},{128,96},{160,128},{192,160},{224,192},{0,2... | collective-permute-start | bytes 122888 | tf_op jit(solution)/shard_map/ppermute | solution.py:742
  39.4 4.1 %collective-permute-start.3 = (f32[80,128]{1,0:T(8,128)S(1)}, f32[80,128]{1,0:T(8,128)S(1)}, u32[]{:S(2)}, u32[]{:S(2)}) collective-permute-start(f32[80,128]{1,0:T(8,128)S(1)} %get-tuple-element.53), channel_id=1, source_target_pairs={{224,0},{0,32},{32,64},{64,96},{96,128},{128,160},{160,192},{192,2... | collective-permute-start | bytes 122888 | tf_op jit(solution)/shard_map/ppermute | solution.py:742
  43.9 16.0 %copy-start.7 = (f32[32,64]{1,0:T(8,128)S(1)}, f32[32,64]{1,0:T(8,128)}, u32[]{:S(2)}) copy-start(f32[32,64]{1,0:T(8,128)} %constant.44.clone.r_6_) | copy-start | bytes 24580
  74.6 2.9 %collective-permute-start.4 = (f32[80,128]{1,0:T(8,128)S(1)}, f32[80,128]{1,0:T(8,128)S(1)}, u32[]{:S(2)}, u32[]{:S(2)}) collective-permute-start(f32[80,128]{1,0:T(8,128)S(1)} %get-tuple-element.63), channel_id=1, source_target_pairs={{32,0},{64,32},{96,64},{128,96},{160,128},{192,160},{224,192},{0,2... | collective-permute-start | bytes 122888 | tf_op jit(solution)/shard_map/ppermute | solution.py:742
  74.7 4.1 %collective-permute-start.5 = (f32[80,128]{1,0:T(8,128)S(1)}, f32[80,128]{1,0:T(8,128)S(1)}, u32[]{:S(2)}, u32[]{:S(2)}) collective-permute-start(f32[80,128]{1,0:T(8,128)S(1)} %get-tuple-element.64), channel_id=1, source_target_pairs={{224,0},{0,32},{32,64},{64,96},{96,128},{128,160},{160,192},{192,2... | collective-permute-start | bytes 122888 | tf_op jit(solution)/shard_map/ppermute | solution.py:742
  94.1 12.8 %all-to-all-start.5 = ((f32[32,8,256]{2,1,0:T(8,128)}), f32[32,8,256]{2,1,0:T(8,128)S(1)}, u32[]{:S(2)}, u32[]{:S(2)}) async-start(f32[32,8,256]{2,1,0:T(8,128)} %bitcast.11), calls=%async_computation.5 | async-start | bytes 524288 | tf_op jit(solution)/shard_map/all_to_all | solution.py:737
  97.9 9.1 %copy-start.4 = (f32[135,256]{1,0:T(8,128)S(1)}, f32[135,256]{1,0:T(8,128)}, u32[]{:S(2)}) copy-start(f32[135,256]{1,0:T(8,128)} %r_3_.1) | copy-start | bytes 414724
  97.9 6.7 %collective-permute-start.8 = (f32[8,128]{1,0:T(8,128)S(1)}, f32[8,128]{1,0:T(8,128)S(1)}, u32[]{:S(2)}, u32[]{:S(2)}) collective-permute-start(f32[8,128]{1,0:T(8,128)S(1)} %gather.1.r_5_), channel_id=1, source_target_pairs={{128,0},{160,32},{192,64},{224,96},{0,128},{32,160},{64,192},{96,2... | collective-permute-start | bytes 12296 | tf_op jit(solution)/shard_map/ppermute | solution.py:742
  99.1 5.5 %collective-permute-start.7 = (f32[8,128]{1,0:T(8,128)S(1)}, f32[8,128]{1,0:T(8,128)S(1)}, u32[]{:S(2)}, u32[]{:S(2)}) collective-permute-start(f32[8,128]{1,0:T(8,128)S(1)} %gather.1.r_5_), channel_id=1, source_target_pairs={{192,0},{224,32},{0,64},{32,96},{64,128},{96,160},{128,192},{160,2... | collective-permute-start | bytes 12296 | tf_op jit(solution)/shard_map/ppermute | solution.py:742
  99.8 5.2 %collective-permute-start.6 = (f32[8,128]{1,0:T(8,128)S(1)}, f32[8,128]{1,0:T(8,128)S(1)}, u32[]{:S(2)}, u32[]{:S(2)}) collective-permute-start(f32[8,128]{1,0:T(8,128)S(1)} %gather.1.r_5_), channel_id=1, source_target_pairs={{64,0},{96,32},{128,64},{160,96},{192,128},{224,160},{0,192},{32,2... | collective-permute-start | bytes 12296 | tf_op jit(solution)/shard_map/ppermute | solution.py:742

commit v12 on v11

--- a/solution.py
+++ b/solution.py
@@ -472,17 +472,22 @@
     half, rows = block // 2, count * block
     scaled = spec_ref[...] * scale_ref[...]
     scaled_ref[...] = scaled
+    coarse, rest = split(scaled)
+
+    def applied(matrix, at):
+        return product(split(matrix), (coarse[at], rest[at]))
+
     for b in range(count):
         at = slice(b * block, (b + 1) * block)
-        part_ref[at, :] = dot(aligned_ref[b], scaled[at])
+        part_ref[at, :] = applied(aligned_ref[b], at)
     for b in range(count - 1):
         at = slice(half + b * block, half + (b + 1) * block)
-        part_ref[at, :] = part_ref[at, :] + dot(stag_ref[b], scaled[at])
+        part_ref[at, :] = part_ref[at, :] + applied(stag_ref[b], at)
     first, last = slice(0, half), slice(rows - half, rows)
-    part_ref[first, :] = part_ref[first, :] + flags_ref[1:2, :] * dot(
-        stag_below_ref[ROWS : ROWS + half, half:], scaled[first]
-    )
-    part_ref[last, :] = part_ref[last, :] + dot(stag_ref[count - 1, :half, :half], scaled[last])
+    part_ref[first, :] = part_ref[first, :] + flags_ref[1:2, :] * applied(
+        stag_below_ref[ROWS : ROWS + half, half:], first
+    )
+    part_ref[last, :] = part_ref[last, :] + applied(stag_ref[count - 1, :half, :half], last)
     total = total_of(scaled * part_ref[...], length) * (flags_ref[2:3, :1] * norm)
     small = lanes((8, 128))
     own = jnp.where(small == SCALARS - 128 + 2, total, sums_ref[...])

time: 108 us -> 108 us (level)
  no operation moved by 1% of the time
where the time goes in v12:
time: 108 us
  blocking collectives  59.5 us (55%)
  starting transfers between devices  23.8 us (22%)
  waiting for transfers between devices  12.3 us (11%)
  Pallas kernels  8.84 us (8%)
  local copies, waits for them, and re-layouts  1.43 us (1%)
  other arithmetic  1.18 us (1%)
    all_to_all x4, blocking collectives, exchanged(): lax.all_to_all(parts, LON, split_axis=0, concat_axis=0, tiled=True)  59.5 us
    ppermute x9, starting transfers between devices, from_lat(): lax.ppermute(value, 'lat', [((d + steps) % count, d) for d in range(count)])  16.2 us
    ppermute x9, waiting for transfers between devices, from_lat(): lax.ppermute(value, 'lat', [((d + steps) % count, d) for d in range(count)])  10.3 us
    all_to_all x2, starting transfers between devices, exchanged(): lax.all_to_all(parts, LON, split_axis=0, concat_axis=0, tiled=True)  7.55 us
  transfers between devices with their start and end apart: 11, of which 8 were waited for; matrix products, arithmetic and copies ran while one was open for 1% of the time, Pallas kernels for 2%

profile of v12, /device:TPU:1, one launch (start us, length us, event | category | flops | bytes accessed | tf_op | source)
XLA Modules:
  0.0 107.9 jit_solution(6299149198825181130)
XLA Ops:
  0.6 1.1 convert_multiply_fusion
  1.7 0.0 copy-start.1
  1.7 0.0 copy-start.5
  1.7 0.1 pack.1
  1.9 0.0 copy-start
  1.9 17.5 %all_to_all.30 = f32[32,8,256]{2,1,0:T(8,128)S(1)} all-to-all(f32[32,8,256]{2,1,0:T(8,128)S(1)} %bitcast.26), channel_id=1, replica_groups=mesh['lat'=8,'lon_0'=4,'lon_1'=4,'lon_2'=2] {'lon_0','lon_1','lon_2'}, dimensions={0} | all-to-all | bytes 524288 | tf_op jit(solution)/shard_map/all_to_all | solution.py:742
  19.4 0.1 pack_more.1.r_1_
  19.5 1.2 %forward.1 = f32[256,256]{1,0:T(8,128)} custom-call(f32[256,256]{1,0:T(8,128)S(1)} %bitcast.16, f32[256,256]{1,0:T(8,128)S(1)} %pack_more.1.r_1_, bf16[2,576,256]{2,1,0:T(8,128)(2,1)S(1)} %copy-done), custom_call_target="tpu_custom_call" | custom-call | tf_op jit(solution)/shard_map/forward/pallas_call | solution.py:785
  20.7 3.8 %all-to-all-start.1 = ((f32[32,8,256]{2,1,0:T(8,128)}), f32[32,8,256]{2,1,0:T(8,128)S(1)}, u32[]{:S(2)}, u32[]{:S(2)}) async-start(f32[32,8,256]{2,1,0:T(8,128)} %bitcast.2), calls=%async_computation.1 | async-start | bytes 524288 | tf_op jit(solution)/shard_map/all_to_all | solution.py:742
  24.6 0.1 edges.1
  24.7 5.7 %collective-permute-start = (f32[8,256]{1,0:T(8,128)S(1)}, f32[8,256]{1,0:T(8,128)S(1)}, u32[]{:S(2)}, u32[]{:S(2)}) collective-permute-start(f32[8,256]{1,0:T(8,128)S(1)} %get-tuple-element.44), channel_id=1, source_target_pairs={{32,0},{64,32},{96,64},{128,96},{160,128},{192,160},{224,192},{0,2... | collective-permute-start | bytes 24584 | tf_op jit(solution)/shard_map/ppermute | solution.py:747
  30.4 0.0 collective-permute-start.1
  30.4 0.7 constant_dynamic-slice_fusion
  31.1 0.7 copy-done.8
  31.7 0.1 add_rsqrt_fusion.scale_ref.r_2_.r_1_
  31.9 0.0 copy-start.3
  31.9 0.0 collective-permute-done.wet_above_ref
  31.9 2.5 %collective-permute-done.1.from_below_ref.r_6_.r_4_ = f32[80,128]{1,0:T(8,128)S(1)} collective-permute-done((f32[80,128]{1,0:T(8,128)S(1)}, f32[80,128]{1,0:T(8,128)S(1)}, u32[]{:S(2)}, u32[]{:S(2)}) %collective-permute-start.1) | collective-permute-done | bytes 40992 | tf_op jit(solution)/shard_map/ppermute | solution.py:747
  34.4 0.6 pack_rest.1.r_8_
  35.0 0.2 blocks.1
  35.2 4.2 %collective-permute-start.2 = (f32[80,128]{1,0:T(8,128)S(1)}, f32[80,128]{1,0:T(8,128)S(1)}, u32[]{:S(2)}, u32[]{:S(2)}) collective-permute-start(f32[80,128]{1,0:T(8,128)S(1)} %get-tuple-element.52), channel_id=1, source_target_pairs={{32,0},{64,32},{96,64},{128,96},{160,128},{192,160},{224,192},{0,2... | collective-permute-start | bytes 122888 | tf_op jit(solution)/shard_map/ppermute | solution.py:747
  39.4 0.3 inner.1.r_1_
  39.8 0.5 coefficients.1
  40.3 0.2 collective-permute-done.2.r_3_
  40.5 3.0 %collective-permute-done.3.r_4_ = f32[80,128]{1,0:T(8,128)S(1)} collective-permute-done((f32[80,128]{1,0:T(8,128)S(1)}, f32[80,128]{1,0:T(8,128)S(1)}, u32[]{:S(2)}, u32[]{:S(2)}) %collective-permute-start.3) | collective-permute-done | bytes 40992 | tf_op jit(solution)/shard_map/ppermute | solution.py:747
  43.5 0.4 halo.1
  43.9 0.0 copy-start.7
  43.9 16.0 %all_to_all.31 = f32[32,8,384]{2,1,0:T(8,128)S(1)} all-to-all(f32[32,8,384]{2,1,0:T(8,128)S(1)} %bitcast.24), channel_id=1, replica_groups=mesh['lat'=8,'lon_0'=4,'lon_1'=4,'lon_2'=2] {'lon_0','lon_1','lon_2'}, dimensions={0} | all-to-all | bytes 786432 | tf_op jit(solution)/shard_map/all_to_all | solution.py:742
  60.0 1.8 %step.1 = (f32[256,256]{1,0:T(8,128)S(1)}, f32[256,256]{1,0:T(8,128)S(1)}, f32[256,256]{1,0:T(8,128)S(1)}, f32[8,128]{1,0:T(8,128)S(1)}) custom-call(f32[256,384]{1,0:T(8,128)S(1)} %bitcast.23, f32[256,256]{1,0:T(8,128)S(1)} %bitcast.18, f32[256,256]{1,0:T(8,128)S(1)} %get-tuple-element.55.r_2_.r_1_, f32[256,256]{1,0:T(8,128)S(1)} %get-tuple-element.56.r_3_, ...), custom_call_target="tpu_custom_call" | custom-call | tf_op jit(solution)/shard_map/step/pallas_call | solution.py:839
  61.8 12.3 %all_to_all.32 = f32[32,8,256]{2,1,0:T(8,128)S(1)} all-to-all(f32[32,8,256]{2,1,0:T(8,128)S(1)} %bitcast.28), channel_id=1, replica_groups=mesh['lat'=8,'lon_0'=4,'lon_1'=4,'lon_2'=2] {'lon_0','lon_1','lon_2'}, dimensions={0} | all-to-all | bytes 524288 | tf_op jit(solution)/shard_map/all_to_all | solution.py:742
  74.1 0.5 sums.1
  74.6 0.1 collective-permute-start.4
  74.7 1.5 %collective-permute-start.5 = (f32[80,128]{1,0:T(8,128)S(1)}, f32[80,128]{1,0:T(8,128)S(1)}, u32[]{:S(2)}, u32[]{:S(2)}) collective-permute-start(f32[80,128]{1,0:T(8,128)S(1)} %get-tuple-element.64), channel_id=1, source_target_pairs={{224,0},{0,32},{32,64},{64,96},{96,128},{128,160},{160,192},{192,2... | collective-permute-start | bytes 122888 | tf_op jit(solution)/shard_map/ppermute | solution.py:747
  76.2 0.2 unpack_first.1
  76.4 1.2 %collective-permute-done.4.r_3_ = f32[80,128]{1,0:T(8,128)S(1)} collective-permute-done((f32[80,128]{1,0:T(8,128)S(1)}, f32[80,128]{1,0:T(8,128)S(1)}, u32[]{:S(2)}, u32[]{:S(2)}) %collective-permute-start.4) | collective-permute-done | bytes 40992 | tf_op jit(solution)/shard_map/ppermute | solution.py:747
  77.6 1.3 %collective-permute-done.5.r_4_ = f32[80,128]{1,0:T(8,128)S(1)} collective-permute-done((f32[80,128]{1,0:T(8,128)S(1)}, f32[80,128]{1,0:T(8,128)S(1)}, u32[]{:S(2)}, u32[]{:S(2)}) %collective-permute-start.5) | collective-permute-done | bytes 40992 | tf_op jit(solution)/shard_map/ppermute | solution.py:747
  78.9 0.4 ends.1
  79.3 13.6 %all_to_all.33 = f32[32,8,256]{2,1,0:T(8,128)S(1)} all-to-all(f32[32,8,256]{2,1,0:T(8,128)S(1)} %bitcast.27), channel_id=1, replica_groups=mesh['lat'=8,'lon_0'=4,'lon_1'=4,'lon_2'=2] {'lon_0','lon_1','lon_2'}, dimensions={0} | all-to-all | bytes 524288 | tf_op jit(solution)/shard_map/all_to_all | solution.py:742
  92.9 1.2 %last.1 = f32[256,256]{1,0:T(8,128)} custom-call(f32[256,256]{1,0:T(8,128)S(1)} %bitcast.13, f32[256,256]{1,0:T(8,128)S(1)} %get-tuple-element.55.r_2_.r_1_, f32[256,256]{1,0:T(8,128)S(1)} %get-tuple-element.69.r_2_, f32[256,256]{1,0:T(8,128)S(1)} %get-tuple-element.66.r_1_.r_3_, bf16[2,576,256]{2,1,0:T(8,128)(2,1)S(1)} %copy-done), custom_call_target="tpu_custom_call" | custom-call | tf_op jit(solution)/shard_map/last/pallas_call | solution.py:864
  94.1 3.7 %all-to-all-start.5 = ((f32[32,8,256]{2,1,0:T(8,128)}), f32[32,8,256]{2,1,0:T(8,128)S(1)}, u32[]{:S(2)}, u32[]{:S(2)}) async-start(f32[32,8,256]{2,1,0:T(8,128)} %bitcast.11), calls=%async_computation.5 | async-start | bytes 524288 | tf_op jit(solution)/shard_map/all_to_all | solution.py:742
  97.9 1.2 %collective-permute-start.8 = (f32[8,128]{1,0:T(8,128)S(1)}, f32[8,128]{1,0:T(8,128)S(1)}, u32[]{:S(2)}, u32[]{:S(2)}) collective-permute-start(f32[8,128]{1,0:T(8,128)S(1)} %gather.1.r_5_), channel_id=1, source_target_pairs={{128,0},{160,32},{192,64},{224,96},{0,128},{32,160},{64,192},{96,2... | collective-permute-start | bytes 12296 | tf_op jit(solution)/shard_map/ppermute | solution.py:747
  99.1 0.6 collective-permute-start.7
  99.8 2.9 %collective-permute-start.6 = (f32[8,128]{1,0:T(8,128)S(1)}, f32[8,128]{1,0:T(8,128)S(1)}, u32[]{:S(2)}, u32[]{:S(2)}) collective-permute-start(f32[8,128]{1,0:T(8,128)S(1)} %gather.1.r_5_), channel_id=1, source_target_pairs={{64,0},{96,32},{128,64},{160,96},{192,128},{224,160},{0,192},{32,2... | collective-permute-start | bytes 12296 | tf_op jit(solution)/shard_map/ppermute | solution.py:747
  102.7 0.1 unpack_image.1.r_2_
  102.8 1.8 %collective-permute-done.8.r_8_ = f32[8,128]{1,0:T(8,128)S(1)} collective-permute-done((f32[8,128]{1,0:T(8,128)S(1)}, f32[8,128]{1,0:T(8,128)S(1)}, u32[]{:S(2)}, u32[]{:S(2)}) %collective-permute-start.8) | collective-permute-done | bytes 4128 | tf_op jit(solution)/shard_map/ppermute | solution.py:747
  104.6 0.3 collective-permute-done.6.r_6_
  104.9 2.0 %all-to-all-done.5 = f32[32,8,256]{2,1,0:T(8,128)S(1)} async-done(((f32[32,8,256]{2,1,0:T(8,128)}), f32[32,8,256]{2,1,0:T(8,128)S(1)}, u32[]{:S(2)}, u32[]{:S(2)}) %all-to-all-start.5) | async-done | bytes 262176 | tf_op jit(solution)/shard_map/all_to_all | solution.py:742
  107.0 1.0 finish.1
  (18 shorter events, 0.1 us)
Async XLA Ops:
  1.7 17.7 %copy-start.1 = (s32[135,256]{1,0:T(8,128)S(1)}, s32[135,256]{1,0:T(8,128)}, u32[]{:S(2)}) copy-start(s32[135,256]{1,0:T(8,128)} %r_4_.2) | copy-start | bytes 414724
  1.7 17.7 %copy-start.5 = (f32[135,256]{1,0:T(8,128)S(1)}, f32[135,256]{1,0:T(8,128)}, u32[]{:S(2)}) copy-start(f32[135,256]{1,0:T(8,128)} %east_ref.1) | copy-start | bytes 414724
  1.9 17.7 %copy-start = (bf16[2,576,256]{2,1,0:T(8,128)(2,1)S(1)}, bf16[2,576,256]{2,1,0:T(8,128)(2,1)}, u32[]{:S(2)}) copy-start(bf16[2,576,256]{2,1,0:T(8,128)(2,1)} %constant.42.clone.r_2_.r_5_.r_4_) | copy-start | bytes 1769476
  20.7 3.9 %copy-start.2 = (f32[2,128,128]{2,1,0:T(8,128)S(1)}, f32[2,128,128]{2,1,0:T(8,128)}, u32[]{:S(2)}) copy-start(f32[2,128,128]{2,1,0:T(8,128)} %r_5_.2) | copy-start | bytes 393220
  20.7 3.9 %copy-start.6 = (f32[135,256]{1,0:T(8,128)S(1)}, f32[135,256]{1,0:T(8,128)}, u32[]{:S(2)}) copy-start(f32[135,256]{1,0:T(8,128)} %north_ref.1) | copy-start | bytes 414724
  20.7 14.3 %all-to-all-start.1 = ((f32[32,8,256]{2,1,0:T(8,128)}), f32[32,8,256]{2,1,0:T(8,128)S(1)}, u32[]{:S(2)}, u32[]{:S(2)}) async-start(f32[32,8,256]{2,1,0:T(8,128)} %bitcast.2), calls=%async_computation.1 | async-start | bytes 524288 | tf_op jit(solution)/shard_map/all_to_all | solution.py:742
  24.7 7.2 %collective-permute-start = (f32[8,256]{1,0:T(8,128)S(1)}, f32[8,256]{1,0:T(8,128)S(1)}, u32[]{:S(2)}, u32[]{:S(2)}) collective-permute-start(f32[8,256]{1,0:T(8,128)S(1)} %get-tuple-element.44), channel_id=1, source_target_pairs={{32,0},{64,32},{96,64},{128,96},{160,128},{192,160},{224,192},{0,2... | collective-permute-start | bytes 24584 | tf_op jit(solution)/shard_map/ppermute | solution.py:747
  30.4 4.1 %collective-permute-start.1 = (f32[80,128]{1,0:T(8,128)S(1)}, f32[80,128]{1,0:T(8,128)S(1)}, u32[]{:S(2)}, u32[]{:S(2)}) collective-permute-start(f32[80,128]{1,0:T(8,128)S(1)} %get-tuple-element.48), channel_id=1, source_target_pairs={{224,0},{0,32},{32,64},{64,96},{96,128},{128,160},{160,192},{192,2... | collective-permute-start | bytes 122888 | tf_op jit(solution)/shard_map/ppermute | solution.py:747
  31.1 0.7 copy-start.8
  31.9 3.1 %copy-start.3 = (f32[2,128,128]{2,1,0:T(8,128)S(1)}, f32[2,128,128]{2,1,0:T(8,128)}, u32[]{:S(2)}) copy-start(f32[2,128,128]{2,1,0:T(8,128)} %r_2_.2) | copy-start | bytes 393220
  35.2 5.3 %collective-permute-start.2 = (f32[80,128]{1,0:T(8,128)S(1)}, f32[80,128]{1,0:T(8,128)S(1)}, u32[]{:S(2)}, u32[]{:S(2)}) collective-permute-start(f32[80,128]{1,0:T(8,128)S(1)} %get-tuple-element.52), channel_id=1, source_target_pairs={{32,0},{64,32},{96,64},{128,96},{160,128},{192,160},{224,192},{0,2... | collective-permute-start | bytes 122888 | tf_op jit(solution)/shard_map/ppermute | solution.py:747
  39.4 4.1 %collective-permute-start.3 = (f32[80,128]{1,0:T(8,128)S(1)}, f32[80,128]{1,0:T(8,128)S(1)}, u32[]{:S(2)}, u32[]{:S(2)}) collective-permute-start(f32[80,128]{1,0:T(8,128)S(1)} %get-tuple-element.53), channel_id=1, source_target_pairs={{224,0},{0,32},{32,64},{64,96},{96,128},{128,160},{160,192},{192,2... | collective-permute-start | bytes 122888 | tf_op jit(solution)/shard_map/ppermute | solution.py:747
  43.9 16.0 %copy-start.7 = (f32[32,64]{1,0:T(8,128)S(1)}, f32[32,64]{1,0:T(8,128)}, u32[]{:S(2)}) copy-start(f32[32,64]{1,0:T(8,128)} %constant.44.clone.r_6_) | copy-start | bytes 24580
  74.6 2.9 %collective-permute-start.4 = (f32[80,128]{1,0:T(8,128)S(1)}, f32[80,128]{1,0:T(8,128)S(1)}, u32[]{:S(2)}, u32[]{:S(2)}) collective-permute-start(f32[80,128]{1,0:T(8,128)S(1)} %get-tuple-element.63), channel_id=1, source_target_pairs={{32,0},{64,32},{96,64},{128,96},{160,128},{192,160},{224,192},{0,2... | collective-permute-start | bytes 122888 | tf_op jit(solution)/shard_map/ppermute | solution.py:747
  74.7 4.1 %collective-permute-start.5 = (f32[80,128]{1,0:T(8,128)S(1)}, f32[80,128]{1,0:T(8,128)S(1)}, u32[]{:S(2)}, u32[]{:S(2)}) collective-permute-start(f32[80,128]{1,0:T(8,128)S(1)} %get-tuple-element.64), channel_id=1, source_target_pairs={{224,0},{0,32},{32,64},{64,96},{96,128},{128,160},{160,192},{192,2... | collective-permute-start | bytes 122888 | tf_op jit(solution)/shard_map/ppermute | solution.py:747
  94.1 12.8 %all-to-all-start.5 = ((f32[32,8,256]{2,1,0:T(8,128)}), f32[32,8,256]{2,1,0:T(8,128)S(1)}, u32[]{:S(2)}, u32[]{:S(2)}) async-start(f32[32,8,256]{2,1,0:T(8,128)} %bitcast.11), calls=%async_computation.5 | async-start | bytes 524288 | tf_op jit(solution)/shard_map/all_to_all | solution.py:742
  97.9 9.1 %copy-start.4 = (f32[135,256]{1,0:T(8,128)S(1)}, f32[135,256]{1,0:T(8,128)}, u32[]{:S(2)}) copy-start(f32[135,256]{1,0:T(8,128)} %r_3_.1) | copy-start | bytes 414724
  97.9 6.7 %collective-permute-start.8 = (f32[8,128]{1,0:T(8,128)S(1)}, f32[8,128]{1,0:T(8,128)S(1)}, u32[]{:S(2)}, u32[]{:S(2)}) collective-permute-start(f32[8,128]{1,0:T(8,128)S(1)} %gather.1.r_5_), channel_id=1, source_target_pairs={{128,0},{160,32},{192,64},{224,96},{0,128},{32,160},{64,192},{96,2... | collective-permute-start | bytes 12296 | tf_op jit(solution)/shard_map/ppermute | solution.py:747
  99.1 5.5 %collective-permute-start.7 = (f32[8,128]{1,0:T(8,128)S(1)}, f32[8,128]{1,0:T(8,128)S(1)}, u32[]{:S(2)}, u32[]{:S(2)}) collective-permute-start(f32[8,128]{1,0:T(8,128)S(1)} %gather.1.r_5_), channel_id=1, source_target_pairs={{192,0},{224,32},{0,64},{32,96},{64,128},{96,160},{128,192},{160,2... | collective-permute-start | bytes 12296 | tf_op jit(solution)/shard_map/ppermute | solution.py:747
  99.8 5.2 %collective-permute-start.6 = (f32[8,128]{1,0:T(8,128)S(1)}, f32[8,128]{1,0:T(8,128)S(1)}, u32[]{:S(2)}, u32[]{:S(2)}) collective-permute-start(f32[8,128]{1,0:T(8,128)S(1)} %gather.1.r_5_), channel_id=1, source_target_pairs={{64,0},{96,32},{128,64},{160,96},{192,128},{224,160},{0,192},{32,2... | collective-permute-start | bytes 12296 | tf_op jit(solution)/shard_map/ppermute | solution.py:747

commit v13 on v11

--- a/solution.py
+++ b/solution.py
@@ -308,7 +308,21 @@
     return both[:, :WIDE], both[:, WIDE:]
 
 
-def forward_kernel(groups, field_ref, rest_ref, matrix_ref, out_ref, left, right, twiddle_ref):
+def forward_kernel(
+    groups,
+    field_ref,
+    own_ref,
+    mask_ref,
+    east_ref,
+    matrix_ref,
+    out_ref,
+    left,
+    right,
+    twiddle_ref,
+    rest_ref,
+    tall,
+):
+    pack_more_kernel(own_ref, mask_ref, east_ref, rest_ref, tall)
     load_twiddle(matrix_ref, twiddle_ref)
     chunks = [field_ref[rows_of(p), :] for p in range(groups)]
     spectrum = transform(chunks, matrix_ref, twiddle_ref, left, right)
@@ -776,9 +790,8 @@
     slab = exchanged(packed)
 
     mask, east_cells = lax.optimization_barrier((ocean_mask, east_coupling, slab))[:2]
-    more = call(pack_more_kernel, wide, [wide], name="pack_more")(own_cells, mask, east_cells)
-    spectrum = call(lambda *r: forward_kernel(groups, *r), wide, transforms + turns, name="forward")(
-        slab, more, matrices
+    spectrum = call(lambda *r: forward_kernel(groups, *r), wide, transforms + turns + [wide] * 2, name="forward")(
+        slab, own_cells, mask, east_cells, matrices
     )
     spec_rhs = exchanged(spectrum)
 

time: 108 us -> 108 us (level)
  no operation moved by 1% of the time
where the time goes in v13:
time: 108 us
  blocking collectives  59.5 us (55%)
  starting transfers between devices  23.8 us (22%)
  waiting for transfers between devices  12.3 us (11%)
  Pallas kernels  8.72 us (8%)
  local copies, waits for them, and re-layouts  1.43 us (1%)
  other arithmetic  1.18 us (1%)
    all_to_all x4, blocking collectives, exchanged(): lax.all_to_all(parts, LON, split_axis=0, concat_axis=0, tiled=True)  59.5 us
    ppermute x9, starting transfers between devices, from_lat(): lax.ppermute(value, 'lat', [((d + steps) % count, d) for d in range(count)])  16.2 us
    ppermute x9, waiting for transfers between devices, from_lat(): lax.ppermute(value, 'lat', [((d + steps) % count, d) for d in range(count)])  10.3 us
    all_to_all x2, starting transfers between devices, exchanged(): lax.all_to_all(parts, LON, split_axis=0, concat_axis=0, tiled=True)  7.54 us
  transfers between devices with their start and end apart: 11, of which 8 were waited for; matrix products, arithmetic and copies ran while one was open for 1% of the time, Pallas kernels for 2%

profile of v13, /device:TPU:1, one launch (start us, length us, event | category | flops | bytes accessed | tf_op | source)
XLA Modules:
  0.0 107.8 jit_solution(2060893104742327207)
XLA Ops:
  0.6 1.1 convert_multiply_fusion
  1.7 0.0 copy-start
  1.7 0.1 pack.1
  1.9 0.0 copy-start.1
  1.9 0.0 copy-start.4
  1.9 17.5 %all_to_all.30 = f32[32,8,256]{2,1,0:T(8,128)S(1)} all-to-all(f32[32,8,256]{2,1,0:T(8,128)S(1)} %bitcast.26), channel_id=1, replica_groups=mesh['lat'=8,'lon_0'=4,'lon_1'=4,'lon_2'=2] {'lon_0','lon_1','lon_2'}, dimensions={0} | all-to-all | bytes 524288 | tf_op jit(solution)/shard_map/all_to_all | solution.py:751
  19.4 1.2 %forward.1 = f32[256,256]{1,0:T(8,128)} custom-call(f32[256,256]{1,0:T(8,128)S(1)} %bitcast.16, f32[135,256]{1,0:T(8,128)S(1)} %get-tuple-element.71.own_ref.r_1_, s32[135,256]{1,0:T(8,128)S(1)} %copy-done.1, f32[135,256]{1,0:T(8,128)S(1)} %copy-done.4, bf16[2,576,256]{2,1,0:T(8,128)(2,1)S(1)} %copy-done), custom_call_target="tpu_custom_call" | custom-call | tf_op jit(solution)/shard_map/forward/pallas_call | solution.py:793
  20.6 3.8 %all-to-all-start.1 = ((f32[32,8,256]{2,1,0:T(8,128)}), f32[32,8,256]{2,1,0:T(8,128)S(1)}, u32[]{:S(2)}, u32[]{:S(2)}) async-start(f32[32,8,256]{2,1,0:T(8,128)} %bitcast.2), calls=%async_computation.1 | async-start | bytes 524288 | tf_op jit(solution)/shard_map/all_to_all | solution.py:751
  24.4 0.1 edges.1
  24.6 5.7 %collective-permute-start = (f32[8,256]{1,0:T(8,128)S(1)}, f32[8,256]{1,0:T(8,128)S(1)}, u32[]{:S(2)}, u32[]{:S(2)}) collective-permute-start(f32[8,256]{1,0:T(8,128)S(1)} %get-tuple-element.44), channel_id=1, source_target_pairs={{32,0},{64,32},{96,64},{128,96},{160,128},{192,160},{224,192},{0,2... | collective-permute-start | bytes 24584 | tf_op jit(solution)/shard_map/ppermute | solution.py:756
  30.2 0.0 collective-permute-start.1
  30.2 0.7 constant_dynamic-slice_fusion
  30.9 0.7 copy-done.8
  31.6 0.1 add_rsqrt_fusion.scale_ref.r_2_.r_1_
  31.8 0.0 copy-start.3
  31.8 0.0 collective-permute-done.wet_above_ref
  31.8 2.5 %collective-permute-done.1.from_below_ref.r_6_.r_4_ = f32[80,128]{1,0:T(8,128)S(1)} collective-permute-done((f32[80,128]{1,0:T(8,128)S(1)}, f32[80,128]{1,0:T(8,128)S(1)}, u32[]{:S(2)}, u32[]{:S(2)}) %collective-permute-start.1) | collective-permute-done | bytes 40992 | tf_op jit(solution)/shard_map/ppermute | solution.py:756
  34.3 0.6 pack_rest.1.r_8_
  34.9 0.2 blocks.1
  35.1 4.2 %collective-permute-start.2 = (f32[80,128]{1,0:T(8,128)S(1)}, f32[80,128]{1,0:T(8,128)S(1)}, u32[]{:S(2)}, u32[]{:S(2)}) collective-permute-start(f32[80,128]{1,0:T(8,128)S(1)} %get-tuple-element.52), channel_id=1, source_target_pairs={{32,0},{64,32},{96,64},{128,96},{160,128},{192,160},{224,192},{0,2... | collective-permute-start | bytes 122888 | tf_op jit(solution)/shard_map/ppermute | solution.py:756
  39.3 0.0 collective-permute-start.3
  39.3 0.3 inner.1.r_1_
  39.6 0.5 coefficients.1
  40.2 0.2 collective-permute-done.2.r_3_
  40.4 3.0 %collective-permute-done.3.r_4_ = f32[80,128]{1,0:T(8,128)S(1)} collective-permute-done((f32[80,128]{1,0:T(8,128)S(1)}, f32[80,128]{1,0:T(8,128)S(1)}, u32[]{:S(2)}, u32[]{:S(2)}) %collective-permute-start.3) | collective-permute-done | bytes 40992 | tf_op jit(solution)/shard_map/ppermute | solution.py:756
  43.4 0.4 halo.1
  43.8 0.0 copy-start.7
  43.8 16.0 %all_to_all.31 = f32[32,8,384]{2,1,0:T(8,128)S(1)} all-to-all(f32[32,8,384]{2,1,0:T(8,128)S(1)} %bitcast.24), channel_id=1, replica_groups=mesh['lat'=8,'lon_0'=4,'lon_1'=4,'lon_2'=2] {'lon_0','lon_1','lon_2'}, dimensions={0} | all-to-all | bytes 786432 | tf_op jit(solution)/shard_map/all_to_all | solution.py:751
  59.8 1.8 %step.1 = (f32[256,256]{1,0:T(8,128)S(1)}, f32[256,256]{1,0:T(8,128)S(1)}, f32[256,256]{1,0:T(8,128)S(1)}, f32[8,128]{1,0:T(8,128)S(1)}) custom-call(f32[256,384]{1,0:T(8,128)S(1)} %bitcast.23, f32[256,256]{1,0:T(8,128)S(1)} %bitcast.18, f32[256,256]{1,0:T(8,128)S(1)} %get-tuple-element.55.r_2_.r_1_, f32[256,256]{1,0:T(8,128)S(1)} %get-tuple-element.56.r_3_, ...), custom_call_target="tpu_custom_call" | custom-call | tf_op jit(solution)/shard_map/step/pallas_call | solution.py:847
  61.7 12.3 %all_to_all.32 = f32[32,8,256]{2,1,0:T(8,128)S(1)} all-to-all(f32[32,8,256]{2,1,0:T(8,128)S(1)} %bitcast.28), channel_id=1, replica_groups=mesh['lat'=8,'lon_0'=4,'lon_1'=4,'lon_2'=2] {'lon_0','lon_1','lon_2'}, dimensions={0} | all-to-all | bytes 524288 | tf_op jit(solution)/shard_map/all_to_all | solution.py:751
  74.0 0.5 sums.1
  74.5 0.1 collective-permute-start.4
  74.6 1.5 %collective-permute-start.5 = (f32[80,128]{1,0:T(8,128)S(1)}, f32[80,128]{1,0:T(8,128)S(1)}, u32[]{:S(2)}, u32[]{:S(2)}) collective-permute-start(f32[80,128]{1,0:T(8,128)S(1)} %get-tuple-element.64), channel_id=1, source_target_pairs={{224,0},{0,32},{32,64},{64,96},{96,128},{128,160},{160,192},{192,2... | collective-permute-start | bytes 122888 | tf_op jit(solution)/shard_map/ppermute | solution.py:756
  76.1 0.2 unpack_first.1
  76.3 1.2 %collective-permute-done.4.r_3_ = f32[80,128]{1,0:T(8,128)S(1)} collective-permute-done((f32[80,128]{1,0:T(8,128)S(1)}, f32[80,128]{1,0:T(8,128)S(1)}, u32[]{:S(2)}, u32[]{:S(2)}) %collective-permute-start.4) | collective-permute-done | bytes 40992 | tf_op jit(solution)/shard_map/ppermute | solution.py:756
  77.4 1.3 %collective-permute-done.5.r_4_ = f32[80,128]{1,0:T(8,128)S(1)} collective-permute-done((f32[80,128]{1,0:T(8,128)S(1)}, f32[80,128]{1,0:T(8,128)S(1)}, u32[]{:S(2)}, u32[]{:S(2)}) %collective-permute-start.5) | collective-permute-done | bytes 40992 | tf_op jit(solution)/shard_map/ppermute | solution.py:756
  78.8 0.4 ends.1
  79.2 13.6 %all_to_all.33 = f32[32,8,256]{2,1,0:T(8,128)S(1)} all-to-all(f32[32,8,256]{2,1,0:T(8,128)S(1)} %bitcast.27), channel_id=1, replica_groups=mesh['lat'=8,'lon_0'=4,'lon_1'=4,'lon_2'=2] {'lon_0','lon_1','lon_2'}, dimensions={0} | all-to-all | bytes 524288 | tf_op jit(solution)/shard_map/all_to_all | solution.py:751
  92.8 1.2 %last.1 = f32[256,256]{1,0:T(8,128)} custom-call(f32[256,256]{1,0:T(8,128)S(1)} %bitcast.13, f32[256,256]{1,0:T(8,128)S(1)} %get-tuple-element.55.r_2_.r_1_, f32[256,256]{1,0:T(8,128)S(1)} %get-tuple-element.69.r_2_, f32[256,256]{1,0:T(8,128)S(1)} %get-tuple-element.66.r_1_.r_3_, bf16[2,576,256]{2,1,0:T(8,128)(2,1)S(1)} %copy-done), custom_call_target="tpu_custom_call" | custom-call | tf_op jit(solution)/shard_map/last/pallas_call | solution.py:872
  94.0 3.7 %all-to-all-start.5 = ((f32[32,8,256]{2,1,0:T(8,128)}), f32[32,8,256]{2,1,0:T(8,128)S(1)}, u32[]{:S(2)}, u32[]{:S(2)}) async-start(f32[32,8,256]{2,1,0:T(8,128)} %bitcast.11), calls=%async_computation.5 | async-start | bytes 524288 | tf_op jit(solution)/shard_map/all_to_all | solution.py:751
  97.8 1.3 %collective-permute-start.8 = (f32[8,128]{1,0:T(8,128)S(1)}, f32[8,128]{1,0:T(8,128)S(1)}, u32[]{:S(2)}, u32[]{:S(2)}) collective-permute-start(f32[8,128]{1,0:T(8,128)S(1)} %gather.1.r_5_), channel_id=1, source_target_pairs={{128,0},{160,32},{192,64},{224,96},{0,128},{32,160},{64,192},{96,2... | collective-permute-start | bytes 12296 | tf_op jit(solution)/shard_map/ppermute | solution.py:756
  99.0 0.6 collective-permute-start.7
  99.7 2.9 %collective-permute-start.6 = (f32[8,128]{1,0:T(8,128)S(1)}, f32[8,128]{1,0:T(8,128)S(1)}, u32[]{:S(2)}, u32[]{:S(2)}) collective-permute-start(f32[8,128]{1,0:T(8,128)S(1)} %gather.1.r_5_), channel_id=1, source_target_pairs={{64,0},{96,32},{128,64},{160,96},{192,128},{224,160},{0,192},{32,2... | collective-permute-start | bytes 12296 | tf_op jit(solution)/shard_map/ppermute | solution.py:756
  102.6 0.1 unpack_image.1.r_2_
  102.7 1.8 %collective-permute-done.8.r_8_ = f32[8,128]{1,0:T(8,128)S(1)} collective-permute-done((f32[8,128]{1,0:T(8,128)S(1)}, f32[8,128]{1,0:T(8,128)S(1)}, u32[]{:S(2)}, u32[]{:S(2)}) %collective-permute-start.8) | collective-permute-done | bytes 4128 | tf_op jit(solution)/shard_map/ppermute | solution.py:756
  104.5 0.3 collective-permute-done.6.r_6_
  104.8 2.0 %all-to-all-done.5 = f32[32,8,256]{2,1,0:T(8,128)S(1)} async-done(((f32[32,8,256]{2,1,0:T(8,128)}), f32[32,8,256]{2,1,0:T(8,128)S(1)}, u32[]{:S(2)}, u32[]{:S(2)}) %all-to-all-start.5) | async-done | bytes 262176 | tf_op jit(solution)/shard_map/all_to_all | solution.py:751
  106.8 1.0 finish.1
  (17 shorter events, 0.1 us)
Async XLA Ops:
  1.7 17.7 %copy-start = (bf16[2,576,256]{2,1,0:T(8,128)(2,1)S(1)}, bf16[2,576,256]{2,1,0:T(8,128)(2,1)}, u32[]{:S(2)}) copy-start(bf16[2,576,256]{2,1,0:T(8,128)(2,1)} %constant.42.clone.r_4_.r_5_) | copy-start | bytes 1769476
  1.9 17.5 %copy-start.1 = (s32[135,256]{1,0:T(8,128)S(1)}, s32[135,256]{1,0:T(8,128)}, u32[]{:S(2)}) copy-start(s32[135,256]{1,0:T(8,128)} %r_4_.3) | copy-start | bytes 414724
  1.9 17.5 %copy-start.4 = (f32[135,256]{1,0:T(8,128)S(1)}, f32[135,256]{1,0:T(8,128)}, u32[]{:S(2)}) copy-start(f32[135,256]{1,0:T(8,128)} %east_ref) | copy-start | bytes 414724
  20.6 3.9 %copy-start.2 = (f32[2,128,128]{2,1,0:T(8,128)S(1)}, f32[2,128,128]{2,1,0:T(8,128)}, u32[]{:S(2)}) copy-start(f32[2,128,128]{2,1,0:T(8,128)} %r_5_.2) | copy-start | bytes 393220
  20.6 3.9 %copy-start.6 = (f32[135,256]{1,0:T(8,128)S(1)}, f32[135,256]{1,0:T(8,128)}, u32[]{:S(2)}) copy-start(f32[135,256]{1,0:T(8,128)} %north_ref.1) | copy-start | bytes 414724
  20.6 14.3 %all-to-all-start.1 = ((f32[32,8,256]{2,1,0:T(8,128)}), f32[32,8,256]{2,1,0:T(8,128)S(1)}, u32[]{:S(2)}, u32[]{:S(2)}) async-start(f32[32,8,256]{2,1,0:T(8,128)} %bitcast.2), calls=%async_computation.1 | async-start | bytes 524288 | tf_op jit(solution)/shard_map/all_to_all | solution.py:751
  24.6 7.2 %collective-permute-start = (f32[8,256]{1,0:T(8,128)S(1)}, f32[8,256]{1,0:T(8,128)S(1)}, u32[]{:S(2)}, u32[]{:S(2)}) collective-permute-start(f32[8,256]{1,0:T(8,128)S(1)} %get-tuple-element.44), channel_id=1, source_target_pairs={{32,0},{64,32},{96,64},{128,96},{160,128},{192,160},{224,192},{0,2... | collective-permute-start | bytes 24584 | tf_op jit(solution)/shard_map/ppermute | solution.py:756
  30.2 4.1 %collective-permute-start.1 = (f32[80,128]{1,0:T(8,128)S(1)}, f32[80,128]{1,0:T(8,128)S(1)}, u32[]{:S(2)}, u32[]{:S(2)}) collective-permute-start(f32[80,128]{1,0:T(8,128)S(1)} %get-tuple-element.48), channel_id=1, source_target_pairs={{224,0},{0,32},{32,64},{64,96},{96,128},{128,160},{160,192},{192,2... | collective-permute-start | bytes 122888 | tf_op jit(solution)/shard_map/ppermute | solution.py:756
  30.9 0.7 copy-start.8
  31.8 3.1 %copy-start.3 = (f32[2,128,128]{2,1,0:T(8,128)S(1)}, f32[2,128,128]{2,1,0:T(8,128)}, u32[]{:S(2)}) copy-start(f32[2,128,128]{2,1,0:T(8,128)} %r_2_.2) | copy-start | bytes 393220
  35.1 5.3 %collective-permute-start.2 = (f32[80,128]{1,0:T(8,128)S(1)}, f32[80,128]{1,0:T(8,128)S(1)}, u32[]{:S(2)}, u32[]{:S(2)}) collective-permute-start(f32[80,128]{1,0:T(8,128)S(1)} %get-tuple-element.52), channel_id=1, source_target_pairs={{32,0},{64,32},{96,64},{128,96},{160,128},{192,160},{224,192},{0,2... | collective-permute-start | bytes 122888 | tf_op jit(solution)/shard_map/ppermute | solution.py:756
  39.3 4.1 %collective-permute-start.3 = (f32[80,128]{1,0:T(8,128)S(1)}, f32[80,128]{1,0:T(8,128)S(1)}, u32[]{:S(2)}, u32[]{:S(2)}) collective-permute-start(f32[80,128]{1,0:T(8,128)S(1)} %get-tuple-element.53), channel_id=1, source_target_pairs={{224,0},{0,32},{32,64},{64,96},{96,128},{128,160},{160,192},{192,2... | collective-permute-start | bytes 122888 | tf_op jit(solution)/shard_map/ppermute | solution.py:756
  43.8 16.0 %copy-start.7 = (f32[32,64]{1,0:T(8,128)S(1)}, f32[32,64]{1,0:T(8,128)}, u32[]{:S(2)}) copy-start(f32[32,64]{1,0:T(8,128)} %constant.44.clone.r_6_) | copy-start | bytes 24580
  74.5 2.9 %collective-permute-start.4 = (f32[80,128]{1,0:T(8,128)S(1)}, f32[80,128]{1,0:T(8,128)S(1)}, u32[]{:S(2)}, u32[]{:S(2)}) collective-permute-start(f32[80,128]{1,0:T(8,128)S(1)} %get-tuple-element.63), channel_id=1, source_target_pairs={{32,0},{64,32},{96,64},{128,96},{160,128},{192,160},{224,192},{0,2... | collective-permute-start | bytes 122888 | tf_op jit(solution)/shard_map/ppermute | solution.py:756
  74.6 4.1 %collective-permute-start.5 = (f32[80,128]{1,0:T(8,128)S(1)}, f32[80,128]{1,0:T(8,128)S(1)}, u32[]{:S(2)}, u32[]{:S(2)}) collective-permute-start(f32[80,128]{1,0:T(8,128)S(1)} %get-tuple-element.64), channel_id=1, source_target_pairs={{224,0},{0,32},{32,64},{64,96},{96,128},{128,160},{160,192},{192,2... | collective-permute-start | bytes 122888 | tf_op jit(solution)/shard_map/ppermute | solution.py:756
  94.0 12.8 %all-to-all-start.5 = ((f32[32,8,256]{2,1,0:T(8,128)}), f32[32,8,256]{2,1,0:T(8,128)S(1)}, u32[]{:S(2)}, u32[]{:S(2)}) async-start(f32[32,8,256]{2,1,0:T(8,128)} %bitcast.11), calls=%async_computation.5 | async-start | bytes 524288 | tf_op jit(solution)/shard_map/all_to_all | solution.py:751
  97.8 9.1 %copy-start.5 = (f32[135,256]{1,0:T(8,128)S(1)}, f32[135,256]{1,0:T(8,128)}, u32[]{:S(2)}) copy-start(f32[135,256]{1,0:T(8,128)} %r_3_.2) | copy-start | bytes 414724
  97.8 6.7 %collective-permute-start.8 = (f32[8,128]{1,0:T(8,128)S(1)}, f32[8,128]{1,0:T(8,128)S(1)}, u32[]{:S(2)}, u32[]{:S(2)}) collective-permute-start(f32[8,128]{1,0:T(8,128)S(1)} %gather.1.r_5_), channel_id=1, source_target_pairs={{128,0},{160,32},{192,64},{224,96},{0,128},{32,160},{64,192},{96,2... | collective-permute-start | bytes 12296 | tf_op jit(solution)/shard_map/ppermute | solution.py:756
  99.0 5.5 %collective-permute-start.7 = (f32[8,128]{1,0:T(8,128)S(1)}, f32[8,128]{1,0:T(8,128)S(1)}, u32[]{:S(2)}, u32[]{:S(2)}) collective-permute-start(f32[8,128]{1,0:T(8,128)S(1)} %gather.1.r_5_), channel_id=1, source_target_pairs={{192,0},{224,32},{0,64},{32,96},{64,128},{96,160},{128,192},{160,2... | collective-permute-start | bytes 12296 | tf_op jit(solution)/shard_map/ppermute | solution.py:756
  99.7 5.1 %collective-permute-start.6 = (f32[8,128]{1,0:T(8,128)S(1)}, f32[8,128]{1,0:T(8,128)S(1)}, u32[]{:S(2)}, u32[]{:S(2)}) collective-permute-start(f32[8,128]{1,0:T(8,128)S(1)} %gather.1.r_5_), channel_id=1, source_target_pairs={{64,0},{96,32},{128,64},{160,96},{192,128},{224,160},{0,192},{32,2... | collective-permute-start | bytes 12296 | tf_op jit(solution)/shard_map/ppermute | solution.py:756
